TPU v7x, 32 devices: a whole 2x2x4 slice. The times are simulated.
32 devices in a mesh: rows: 4 (over y, x), seq: 8 (over z, core).
Axes of the slice: x: 2, y: 2, z: 4, core: 2. Of those that a mesh axis runs over, the one named last changes fastest.
Arguments:
- layer_input: bfloat16 [8, 512, 2048], P('rows', 'seq')
- output_gradient: bfloat16 [8, 512, 2048], P('rows', 'seq')
- norm_gain_vectors: float32 [2, 2048], replicated, may hold values from 0.1 to 1.9
- query_output_frozen: bfloat16 [2, 2048, 2048], P(None, 'seq'), may hold values from -0.125 to 0.125
- key_value_frozen: bfloat16 [2, 2048, 512], P(None, 'seq'), may hold values from -0.125 to 0.125
- gate_up_frozen: bfloat16 [2, 2048, 8192], P(None, 'seq'), may hold values from -0.125 to 0.125
- down_frozen_weight: bfloat16 [8192, 2048], P('seq'), may hold values from -0.0625 to 0.0625
- attention_adapter_a: float32 [4, 16, 2048], replicated, may hold values from -0.125 to 0.125
- query_output_adapter_b: float32 [2, 16, 2048], replicated, may hold values from -0.3125 to 0.3125
- key_value_adapter_b: float32 [2, 16, 512], replicated, may hold values from -0.3125 to 0.3125
- query_magnitude: float32 [2048], replicated, may hold values from 0.8 to 1.6
- key_value_magnitude: float32 [2, 512], replicated, may hold values from 0.8 to 1.6
- output_magnitude: float32 [2048], replicated, may hold values from 3 to 12
- gate_up_adapter_a: float32 [2, 16, 2048], replicated, may hold values from -0.125 to 0.125
- gate_up_adapter_b: float32 [2, 16, 8192], replicated, may hold values from -0.3125 to 0.3125
- gate_up_magnitude: float32 [2, 8192], replicated, may hold values from 0.6 to 1.8
- down_adapter_a: float32 [16, 8192], replicated, may hold values from -0.0625 to 0.0625
- down_adapter_b: float32 [16, 2048], replicated, may hold values from -0.3125 to 0.3125
- down_magnitude: float32 [2048], replicated, may hold values from 0.7 to 2.5
- prompt_length_list: int32 [4], P('rows'), may hold values from 64 to 256, as said below
- response_length_list: int32 [8], P('rows'), may hold values from 1 to 448
Outputs:
- out: bfloat16 [8, 512, 2048], P('rows', 'seq')
- grad_x: float32 [8, 512, 2048], P('rows', 'seq')
- grad_attn_lora_a: float32 [4, 16, 2048], replicated
- grad_query_out_lora_b: float32 [2, 16, 2048], replicated
- grad_key_value_lora_b: float32 [2, 16, 512], replicated
- grad_query_mag: float32 [2048], replicated
- grad_key_value_mag: float32 [2, 512], replicated
- grad_out_mag: float32 [2048], replicated
- grad_gate_up_lora_a: float32 [2, 16, 2048], replicated
- grad_gate_up_lora_b: float32 [2, 16, 8192], replicated
- grad_gate_up_mag: float32 [2, 8192], replicated
- grad_down_lora_a: float32 [16, 8192], replicated
- grad_down_lora_b: float32 [16, 2048], replicated
- grad_down_mag: float32 [2048], replicated
- stats: float32 [7, 2], replicated
Inputs may be any that keep to these rules, and one draw needn't show every extreme that they name: prompt_length_list[p] + response_length_list[r] <= 512 for both rows r = 2 p and 2 p + 1 of pair p, and row 0 fills all 512 positions.
All inputs are finite; a program needn't handle non-finite values.
Results may differ from a plain program's by a relative error of at most 0.023.
Values may be sent and summed in bfloat16 or wider, within the bound.
A program may use at most 384 MiB of HBM per device.

v0:
```python
import jax
import jax.numpy as jnp
from jax import lax
from jax.sharding import PartitionSpec as P

HEADS = 32
KV_HEADS = 8
HEAD_DIM = 64
ADAPTER_RANK = 16
ALPHA = 32


highest = lax.Precision.HIGHEST
last_last = (((1,), (1,)), ((), ()))
first_first = (((0,), (0,)), ((), ()))


def rms_scale(values, gain):
    inverse = lax.rsqrt(jnp.mean(values * values, axis=-1, keepdims=True) + 1e-05)
    return values * inverse * gain


def rotate(values, positions, direction_sign):
    half_dim = values.shape[-1] // 2
    frequency = 500000.0 ** (-(jnp.arange(half_dim, dtype=jnp.float32) * 2.0) / values.shape[-1])
    angles = positions.astype(jnp.float32)[:, None] * frequency[None, :]
    cosine = jnp.cos(angles)[:, None, :]
    sine_part = direction_sign * jnp.sin(angles)[:, None, :]
    first_half = values[..., :half_dim]
    second_half = values[..., half_dim:]
    return jnp.concatenate(
        [
            first_half * cosine - second_half * sine_part,
            second_half * cosine + first_half * sine_part,
        ],
        axis=-1,
    )


def prepare_weights(merged_weight, adapter_factor_a, adapter_factor_b):
    scale = ALPHA / ADAPTER_RANK
    down_factor_a = adapter_factor_a.astype(jnp.bfloat16)
    down_factor_b = adapter_factor_b.astype(jnp.bfloat16)
    a_wide = down_factor_a.astype(jnp.float32)
    b_wide = down_factor_b.astype(jnp.float32)
    cross = jnp.dot(down_factor_a, merged_weight, preferred_element_type=jnp.float32)
    gram = jnp.dot(a_wide, a_wide.T, precision=highest)
    squares = jnp.sum(jnp.square(merged_weight.astype(jnp.float32)), axis=0)
    squares = squares + 2.0 * scale * jnp.sum(b_wide * cross, axis=0)
    squares = squares + scale * scale * jnp.sum(
        b_wide * jnp.dot(gram, b_wide, precision=highest), axis=0
    )
    norms = jnp.sqrt(squares + 1e-06)
    return (down_factor_a, down_factor_b, cross, gram, norms)


def project(input_rows, merged_weight, prepared, magnitude_vector):
    down_factor_a, down_factor_b, cross, gram, norms = prepared
    base_out = jnp.dot(input_rows, merged_weight, preferred_element_type=jnp.float32)
    inner_low = lax.dot_general(
        input_rows, down_factor_a, last_last, preferred_element_type=jnp.float32
    ).astype(jnp.bfloat16)
    before = base_out + ALPHA / ADAPTER_RANK * jnp.dot(
        inner_low, down_factor_b, preferred_element_type=jnp.float32
    )
    return (before * (magnitude_vector / norms), before, inner_low)


def project_back(
    upstream, input_rows, merged_weight, prepared, magnitude_vector, before, inner_low
):
    down_factor_a, down_factor_b, cross, gram, norms = prepared
    scale = ALPHA / ADAPTER_RANK
    grad_before = (upstream * (magnitude_vector / norms)).astype(jnp.bfloat16)
    grad_inner = (
        scale
        * lax.dot_general(grad_before, down_factor_b, last_last, preferred_element_type=jnp.float32)
    ).astype(jnp.bfloat16)
    grad_inputs = lax.dot_general(
        grad_before, merged_weight, last_last, preferred_element_type=jnp.float32
    )
    grad_inputs = grad_inputs + jnp.dot(
        grad_inner, down_factor_a, preferred_element_type=jnp.float32
    )
    grad_mag = jnp.sum(upstream * before, axis=0) / norms
    column = -grad_mag * magnitude_vector / (norms * norms)
    a_wide = down_factor_a.astype(jnp.float32)
    b_wide = down_factor_b.astype(jnp.float32)
    weighted = b_wide * column
    upper_part = weighted.astype(jnp.bfloat16)
    lower_part = (weighted - upper_part.astype(jnp.float32)).astype(jnp.bfloat16)
    spread = lax.dot_general(
        upper_part, merged_weight, last_last, preferred_element_type=jnp.float32
    )
    spread = spread + lax.dot_general(
        lower_part, merged_weight, last_last, preferred_element_type=jnp.float32
    )
    spread = spread + scale * jnp.dot(
        jnp.dot(weighted, b_wide.T, precision=highest), a_wide, precision=highest
    )
    grad_a = (
        lax.dot_general(grad_inner, input_rows, first_first, preferred_element_type=jnp.float32)
        + scale * spread
    )
    grad_b = scale * lax.dot_general(
        inner_low, grad_before, first_first, preferred_element_type=jnp.float32
    )
    grad_b = grad_b + scale * (cross + scale * jnp.dot(gram, b_wide, precision=highest)) * column
    return (grad_inputs, grad_a, grad_b, grad_mag)


def to_heads(flat, pair_rows, span_len, group_count, ratio, head_dim):
    shaped = flat.reshape(pair_rows, span_len, group_count, ratio, head_dim)
    return shaped.transpose(2, 0, 3, 1, 4).reshape(
        group_count, pair_rows, ratio * span_len, head_dim
    )


def from_heads(stacked, pair_rows, span_len, group_count, ratio, head_dim):
    shaped = stacked.reshape(group_count, pair_rows, ratio, span_len, head_dim)
    return shaped.transpose(1, 3, 0, 2, 4).reshape(
        pair_rows * span_len, group_count * ratio * head_dim
    )


def keys_to_heads(whole, group_count, head_dim):
    pair_rows, length_all, _ = whole.shape
    return whole.reshape(pair_rows, length_all, group_count, head_dim).transpose(2, 0, 1, 3)


def keys_from_heads(stacked):
    group_count, pair_rows, length_all, head_dim = stacked.shape
    return stacked.transpose(1, 2, 0, 3).reshape(pair_rows, length_all, group_count * head_dim)


def score_block(head_q, head_k, row_pos, key_pos, valid_len):
    scores = jnp.einsum(
        "rqd,rkd->rqk", head_q, head_k, preferred_element_type=jnp.float32
    ) * head_q.shape[-1] ** (-0.5)
    allowed = (key_pos[None, None, :] <= row_pos[None, :, None]) & (
        key_pos[None, None, :] < valid_len[:, None, None]
    )
    return (scores, allowed)


def drift_stats(magnitude_vector, norms):
    drift = jnp.sqrt(jnp.mean(jnp.square(magnitude_vector - norms))) / jnp.sqrt(
        jnp.mean(jnp.square(magnitude_vector)) + 1e-06
    )
    return jnp.stack([drift, jnp.mean(norms)])


def local(
    layer_input,
    output_gradient,
    norm_gain_vectors,
    query_output_frozen,
    key_value_frozen,
    gate_up_frozen,
    down_frozen_weight,
    attention_adapter_a,
    query_output_adapter_b,
    key_value_adapter_b,
    query_magnitude,
    key_value_magnitude,
    output_magnitude,
    gate_up_adapter_a,
    gate_up_adapter_b,
    gate_up_magnitude,
    down_adapter_a,
    down_adapter_b,
    down_magnitude,
    prompt_length_list,
    response_length_list,
):
    pair_rows, span_len, model_width = layer_input.shape
    token_count = pair_rows * span_len
    head_count = HEADS
    group_count = KV_HEADS
    head_dim = HEAD_DIM
    ratio = head_count // group_count
    kv_width = group_count * head_dim
    collected_query_output, collected_key_value, collected_feedfwd, collected_down = (
        lax.all_gather(query_output_frozen, "seq", axis=1, tiled=True),
        lax.all_gather(key_value_frozen, "seq", axis=1, tiled=True),
        lax.all_gather(gate_up_frozen, "seq", axis=1, tiled=True),
        lax.all_gather(down_frozen_weight, "seq", axis=0, tiled=True),
    )
    query_components = prepare_weights(
        collected_query_output[0], attention_adapter_a[0], query_output_adapter_b[0]
    )
    key_components = prepare_weights(
        collected_key_value[0], attention_adapter_a[1], key_value_adapter_b[0]
    )
    value_components = prepare_weights(
        collected_key_value[1], attention_adapter_a[2], key_value_adapter_b[1]
    )
    output_components = prepare_weights(
        collected_query_output[1], attention_adapter_a[3], query_output_adapter_b[1]
    )
    gate_components = prepare_weights(
        collected_feedfwd[0], gate_up_adapter_a[0], gate_up_adapter_b[0]
    )
    lift_components = prepare_weights(
        collected_feedfwd[1], gate_up_adapter_a[1], gate_up_adapter_b[1]
    )
    down_components = prepare_weights(collected_down, down_adapter_a, down_adapter_b)
    seq_index = lax.axis_index("seq")
    query_pos = seq_index * span_len + jnp.arange(span_len, dtype=jnp.int32)
    positions = jnp.tile(query_pos, pair_rows)
    row_pos = jnp.tile(query_pos, ratio)
    key_pos = jnp.arange(span_len * lax.axis_size("seq"), dtype=jnp.int32)
    valid_len = prompt_length_list[0] + response_length_list
    token_rows = layer_input.reshape(token_count, model_width).astype(jnp.float32)
    first_input = rms_scale(token_rows, norm_gain_vectors[0]).astype(jnp.bfloat16)
    query_unnormed, query_before, query_inner = project(
        first_input, collected_query_output[0], query_components, query_magnitude
    )
    key_unnormed, key_before, key_inner = project(
        first_input, collected_key_value[0], key_components, key_value_magnitude[0]
    )
    value_unnormed, value_before, value_inner = project(
        first_input, collected_key_value[1], value_components, key_value_magnitude[1]
    )
    queries = rotate(
        query_unnormed.reshape(token_count, head_count, head_dim), positions, 1.0
    ).astype(jnp.bfloat16)
    key_rows = rotate(
        key_unnormed.reshape(token_count, group_count, head_dim), positions, 1.0
    ).astype(jnp.bfloat16)
    keys_local = key_rows.reshape(pair_rows, span_len, kv_width)
    values_local = value_unnormed.astype(jnp.bfloat16).reshape(pair_rows, span_len, kv_width)
    keys_all, values_all = (
        lax.all_gather(keys_local, "seq", axis=1, tiled=True),
        lax.all_gather(values_local, "seq", axis=1, tiled=True),
    )
    query_heads = to_heads(
        queries.reshape(token_count, model_width), pair_rows, span_len, group_count, ratio, head_dim
    )
    key_heads = keys_to_heads(keys_all, group_count, head_dim)
    value_heads = keys_to_heads(values_all, group_count, head_dim)

    def forward_head(operands):
        head_q, head_k, head_v = operands
        scores, allowed = score_block(head_q, head_k, row_pos, key_pos, valid_len)
        masked = jnp.where(allowed, scores, -1e30)
        row_max = jnp.max(masked, axis=-1, keepdims=True)
        unscaled = jnp.exp(masked - row_max)
        row_total = jnp.sum(unscaled, axis=-1, keepdims=True)
        shares = unscaled / row_total
        mixed_out = jnp.einsum(
            "rqk,rkd->rqd", shares.astype(jnp.bfloat16), head_v, preferred_element_type=jnp.float32
        )
        return (mixed_out, (row_max + jnp.log(row_total))[..., 0])

    mixed_heads, log_totals = lax.map(forward_head, (query_heads, key_heads, value_heads))
    attention_result = from_heads(
        mixed_heads, pair_rows, span_len, group_count, ratio, head_dim
    ).astype(jnp.bfloat16)
    out_raw, out_before, out_inner = project(
        attention_result, collected_query_output[1], output_components, output_magnitude
    )
    residual_stream = token_rows + out_raw
    second_input = rms_scale(residual_stream, norm_gain_vectors[1]).astype(jnp.bfloat16)
    gate_output, gate_before, gate_inner = project(
        second_input, collected_feedfwd[0], gate_components, gate_up_magnitude[0]
    )
    lift_output, lift_before, lift_inner = project(
        second_input, collected_feedfwd[1], lift_components, gate_up_magnitude[1]
    )
    hidden_rows = (jax.nn.sigmoid(gate_output) * gate_output * lift_output).astype(jnp.bfloat16)
    down_raw, down_before, down_inner = project(
        hidden_rows, collected_down, down_components, down_magnitude
    )
    layer_result = (
        (residual_stream + down_raw).astype(jnp.bfloat16).reshape(pair_rows, span_len, model_width)
    )
    back_qo, back_kv, back_ff, back_down = (
        lax.all_gather(query_output_frozen, "seq", axis=1, tiled=True),
        lax.all_gather(key_value_frozen, "seq", axis=1, tiled=True),
        lax.all_gather(gate_up_frozen, "seq", axis=1, tiled=True),
        lax.all_gather(down_frozen_weight, "seq", axis=0, tiled=True),
    )
    keys_back, values_back = (
        lax.all_gather(keys_local, "seq", axis=1, tiled=True),
        lax.all_gather(values_local, "seq", axis=1, tiled=True),
    )
    key_heads_back = keys_to_heads(keys_back, group_count, head_dim)
    value_heads_back = keys_to_heads(values_back, group_count, head_dim)
    upstream = output_gradient.reshape(token_count, model_width).astype(jnp.float32)
    grad_hidden, grad_a_down, grad_b_down, grad_m_down = project_back(
        upstream, hidden_rows, back_down, down_components, down_magnitude, down_before, down_inner
    )
    _, swish_pull = jax.vjp(
        lambda gate_in, lift_in: jax.nn.sigmoid(gate_in) * gate_in * lift_in,
        gate_output,
        lift_output,
    )
    grad_gate, grad_lift = swish_pull(grad_hidden)
    gate_in_grad, grad_a_gate, grad_b_gate, grad_m_gate = project_back(
        grad_gate,
        second_input,
        back_ff[0],
        gate_components,
        gate_up_magnitude[0],
        gate_before,
        gate_inner,
    )
    lift_in_grad, grad_a_lift, grad_b_lift, grad_m_lift = project_back(
        grad_lift,
        second_input,
        back_ff[1],
        lift_components,
        gate_up_magnitude[1],
        lift_before,
        lift_inner,
    )
    _, second_pull = jax.vjp(
        lambda values: rms_scale(values, norm_gain_vectors[1]), residual_stream
    )
    grad_residual = upstream + second_pull(gate_in_grad + lift_in_grad)[0]
    grad_attended, grad_a_out, grad_b_out, grad_m_out = project_back(
        grad_residual,
        attention_result,
        back_qo[1],
        output_components,
        output_magnitude,
        out_before,
        out_inner,
    )
    grad_att_heads = to_heads(
        grad_attended.astype(jnp.bfloat16), pair_rows, span_len, group_count, ratio, head_dim
    )
    scale_factor = head_dim ** (-0.5)

    def backward_head(operands):
        head_q, head_k, head_v, head_lse, head_grad = operands
        scores, allowed = score_block(head_q, head_k, row_pos, key_pos, valid_len)
        shares = jnp.where(allowed, jnp.exp(scores - head_lse[..., None]), 0.0)
        grad_shares = jnp.einsum(
            "rqd,rkd->rqk", head_grad, head_v, preferred_element_type=jnp.float32
        )
        centre = jnp.sum(shares * grad_shares, axis=-1, keepdims=True)
        grad_scores = (shares * (grad_shares - centre)).astype(jnp.bfloat16)
        grad_q = (
            jnp.einsum("rqk,rkd->rqd", grad_scores, head_k, preferred_element_type=jnp.float32)
            * scale_factor
        )
        grad_k = (
            jnp.einsum("rqk,rqd->rkd", grad_scores, head_q, preferred_element_type=jnp.float32)
            * scale_factor
        )
        grad_v = jnp.einsum(
            "rqk,rqd->rkd",
            shares.astype(jnp.bfloat16),
            head_grad,
            preferred_element_type=jnp.float32,
        )
        return (grad_q, grad_k, grad_v)

    grad_q_heads, grad_k_heads, grad_v_heads = lax.map(
        backward_head, (query_heads, key_heads_back, value_heads_back, log_totals, grad_att_heads)
    )
    key_grads, value_grads = (
        lax.psum_scatter(
            keys_from_heads(grad_k_heads).astype(jnp.bfloat16),
            "seq",
            scatter_dimension=1,
            tiled=True,
        ).astype(jnp.float32),
        lax.psum_scatter(
            keys_from_heads(grad_v_heads).astype(jnp.bfloat16),
            "seq",
            scatter_dimension=1,
            tiled=True,
        ).astype(jnp.float32),
    )
    grad_query = from_heads(grad_q_heads, pair_rows, span_len, group_count, ratio, head_dim)
    grad_query = (
        grad_query.astype(jnp.bfloat16)
        .astype(jnp.float32)
        .reshape(token_count, head_count, head_dim)
    )
    grad_query = rotate(grad_query, positions, -1.0).reshape(token_count, model_width)
    grad_key = (
        key_grads.reshape(token_count, group_count, head_dim)
        .astype(jnp.bfloat16)
        .astype(jnp.float32)
    )
    grad_key = rotate(grad_key, positions, -1.0).reshape(token_count, kv_width)
    grad_value = value_grads.reshape(token_count, kv_width).astype(jnp.bfloat16).astype(jnp.float32)
    query_in_grad, grad_a_query, grad_b_query, grad_m_query = project_back(
        grad_query,
        first_input,
        back_qo[0],
        query_components,
        query_magnitude,
        query_before,
        query_inner,
    )
    key_in_grad, grad_a_key, grad_b_key, grad_m_key = project_back(
        grad_key,
        first_input,
        back_kv[0],
        key_components,
        key_value_magnitude[0],
        key_before,
        key_inner,
    )
    value_in_grad, grad_a_value, grad_b_value, grad_m_value = project_back(
        grad_value,
        first_input,
        back_kv[1],
        value_components,
        key_value_magnitude[1],
        value_before,
        value_inner,
    )
    _, first_pull = jax.vjp(lambda values: rms_scale(values, norm_gain_vectors[0]), token_rows)
    grad_inputs = grad_residual + first_pull(query_in_grad + key_in_grad + value_in_grad)[0]
    grad_inputs = grad_inputs.reshape(pair_rows, span_len, model_width)
    summed = lax.psum(
        (
            jnp.stack([grad_a_query, grad_a_key, grad_a_value, grad_a_out]),
            jnp.stack([grad_b_query, grad_b_out]),
            jnp.stack([grad_b_key, grad_b_value]),
            grad_m_query,
            jnp.stack([grad_m_key, grad_m_value]),
            grad_m_out,
            jnp.stack([grad_a_gate, grad_a_lift]),
            jnp.stack([grad_b_gate, grad_b_lift]),
            jnp.stack([grad_m_gate, grad_m_lift]),
            grad_a_down,
            grad_b_down,
            grad_m_down,
        ),
        ("rows", "seq"),
    )
    stats = jnp.stack(
        [
            drift_stats(query_magnitude, query_components[4]),
            drift_stats(key_value_magnitude[0], key_components[4]),
            drift_stats(key_value_magnitude[1], value_components[4]),
            drift_stats(output_magnitude, output_components[4]),
            drift_stats(gate_up_magnitude[0], gate_components[4]),
            drift_stats(gate_up_magnitude[1], lift_components[4]),
            drift_stats(down_magnitude, down_components[4]),
        ]
    )
    return (
        layer_result,
        grad_inputs,
        summed[0],
        summed[1],
        summed[2],
        summed[3],
        summed[4],
        summed[5],
        summed[6],
        summed[7],
        summed[8],
        summed[9],
        summed[10],
        summed[11],
        stats,
    )


def solution(mesh):
    return jax.shard_map(
        local,
        mesh=mesh,
        in_specs=(
            P("rows", "seq", None),
            P("rows", "seq", None),
            P(),
            P(None, "seq", None),
            P(None, "seq", None),
            P(None, "seq", None),
            P("seq", None),
            P(),
            P(),
            P(),
            P(),
            P(),
            P(),
            P(),
            P(),
            P(),
            P(),
            P(),
            P(),
            P("rows"),
            P("rows"),
        ),
        out_specs=(
            P("rows", "seq", None),
            P("rows", "seq", None),
            P(),
            P(),
            P(),
            P(),
            P(),
            P(),
            P(),
            P(),
            P(),
            P(),
            P(),
            P(),
            P(),
        ),
        check_vma=False,
    )
```

profile of v0, /device:TPU:0, one launch (start us, length us, event | category | flops | bytes accessed | tf_op | source)
XLA Modules:
  0.0 1713.6 jit_solution(3727778190780617007)
XLA Ops:
  16.5 42.8 %all-gather.9.cloned.1.call-done = bf16[2,2048,512]{2,1,0:T(8,128)(2,1)} async-done(((bf16[2,256,512]{2,1,0:T(8,128)(2,1)}), bf16[2,2048,512]{2,1,0:T(8,128)(2,1)}) %all-gather.9.cloned.1.call-update) | async-done | bytes 4194320 | tf_op jit(solution)/shard_map/all_gather | solution.py:185
  59.3 3.2 multiply_reduce_fusion.8
  87.7 5.3 all-gather.11.cloned.1.call-done
  96.8 20.1 %all-gather.13.cloned.1.call-done = bf16[2,512,512]{2,0,1:T(2,128)(2,1)} async-done(((bf16[2,64,512]{2,0,1:T(2,128)(2,1)}), bf16[2,512,512]{2,0,1:T(2,128)(2,1)}) %all-gather.13.cloned.1.call-update) | async-done | bytes 1048592 | tf_op jit(solution)/shard_map/all_gather | solution.py:235
  116.9 3.7 copy.129
  122.8 146.3 %all-gather.7.cloned.1.call-done = bf16[2,2048,2048]{2,1,0:T(8,128)(2,1)} async-done(((bf16[2,256,2048]{2,1,0:T(8,128)(2,1)}), bf16[2,2048,2048]{2,1,0:T(8,128)(2,1)}) %all-gather.7.cloned.1.call-update) | async-done | bytes 16777232 | tf_op jit(solution)/shard_map/all_gather | solution.py:184
  269.1 5.2 fusion.188
  274.3 10.0 multiply_reduce_fusion.4
  285.0 5.6 copy-done
  294.7 262.7 %all-gather.17.cloned.1.call-done = bf16[8192,2048]{1,0:T(8,128)(2,1)} async-done(((bf16[1024,2048]{1,0:T(8,128)(2,1)}), bf16[8192,2048]{1,0:T(8,128)(2,1)}) %all-gather.17.cloned.1.call-update) | async-done | bytes 33554448 | tf_op jit(solution)/shard_map/all_gather | solution.py:187
  557.4 19.0 %multiply_reduce_fusion.1 = f32[2048]{0:T(1024)S(1)} fusion(bf16[8192,2048]{1,0:T(8,128)(2,1)} %all-gather.17.cloned.1.call-done), kind=kLoop, calls=%fused_computation.63 | loop fusion | flops 50329600 | bytes 33562624 | tf_op jit(solution)/shard_map/reduce_sum | solution.py:48
  576.5 18.3 %fusion.191 = (f32[2048]{0:T(1024)S(1)}, f32[2048]{0:T(1024)S(1)}, f32[16,2048]{1,0:T(8,128)}) fusion(bf16[16,2048]{1,0:T(8,128)(2,1)S(1)} %convert_element_type.646, f32[16,2048]{1,0:T(8,128)S(1)} %fusion.292, bf16[16,8192]{1,0:T(8,128)(2,1)S(1)} %convert_element_type.644, bf16[8192,2048]{1,0:T(8,128)(2,1)} %all-gather.17.cloned.1.call-done), kind=kOutput, calls=%fused_computation.330 | convolution fusion | flops 537030656 | bytes 34160640 | tf_op jit(solution)/shard_map/dot_general | solution.py:46
  610.0 29.6 %while.30 = (s32[]{:T(128)}, bf16[8,2,256,64]{2,3,1,0:T(8,128)(2,1)}, f32[8,2,256]{2,1,0:T(2,128)}, s32[2]{0:T(128)S(1)}, bf16[8,2,256,64]{2,3,1,0:T(8,128)(2,1)...) while((s32[]{:T(128)}, ...), condition=%wide.region_13.0_spmd.clone.clone, body=%wide.region_10.13_spmd.clone.clone.sunk | while | flops 69599744 | bytes 3892593 | solution.py:256
  639.6 3.0 convert_element_type.618
  642.6 3.4 copy.132
  648.8 4.8 fusion.82
  657.0 16.2 fusion.293
  675.9 445.1 %all-gather.15.cloned.1.call-done = bf16[2,2048,8192]{2,1,0:T(8,128)(2,1)} async-done(((bf16[2,256,8192]{2,1,0:T(8,128)(2,1)}), bf16[2,2048,8192]{2,1,0:T(8,128)(2,1)}) %all-gather.15.cloned.1.call-update) | async-done | bytes 67108880 | tf_op jit(solution)/shard_map/all_gather | solution.py:186
  1121.1 21.8 %multiply_reduce_fusion.3 = (f32[8192]{0:T(1024)S(1)}, f32[8192]{0:T(1024)S(1)}) fusion(bf16[2,2048,8192]{2,1,0:T(8,128)(2,1)} %all-gather.15.cloned.1.call-done), kind=kLoop, calls=%fused_computation.65 | loop fusion | flops 100646912 | bytes 67174400 | tf_op jit(solution)/shard_map/reduce_sum | solution.py:48
  1142.9 14.2 fusion.147
  1157.1 13.9 fusion.145
  1171.8 15.0 fusion.60
  1186.8 4.9 fusion.62
  1191.8 15.0 fusion.55
  1206.9 6.9 multiply_reduce_fusion.7
  1221.7 16.5 fusion.53
  1240.7 16.6 fusion.58
  1259.4 13.3 fusion.290
  1276.4 6.3 fusion.80
  1292.2 84.6 %while.31 = (s32[]{:T(128)}, bf16[8,2,256,64]{2,3,1,0:T(8,128)(2,1)}, bf16[8,2,512,64]{2,3,0,1:T(8,128)(2,1)}, bf16[8,2,512,64]{2,3,0,1:T(8,128)(2,1)}, s32[2]{0...) while((s32[]{:T(128)}, ...), condition=%wide.region_30.31_spmd.clone.clone, body=%wide.region_28.30_spmd.clone.clone.sunk | while | flops 170623488 | bytes 9459081 | solution.py:361
  1376.9 3.0 reshape.1143
  1379.9 4.6 copy.221
  1384.4 3.4 reshape.1132
  1391.3 4.1 copy.138
  1395.4 3.7 copy.143
  1406.8 14.5 fusion.56
  1421.4 14.6 fusion.117
  1437.1 14.5 fusion.51
  1451.6 14.6 fusion.118
  1468.7 6.3 fusion.75
  1476.6 5.6 fusion.78
  1482.3 5.7 fusion.115
  1488.3 5.7 fusion.73
  1494.2 5.9 fusion.116
  1505.4 14.9 fusion.228
  1520.4 14.8 convolution_add_fusion.1
  1570.7 40.9 %all-reduce.2 = (f32[2048]{0:T(1024)}, f32[2,512]{1,0:T(2,128)}, f32[2048]{0:T(1024)}, f32[2048]{0:T(1024)}) all-reduce(f32[2048]{0:T(1024)S(1)} %copy-done.163, f32[2,512]{1,0:T(2,128)S(1)} %pad_maximum_fusion.9, f32[2048]{0:T(1024)S(1)} %copy-done.162, f32[2048]{0:T(1024)S(1)} %copy-done.164), channel_id=1, replica_groups=mesh['rows'=4,'seq'=8] {'rows','seq'}, use_global_device_ids=true, to_apply=%region_41.42 | all-reduce | flops 7168 | bytes 57344 | tf_op jit(solution)/shard_map/psum | solution.py:422
  1611.6 83.7 %all-reduce.8.cloned.1.call-done = (f32[4,16,2048]{2,1,0:T(8,128)}, f32[2,16,2048]{2,1,0:T(8,128)}, f32[2,16,512]{2,1,0:T(8,128)}, f32[2,16,2048]{2,1,0:T(8,128)...) async-done(((f32[4,16,2048]{2,1,0:T(8,128)}, f32[2,16,2048]{2,1,0:T(8,128)}, f32[2,16,512]{2,1,0:T(8,128)}, ...) | async-done | bytes 2883600 | tf_op jit(solution)/shard_map/psum | solution.py:422
  (744 shorter events, 261.9 us)
Async XLA Ops:
  7.2 52.1 %all-gather.9.cloned.1.call-start = ((), (), s32[]{:S(2)}) async-start(), calls=%async_computation.1 | async-start | bytes 4718592 | tf_op jit(solution)/shard_map/all_gather | solution.py:185
  7.9 85.1 %all-gather.11.cloned.1.call-start = ((), (), s32[]{:S(2)}) async-start(), calls=%async_computation.2 | async-start | bytes 1179648 | tf_op jit(solution)/shard_map/all_gather | solution.py:234
  11.4 590.2 %copy-start.79 = (f32[128,32]{0,1:T(8,128)}, f32[128,32]{0,1:T(8,128)S(1)}, u32[]{:S(2)}) copy-start(f32[128,32]{0,1:T(8,128)S(1)} %get-tuple-element.546) | copy-start | bytes 49156
  12.2 51.5 %copy-start.59 = (bf16[1,16,512]{2,1,0:T(8,128)(2,1)}, bf16[1,16,512]{2,1,0:T(8,128)(2,1)S(1)}, u32[]{:S(2)}) copy-start(bf16[1,16,512]{2,1,0:T(8,128)(2,1)S(1)} %get-tuple-element.526) | copy-start | bytes 49156
  12.2 59.8 %copy-start.61 = (bf16[1,16,512]{2,1,0:T(8,128)(2,1)}, bf16[1,16,512]{2,1,0:T(8,128)(2,1)S(1)}, u32[]{:S(2)}) copy-start(bf16[1,16,512]{2,1,0:T(8,128)(2,1)S(1)} %get-tuple-element.525) | copy-start | bytes 49156
  13.3 50.4 %copy-start.49 = (bf16[16,2048]{1,0:T(8,128)(2,1)}, bf16[16,2048]{1,0:T(8,128)(2,1)S(1)}, u32[]{:S(2)}) copy-start(bf16[16,2048]{1,0:T(8,128)(2,1)S(1)} %get-tuple-element.504) | copy-start | bytes 196612
  13.3 58.4 %copy-start.42 = (bf16[16,2048]{1,0:T(8,128)(2,1)}, bf16[16,2048]{1,0:T(8,128)(2,1)S(1)}, u32[]{:S(2)}) copy-start(bf16[16,2048]{1,0:T(8,128)(2,1)S(1)} %get-tuple-element.506) | copy-start | bytes 196612
  13.4 271.6 %copy-start.44 = (bf16[16,2048]{1,0:T(8,128)(2,1)}, bf16[16,2048]{1,0:T(8,128)(2,1)S(1)}, u32[]{:S(2)}) copy-start(bf16[16,2048]{1,0:T(8,128)(2,1)S(1)} %get-tuple-element.505) | copy-start | bytes 196612
  13.4 635.1 %copy-start.46 = (bf16[16,2048]{1,0:T(8,128)(2,1)}, bf16[16,2048]{1,0:T(8,128)(2,1)S(1)}, u32[]{:S(2)}) copy-start(bf16[16,2048]{1,0:T(8,128)(2,1)S(1)} %get-tuple-element.503) | copy-start | bytes 196612
  13.7 50.1 %copy-start.82 = (f32[16,512]{1,0:T(8,128)}, f32[16,512]{1,0:T(8,128)S(1)}, u32[]{:S(2)}) copy-start(f32[16,512]{1,0:T(8,128)S(1)} %fusion.256) | copy-start | bytes 98308
  14.0 49.8 %copy-start.84 = (f32[16,512]{1,0:T(8,128)}, f32[16,512]{1,0:T(8,128)S(1)}, u32[]{:S(2)}) copy-start(f32[16,512]{1,0:T(8,128)S(1)} %fusion.261) | copy-start | bytes 98308
  14.8 49.0 %copy-start.94 = (f32[1,2048]{1,0:T(1,128)}, f32[1,2048]{1,0:T(1,128)S(1)}, u32[]{:S(2)}) copy-start(f32[1,2048]{1,0:T(1,128)S(1)} %get-tuple-element.532) | copy-start | bytes 24580
  16.3 48.5 %copy-start.132 = (bf16[128,16]{0,1:T(8,128)(2,1)}, bf16[128,16]{0,1:T(8,128)(2,1)S(1)}, u32[]{:S(2)}) copy-start(bf16[128,16]{0,1:T(8,128)(2,1)S(1)} %convolution_convert_fusion.5) | copy-start | bytes 12292
  16.5 50.6 %copy-start.148 = (f32[2,512]{1,0:T(2,128)S(1)}, f32[2,512]{1,0:T(2,128)}, u32[]{:S(2)}) copy-start(f32[2,512]{1,0:T(2,128)} %param.36) | copy-start | bytes 12292
  71.7 45.1 %all-gather.13.cloned.1.call-start = ((), (), s32[]{:S(2)}) async-start(), calls=%async_computation.3 | async-start | bytes 1179648 | tf_op jit(solution)/shard_map/all_gather | solution.py:235
  75.8 193.2 %all-gather.7.cloned.1.call-start = ((), (), s32[]{:S(2)}) async-start(), calls=%async_computation | async-start | bytes 18874368 | tf_op jit(solution)/shard_map/all_gather | solution.py:184
  76.4 481.0 %all-gather.17.cloned.1.call-start = ((), (), s32[]{:S(2)}) async-start(), calls=%async_computation.5 | async-start | bytes 37748736 | tf_op jit(solution)/shard_map/all_gather | solution.py:187
  77.1 1044.0 %all-gather.15.cloned.1.call-start = ((), (), s32[]{:S(2)}) async-start(), calls=%async_computation.4 | async-start | bytes 75497472 | tf_op jit(solution)/shard_map/all_gather | solution.py:186
  77.7 1462.0 %all-reduce.10.cloned.1.call-start = ((), (), s32[]{:S(2)}) async-start(), calls=%async_computation.7 | async-start | bytes 4194304
  78.4 577.5 %copy-start.20 = (bf16[16,2048]{1,0:T(8,128)(2,1)}, bf16[16,2048]{1,0:T(8,128)(2,1)S(1)}, u32[]{:S(2)}) copy-start(bf16[16,2048]{1,0:T(8,128)(2,1)S(1)} %convert_element_type.646) | copy-start | bytes 196612
  78.5 1139.6 %copy-start.3 = (bf16[16,8192]{1,0:T(8,128)(2,1)}, bf16[16,8192]{1,0:T(8,128)(2,1)S(1)}, u32[]{:S(2)}) copy-start(bf16[16,8192]{1,0:T(8,128)(2,1)S(1)} %convert_element_type.644) | copy-start | bytes 786436
  81.3 1156.9 %copy-start.38 = (bf16[16,2048]{1,0:T(8,128)(2,1)}, bf16[16,2048]{1,0:T(8,128)(2,1)S(1)}, u32[]{:S(2)}) copy-start(bf16[16,2048]{1,0:T(8,128)(2,1)S(1)} %get-tuple-element.513) | copy-start | bytes 196612
  81.3 1176.0 %copy-start.40 = (bf16[16,2048]{1,0:T(8,128)(2,1)}, bf16[16,2048]{1,0:T(8,128)(2,1)S(1)}, u32[]{:S(2)}) copy-start(bf16[16,2048]{1,0:T(8,128)(2,1)S(1)} %get-tuple-element.514) | copy-start | bytes 196612
  81.7 514.5 %copy-start.24 = (bf16[1,16,2048]{2,1,0:T(8,128)(2,1)}, bf16[1,16,2048]{2,1,0:T(8,128)(2,1)S(1)}, u32[]{:S(2)}) copy-start(bf16[1,16,2048]{2,1,0:T(8,128)(2,1)S(1)} %get-tuple-element.516) | copy-start | bytes 196612
  81.7 571.9 %copy-start.22 = (bf16[1,16,2048]{2,1,0:T(8,128)(2,1)}, bf16[1,16,2048]{2,1,0:T(8,128)(2,1)S(1)}, u32[]{:S(2)}) copy-start(bf16[1,16,2048]{2,1,0:T(8,128)(2,1)S(1)} %get-tuple-element.515) | copy-start | bytes 196612
  81.9 187.2 %copy-start.67 = (f32[16,2048]{1,0:T(8,128)}, f32[16,2048]{1,0:T(8,128)S(1)}, u32[]{:S(2)}) copy-start(f32[16,2048]{1,0:T(8,128)S(1)} %fusion.217) | copy-start | bytes 393220
  82.3 494.1 %copy-start.63 = (f32[16,2048]{1,0:T(8,128)}, f32[16,2048]{1,0:T(8,128)S(1)}, u32[]{:S(2)}) copy-start(f32[16,2048]{1,0:T(8,128)S(1)} %fusion.292) | copy-start | bytes 393220
  82.6 202.4 %copy-start.65 = (f32[16,2048]{1,0:T(8,128)}, f32[16,2048]{1,0:T(8,128)S(1)}, u32[]{:S(2)}) copy-start(f32[16,2048]{1,0:T(8,128)S(1)} %fusion.222) | copy-start | bytes 393220
  82.8 513.4 %copy-start.136 = (bf16[128,16]{0,1:T(8,128)(2,1)}, bf16[128,16]{0,1:T(8,128)(2,1)S(1)}, u32[]{:S(2)}) copy-start(bf16[128,16]{0,1:T(8,128)(2,1)S(1)} %convolution_convert_fusion.6) | copy-start | bytes 12292
  84.1 1132.4 %copy-start.9 = (bf16[1,16,8192]{2,1,0:T(8,128)(2,1)}, bf16[1,16,8192]{2,1,0:T(8,128)(2,1)S(1)}, u32[]{:S(2)}) copy-start(bf16[1,16,8192]{2,1,0:T(8,128)(2,1)S(1)} %get-tuple-element.497) | copy-start | bytes 786436
  274.3 16.3 copy-start
  290.6 363.0 %copy-start.112 = (f32[2048]{0:T(1024)}, f32[2048]{0:T(1024)S(1)}, u32[]{:S(2)}) copy-start(f32[2048]{0:T(1024)S(1)} %div.227) | copy-start | bytes 24580
  576.4 18.3 %copy-start.120 = (f32[2048]{0:T(1024)S(1)}, f32[2048]{0:T(1024)}, u32[]{:S(2)}) copy-start(f32[2048]{0:T(1024)} %param.35) | copy-start | bytes 24580
  576.5 18.3 %copy-start.121 = (f32[2048]{0:T(1024)S(1)}, f32[2048]{0:T(1024)}, u32[]{:S(2)}) copy-start(f32[2048]{0:T(1024)} %param.43) | copy-start | bytes 24580
  595.5 53.0 %copy-start.123 = (f32[2048]{0:T(1024)}, f32[2048]{0:T(1024)S(1)}, u32[]{:S(2)}) copy-start(f32[2048]{0:T(1024)S(1)} %get-tuple-element.450) | copy-start | bytes 24580
  655.2 536.6 %copy-start.7 = (bf16[128,2048]{1,0:T(8,128)(2,1)}, bf16[128,2048]{1,0:T(8,128)(2,1)S(1)}, u32[]{:S(2)}) copy-start(bf16[128,2048]{1,0:T(8,128)(2,1)S(1)} %multiply_convert_fusion.7) | copy-start | bytes 1572868
  655.5 531.3 %copy-start.150 = (bf16[128,16]{0,1:T(8,128)(2,1)}, bf16[128,16]{0,1:T(8,128)(2,1)S(1)}, u32[]{:S(2)}) copy-start(bf16[128,16]{0,1:T(8,128)(2,1)S(1)} %convolution_convert_fusion.1) | copy-start | bytes 12292
  655.7 551.1 %copy-start.174 = (bf16[128,16]{0,1:T(8,128)(2,1)}, bf16[128,16]{0,1:T(8,128)(2,1)S(1)}, u32[]{:S(2)}) copy-start(bf16[128,16]{0,1:T(8,128)(2,1)S(1)} %convolution_convert_fusion.2) | copy-start | bytes 12292
  675.9 466.9 %copy-start.30 = (f32[16,8192]{1,0:T(8,128)S(1)}, f32[16,8192]{1,0:T(8,128)}, u32[]{:S(2)}) copy-start(f32[16,8192]{1,0:T(8,128)} %fusion.169) | copy-start | bytes 1572868
  1213.8 27.0 %copy-start.18 = (bf16[128,8192]{1,0:T(8,128)(2,1)}, bf16[128,8192]{1,0:T(8,128)(2,1)S(1)}, u32[]{:S(2)}) copy-start(bf16[128,8192]{1,0:T(8,128)(2,1)S(1)} %get-tuple-element.485) | copy-start | bytes 6291460
  1218.8 54.0 %copy-start.140 = (bf16[128,16]{0,1:T(8,128)(2,1)}, bf16[128,16]{0,1:T(8,128)(2,1)S(1)}, u32[]{:S(2)}) copy-start(bf16[128,16]{0,1:T(8,128)(2,1)S(1)} %convolution_convert_fusion) | copy-start | bytes 12292
  1221.0 17.2 %copy-start.146 = (bf16[128,16]{0,1:T(8,128)(2,1)}, bf16[128,16]{0,1:T(8,128)(2,1)S(1)}, u32[]{:S(2)}) copy-start(bf16[128,16]{0,1:T(8,128)(2,1)S(1)} %fusion.126) | copy-start | bytes 12292
  1221.7 35.7 %copy-start.152 = (bf16[128,16]{0,1:T(8,128)(2,1)}, bf16[128,16]{0,1:T(8,128)(2,1)S(1)}, u32[]{:S(2)}) copy-start(bf16[128,16]{0,1:T(8,128)(2,1)S(1)} %fusion.127) | copy-start | bytes 12292
  1451.6 17.1 copy-start.58
  1476.4 219.0 %all-reduce.8.cloned.1.call-start = ((), (), s32[]{:S(2)}) async-start(), calls=%async_computation.6 | async-start | bytes 5767168 | tf_op jit(solution)/shard_map/psum | solution.py:422
  1552.2 18.5 %copy-start.162 = (f32[2048]{0:T(1024)S(1)}, f32[2048]{0:T(1024)}, u32[]{:S(2)}) copy-start(f32[2048]{0:T(1024)} %get-tuple-element.470) | copy-start | bytes 24580
  1552.2 18.5 %copy-start.163 = (f32[2048]{0:T(1024)S(1)}, f32[2048]{0:T(1024)}, u32[]{:S(2)}) copy-start(f32[2048]{0:T(1024)} %get-tuple-element.467) | copy-start | bytes 24580
  1552.2 18.5 %copy-start.164 = (f32[2048]{0:T(1024)S(1)}, f32[2048]{0:T(1024)}, u32[]{:S(2)}) copy-start(f32[2048]{0:T(1024)} %get-tuple-element.459) | copy-start | bytes 24580
  (145 other events, 1049.4 us)
Sparse Core Ops, SparseCore 0:
  9.6 49.6 all-gather.8
  71.9 21.1 all-gather.10
  95.2 21.6 all-gather.12
  118.3 150.7 all-gather.6
  270.5 286.8 all-gather.16
  558.9 562.1 all-gather.14
  1476.5 63.0 all-reduce.9
  1555.4 139.9 all-reduce.7
where the time goes:
time: 1720 us; the launch traced here: 1710 us
  waiting for transfers between devices  1010 us (59%)
  matrix products  428 us (25%)
  local copies, waits for them, and re-layouts  101 us (6%)
  other arithmetic  100 us (6%)
  blocking collectives  40.9 us (2%)
  between operations  31.6 us (2%)
    all_gather x1, waiting for transfers between devices, local(): lax.all_gather(gate_up_frozen, 'seq', axis=1, tiled=True)  445 us
    all_gather x1, waiting for transfers between devices, local(): lax.all_gather(down_frozen_weight, 'seq', axis=0, tiled=True)  263 us
    all_gather x1, waiting for transfers between devices, local(): lax.all_gather(query_output_frozen, 'seq', axis=1, tiled=True)  146 us
    psum x1, waiting for transfers between devices, local(): lax.psum((jnp.stack([grad_a_query, grad_a_key, grad_a_value, grad_a_out])...  83.7 us
    dot_general x7, matrix products, project_back(): lax.dot_general(grad_before, merged_weight, last_last, preferred_element_...  65.6 us
    dot_general x7, matrix products, project_back(): lax.dot_general(upper_part, merged_weight, last_last, preferred_element_t...  57 us
    dot_general x7, matrix products, project_back(): lax.dot_general(lower_part, merged_weight, last_last, preferred_element_t...  56.4 us
    dot_general x7, matrix products, project(): jnp.dot(input_rows, merged_weight, preferred_element_type=jnp.float32)  55.9 us
  transfers between devices with their start and end apart: 8, of which 8 were waited for; matrix products, arithmetic and copies ran while one was open for 13% of the time, Pallas kernels for 0%

commit v1 on v0

v1 whole, which is shorter than its diff:
```python
import jax
import jax.numpy as jnp
from jax import lax
from jax.sharding import PartitionSpec as P

HEADS = 32
KV_HEADS = 8
HEAD_DIM = 64
ADAPTER_RANK = 16
ALPHA = 32


highest = lax.Precision.HIGHEST
last_last = (((1,), (1,)), ((), ()))
first_first = (((0,), (0,)), ((), ()))


def rms_scale(values, gain):
    inverse = lax.rsqrt(jnp.mean(values * values, axis=-1, keepdims=True) + 1e-05)
    return values * inverse * gain


def rotate(values, positions, direction_sign):
    half_dim = values.shape[-1] // 2
    frequency = 500000.0 ** (-(jnp.arange(half_dim, dtype=jnp.float32) * 2.0) / values.shape[-1])
    angles = positions.astype(jnp.float32)[:, None] * frequency[None, :]
    cosine = jnp.cos(angles)[:, None, :]
    sine_part = direction_sign * jnp.sin(angles)[:, None, :]
    first_half = values[..., :half_dim]
    second_half = values[..., half_dim:]
    return jnp.concatenate(
        [
            first_half * cosine - second_half * sine_part,
            second_half * cosine + first_half * sine_part,
        ],
        axis=-1,
    )


SCALE = ALPHA / ADAPTER_RANK


def dot_f32(a, b):
    return jnp.dot(a, b, preferred_element_type=jnp.float32)


def dot_nt(a, b):
    return lax.dot_general(a, b, last_last, preferred_element_type=jnp.float32)


def dot_tn(a, b):
    return lax.dot_general(a, b, first_first, preferred_element_type=jnp.float32)


def block_rows(blocks):
    total = sum(b.shape[1] for b in blocks)
    rows, start = [], 0
    for b in blocks:
        rows.append(jnp.pad(b, ((0, 0), (start, total - start - b.shape[1]))))
        start += b.shape[1]
    return jnp.concatenate(rows, axis=0)


def square_terms(weight, a_low, b_low):
    cross = dot_f32(a_low, weight)
    squares = jnp.sum(jnp.square(weight.astype(jnp.float32)), axis=0)
    return squares + 2.0 * SCALE * jnp.sum(b_low.astype(jnp.float32) * cross, axis=0), cross


def gram_times_b(a_low, b_low):
    a_wide = a_low.astype(jnp.float32)
    return jnp.dot(
        jnp.dot(a_wide, a_wide.T, precision=highest), b_low.astype(jnp.float32), precision=highest
    )


def project(rows, weight, a_low, b_low):
    base = dot_f32(rows, weight)
    inner = dot_nt(rows, a_low).astype(jnp.bfloat16)
    return base + SCALE * dot_f32(inner, b_low), inner


def back_low(grad_before, a_low, b_low):
    return (SCALE * dot_nt(grad_before, b_low)).astype(jnp.bfloat16)


def spread_term(weight, a_low, b_low, column):
    b_wide = b_low.astype(jnp.float32)
    weighted = b_wide * column
    upper = weighted.astype(jnp.bfloat16)
    lower = (weighted - upper.astype(jnp.float32)).astype(jnp.bfloat16)
    rank = b_low.shape[0]
    both = dot_nt(jnp.concatenate([upper, lower], axis=0), weight)
    inner = jnp.dot(weighted, b_wide.T, precision=highest)
    return (
        both[:rank]
        + both[rank:]
        + SCALE * jnp.dot(inner, a_low.astype(jnp.float32), precision=highest)
    )

def to_heads(flat, pair_rows, span_len, group_count, ratio, head_dim):
    shaped = flat.reshape(pair_rows, span_len, group_count, ratio, head_dim)
    return shaped.transpose(2, 0, 3, 1, 4).reshape(
        group_count, pair_rows, ratio * span_len, head_dim
    )


def from_heads(stacked, pair_rows, span_len, group_count, ratio, head_dim):
    shaped = stacked.reshape(group_count, pair_rows, ratio, span_len, head_dim)
    return shaped.transpose(1, 3, 0, 2, 4).reshape(
        pair_rows * span_len, group_count * ratio * head_dim
    )


def keys_to_heads(whole, group_count, head_dim):
    pair_rows, length_all, _ = whole.shape
    return whole.reshape(pair_rows, length_all, group_count, head_dim).transpose(2, 0, 1, 3)


def keys_from_heads(stacked):
    group_count, pair_rows, length_all, head_dim = stacked.shape
    return stacked.transpose(1, 2, 0, 3).reshape(pair_rows, length_all, group_count * head_dim)


def score_block(head_q, head_k, row_pos, key_pos, valid_len):
    scores = jnp.einsum(
        "rqd,rkd->rqk", head_q, head_k, preferred_element_type=jnp.float32
    ) * head_q.shape[-1] ** (-0.5)
    allowed = (key_pos[None, None, :] <= row_pos[None, :, None]) & (
        key_pos[None, None, :] < valid_len[:, None, None]
    )
    return (scores, allowed)


def drift_stats(magnitude_vector, norms):
    drift = jnp.sqrt(jnp.mean(jnp.square(magnitude_vector - norms))) / jnp.sqrt(
        jnp.mean(jnp.square(magnitude_vector)) + 1e-06
    )
    return jnp.stack([drift, jnp.mean(norms)])


def local(
    layer_input,
    output_gradient,
    norm_gain_vectors,
    query_output_frozen,
    key_value_frozen,
    gate_up_frozen,
    down_frozen_weight,
    attention_adapter_a,
    query_output_adapter_b,
    key_value_adapter_b,
    query_magnitude,
    key_value_magnitude,
    output_magnitude,
    gate_up_adapter_a,
    gate_up_adapter_b,
    gate_up_magnitude,
    down_adapter_a,
    down_adapter_b,
    down_magnitude,
    prompt_length_list,
    response_length_list,
):
    pair_rows, span_len, model_width = layer_input.shape
    token_count = pair_rows * span_len
    head_count, group_count, head_dim = HEADS, KV_HEADS, HEAD_DIM
    ratio = head_count // group_count
    kv_width = group_count * head_dim
    seq_size = lax.axis_size("seq")
    seq_index = lax.axis_index("seq")
    first_member = (seq_index == 0).astype(jnp.float32)
    low = jnp.bfloat16
    rank = ADAPTER_RANK

    qkv_local = jnp.concatenate(
        [query_output_frozen[0], key_value_frozen[0], key_value_frozen[1]], axis=1
    )
    weight_qkv = lax.all_gather(qkv_local, "seq", axis=0, tiled=True)
    weight_o = lax.all_gather(query_output_frozen[1], "seq", axis=0, tiled=True)
    weight_gu = lax.all_to_all(gate_up_frozen, "seq", split_axis=2, concat_axis=1, tiled=True)
    weight_d = down_frozen_weight
    slice_units = weight_d.shape[0]

    a_qkv = attention_adapter_a[:3].reshape(3 * rank, model_width).astype(low)
    b_qkv = block_rows(
        [query_output_adapter_b[0], key_value_adapter_b[0], key_value_adapter_b[1]]
    ).astype(low)
    m_qkv = jnp.concatenate([query_magnitude, key_value_magnitude[0], key_value_magnitude[1]])
    a_o = attention_adapter_a[3].astype(low)
    b_o = query_output_adapter_b[1].astype(low)
    a_gu = gate_up_adapter_a.astype(low)
    start = seq_index * slice_units
    b_gu = lax.dynamic_slice_in_dim(gate_up_adapter_b, start, slice_units, 2).astype(low)
    m_gu = lax.dynamic_slice_in_dim(gate_up_magnitude, start, slice_units, 1)
    a_d = down_adapter_a.astype(low)
    a_d_local = lax.dynamic_slice_in_dim(a_d, start, slice_units, 1)
    b_d = down_adapter_b.astype(low)

    def norms_of(squares, a_low, b_low):
        b_wide = b_low.astype(jnp.float32)
        gram_b = gram_times_b(a_low, b_low)
        return jnp.sqrt(squares + SCALE * SCALE * jnp.sum(b_wide * gram_b, axis=0) + 1e-06), gram_b

    sq_d, cross_d = square_terms(weight_d, a_d_local, b_d)
    sq_d = lax.psum(sq_d, "seq")
    n_d, gram_d = norms_of(sq_d, a_d, b_d)
    ratio_d = down_magnitude / n_d

    sq_qkv, cross_qkv = square_terms(weight_qkv, a_qkv, b_qkv)
    n_qkv, gram_qkv = norms_of(sq_qkv, a_qkv, b_qkv)
    ratio_qkv = m_qkv / n_qkv
    sq_o, cross_o = square_terms(weight_o, a_o, b_o)
    n_o, gram_o = norms_of(sq_o, a_o, b_o)
    ratio_o = output_magnitude / n_o

    query_pos = seq_index * span_len + jnp.arange(span_len, dtype=jnp.int32)
    positions = jnp.tile(query_pos, pair_rows)
    row_pos = jnp.tile(query_pos, ratio)
    key_pos = jnp.arange(span_len * seq_size, dtype=jnp.int32)
    valid_len = prompt_length_list[0] + response_length_list

    token_rows = layer_input.reshape(token_count, model_width).astype(jnp.float32)
    first_input = rms_scale(token_rows, norm_gain_vectors[0]).astype(low)
    before_qkv, inner_qkv = project(first_input, weight_qkv, a_qkv, b_qkv)
    qkv = before_qkv * ratio_qkv
    q_flat = qkv[:, :model_width]
    k_flat = qkv[:, model_width : model_width + kv_width]
    v_flat = qkv[:, model_width + kv_width :]
    queries = rotate(q_flat.reshape(token_count, head_count, head_dim), positions, 1.0).astype(low)
    key_rows = rotate(k_flat.reshape(token_count, group_count, head_dim), positions, 1.0).astype(
        low
    )
    keys_values = jnp.concatenate(
        [key_rows.reshape(token_count, kv_width), v_flat.astype(low)], axis=1
    ).reshape(pair_rows, span_len, 2 * kv_width)
    kv_all = lax.all_gather(keys_values, "seq", axis=1, tiled=True)
    query_heads = to_heads(
        queries.reshape(token_count, model_width), pair_rows, span_len, group_count, ratio, head_dim
    )
    key_heads = keys_to_heads(kv_all[..., :kv_width], group_count, head_dim)
    value_heads = keys_to_heads(kv_all[..., kv_width:], group_count, head_dim)

    def forward_head(operands):
        head_q, head_k, head_v = operands
        scores, allowed = score_block(head_q, head_k, row_pos, key_pos, valid_len)
        masked = jnp.where(allowed, scores, -1e30)
        row_max = jnp.max(masked, axis=-1, keepdims=True)
        unscaled = jnp.exp(masked - row_max)
        row_total = jnp.sum(unscaled, axis=-1, keepdims=True)
        shares = unscaled / row_total
        mixed_out = jnp.einsum(
            "rqk,rkd->rqd", shares.astype(jnp.bfloat16), head_v, preferred_element_type=jnp.float32
        )
        return (mixed_out, (row_max + jnp.log(row_total))[..., 0])

    mixed_heads, log_totals = lax.map(forward_head, (query_heads, key_heads, value_heads))
    attended = from_heads(
        mixed_heads, pair_rows, span_len, group_count, ratio, head_dim
    ).astype(low)
    before_o, inner_o = project(attended, weight_o, a_o, b_o)
    residual = token_rows + before_o * ratio_o
    second_input = rms_scale(residual, norm_gain_vectors[1]).astype(low)

    u2 = lax.all_gather(second_input, "seq", axis=0, tiled=True)
    grad_out_rows = output_gradient.reshape(token_count, model_width)
    gy_all = lax.all_gather(grad_out_rows, "seq", axis=0, tiled=True)
    gb_d = (gy_all.astype(jnp.float32) * ratio_d).astype(low)
    gi_d = back_low(gb_d, a_d, b_d)
    grad_hidden = dot_nt(gb_d, weight_d) + dot_f32(gi_d, a_d_local)

    branch = []
    for i in range(2):
        sq, cross = square_terms(weight_gu[i], a_gu[i], b_gu[i])
        norm, gram_b = norms_of(sq, a_gu[i], b_gu[i])
        before, inner = project(u2, weight_gu[i], a_gu[i], b_gu[i])
        branch.append((norm, gram_b, cross, m_gu[i] / norm, before, inner))
    gate = branch[0][4] * branch[0][3]
    lift = branch[1][4] * branch[1][3]
    sig = jax.nn.sigmoid(gate)
    silu = sig * gate
    hidden = (silu * lift).astype(low)
    down_partial = dot_f32(hidden, weight_d)
    inner_d_partial = dot_nt(hidden, a_d_local)
    down_sum = lax.psum_scatter(down_partial.astype(low), "seq", scatter_dimension=0, tiled=True)
    inner_d = lax.psum_scatter(inner_d_partial, "seq", scatter_dimension=0, tiled=True).astype(low)
    before_d = down_sum.astype(jnp.float32) + SCALE * dot_f32(inner_d, b_d)
    layer_result = (residual + before_d * ratio_d).astype(low)

    grad_rows = grad_out_rows.astype(jnp.float32)
    gm_d = jnp.sum(grad_rows * before_d, axis=0) / n_d
    gm_d_line = lax.psum(gm_d, "seq")
    c_d = -gm_d_line * down_magnitude / (n_d * n_d)
    gb_d_own = (grad_rows * ratio_d).astype(low)
    spread_d = spread_term(weight_d, jnp.zeros_like(a_d_local), b_d, c_d)
    weighted_d = b_d.astype(jnp.float32) * c_d
    spread_d = spread_d + SCALE * jnp.dot(
        jnp.dot(weighted_d, b_d.astype(jnp.float32).T, precision=highest),
        a_d_local.astype(jnp.float32),
        precision=highest,
    )
    ga_d = dot_tn(gi_d, hidden) + SCALE * spread_d
    gB_d = SCALE * dot_tn(inner_d, gb_d_own) + SCALE * c_d * (
        cross_d + first_member * SCALE * gram_d
    )

    ggate = grad_hidden * lift * sig * (1.0 + gate * (1.0 - sig))
    glift = grad_hidden * silu
    grad_in = None
    ga_gu, gB_gu, gm_gu = [], [], []
    for i, g in enumerate((ggate, glift)):
        norm, gram_b, cross, rat, before, inner = branch[i]
        gb = (g * rat).astype(low)
        gi = back_low(gb, a_gu[i], b_gu[i])
        term = dot_nt(gb, weight_gu[i])
        gm = jnp.sum(g * before, axis=0) / norm
        c = -gm * m_gu[i] / (norm * norm)
        grad_in = term if grad_in is None else grad_in + term
        low_term = dot_f32(gi, a_gu[i])
        grad_in = grad_in + low_term
        ga_gu.append(dot_tn(gi, u2) + SCALE * spread_term(weight_gu[i], a_gu[i], b_gu[i], c))
        gB_gu.append(SCALE * dot_tn(inner, gb) + SCALE * c * (cross + SCALE * gram_b))
        gm_gu.append(gm)
    in_grad = lax.psum_scatter(grad_in.astype(low), "seq", scatter_dimension=0, tiled=True)
    _, second_pull = jax.vjp(lambda v: rms_scale(v, norm_gain_vectors[1]), residual)
    grad_residual = grad_rows + second_pull(in_grad.astype(jnp.float32))[0]

    def back_full(upstream, rows, weight, a_low, b_low, ratio_p, norm, magnitude, before, inner, cross, gram_b):
        gb = (upstream * ratio_p).astype(low)
        gi = back_low(gb, a_low, b_low)
        grad_rows_in = dot_nt(gb, weight) + dot_f32(gi, a_low)
        gm = jnp.sum(upstream * before, axis=0) / norm
        c = -gm * magnitude / (norm * norm)
        ga = dot_tn(gi, rows) + SCALE * spread_term(weight, a_low, b_low, c)
        gB = SCALE * dot_tn(inner, gb) + SCALE * c * (cross + SCALE * gram_b)
        return grad_rows_in, ga, gB, gm

    grad_att, ga_o, gB_o, gm_o = back_full(
        grad_residual, attended, weight_o, a_o, b_o, ratio_o, n_o, output_magnitude,
        before_o, inner_o, cross_o, gram_o,
    )
    grad_att_heads = to_heads(
        grad_att.astype(low), pair_rows, span_len, group_count, ratio, head_dim
    )
    scale_factor = head_dim ** (-0.5)

    def backward_head(operands):
        head_q, head_k, head_v, head_lse, head_grad = operands
        scores, allowed = score_block(head_q, head_k, row_pos, key_pos, valid_len)
        shares = jnp.where(allowed, jnp.exp(scores - head_lse[..., None]), 0.0)
        grad_shares = jnp.einsum(
            "rqd,rkd->rqk", head_grad, head_v, preferred_element_type=jnp.float32
        )
        centre = jnp.sum(shares * grad_shares, axis=-1, keepdims=True)
        grad_scores = (shares * (grad_shares - centre)).astype(jnp.bfloat16)
        grad_q = (
            jnp.einsum("rqk,rkd->rqd", grad_scores, head_k, preferred_element_type=jnp.float32)
            * scale_factor
        )
        grad_k = (
            jnp.einsum("rqk,rqd->rkd", grad_scores, head_q, preferred_element_type=jnp.float32)
            * scale_factor
        )
        grad_v = jnp.einsum(
            "rqk,rqd->rkd",
            shares.astype(jnp.bfloat16),
            head_grad,
            preferred_element_type=jnp.float32,
        )
        return (grad_q, grad_k, grad_v)

    grad_q_heads, grad_k_heads, grad_v_heads = lax.map(
        backward_head, (query_heads, key_heads, value_heads, log_totals, grad_att_heads)
    )
    kv_grads = jnp.concatenate(
        [keys_from_heads(grad_k_heads).astype(low), keys_from_heads(grad_v_heads).astype(low)],
        axis=2,
    )
    kv_grads = lax.psum_scatter(kv_grads, "seq", scatter_dimension=1, tiled=True)
    kv_grads = kv_grads.reshape(token_count, 2 * kv_width).astype(jnp.float32)
    grad_query = from_heads(grad_q_heads, pair_rows, span_len, group_count, ratio, head_dim)
    grad_query = (
        grad_query.astype(low).astype(jnp.float32).reshape(token_count, head_count, head_dim)
    )
    grad_query = rotate(grad_query, positions, -1.0).reshape(token_count, model_width)
    grad_key = kv_grads[:, :kv_width].reshape(token_count, group_count, head_dim)
    grad_key = rotate(grad_key, positions, -1.0).reshape(token_count, kv_width)
    grad_qkv = jnp.concatenate([grad_query, grad_key, kv_grads[:, kv_width:]], axis=1)
    first_grad, ga_qkv, gB_qkv, gm_qkv = back_full(
        grad_qkv, first_input, weight_qkv, a_qkv, b_qkv, ratio_qkv, n_qkv, m_qkv,
        before_qkv, inner_qkv, cross_qkv, gram_qkv,
    )
    _, first_pull = jax.vjp(lambda v: rms_scale(v, norm_gain_vectors[0]), token_rows)
    grad_inputs = grad_residual + first_pull(first_grad)[0]

    k_end = model_width + kv_width
    full_units = gate_up_magnitude.shape[1]

    def place(piece, axis):
        shape = list(piece.shape)
        shape[axis] = full_units
        return lax.dynamic_update_slice_in_dim(
            jnp.zeros(shape, piece.dtype), piece, start, axis
        )

    summed = lax.psum(
        (
            jnp.concatenate([ga_qkv, ga_o], axis=0).reshape(4, rank, model_width),
            jnp.stack([gB_qkv[:rank, :model_width], gB_o]),
            jnp.stack(
                [gB_qkv[rank : 2 * rank, model_width:k_end], gB_qkv[2 * rank :, k_end:]]
            ),
            gm_qkv[:model_width],
            gm_qkv[model_width:].reshape(2, kv_width),
            gm_o,
            jnp.stack(ga_gu),
            place(jnp.stack(gB_gu), 2),
            place(jnp.stack(gm_gu), 1),
            place(ga_d, 1),
            gB_d,
            gm_d,
        ),
        ("rows", "seq"),
    )
    norms_gu = lax.all_gather(
        jnp.stack([branch[0][0], branch[1][0]]), "seq", axis=1, tiled=True
    )
    stats = jnp.stack(
        [
            drift_stats(query_magnitude, n_qkv[:model_width]),
            drift_stats(key_value_magnitude[0], n_qkv[model_width:k_end]),
            drift_stats(key_value_magnitude[1], n_qkv[k_end:]),
            drift_stats(output_magnitude, n_o),
            drift_stats(gate_up_magnitude[0], norms_gu[0]),
            drift_stats(gate_up_magnitude[1], norms_gu[1]),
            drift_stats(down_magnitude, n_d),
        ]
    )
    shape = (pair_rows, span_len, model_width)
    return (layer_result.reshape(shape), grad_inputs.reshape(shape), *summed, stats)


def solution(mesh):
    return jax.shard_map(
        local,
        mesh=mesh,
        in_specs=(
            P("rows", "seq", None),
            P("rows", "seq", None),
            P(),
            P(None, "seq", None),
            P(None, "seq", None),
            P(None, "seq", None),
            P("seq", None),
            P(),
            P(),
            P(),
            P(),
            P(),
            P(),
            P(),
            P(),
            P(),
            P(),
            P(),
            P(),
            P("rows"),
            P("rows"),
        ),
        out_specs=(
            P("rows", "seq", None),
            P("rows", "seq", None),
            P(),
            P(),
            P(),
            P(),
            P(),
            P(),
            P(),
            P(),
            P(),
            P(),
            P(),
            P(),
            P(),
        ),
        check_vma=False,
    )
```

time: 1720 us -> 1150 us (0.67)
  waiting for transfers between devices: 1010 us -> 350 us
  blocking collectives: 40.9 us -> 277 us
  matrix products: 428 us -> 263 us
  local copies, waits for them, and re-layouts: 101 us -> 138 us
  other arithmetic: 100 us -> 70 us
    all_gather x6 -> x5, waiting for transfers between devices: 922 us -> 153 us  [the longest x1 113 us: local(): weight_qkv = lax.all_gather(qkv_local, 'seq', axis=0, tiled=True)]
    psum x1 -> x3, blocking collectives: 40.9 us -> 259 us  [the longest x1 204 us: local(): sq_d = lax.psum(sq_d, 'seq')]
    dot_general x105 -> x71, matrix products: 344 us -> 172 us  [the longest x20 78.2 us: dot_f32(): return jnp.dot(a, b, preferred_element_type=jnp.float32)]
    reduce_scatter x0 -> x3, waiting for transfers between devices: none -> 73.2 us  [the longest x1 50.6 us: local(): lax.psum_scatter(down_partial.astype(low), 'seq', scatter_dimension=0, ti...]
    unnamed x9 -> x11, waiting for transfers between devices: 4.22 us -> 38.2 us
    slice x7 -> x20, local copies, waits for them, and re-layouts: 4.57 us -> 34.8 us  [the longest x3 18.6 us: local(): before, inner = project(u2, weight_gu[i], a_gu[i], b_gu[i])]
    reduce_sum x6 -> x8, other arithmetic: 55.8 us -> 26.1 us  [the longest x4 21.5 us: square_terms(): squares = jnp.sum(jnp.square(weight.astype(jnp.float32)), axis=0)]
    all_gather x0 -> x1, blocking collectives: none -> 18.1 us  [local(): lax.all_gather(jnp.stack([branch[0][0], branch[1][0]]), 'seq', axis=1, ti...]
  transfers between devices with their start and end apart: 8 -> 11, of which waited for: 8 -> 6; matrix products, arithmetic and copies ran while one was open for 13% -> 24% of each run, Pallas kernels for 0% -> 0%
where the time goes in v1:
time: 1150 us; the launch traced here: 1140 us
  waiting for transfers between devices  350 us (30%)
  blocking collectives  277 us (24%)
  matrix products  263 us (23%)
  local copies, waits for them, and re-layouts  138 us (12%)
  other arithmetic  70 us (6%)
  between operations  31.4 us (3%)
    psum x1, blocking collectives, local(): sq_d = lax.psum(sq_d, 'seq')  204 us
    all_gather x1, waiting for transfers between devices, local(): weight_qkv = lax.all_gather(qkv_local, 'seq', axis=0, tiled=True)  113 us
    psum x1, waiting for transfers between devices, local(): lax.psum((jnp.concatenate([ga_qkv, ga_o], axis=0).reshape(4, rank, model_...  85.3 us
    dot_general x20, matrix products, dot_f32(): return jnp.dot(a, b, preferred_element_type=jnp.float32)  78.2 us
    dot_general x20, matrix products, dot_nt(): return lax.dot_general(a, b, last_last, preferred_element_type=jnp.float32)  72.1 us
    reduce_scatter x1, waiting for transfers between devices, local(): lax.psum_scatter(down_partial.astype(low), 'seq', scatter_dimension=0, ti...  50.6 us
    unnamed x263, local copies, waits for them, and re-layouts  41.5 us
    psum x1, blocking collectives, local(): lax.psum((jnp.concatenate([ga_qkv, ga_o], axis=0).reshape(4, rank, model_...  40.9 us
  transfers between devices with their start and end apart: 11, of which 6 were waited for; matrix products, arithmetic and copies ran while one was open for 24% of the time, Pallas kernels for 0%

profile of v1, /device:TPU:0, one launch (start us, length us, event | category | flops | bytes accessed | tf_op | source)
XLA Modules:
  0.0 1135.6 jit_solution(551093892239770717)
XLA Ops:
  18.7 113.4 %all-gather.7.cloned.1.call-done = bf16[2048,3072]{1,0:T(8,128)(2,1)} async-done(((bf16[256,3072]{1,0:T(8,128)(2,1)}), bf16[2048,3072]{1,0:T(8,128)(2,1)}) %all-gather.7.cloned.1.call-update) | async-done | bytes 12582928 | tf_op jit(solution)/shard_map/all_gather | solution.py:179
  132.2 7.7 fusion.112
  139.9 8.1 multiply_reduce_fusion.1
  148.6 6.4 fusion.256
  163.5 21.1 %copy.124 = bf16[2,256,8192]{1,0,2:T(2,128)(2,1)} copy(bf16[2,256,8192]{2,1,0:T(8,128)(2,1)} %param.30) | data formatting | bytes 16777216 | tf_op args[5]
  184.6 5.0 all-to-all-start
  192.7 3.7 multiply_reduce_fusion.3
  202.9 203.6 %psum.98 = f32[2048]{0:T(1024)} all-reduce(f32[2048]{0:T(1024)} %multiply_add_fusion.4), channel_id=1, replica_groups=mesh['rows'=4,'seq'=8] {'seq'}, use_global_device_ids=true, to_apply=%region_22.23 | all-reduce | flops 2048 | bytes 16384 | tf_op jit(solution)/shard_map/psum | solution.py:206
  409.3 5.3 multiply_reduce_fusion.2
  433.6 3.0 fusion.245
  443.6 36.3 %while.30 = (s32[]{:T(128)}, bf16[8,2,256,64]{2,3,1,0:T(8,128)(2,1)}, f32[8,2,256]{2,1,0:T(2,128)}, s32[2]{0:T(128)S(1)}, bf16[8,2,256,64]{2,3,1,0:T(8,128)(2,1)...) while((s32[]{:T(128)}, ...), condition=%wide.region_7.8_spmd.clone.clone, body=%wide.region_4.7_spmd.clone.clone.sunk | while | flops 69599744 | bytes 3892593 | solution.py:257
  479.9 3.0 convert_element_type.364
  482.9 3.4 copy.123
  490.5 4.7 fusion.57
  500.3 7.8 copy.125
  508.1 5.8 fusion.243
  513.9 6.4 copy.126
  520.3 6.4 copy.127
  530.9 4.4 multiply_reduce_fusion.5
  535.4 3.5 fusion.96
  539.0 6.4 fusion.62
  545.4 3.5 convolution_add_fusion.3
  548.9 39.4 %all-gather.11.cloned.1.call-done = bf16[1024,2048]{1,0:T(8,128)(2,1)} async-done(((bf16[128,2048]{1,0:T(8,128)(2,1)}), bf16[1024,2048]{1,0:T(8,128)(2,1)}) %all-gather.11.cloned.1.call-update) | async-done | bytes 4194320 | tf_op jit(solution)/shard_map/all_gather | solution.py:265
  588.3 3.5 convolution_convert_fusion.1
  591.8 6.5 fusion.259
  601.3 4.5 fusion.258
  605.8 4.9 multiply_reduce_fusion.7
  611.9 6.9 fusion.261
  619.5 7.0 fusion.262
  627.8 9.3 add_convert_fusion
  640.2 9.4 convolution_convert_fusion
  655.8 18.1 %all_gather.23 = f32[2,8192]{1,0:T(2,128)S(1)} all-gather(f32[2,1024]{1,0:T(2,128)S(1)} %pad_maximum_fusion.12), channel_id=1, replica_groups=mesh['rows'=4,'seq'=8] {'seq'}, dimensions={1}, use_global_device_ids=true | all-gather | bytes 73728 | tf_op jit(solution)/shard_map/all_gather | solution.py:425
  699.8 22.6 %reduce-scatter.6.cloned.1.call-done = f32[128,16]{0,1:T(8,128)} async-done(((f32[1024,16]{0,1:T(8,128)}), f32[128,16]{0,1:T(8,128)}) %reduce-scatter.6.cloned.1.call-update) | async-done | bytes 8208 | tf_op jit(solution)/shard_map/reduce_scatter | solution.py:286
  722.3 50.6 %reduce-scatter.4.cloned.1.call-done = bf16[128,2048]{1,0:T(8,128)(2,1)} async-done(((bf16[1024,2048]{1,0:T(8,128)(2,1)}), bf16[128,2048]{1,0:T(8,128)(2,1)}) %reduce-scatter.4.cloned.1.call-update) | async-done | bytes 524304 | tf_op jit(solution)/shard_map/reduce_scatter | solution.py:285
  772.9 3.2 fusion.99
  777.6 14.5 %psum.108 = f32[2048]{0:T(1024)S(1)} all-reduce(f32[2048]{0:T(1024)S(1)} %div.228), channel_id=1, replica_groups=mesh['rows'=4,'seq'=8] {'seq'}, use_global_device_ids=true, to_apply=%region_45.46 | all-reduce | flops 2048 | bytes 16384 | tf_op jit(solution)/shard_map/psum | solution.py:292
  794.6 6.3 fusion.53
  811.3 74.6 %while.31 = (s32[]{:T(128)}, bf16[8,2,256,64]{2,3,1,0:T(8,128)(2,1)}, bf16[8,2,512,64]{2,3,0,1:T(8,128)(2,1)}, bf16[8,2,512,64]{2,3,0,1:T(8,128)(2,1)}, s32[2]{0...) while((s32[]{:T(128)}, ...), condition=%wide.region_28.29_spmd.clone.clone, body=%wide.region_26.28_spmd.clone.clone.sunk | while | flops 170623488 | bytes 9459081 | solution.py:372
  885.9 3.1 pad_maximum_fusion
  889.0 6.3 copy.134
  897.6 4.7 copy.198
  906.8 3.6 fusion.141
  910.7 6.2 fusion.51
  921.8 36.9 %all-reduce.9.cloned.1.call-done = bf16[2,512,1024]{2,0,1:T(2,128)(2,1)} async-done(((bf16[2,512,1024]{2,0,1:T(2,128)(2,1)}), bf16[2,512,1024]{2,0,1:T(2,128)(2,1)}) %all-reduce.9.cloned.1.call-update) | async-done | bytes 2097168
  967.8 8.6 fusion.114
  977.7 9.8 fusion.263
  988.3 40.9 %all-reduce.4 = (f32[2048]{0:T(1024)}, f32[2,512]{1,0:T(2,128)}, f32[2048]{0:T(1024)}, f32[2048]{0:T(1024)}) all-reduce(f32[2048]{0:T(1024)S(1)} %slice.303, f32[2,512]{1,0:T(2,128)S(1)} %reshape.792, f32[2048]{0:T(1024)S(1)} %copy-done.108, f32[2048]{0:T(1024)S(1)} %copy-done.81), channel_id=1, replica_groups=mesh['rows'=4,'seq'=8] {'rows','seq'}, use_global_device_ids=true, to_apply=%region_36.37 | all-reduce | flops 7168 | bytes 57344 | tf_op jit(solution)/shard_map/psum | solution.py:406
  1032.2 85.3 %all-reduce.11.cloned.1.call-done = (f32[4,16,2048]{2,1,0:T(8,128)}, f32[2,16,2048]{2,1,0:T(8,128)}, f32[2,16,512]{2,1,0:T(8,128)}, f32[2,16,2048]{2,1,0:T(8,128...) async-done(((f32[4,16,2048]{2,1,0:T(8,128)}, f32[2,16,2048]{2,1,0:T(8,128)}, f32[2,16,512]{2,1,0:T(8,128)}, ...) | async-done | bytes 2883600 | tf_op jit(solution)/shard_map/psum | solution.py:406
  (613 shorter events, 259.1 us)
Async XLA Ops:
  7.2 492.4 %copy-start = (f32[2,16,8192]{2,1,0:T(8,128)S(1)}, f32[2,16,8192]{2,1,0:T(8,128)}, u32[]{:S(2)}) copy-start(f32[2,16,8192]{2,1,0:T(8,128)} %param.39) | copy-start | bytes 3145732
  7.2 125.0 %all-gather.7.cloned.1.call-start = ((), (), s32[]{:S(2)}) async-start(), calls=%async_computation.4 | async-start | bytes 14155776 | tf_op jit(solution)/shard_map/all_gather | solution.py:179
  12.5 396.8 %all-gather.15.cloned.1.call-start = ((), (), s32[]{:S(2)}) async-start(), calls=%async_computation.11 | async-start | bytes 9437184 | tf_op jit(solution)/shard_map/all_gather | solution.py:180
  13.3 420.3 %all-gather.9.cloned.1.call-start = ((), (), s32[]{:S(2)}) async-start(), calls=%async_computation.5 | async-start | bytes 2359296 | tf_op jit(solution)/shard_map/all_gather | solution.py:237
  14.8 117.4 %copy-start.116 = (f32[128]{0:T(128)}, f32[128]{0:T(128)S(1)}, u32[]{:S(2)}) copy-start(f32[128]{0:T(128)S(1)} %rsqrt.65) | copy-start | bytes 1540
  15.9 124.0 %copy-start.17 = (bf16[3,16,2048]{2,1,0:T(8,128)(2,1)}, bf16[3,16,2048]{2,1,0:T(8,128)(2,1)S(1)}, u32[]{:S(2)}) copy-start(bf16[3,16,2048]{2,1,0:T(8,128)(2,1)S(1)} %slice.444) | copy-start | bytes 589828
  15.9 132.7 %copy-start.109 = (f32[1,512]{1,0:T(1,128)}, f32[1,512]{1,0:T(1,128)S(1)}, u32[]{:S(2)}) copy-start(f32[1,512]{1,0:T(1,128)S(1)} %get-tuple-element.525) | copy-start | bytes 6148
  15.9 132.7 %copy-start.112 = (f32[1,512]{1,0:T(1,128)}, f32[1,512]{1,0:T(1,128)S(1)}, u32[]{:S(2)}) copy-start(f32[1,512]{1,0:T(1,128)S(1)} %get-tuple-element.526) | copy-start | bytes 6148
  15.9 139.2 %copy-start.50 = (bf16[16,512]{1,0:T(8,128)(2,1)}, bf16[16,512]{1,0:T(8,128)(2,1)S(1)}, u32[]{:S(2)}) copy-start(bf16[16,512]{1,0:T(8,128)(2,1)S(1)} %get-tuple-element.515) | copy-start | bytes 49156
  15.9 139.2 %copy-start.52 = (bf16[16,512]{1,0:T(8,128)(2,1)}, bf16[16,512]{1,0:T(8,128)(2,1)S(1)}, u32[]{:S(2)}) copy-start(bf16[16,512]{1,0:T(8,128)(2,1)S(1)} %get-tuple-element.516) | copy-start | bytes 49156
  16.7 141.6 %copy-start.58 = (f32[128,32]{0,1:T(8,128)}, f32[128,32]{0,1:T(8,128)S(1)}, u32[]{:S(2)}) copy-start(f32[128,32]{0,1:T(8,128)S(1)} %get-tuple-element.528) | copy-start | bytes 49156
  16.7 405.9 %copy-start.45 = (f32[128,32]{0,1:T(8,128)}, f32[128,32]{0,1:T(8,128)S(1)}, u32[]{:S(2)}) copy-start(f32[128,32]{0,1:T(8,128)S(1)} %get-tuple-element.529) | copy-start | bytes 49156
  16.9 138.2 %copy-start.35 = (bf16[16,2048]{1,0:T(8,128)(2,1)}, bf16[16,2048]{1,0:T(8,128)(2,1)S(1)}, u32[]{:S(2)}) copy-start(bf16[16,2048]{1,0:T(8,128)(2,1)S(1)} %get-tuple-element.497) | copy-start | bytes 196612
  17.3 122.5 %copy-start.28 = (f32[48,3072]{1,0:T(8,128)}, f32[48,3072]{1,0:T(8,128)S(1)}, u32[]{:S(2)}) copy-start(f32[48,3072]{1,0:T(8,128)S(1)} %fusion.238) | copy-start | bytes 1769476
  18.0 121.9 %copy-start.61 = (f32[1,2048]{1,0:T(1,128)}, f32[1,2048]{1,0:T(1,128)S(1)}, u32[]{:S(2)}) copy-start(f32[1,2048]{1,0:T(1,128)S(1)} %get-tuple-element.519) | copy-start | bytes 24580
  18.5 136.6 %copy-start.66 = (bf16[128,48]{0,1:T(8,128)(2,1)}, bf16[128,48]{0,1:T(8,128)(2,1)S(1)}, u32[]{:S(2)}) copy-start(bf16[128,48]{0,1:T(8,128)(2,1)S(1)} %convolution_convert_fusion.3) | copy-start | bytes 36868
  18.7 129.9 %copy-start.21 = (bf16[128,2048]{1,0:T(8,128)(2,1)}, bf16[128,2048]{1,0:T(8,128)(2,1)S(1)}, u32[]{:S(2)}) copy-start(bf16[128,2048]{1,0:T(8,128)(2,1)S(1)} %fusion.106) | copy-start | bytes 1572868
  184.6 315.7 %all-to-all-start = ((bf16[2,256,8192]{1,0,2:T(2,128)(2,1)}), bf16[2,256,8192]{1,0,2:T(2,128)(2,1)}, u32[]{:S(2)}, u32[]{:S(2)}) async-start(bf16[2,256,8192]{1,0,2:T(2,128)(2,1)} %copy.124), calls=%async_computation | async-start | bytes 16777216 | tf_op jit(solution)/shard_map/all_to_all | solution.py:181
  189.7 345.7 %all-gather.13.cloned.1.call-start = ((), (), s32[]{:S(2)}) async-start(), calls=%async_computation.9 | async-start | bytes 4718592 | tf_op jit(solution)/shard_map/all_gather | solution.py:267
  190.2 398.1 %all-gather.11.cloned.1.call-start = ((), (), s32[]{:S(2)}) async-start(), calls=%async_computation.6 | async-start | bytes 4718592 | tf_op jit(solution)/shard_map/all_gather | solution.py:265
  196.5 218.2 %copy-start.27 = (bf16[16,8192]{1,0:T(8,128)(2,1)}, bf16[16,8192]{1,0:T(8,128)(2,1)S(1)}, u32[]{:S(2)}) copy-start(bf16[16,8192]{1,0:T(8,128)(2,1)S(1)} %convert_element_type.386) | copy-start | bytes 786436
  498.5 199.9 %reduce-scatter.8.cloned.1.call-start = ((), (), s32[]{:S(2)}) async-start(), calls=%async_computation.10 | async-start | bytes 4718592 | tf_op jit(solution)/shard_map/reduce_scatter | solution.py:324
  500.3 38.7 %copy-start.73 = (f32[2048]{0:T(1024)}, f32[2048]{0:T(1024)S(1)}, u32[]{:S(2)}) copy-start(f32[2048]{0:T(1024)S(1)} %div.214) | copy-start | bytes 24580
  611.9 14.6 %copy-start.47 = (bf16[1024,16]{0,1:T(8,128)(2,1)}, bf16[1024,16]{0,1:T(8,128)(2,1)S(1)}, u32[]{:S(2)}) copy-start(bf16[1024,16]{0,1:T(8,128)(2,1)S(1)} %fusion.94) | copy-start | bytes 98308
  637.2 85.2 %reduce-scatter.6.cloned.1.call-start = ((), (), s32[]{:S(2)}) async-start(), calls=%async_computation.8 | async-start | bytes 73728 | tf_op jit(solution)/shard_map/reduce_scatter | solution.py:286
  640.1 132.8 %reduce-scatter.4.cloned.1.call-start = ((), (), s32[]{:S(2)}) async-start(), calls=%async_computation.7 | async-start | bytes 4718592 | tf_op jit(solution)/shard_map/reduce_scatter | solution.py:285
  649.5 29.6 %copy-start.87 = (f32[2048]{0:T(1024)S(1)}, f32[2048]{0:T(1024)}, u32[]{:S(2)}) copy-start(f32[2048]{0:T(1024)} %param.35) | copy-start | bytes 24580
  649.5 29.6 %copy-start.97 = (f32[3072]{0:T(1024)S(1)}, f32[3072]{0:T(1024)}, u32[]{:S(2)}) copy-start(f32[3072]{0:T(1024)} %get-tuple-element.444) | copy-start | bytes 36868
  649.5 32.2 %copy-start.110 = (f32[1,512]{1,0:T(1,128)S(1)}, f32[1,512]{1,0:T(1,128)}, u32[]{:S(2)}) copy-start(f32[1,512]{1,0:T(1,128)} %copy-done.109) | copy-start | bytes 6148
  649.6 32.2 %copy-start.113 = (f32[1,512]{1,0:T(1,128)S(1)}, f32[1,512]{1,0:T(1,128)}, u32[]{:S(2)}) copy-start(f32[1,512]{1,0:T(1,128)} %copy-done.112) | copy-start | bytes 6148
  649.6 309.1 %all-reduce.9.cloned.1.call-start = ((), (), s32[]{:S(2)}) async-start(), calls=%async_computation.12 | async-start | bytes 4194304
  695.1 77.8 %copy-start.24 = (bf16[2,64,2048]{2,1,0:T(8,128)(2,1)S(1)}, bf16[2,64,2048]{2,1,0:T(8,128)(2,1)}, u32[]{:S(2)}) copy-start(bf16[2,64,2048]{2,1,0:T(8,128)(2,1)} %param.26) | copy-start | bytes 1572868
  695.1 77.8 %copy-start.74 = (f32[2048]{0:T(1024)S(1)}, f32[2048]{0:T(1024)}, u32[]{:S(2)}) copy-start(f32[2048]{0:T(1024)} %copy-done.73) | copy-start | bytes 24580
  695.1 77.8 %copy-start.119 = (f32[128]{0:T(128)S(1)}, f32[128]{0:T(128)}, u32[]{:S(2)}) copy-start(f32[128]{0:T(128)} %copy-done.118) | copy-start | bytes 1540
  697.4 78.7 %copy-start.83 = (f32[2048]{0:T(1024)S(1)}, f32[2048]{0:T(1024)}, u32[]{:S(2)}) copy-start(f32[2048]{0:T(1024)} %param.37) | copy-start | bytes 24580
  697.4 78.7 %copy-start.85 = (f32[2048]{0:T(1024)S(1)}, f32[2048]{0:T(1024)}, u32[]{:S(2)}) copy-start(f32[2048]{0:T(1024)} %copy-done.84) | copy-start | bytes 24580
  698.4 93.7 %copy-start.79 = (f32[2048]{0:T(1024)S(1)}, f32[2048]{0:T(1024)}, u32[]{:S(2)}) copy-start(f32[2048]{0:T(1024)} %param.43) | copy-start | bytes 24580
  698.4 94.4 %copy-start.41 = (f32[16,2048]{1,0:T(8,128)S(1)}, f32[16,2048]{1,0:T(8,128)}, u32[]{:S(2)}) copy-start(f32[16,2048]{1,0:T(8,128)} %param.42) | copy-start | bytes 393220
  777.6 16.0 %copy-start.80 = (f32[2048]{0:T(1024)}, f32[2048]{0:T(1024)S(1)}, u32[]{:S(2)}) copy-start(f32[2048]{0:T(1024)S(1)} %div.228) | copy-start | bytes 24580
  895.3 222.1 %all-reduce.11.cloned.1.call-start = ((), (), s32[]{:S(2)}) async-start(), calls=%async_computation.13 | async-start | bytes 5767168 | tf_op jit(solution)/shard_map/psum | solution.py:406
  917.8 43.3 %copy-start.71 = (f32[3072]{0:T(1024)S(1)}, f32[3072]{0:T(1024)}, u32[]{:S(2)}) copy-start(f32[3072]{0:T(1024)} %copy-done.70) | copy-start | bytes 36868
  918.8 44.4 %copy-start.31 = (f32[16,8192]{1,0:T(8,128)}, f32[16,8192]{1,0:T(8,128)S(1)}, u32[]{:S(2)}) copy-start(f32[16,8192]{1,0:T(8,128)S(1)} %fusion.88) | copy-start | bytes 1572868
  977.7 10.6 copy-start.81
  977.7 51.5 %copy-start.12 = (bf16[2,64,2048]{2,1,0:T(8,128)(2,1)S(1)}, bf16[2,64,2048]{2,1,0:T(8,128)(2,1)}, u32[]{:S(2)}) copy-start(bf16[2,64,2048]{2,1,0:T(8,128)(2,1)} %param.25) | copy-start | bytes 1572868
  977.7 51.5 %copy-start.62 = (f32[1,2048]{1,0:T(1,128)S(1)}, f32[1,2048]{1,0:T(1,128)}, u32[]{:S(2)}) copy-start(f32[1,2048]{1,0:T(1,128)} %copy-done.61) | copy-start | bytes 24580
  977.7 53.2 %copy-start.123 = (f32[128]{0:T(128)S(1)}, f32[128]{0:T(128)}, u32[]{:S(2)}) copy-start(f32[128]{0:T(128)} %copy-done.122) | copy-start | bytes 1540
  977.7 53.2 %copy-start.117 = (f32[128]{0:T(128)S(1)}, f32[128]{0:T(128)}, u32[]{:S(2)}) copy-start(f32[128]{0:T(128)} %copy-done.116) | copy-start | bytes 1540
  1030.9 97.7 %copy-start.1 = (f32[2,16,8192]{2,1,0:T(8,128)S(1)}, f32[2,16,8192]{2,1,0:T(8,128)}, u32[]{:S(2)}) copy-start(f32[2,16,8192]{2,1,0:T(8,128)} %param.39) | copy-start | bytes 3145732
  (88 other events, 470.9 us)
Sparse Core Ops, SparseCore 0:
  12.6 119.4 all-gather.6
  134.3 101.5 all-gather.14
  238.2 66.2 all-gather.8
  305.9 111.5 all-gather.12
  498.6 89.6 all-gather.10
  637.3 54.0 reduce-scatter.7
  694.2 28.1 reduce-scatter.5
  724.7 48.1 reduce-scatter.3
  895.4 63.1 all-reduce.8
  977.8 139.5 all-reduce.10

commit v2 on v1

--- a/solution.py
+++ b/solution.py
@@ -1,6 +1,10 @@
+import functools
+
 import jax
 import jax.numpy as jnp
 from jax import lax
+from jax.experimental import pallas as pl
+from jax.experimental.pallas import tpu as pltpu
 from jax.sharding import PartitionSpec as P
 
 HEADS = 32
@@ -35,6 +39,431 @@
         ],
         axis=-1,
     )
+
+
+MESH = pl.DeviceIdType.MESH
+
+
+def place_in_seq():
+    s = lax.axis_index("seq")
+    return s, s // 2, lax.rem(s, 2)
+
+
+def greet(nc, q, s):
+    barrier = pltpu.get_barrier_semaphore()
+
+    def signal(target):
+        pl.semaphore_signal(barrier, inc=1, device_id={"seq": target}, device_id_type=MESH)
+
+    sibling = s + 1 - 2 * lax.rem(s, 2)
+    signal(sibling)
+    pl.when(q > 0)(lambda: signal(s - 2))
+    pl.when(q < nc - 1)(lambda: signal(s + 2))
+    pl.semaphore_wait(barrier, 1 + jnp.where(q > 0, 1, 0) + jnp.where(q < nc - 1, 1, 0))
+    return sibling
+
+
+def gather_kernel(n, count, *refs):
+    nc = n // 2
+    xs, outs = refs[:count], refs[count : 2 * count]
+    local_sem, to_sib, to_left, to_right, recv = refs[2 * count :]
+    s, q, c = place_in_seq()
+    sibling = greet(nc, q, s)
+    locals_ = [
+        pltpu.make_async_copy(xs[k], outs[k].at[s], local_sem.at[k]) for k in range(count)
+    ]
+    for cp in locals_:
+        cp.start()
+
+    def copy(k, src, slot, sems, target):
+        return pltpu.make_async_remote_copy(
+            src_ref=src,
+            dst_ref=outs[k].at[slot],
+            send_sem=sems.at[k, slot],
+            recv_sem=recv.at[k, slot],
+            device_id={"seq": target},
+            device_id_type=MESH,
+        )
+
+    for k in range(count):
+        pl.when(q > 0)(lambda k=k: copy(k, xs[k], s, to_left, s - 2).start())
+        pl.when(q < nc - 1)(lambda k=k: copy(k, xs[k], s, to_right, s + 2).start())
+        copy(k, xs[k], s, to_sib, sibling).start()
+    for t in range(1, nc):
+
+        @pl.when(q - t >= 0)
+        def _(t=t):
+            slot = s - 2 * t
+            for k in range(count):
+                src = outs[k].at[slot]
+                copy(k, src, slot, to_right, s).wait_recv()
+                pl.when(q < nc - 1)(
+                    lambda k=k: copy(k, src, slot, to_right, s + 2).start()
+                )
+                copy(k, src, slot, to_sib, sibling).start()
+
+        @pl.when(q + t < nc)
+        def _(t=t):
+            slot = s + 2 * t
+            for k in range(count):
+                src = outs[k].at[slot]
+                copy(k, src, slot, to_left, s).wait_recv()
+                pl.when(q > 0)(lambda k=k: copy(k, src, slot, to_left, s - 2).start())
+                copy(k, src, slot, to_sib, sibling).start()
+
+    for cp in locals_:
+        cp.wait()
+    other = 1 - 2 * c
+    for p in range(nc):
+        mine, theirs = 2 * p + c, 2 * p + c + other
+        for k in range(count):
+            copy(k, outs[k].at[theirs], theirs, to_sib, sibling).wait_recv()
+            copy(k, outs[k].at[mine], mine, to_sib, sibling).wait_send()
+            pl.when((q < nc - 1) & (p <= q))(
+                lambda k=k: copy(k, outs[k].at[mine], mine, to_right, sibling).wait_send()
+            )
+            pl.when((q > 0) & (p >= q))(
+                lambda k=k: copy(k, outs[k].at[mine], mine, to_left, sibling).wait_send()
+            )
+
+
+def gather_seq(n, arrays, collective_id):
+    count = len(arrays)
+    nbytes = sum(a.size * a.dtype.itemsize for a in arrays)
+    dma = pltpu.SemaphoreType.DMA
+    return pl.pallas_call(
+        functools.partial(gather_kernel, n, count),
+        out_shape=tuple(jax.ShapeDtypeStruct((n, *a.shape), a.dtype) for a in arrays),
+        in_specs=[pl.BlockSpec(memory_space=pl.ANY)] * count,
+        out_specs=tuple([pl.BlockSpec(memory_space=pl.ANY)] * count),
+        scratch_shapes=[dma((count,))] + [dma((count, n))] * 4,
+        compiler_params=pltpu.CompilerParams(collective_id=collective_id, has_side_effects=True),
+        cost_estimate=pl.CostEstimate(flops=0, transcendentals=0, bytes_accessed=nbytes * n * 20),
+        name="gather_seq",
+    )(*arrays)
+
+
+def scatter_kernel(n, x_ref, o_ref, own, sib, from_left, from_right, load_sem, to_sib, sib_in, to_right, right_in, to_left, left_in):
+    nc = n // 2
+    s, q, c = place_in_seq()
+    sibling = greet(nc, q, s)
+    theirs = 1 - c
+
+    def load(p):
+        return pltpu.make_async_copy(x_ref.at[2 * p + c], own.at[p], load_sem.at[p])
+
+    def to_sibling(p):
+        return pltpu.make_async_remote_copy(
+            src_ref=x_ref.at[2 * p + theirs],
+            dst_ref=sib.at[p],
+            send_sem=to_sib.at[p],
+            recv_sem=sib_in.at[p],
+            device_id={"seq": sibling},
+            device_id_type=MESH,
+        )
+
+    def rightward(p, target):
+        return pltpu.make_async_remote_copy(
+            src_ref=own.at[p],
+            dst_ref=from_left.at[p],
+            send_sem=to_right.at[p],
+            recv_sem=right_in.at[p],
+            device_id={"seq": target},
+            device_id_type=MESH,
+        )
+
+    def leftward(p, target):
+        return pltpu.make_async_remote_copy(
+            src_ref=own.at[p],
+            dst_ref=from_right.at[p],
+            send_sem=to_left.at[p],
+            recv_sem=left_in.at[p],
+            device_id={"seq": target},
+            device_id_type=MESH,
+        )
+
+    order = []
+    for t in range(nc):
+        for p in (nc - 1 - t, t):
+            if p not in order:
+                order.append(p)
+    for p in order:
+        to_sibling(p).start()
+        load(p).start()
+
+    f32 = jnp.float32
+    for p in order:
+        load(p).wait()
+        to_sibling(p).wait_recv()
+
+        @pl.when(p > q)
+        def _(p=p):
+            @pl.when(q > 0)
+            def _():
+                rightward(p, s).wait_recv()
+                total = own[p].astype(f32) + sib[p].astype(f32) + from_left[p].astype(f32)
+                own[p] = total.astype(own.dtype)
+
+            @pl.when(q == 0)
+            def _():
+                own[p] = (own[p].astype(f32) + sib[p].astype(f32)).astype(own.dtype)
+
+            rightward(p, s + 2).start()
+
+        @pl.when(p < q)
+        def _(p=p):
+            @pl.when(q < nc - 1)
+            def _():
+                leftward(p, s).wait_recv()
+                total = own[p].astype(f32) + sib[p].astype(f32) + from_right[p].astype(f32)
+                own[p] = total.astype(own.dtype)
+
+            @pl.when(q == nc - 1)
+            def _():
+                own[p] = (own[p].astype(f32) + sib[p].astype(f32)).astype(own.dtype)
+
+            leftward(p, s - 2).start()
+
+    o_ref[...] = own[q].astype(f32) + sib[q].astype(f32)
+
+    @pl.when(q > 0)
+    def _():
+        rightward(q, s).wait_recv()
+        o_ref[...] += from_left[q].astype(f32)
+
+    @pl.when(q < nc - 1)
+    def _():
+        leftward(q, s).wait_recv()
+        o_ref[...] += from_right[q].astype(f32)
+
+    for p in range(nc):
+        to_sibling(p).wait_send()
+        pl.when(p > q)(lambda p=p: rightward(p, s).wait_send())
+        pl.when(p < q)(lambda p=p: leftward(p, s).wait_send())
+
+
+def scatter_seq(n, x, collective_id):
+    nc = n // 2
+    _, rows, cols = x.shape
+    dma = pltpu.SemaphoreType.DMA
+    buf = pltpu.VMEM((nc, rows, cols), x.dtype)
+    return pl.pallas_call(
+        functools.partial(scatter_kernel, n),
+        out_shape=jax.ShapeDtypeStruct((rows, cols), jnp.float32),
+        in_specs=[pl.BlockSpec(memory_space=pl.ANY)],
+        out_specs=pl.BlockSpec(memory_space=pltpu.VMEM),
+        scratch_shapes=[buf] * 4 + [dma((nc,))] * 7,
+        compiler_params=pltpu.CompilerParams(
+            collective_id=collective_id, has_side_effects=True, vmem_limit_bytes=32 << 20
+        ),
+        cost_estimate=pl.CostEstimate(flops=0, transcendentals=0, bytes_accessed=x.size * 2 * 20),
+        name="scatter_seq",
+    )(x)
+
+
+def near_first(i, q, nc):
+    short = jnp.where(q <= nc - 1 - q, q, nc - 1 - q)
+    far = jnp.where(q <= nc - 1 - q, i, nc - 1 - i)
+    step = (i + 1) // 2
+    near = q - step if i % 2 else q + step
+    return jnp.where(i <= 2 * short, near, far)
+
+
+def weights_kernel(n, rows, xa, wa, local, edge, a_in, a_sib_in, a_out, a_sib_out):
+    nc, half = n // 2, rows // 2
+    others = half - 1
+    s, q, c = place_in_seq()
+    sibling = s + 1 - 2 * c
+    r = lax.axis_index("rows")
+    a, b = r // 2, lax.rem(r, 2)
+    b_row = r + 1 - 2 * b
+
+    def a_row(k):
+        return lax.rem(a + k + half, half) * 2 + b
+
+    def diagonal(k):
+        return lax.rem(a + k + half, half) * 2 + 1 - b
+
+    barrier = pltpu.get_barrier_semaphore()
+    for t in range(1, n):
+        pl.semaphore_signal(
+            barrier, inc=1, device_id=(r, lax.rem(s + t, n)), device_id_type=MESH
+        )
+    pl.semaphore_signal(barrier, inc=1, device_id=(b_row, s), device_id_type=MESH)
+    for k in range(1, half):
+        pl.semaphore_signal(barrier, inc=1, device_id=(a_row(k), s), device_id_type=MESH)
+    pl.semaphore_wait(barrier, n - 1 + half)
+
+    def remote(src, dst, send, recv, row, seq):
+        return pltpu.make_async_remote_copy(
+            src_ref=src, dst_ref=dst, send_sem=send, recv_sem=recv,
+            device_id=(row, seq), device_id_type=MESH,
+        )
+
+    both, first, second = pl.ds(0, 2), pl.ds(0, 1), pl.ds(1, 1)
+    LINE, FROM_B = 0, 1
+
+    def from_a(k):
+        return 1 + k
+
+    def relay_b(k):
+        return 1 + others + k
+
+    def relay_a(k):
+        return 1 + 2 * others + k
+
+    def a_view(p, core, parts, row):
+        return wa.at[parts, 2 * p + core, row]
+
+    def content(kind):
+        if kind == LINE:
+            return both, r
+        if kind == FROM_B:
+            return both, b_row
+        for k in range(1, half):
+            if kind == from_a(k):
+                return both, a_row(-k)
+            if kind == relay_b(k):
+                return second, diagonal(-k)
+            if kind == relay_a(k):
+                return first, diagonal(-k)
+
+    kinds = 2 + 3 * others
+
+    def a_send(p, parts, row, kind, target_row):
+        return remote(
+            a_view(p, c, parts, row), a_view(p, c, parts, row),
+            a_out.at[p, kind], a_in.at[p, kind], target_row, s,
+        )
+
+    def a_arrival(p, kind):
+        parts, row = content(kind)
+        return a_send(p, parts, row, kind, r)
+
+    def a_to_sibling(p, kind, core):
+        parts, row = content(kind)
+        return remote(
+            a_view(p, core, parts, row), a_view(p, core, parts, row),
+            a_sib_out.at[p, kind], a_sib_in.at[p, kind], r, sibling,
+        )
+
+    def line_send(p, src, sem, target):
+        return remote(src, a_view(p, c, both, r), sem, a_in.at[p, LINE], r, target)
+
+    own = xa.at[both, r]
+    to_left = lambda: line_send(q, own, edge.at[0], s - 2)
+    to_right = lambda: line_send(q, own, edge.at[1], s + 2)
+    pl.when(q > 0)(lambda: to_left().start())
+    pl.when(q < nc - 1)(lambda: to_right().start())
+    order = [near_first(i, q, nc) for i in range(nc)]
+    sib_a = lambda: remote(xa, wa.at[:, s], edge.at[2], edge.at[3], r, sibling)
+    keep_a = pltpu.make_async_copy(xa, wa.at[:, s], local.at[0])
+    sib_a().start()
+    keep_a.start()
+
+    def spread_a(p):
+        a_send(p, both, r, FROM_B, b_row).start()
+        for k in range(1, half):
+            a_send(p, both, r, from_a(k), a_row(k)).start()
+
+    for p in order[1:]:
+        a_arrival(p, LINE).wait_recv()
+        pl.when((p < q) & (q < nc - 1))(
+            lambda p=p: line_send(p, a_view(p, c, both, r), a_out.at[p, LINE], s + 2).start()
+        )
+        pl.when((p > q) & (q > 0))(
+            lambda p=p: line_send(p, a_view(p, c, both, r), a_out.at[p, LINE], s - 2).start()
+        )
+        spread_a(p)
+        a_to_sibling(p, LINE, c).start()
+    for p in order[1:]:
+        a_arrival(p, FROM_B).wait_recv()
+        for k in range(1, half):
+            a_send(p, first, b_row, relay_a(k), a_row(k)).start()
+        a_to_sibling(p, FROM_B, c).start()
+        for k in range(1, half):
+            a_arrival(p, from_a(k)).wait_recv()
+            a_send(p, second, a_row(-k), relay_b(k), b_row).start()
+            a_to_sibling(p, from_a(k), c).start()
+    for p in order[1:]:
+        for k in range(1, half):
+            for kind in (relay_b(k), relay_a(k)):
+                a_arrival(p, kind).wait_recv()
+                a_to_sibling(p, kind, c).start()
+    keep_a.wait()
+    sib_a().wait()
+    pl.when(q > 0)(lambda: to_left().wait_send())
+    pl.when(q < nc - 1)(lambda: to_right().wait_send())
+    for p in order[1:]:
+        pl.when(((p < q) & (q < nc - 1)) | ((p > q) & (q > 0)))(
+            lambda p=p: line_send(p, a_view(p, c, both, r), a_out.at[p, LINE], s).wait_send()
+        )
+        for kind in range(kinds):
+            a_to_sibling(p, kind, c).wait_send()
+            a_to_sibling(p, kind, 1 - c).wait_recv()
+        a_send(p, both, r, FROM_B, b_row).wait_send()
+        for k in range(1, half):
+            a_send(p, both, r, from_a(k), r).wait_send()
+            a_send(p, first, b_row, relay_a(k), r).wait_send()
+            a_send(p, second, a_row(-k), relay_b(k), r).wait_send()
+
+
+def gather_weights(n, rows, xa, collective_id):
+    nc = n // 2
+    block = xa.shape[1]
+    part = block // rows
+    xa = xa.reshape(2, rows, part, xa.shape[2])
+    kinds = 2 + 3 * (rows // 2 - 1)
+    dma = pltpu.SemaphoreType.DMA
+    anywhere = pl.BlockSpec(memory_space=pl.ANY)
+    wa = pl.pallas_call(
+        functools.partial(weights_kernel, n, rows),
+        out_shape=jax.ShapeDtypeStruct((2, n, rows, part, xa.shape[3]), xa.dtype),
+        in_specs=[anywhere],
+        out_specs=anywhere,
+        scratch_shapes=[dma((1,)), dma((4,))] + [dma((nc, kinds))] * 4,
+        compiler_params=pltpu.CompilerParams(collective_id=collective_id, has_side_effects=True),
+        cost_estimate=pl.CostEstimate(
+            flops=0, transcendentals=0, bytes_accessed=250 * 1024 * 1024
+        ),
+        name="gather_weights",
+    )(xa)
+    return wa.reshape(2, n * block, -1)
+
+def reshard_units(gate_up, n, rows):
+    half = rows // 2
+    _, block, units_all = gate_up.shape
+    part, units = block // rows, units_all // n
+    r = lax.axis_index("rows")
+    a, b = r // 2, lax.rem(r, 2)
+    mine = lax.dynamic_slice_in_dim(gate_up, r * part, part, 1)
+    mine = mine.reshape(2, part, n, units).transpose(2, 0, 1, 3)
+    mine = lax.all_to_all(mine, "seq", split_axis=0, concat_axis=0, tiled=True)
+    swap = [(i, i ^ 1) for i in range(rows)]
+    turns = [[(i, (i + 2 * k) % rows) for i in range(rows)] for k in range(1, half)]
+    from_b = lax.ppermute(mine, "rows", swap)
+    from_a = [lax.ppermute(mine, "rows", turn) for turn in turns]
+    pieces, holds = [mine, from_b], [r, 2 * a + 1 - b]
+    for k in range(1, half):
+        a_from = lax.rem(a - k + half, half)
+        pieces.append(from_a[k - 1])
+        holds.append(2 * a_from + b)
+        gate = lax.ppermute(from_b[:, 0], "rows", turns[k - 1])
+        lift = lax.ppermute(from_a[k - 1][:, 1], "rows", swap)
+        pieces.append(jnp.stack([gate, lift], axis=1))
+        holds.append(2 * a_from + 1 - b)
+    return pieces, holds
+
+
+def join_units(pieces, holds):
+    rows = len(pieces)
+    n, _, part, units = pieces[0].shape
+    joined = jnp.zeros((2, n, rows, part, units), pieces[0].dtype)
+    for piece, hold in zip(pieces, holds):
+        joined = lax.dynamic_update_slice_in_dim(
+            joined, piece.transpose(1, 0, 2, 3)[:, :, None], hold, 2
+        )
+    return joined.reshape(2, n * rows * part, units)
 
 
 SCALE = ALPHA / ADAPTER_RANK
@@ -173,12 +602,18 @@
     low = jnp.bfloat16
     rank = ADAPTER_RANK
 
-    qkv_local = jnp.concatenate(
-        [query_output_frozen[0], key_value_frozen[0], key_value_frozen[1]], axis=1
-    )
-    weight_qkv = lax.all_gather(qkv_local, "seq", axis=0, tiled=True)
-    weight_o = lax.all_gather(query_output_frozen[1], "seq", axis=0, tiled=True)
-    weight_gu = lax.all_to_all(gate_up_frozen, "seq", split_axis=2, concat_axis=1, tiled=True)
+    rows_size = lax.axis_size("rows")
+    packed = jnp.stack(
+        [
+            jnp.concatenate([query_output_frozen[0], key_value_frozen[0]], axis=1),
+            jnp.concatenate([key_value_frozen[1], query_output_frozen[1]], axis=1),
+        ]
+    )
+    weight_parts = gather_weights(seq_size, rows_size, packed, 1)
+    weight_qk, weight_v = weight_parts[0], weight_parts[1, :, :kv_width]
+    weight_o = weight_parts[1, :, kv_width:]
+    weight_qkv = jnp.concatenate([weight_qk, weight_v], axis=1)
+    weight_gu = join_units(*reshard_units(gate_up_frozen, seq_size, rows_size))
     weight_d = down_frozen_weight
     slice_units = weight_d.shape[0]
 
@@ -233,8 +668,10 @@
     )
     keys_values = jnp.concatenate(
         [key_rows.reshape(token_count, kv_width), v_flat.astype(low)], axis=1
-    ).reshape(pair_rows, span_len, 2 * kv_width)
-    kv_all = lax.all_gather(keys_values, "seq", axis=1, tiled=True)
+    )
+    (kv_all,) = gather_seq(seq_size, [keys_values], 2)
+    kv_all = kv_all.reshape(seq_size, pair_rows, span_len, 2 * kv_width)
+    kv_all = kv_all.transpose(1, 0, 2, 3).reshape(pair_rows, seq_size * span_len, 2 * kv_width)
     query_heads = to_heads(
         queries.reshape(token_count, model_width), pair_rows, span_len, group_count, ratio, head_dim
     )
@@ -262,7 +699,8 @@
     residual = token_rows + before_o * ratio_o
     second_input = rms_scale(residual, norm_gain_vectors[1]).astype(low)
 
-    u2 = lax.all_gather(second_input, "seq", axis=0, tiled=True)
+    (u2,) = gather_seq(seq_size, [second_input], 3)
+    u2 = u2.reshape(seq_size * token_count, model_width)
     grad_out_rows = output_gradient.reshape(token_count, model_width)
     gy_all = lax.all_gather(grad_out_rows, "seq", axis=0, tiled=True)
     gb_d = (gy_all.astype(jnp.float32) * ratio_d).astype(low)
@@ -321,9 +759,11 @@
         ga_gu.append(dot_tn(gi, u2) + SCALE * spread_term(weight_gu[i], a_gu[i], b_gu[i], c))
         gB_gu.append(SCALE * dot_tn(inner, gb) + SCALE * c * (cross + SCALE * gram_b))
         gm_gu.append(gm)
-    in_grad = lax.psum_scatter(grad_in.astype(low), "seq", scatter_dimension=0, tiled=True)
+    in_grad = scatter_seq(
+        seq_size, grad_in.astype(low).reshape(seq_size, token_count, model_width), 4
+    )
     _, second_pull = jax.vjp(lambda v: rms_scale(v, norm_gain_vectors[1]), residual)
-    grad_residual = grad_rows + second_pull(in_grad.astype(jnp.float32))[0]
+    grad_residual = grad_rows + second_pull(in_grad)[0]
 
     def back_full(upstream, rows, weight, a_low, b_low, ratio_p, norm, magnitude, before, inner, cross, gram_b):
         gb = (upstream * ratio_p).astype(low)
@@ -376,8 +816,13 @@
         [keys_from_heads(grad_k_heads).astype(low), keys_from_heads(grad_v_heads).astype(low)],
         axis=2,
     )
-    kv_grads = lax.psum_scatter(kv_grads, "seq", scatter_dimension=1, tiled=True)
-    kv_grads = kv_grads.reshape(token_count, 2 * kv_width).astype(jnp.float32)
+    kv_grads = kv_grads.reshape(pair_rows, seq_size, span_len, 2 * kv_width)
+    kv_grads = scatter_seq(
+        seq_size,
+        kv_grads.transpose(1, 0, 2, 3).reshape(seq_size, token_count, 2 * kv_width),
+        5,
+    )
+    kv_grads = kv_grads.astype(low).astype(jnp.float32)
     grad_query = from_heads(grad_q_heads, pair_rows, span_len, group_count, ratio, head_dim)
     grad_query = (
         grad_query.astype(low).astype(jnp.float32).reshape(token_count, head_count, head_dim)

time: 1150 us -> 1070 us (0.930)
  Pallas kernels: 0 us -> 333 us
  waiting for transfers between devices: 350 us -> 151 us
  blocking collectives: 277 us -> 84.8 us
  matrix products: 263 us -> 242 us
    pallas_call x0 -> x5, Pallas kernels: none -> 333 us  [the longest x1 153 us: gather_weights(): pl.pallas_call(functools.partial(weights_kernel, n, rows), out_shape=jax....]
    psum x1, blocking collectives: 204 us -> 15.3 us  [local(): sq_d = lax.psum(sq_d, 'seq')]
    all_gather x4 -> x0, waiting for transfers between devices: 153 us -> none  [the longest x1 113 us: local(): weight_qkv = lax.all_gather(qkv_local, 'seq', axis=0, tiled=True)]
    reduce_scatter x1, waiting for transfers between devices: 50.6 us -> 0.01 us  [local(): lax.psum_scatter(down_partial.astype(low), 'seq', scatter_dimension=0, ti...]
    psum x1, waiting for transfers between devices: 85.3 us -> 131 us  [local(): lax.psum((jnp.concatenate([ga_qkv, ga_o], axis=0).reshape(4, rank, model_...]
    unnamed x11 -> x4, waiting for transfers between devices: 38.2 us -> 0.73 us
    reduce_scatter x1, waiting for transfers between devices: 22.6 us -> 0.01 us  [local(): lax.psum_scatter(inner_d_partial, 'seq', scatter_dimension=0, tiled=True)]
    ppermute x0 -> x4, waiting for transfers between devices: none -> 18.6 us  [the longest x1 15.4 us: reshard_units(): gate = lax.ppermute(from_b[:, 0], 'rows', turns[k - 1])]
  transfers between devices with their start and end apart: 11 -> 9, of which waited for: 6 -> 3; matrix products, arithmetic and copies ran while one was open for 24% -> 25% of each run, Pallas kernels for 0% -> 29%
where the time goes in v2:
time: 1070 us; the launch traced here: 1060 us
  Pallas kernels  333 us (31%)
  matrix products  242 us (23%)
  waiting for transfers between devices  151 us (14%)
  local copies, waits for them, and re-layouts  134 us (13%)
  blocking collectives  84.8 us (8%)
  other arithmetic  75.8 us (7%)
  between operations  31 us (3%)
  starting transfers between devices  10.8 us (1%)
    pallas_call x1, Pallas kernels, gather_weights(): pl.pallas_call(functools.partial(weights_kernel, n, rows), out_shape=jax....  153 us
    psum x1, waiting for transfers between devices, local(): lax.psum((jnp.concatenate([ga_qkv, ga_o], axis=0).reshape(4, rank, model_...  131 us
    pallas_call x2, Pallas kernels, scatter_seq(): pl.pallas_call(functools.partial(scatter_kernel, n), out_shape=jax.ShapeD...  115 us
    dot_general x20, matrix products, dot_f32(): return jnp.dot(a, b, preferred_element_type=jnp.float32)  73.3 us
    dot_general x20, matrix products, dot_nt(): return lax.dot_general(a, b, last_last, preferred_element_type=jnp.float32)  68.8 us
    pallas_call x2, Pallas kernels, gather_seq(): pl.pallas_call(functools.partial(gather_kernel, n, count), out_shape=tupl...  65.5 us
    psum x1, blocking collectives, local(): lax.psum((jnp.concatenate([ga_qkv, ga_o], axis=0).reshape(4, rank, model_...  41.7 us
    unnamed x329, local copies, waits for them, and re-layouts  30.6 us
  transfers between devices with their start and end apart: 9, of which 3 were waited for; matrix products, arithmetic and copies ran while one was open for 25% of the time, Pallas kernels for 29%

profile of v2, /device:TPU:0, one launch (start us, length us, event | category | flops | bytes accessed | tf_op | source)
XLA Modules:
  0.0 1062.2 jit_solution(2529844481332003573)
XLA Ops:
  13.8 6.3 all-to-all-start
  34.0 153.2 %gather_weights.1 = bf16[2,8,4,64,2560]{4,3,2,1,0:T(8,128)(2,1)} custom-call(bf16[2,4,64,2560]{3,2,1,0:T(8,128)(2,1)} %maximum_maximum_fusion.xa), custom_call_target="tpu_custom_call" | custom-call | bytes 262144000 | tf_op jit(solution)/shard_map/gather_weights/pallas_call | solution.py:419
  187.3 9.1 slice.233
  198.1 8.0 multiply_reduce_fusion.1
  207.3 6.0 fusion.110
  221.1 3.1 multiply_reduce_fusion.3
  225.3 3.5 fusion.200
  241.9 2.8 maximum_bitcast_fusion.2
  246.5 2.9 reshape.808
  251.0 24.8 %gather_seq.2 = bf16[8,128,1024]{2,1,0:T(8,128)(2,1)} custom-call(bf16[128,1024]{1,0:T(8,128)(2,1)} %pad_maximum_fusion.4.refs_0_), custom_call_target="tpu_custom_call" | custom-call | bytes 41943040 | tf_op jit(solution)/shard_map/gather_seq/pallas_call | solution.py:134
  289.2 37.0 %while.30 = (s32[]{:T(128)}, bf16[8,2,256,64]{2,3,1,0:T(8,128)(2,1)}, f32[8,2,256]{2,1,0:T(2,128)}, s32[2]{0:T(128)S(1)}, bf16[8,2,256,64]{2,3,1,0:T(8,128)(2,1)...) while((s32[]{:T(128)}, ...), condition=%wide.region_7.8_spmd.clone.clone, body=%wide.region_4.7_spmd.clone.clone.sunk | while | flops 69599744 | bytes 3891569 | solution.py:694
  328.2 15.3 %psum.98 = f32[2048]{0:T(1024)S(1)} all-reduce(f32[2048]{0:T(1024)S(1)} %multiply_add_fusion.4), channel_id=1, replica_groups=mesh['rows'=4,'seq'=8] {'seq'}, use_global_device_ids=true, to_apply=%region_22.23 | all-reduce | flops 2048 | bytes 16384 | tf_op jit(solution)/shard_map/psum | solution.py:641
  343.5 5.3 fusion.131
  348.8 5.1 multiply_reduce_fusion.2
  361.3 3.2 convert_element_type.364
  364.5 3.4 copy.99
  367.9 3.0 convert_element_type.366
  372.4 4.9 fusion.54
  393.6 40.7 %gather_seq.3 = bf16[8,128,2048]{2,1,0:T(8,128)(2,1)} custom-call(bf16[128,2048]{1,0:T(8,128)(2,1)} %multiply_convert_fusion.13.refs_0_), custom_call_target="tpu_custom_call" | custom-call | bytes 83886080 | tf_op jit(solution)/shard_map/gather_seq/pallas_call | solution.py:134
  434.8 4.2 convolution_convert_fusion.1
  454.1 15.4 %collective-permute-done.2 = bf16[8,64,1024]{2,1,0:T(8,128)(2,1)S(1)} collective-permute-done((bf16[8,64,1024]{2,1,0:T(8,128)(2,1)}, bf16[8,64,1024]{2,1,0:T(8,128)(2,1)S(1)}, u32[]{:S(2)}, u32[]{:S(2)}) %collective-permute-start.2) | collective-permute-done | bytes 1048608 | tf_op jit(solution)/shard_map/ppermute | solution.py:451
  469.6 3.2 collective-permute-done.3
  482.0 14.0 %all_gather.7 = f32[2,8192]{1,0:T(2,128)S(1)} all-gather(f32[2,1024]{1,0:T(2,128)S(1)} %pad_maximum_fusion.11), channel_id=1, replica_groups=mesh['rows'=4,'seq'=8] {'seq'}, dimensions={1}, use_global_device_ids=true | all-gather | bytes 73728 | tf_op jit(solution)/shard_map/all_gather | solution.py:870
  501.8 7.7 fusion.258
  509.6 2.9 multiply_add_fusion
  514.5 6.1 fusion.257
  520.6 3.5 fusion.94
  524.2 6.4 fusion.58
  534.1 6.1 multiply_reduce_fusion.7
  542.3 8.2 convolution_convert_fusion
  552.8 2.8 multiply_convert_fusion.3
  558.5 6.7 fusion.260
  565.2 6.7 fusion.261
  571.9 7.3 add_convert_fusion
  579.4 85.8 %scatter_seq.2 = f32[128,2048]{1,0:T(8,128)S(1)} custom-call(bf16[8,128,2048]{2,1,0:T(8,128)(2,1)S(1)} %bitcast.467), custom_call_target="tpu_custom_call" | custom-call | bytes 83886080 | tf_op jit(solution)/shard_map/scatter_seq/pallas_call | solution.py:250
  675.8 3.4 fusion.97
  681.9 13.9 %psum.108 = f32[2048]{0:T(1024)S(1)} all-reduce(f32[2048]{0:T(1024)S(1)} %div.239), channel_id=1, replica_groups=mesh['rows'=4,'seq'=8] {'seq'}, use_global_device_ids=true, to_apply=%region_43.44 | all-reduce | flops 2048 | bytes 16384 | tf_op jit(solution)/shard_map/psum | solution.py:730
  699.2 6.4 fusion.52
  711.5 62.4 %while.31 = (s32[]{:T(128)}, bf16[8,2,256,64]{2,3,1,0:T(8,128)(2,1)S(1)}, bf16[8,2,512,64]{2,3,1,0:T(8,128)(2,1)}, bf16[8,2,512,64]{2,3,1,0:T(8,128)(2,1)}, s32[...) while((s32[]{:T(128)}, ...), condition=%wide.region_27.28_spmd.clone.clone, body=%wide.region_25.27_spmd.clone.clone.sunk | while | flops 170623488 | bytes 9459081 | solution.py:812
  774.7 2.7 copy.111
  780.3 2.9 copy.126
  793.9 28.8 %scatter_seq.3 = f32[128,1024]{1,0:T(8,128)S(1)} custom-call(bf16[8,128,1024]{2,1,0:T(8,128)(2,1)S(1)} %bitcast.468), custom_call_target="tpu_custom_call" | custom-call | bytes 41943040 | tf_op jit(solution)/shard_map/scatter_seq/pallas_call | solution.py:250
  831.6 6.0 fusion.51
  842.0 3.6 fusion.139
  850.0 7.2 fusion.112
  860.8 41.7 %all-reduce.3 = (f32[2048]{0:T(1024)}, f32[2,512]{1,0:T(2,128)}, f32[2048]{0:T(1024)}, f32[2048]{0:T(1024)}) all-reduce(f32[2048]{0:T(1024)} %slice.328, f32[2,512]{1,0:T(2,128)} %reshape.835, f32[2048]{0:T(1024)} %get-tuple-element.440, f32[2048]{0:T(1024)S(1)} %copy-done.100), channel_id=1, replica_groups=mesh['rows'=4,'seq'=8] {'rows','seq'}, use_global_device_ids=true, to_apply=%region_34.35 | all-reduce | flops 7168 | bytes 57344 | tf_op jit(solution)/shard_map/psum | solution.py:851
  904.2 7.1 fusion.238
  913.2 131.2 %all-reduce.7.cloned.1.call-done = (f32[4,16,2048]{2,1,0:T(8,128)}, f32[2,16,2048]{2,1,0:T(8,128)}, f32[2,16,512]{2,1,0:T(8,128)}, f32[2,16,2048]{2,1,0:T(8,128)...) async-done(((f32[4,16,2048]{2,1,0:T(8,128)}, f32[2,16,2048]{2,1,0:T(8,128)}, f32[2,16,512]{2,1,0:T(8,128)}, ...) | async-done | bytes 2883600 | tf_op jit(solution)/shard_map/psum | solution.py:851
  (687 shorter events, 288.1 us)
Async XLA Ops:
  7.2 427.1 %copy-start = (f32[2,16,8192]{2,1,0:T(8,128)S(1)}, f32[2,16,8192]{2,1,0:T(8,128)}, u32[]{:S(2)}) copy-start(f32[2,16,8192]{2,1,0:T(8,128)} %param.39) | copy-start | bytes 3145732
  7.2 513.4 %all-gather.2.cloned.1.call-start = ((), (), s32[]{:S(2)}) async-start(), calls=%async_computation.5 | async-start | bytes 4718592 | tf_op jit(solution)/shard_map/all_gather | solution.py:705
  13.8 366.9 %all-to-all-start = ((bf16[8,2,64,1024]{3,2,1,0:T(8,128)(2,1)}), bf16[8,2,64,1024]{3,2,1,0:T(8,128)(2,1)S(1)}, u32[]{:S(2)}, u32[]{:S(2)}) async-start(bf16[8,2,64,1024]{3,2,1,0:T(8,128)(2,1)} %copy.100), calls=%async_computation | async-start | bytes 4194304 | tf_op jit(solution)/shard_map/all_to_all | solution.py:441
  20.1 655.7 %reduce-scatter.5.cloned.1.call-start = ((), (), s32[]{:S(2)}) async-start(), calls=%async_computation.4 | async-start | bytes 73728 | tf_op jit(solution)/shard_map/reduce_scatter | solution.py:724
  22.9 183.6 %copy-start.27 = (bf16[3,16,2048]{2,1,0:T(8,128)(2,1)}, bf16[3,16,2048]{2,1,0:T(8,128)(2,1)S(1)}, u32[]{:S(2)}) copy-start(bf16[3,16,2048]{2,1,0:T(8,128)(2,1)S(1)} %slice.478) | copy-start | bytes 589828
  25.5 190.3 %copy-start.78 = (bf16[16,512]{1,0:T(8,128)(2,1)}, bf16[16,512]{1,0:T(8,128)(2,1)S(1)}, u32[]{:S(2)}) copy-start(bf16[16,512]{1,0:T(8,128)(2,1)S(1)} %get-tuple-element.496) | copy-start | bytes 49156
  25.5 190.3 %copy-start.80 = (bf16[16,512]{1,0:T(8,128)(2,1)}, bf16[16,512]{1,0:T(8,128)(2,1)S(1)}, u32[]{:S(2)}) copy-start(bf16[16,512]{1,0:T(8,128)(2,1)S(1)} %get-tuple-element.497) | copy-start | bytes 49156
  26.5 189.3 %copy-start.54 = (bf16[16,2048]{1,0:T(8,128)(2,1)}, bf16[16,2048]{1,0:T(8,128)(2,1)S(1)}, u32[]{:S(2)}) copy-start(bf16[16,2048]{1,0:T(8,128)(2,1)S(1)} %get-tuple-element.478) | copy-start | bytes 196612
  26.5 350.7 %copy-start.35 = (bf16[1,16,2048]{2,1,0:T(8,128)(2,1)}, bf16[1,16,2048]{2,1,0:T(8,128)(2,1)S(1)}, u32[]{:S(2)}) copy-start(bf16[1,16,2048]{2,1,0:T(8,128)(2,1)S(1)} %get-tuple-element.477) | copy-start | bytes 196612
  28.9 186.9 %copy-start.87 = (bf16[128,48]{0,1:T(8,128)(2,1)}, bf16[128,48]{0,1:T(8,128)(2,1)S(1)}, u32[]{:S(2)}) copy-start(bf16[128,48]{0,1:T(8,128)(2,1)S(1)} %convolution_convert_fusion.3) | copy-start | bytes 36868
  224.3 296.3 %copy-start.48 = (bf16[16,2048]{1,0:T(8,128)(2,1)}, bf16[16,2048]{1,0:T(8,128)(2,1)S(1)}, u32[]{:S(2)}) copy-start(bf16[16,2048]{1,0:T(8,128)(2,1)S(1)} %convert_element_type.388) | copy-start | bytes 196612
  326.2 22.6 %copy-start.112 = (s32[64]{0:T(128)}, s32[64]{0:T(128)S(1)}, u32[]{:S(2)}) copy-start(s32[64]{0:T(128)S(1)} %get-tuple-element.781) | copy-start | bytes 772
  326.2 22.6 %copy-start.114 = (s32[2]{0:T(128)}, s32[2]{0:T(128)S(1)}, u32[]{:S(2)}) copy-start(s32[2]{0:T(128)S(1)} %get-tuple-element.782) | copy-start | bytes 28
  326.4 22.4 %copy-start.50 = (f32[16,2048]{1,0:T(8,128)}, f32[16,2048]{1,0:T(8,128)S(1)}, u32[]{:S(2)}) copy-start(f32[16,2048]{1,0:T(8,128)S(1)} %fusion.173) | copy-start | bytes 393220
  354.6 22.7 %copy-start.103 = (f32[2048]{0:T(1024)}, f32[2048]{0:T(1024)S(1)}, u32[]{:S(2)}) copy-start(f32[2048]{0:T(1024)S(1)} %get-tuple-element.524) | copy-start | bytes 24580
  378.7 55.5 %copy-start.152 = (f32[128]{0:T(128)}, f32[128]{0:T(128)S(1)}, u32[]{:S(2)}) copy-start(f32[128]{0:T(128)S(1)} %get-tuple-element.443) | copy-start | bytes 1540
  378.7 55.5 %copy-start.145 = (f32[128]{0:T(128)}, f32[128]{0:T(128)S(1)}, u32[]{:S(2)}) copy-start(f32[128]{0:T(128)S(1)} %fusion.220) | copy-start | bytes 1540
  382.3 59.3 %collective-permute-start = (bf16[8,2,64,1024]{3,2,0,1:T(8,128)(2,1)}, bf16[8,2,64,1024]{3,2,0,1:T(8,128)(2,1)}, u32[]{:S(2)}, u32[]{:S(2)}) collective-permute-start(bf16[8,2,64,1024]{3,2,0,1:T(8,128)(2,1)} %copy.101), channel_id=1, source_target_pairs={{0,8},{8,0},{16,24},{24,16},{1,9},{9,1},{17,25},{25,17},{2,10},{10... | collective-permute-start | bytes 6291464 | tf_op jit(solution)/shard_map/ppermute | solution.py:444
  384.1 60.9 %collective-permute-start.1 = (bf16[8,2,64,1024]{3,2,0,1:T(8,128)(2,1)}, bf16[8,2,64,1024]{3,2,0,1:T(8,128)(2,1)}, u32[]{:S(2)}, u32[]{:S(2)}) collective-permute-start(bf16[8,2,64,1024]{3,2,0,1:T(8,128)(2,1)} %copy.101), channel_id=1, source_target_pairs={{0,16},{8,24},{16,0},{24,8},{1,17},{9,25},{17,1},{25,9},{2,18},{10... | collective-permute-start | bytes 6291464 | tf_op jit(solution)/shard_map/ppermute | solution.py:445
  386.1 285.0 %copy-start.39 = (bf16[2,16,2048]{2,1,0:T(8,128)(2,1)}, bf16[2,16,2048]{2,1,0:T(8,128)(2,1)S(1)}, u32[]{:S(2)}) copy-start(bf16[2,16,2048]{2,1,0:T(8,128)(2,1)S(1)} %convert_element_type.375) | copy-start | bytes 393220
  443.9 25.6 %collective-permute-start.2 = (bf16[8,64,1024]{2,1,0:T(8,128)(2,1)}, bf16[8,64,1024]{2,1,0:T(8,128)(2,1)S(1)}, u32[]{:S(2)}, u32[]{:S(2)}) collective-permute-start(bf16[8,64,1024]{2,1,0:T(8,128)(2,1)} %slice_bitcast_fusion.9), channel_id=1, source_target_pairs={{0,16},{8,24},{16,0},{24,8},{1,17},{9,25},{17,1},{25,9},{2,18},{10... | collective-permute-start | bytes 3145736 | tf_op jit(solution)/shard_map/ppermute | solution.py:451
  447.3 25.5 %collective-permute-start.3 = (bf16[8,64,1024]{2,1,0:T(8,128)(2,1)}, bf16[8,64,1024]{2,1,0:T(8,128)(2,1)}, u32[]{:S(2)}, u32[]{:S(2)}) collective-permute-start(bf16[8,64,1024]{2,1,0:T(8,128)(2,1)} %slice_bitcast_fusion.8), channel_id=1, source_target_pairs={{0,8},{8,0},{16,24},{24,16},{1,9},{9,1},{17,25},{25,17},{2,10},{10... | collective-permute-start | bytes 3145736 | tf_op jit(solution)/shard_map/ppermute | solution.py:452
  478.9 22.2 %copy-start.148 = (f32[1,2]{0,1:T(2,128)S(1)}, f32[1,2]{0,1:T(2,128)}, u32[]{:S(2)}) copy-start(f32[1,2]{0,1:T(2,128)} %copy.122) | copy-start | bytes 28
  478.9 22.2 %copy-start.149 = (f32[1,2]{0,1:T(2,128)S(1)}, f32[1,2]{0,1:T(2,128)}, u32[]{:S(2)}) copy-start(f32[1,2]{0,1:T(2,128)} %copy.116) | copy-start | bytes 28
  481.4 28.2 %copy-start.123 = (f32[1024]{0:T(1024)}, f32[1024]{0:T(1024)S(1)}, u32[]{:S(2)}) copy-start(f32[1024]{0:T(1024)S(1)} %get-tuple-element.503) | copy-start | bytes 12292
  481.4 28.2 %copy-start.125 = (f32[1024]{0:T(1024)}, f32[1024]{0:T(1024)S(1)}, u32[]{:S(2)}) copy-start(f32[1024]{0:T(1024)S(1)} %get-tuple-element.528) | copy-start | bytes 12292
  542.3 133.5 %reduce-scatter.3.cloned.1.call-start = ((), (), s32[]{:S(2)}) async-start(), calls=%async_computation.3 | async-start | bytes 4718592 | tf_op jit(solution)/shard_map/reduce_scatter | solution.py:723
  550.6 493.8 %all-reduce.7.cloned.1.call-start = ((), (), s32[]{:S(2)}) async-start(), calls=%async_computation.6 | async-start | bytes 5767168 | tf_op jit(solution)/shard_map/psum | solution.py:851
  579.3 86.0 %copy-start.124 = (f32[1024]{0:T(1024)S(1)}, f32[1024]{0:T(1024)}, u32[]{:S(2)}) copy-start(f32[1024]{0:T(1024)} %copy-done.123) | copy-start | bytes 12292
  579.3 86.0 %copy-start.126 = (f32[1024]{0:T(1024)S(1)}, f32[1024]{0:T(1024)}, u32[]{:S(2)}) copy-start(f32[1024]{0:T(1024)} %copy-done.125) | copy-start | bytes 12292
  579.3 86.0 %copy-start.128 = (f32[1024]{0:T(1024)S(1)}, f32[1024]{0:T(1024)}, u32[]{:S(2)}) copy-start(f32[1024]{0:T(1024)} %copy-done.127) | copy-start | bytes 12292
  579.3 86.0 %copy-start.130 = (f32[1024]{0:T(1024)S(1)}, f32[1024]{0:T(1024)}, u32[]{:S(2)}) copy-start(f32[1024]{0:T(1024)} %copy-done.129) | copy-start | bytes 12292
  579.3 86.0 %copy-start.140 = (f32[1024]{0:T(1024)S(1)}, f32[1024]{0:T(1024)}, u32[]{:S(2)}) copy-start(f32[1024]{0:T(1024)} %get-tuple-element.338) | copy-start | bytes 12292
  579.3 86.0 %copy-start.141 = (f32[1024]{0:T(1024)S(1)}, f32[1024]{0:T(1024)}, u32[]{:S(2)}) copy-start(f32[1024]{0:T(1024)} %get-tuple-element.339) | copy-start | bytes 12292
  579.3 87.0 %copy-start.26 = (bf16[1024,1024]{1,0:T(8,128)(2,1)S(1)}, bf16[1024,1024]{1,0:T(8,128)(2,1)}, u32[]{:S(2)}) copy-start(bf16[1024,1024]{1,0:T(8,128)(2,1)} %get-tuple-element.450) | copy-start | bytes 6291460
  579.3 87.0 %copy-start.53 = (f32[16,1024]{1,0:T(8,128)S(1)}, f32[16,1024]{1,0:T(8,128)}, u32[]{:S(2)}) copy-start(f32[16,1024]{1,0:T(8,128)} %fusion.187) | copy-start | bytes 196612
  579.4 87.0 %copy-start.69 = (bf16[1024,16]{0,1:T(8,128)(2,1)S(1)}, bf16[1024,16]{0,1:T(8,128)(2,1)}, u32[]{:S(2)}) copy-start(bf16[1024,16]{0,1:T(8,128)(2,1)} %convolution_convert_fusion.1) | copy-start | bytes 98308
  579.4 87.4 %copy-start.14 = (bf16[1024,1024]{1,0:T(8,128)(2,1)S(1)}, bf16[1024,1024]{1,0:T(8,128)(2,1)}, u32[]{:S(2)}) copy-start(bf16[1024,1024]{1,0:T(8,128)(2,1)} %copy-done.13) | copy-start | bytes 6291460
  579.4 87.4 %copy-start.72 = (f32[16,1024]{1,0:T(8,128)S(1)}, f32[16,1024]{1,0:T(8,128)}, u32[]{:S(2)}) copy-start(f32[16,1024]{1,0:T(8,128)} %get-tuple-element.519) | copy-start | bytes 196612
  579.4 87.4 %copy-start.76 = (bf16[1024,16]{0,1:T(8,128)(2,1)S(1)}, bf16[1024,16]{0,1:T(8,128)(2,1)}, u32[]{:S(2)}) copy-start(bf16[1024,16]{0,1:T(8,128)(2,1)} %convolution_convert_fusion.2) | copy-start | bytes 98308
  674.8 22.5 %copy-start.62 = (f32[16,2048]{1,0:T(8,128)S(1)}, f32[16,2048]{1,0:T(8,128)}, u32[]{:S(2)}) copy-start(f32[16,2048]{1,0:T(8,128)} %param.42) | copy-start | bytes 393220
  674.8 23.1 %copy-start.96 = (f32[2048]{0:T(1024)S(1)}, f32[2048]{0:T(1024)}, u32[]{:S(2)}) copy-start(f32[2048]{0:T(1024)} %copy-done.95) | copy-start | bytes 24580
  793.9 30.1 %copy-start.29 = (f32[128,3072]{1,0:T(8,128)S(1)}, f32[128,3072]{1,0:T(8,128)}, u32[]{:S(2)}) copy-start(f32[128,3072]{1,0:T(8,128)} %get-tuple-element.515) | copy-start | bytes 4718596
  850.0 52.6 %copy-start.32 = (bf16[2,64,2048]{2,1,0:T(8,128)(2,1)S(1)}, bf16[2,64,2048]{2,1,0:T(8,128)(2,1)}, u32[]{:S(2)}) copy-start(bf16[2,64,2048]{2,1,0:T(8,128)(2,1)} %param.26) | copy-start | bytes 1572868
  850.0 52.5 %copy-start.51 = (f32[16,2048]{1,0:T(8,128)S(1)}, f32[16,2048]{1,0:T(8,128)}, u32[]{:S(2)}) copy-start(f32[16,2048]{1,0:T(8,128)} %fusion.200) | copy-start | bytes 393220
  850.0 52.5 %copy-start.63 = (f32[16,2048]{1,0:T(8,128)S(1)}, f32[16,2048]{1,0:T(8,128)}, u32[]{:S(2)}) copy-start(f32[16,2048]{1,0:T(8,128)} %get-tuple-element.518) | copy-start | bytes 393220
  850.0 52.5 %copy-start.94 = (f32[2048]{0:T(1024)S(1)}, f32[2048]{0:T(1024)}, u32[]{:S(2)}) copy-start(f32[2048]{0:T(1024)} %div.225) | copy-start | bytes 24580
  911.9 143.6 %copy-start.1 = (f32[2,16,8192]{2,1,0:T(8,128)S(1)}, f32[2,16,8192]{2,1,0:T(8,128)}, u32[]{:S(2)}) copy-start(f32[2,16,8192]{2,1,0:T(8,128)} %param.39) | copy-start | bytes 3145732
  (120 other events, 770.5 us)
Sparse Core Ops, SparseCore 0:
  9.6 88.9 all-gather.1
  542.4 30.6 reduce-scatter.4
  575.5 81.8 reduce-scatter.2
  904.3 140.0 all-reduce.6

commit v3 on v2

v3 whole, which is shorter than its diff:
```python
import functools

import jax
import jax.numpy as jnp
from jax import lax
from jax.experimental import pallas as pl
from jax.experimental.pallas import tpu as pltpu
from jax.sharding import PartitionSpec as P

HEADS = 32
KV_HEADS = 8
HEAD_DIM = 64
ADAPTER_RANK = 16
ALPHA = 32
SCALE = ALPHA / ADAPTER_RANK
TILE = 512

highest = lax.Precision.HIGHEST
last_last = (((1,), (1,)), ((), ()))
first_first = (((0,), (0,)), ((), ()))

def dot_f32(a, b):
    return jnp.dot(a, b, preferred_element_type=jnp.float32)


def dot_nt(a, b):
    return lax.dot_general(a, b, last_last, preferred_element_type=jnp.float32)


def dot_tn(a, b):
    return lax.dot_general(a, b, first_first, preferred_element_type=jnp.float32)


def unit_rms(v):
    return lax.rsqrt(jnp.mean(v * v, axis=-1, keepdims=True) + 1e-05)


def rms_back(v, gain, upstream):
    r = unit_rms(v)
    scaled = gain * upstream
    return r * scaled - v * (r * r * r) * jnp.mean(scaled * v, axis=-1, keepdims=True)


def turn(z, cosine, sine):
    width = z.shape[1]
    lane = lax.broadcasted_iota(jnp.int32, z.shape, 1)
    half = HEAD_DIM // 2
    other = jnp.where(
        lax.rem(lane, HEAD_DIM) < half, -pltpu.roll(z, width - half, 1), pltpu.roll(z, half, 1)
    )
    copies = width // cosine.shape[1]
    return z * jnp.tile(cosine, (1, copies)) + other * jnp.tile(sine, (1, copies))


def column_norms(w, a, b_wide, cross):
    ones = jnp.ones((16, w.shape[0]), jnp.bfloat16)
    squares = dot_f32(ones, w * w)[:1]
    gram_b = jnp.dot(dot_nt(a, a), b_wide, precision=highest, preferred_element_type=jnp.float32)
    squares = squares + 2.0 * SCALE * jnp.sum(b_wide * cross, axis=0, keepdims=True)
    squares = squares + SCALE * SCALE * jnp.sum(b_wide * gram_b, axis=0, keepdims=True)
    return jnp.sqrt(squares + 1e-06), cross + SCALE * gram_b


def project_kernel(kv_tiles, x_ref, gain_ref, a_ref, w_ref, b_ref, m_ref, cos_ref, sin_ref,
                   u_ref, before_ref, q_ref, kv_ref, n_ref, cross_ref):
    j = pl.program_id(0)
    q_tiles = kv_tiles[0]

    @pl.when(j == 0)
    def _():
        v = x_ref[...].astype(jnp.float32)
        u_ref[...] = (v * unit_rms(v) * gain_ref[...]).astype(jnp.bfloat16)

    a = a_ref[0].astype(jnp.bfloat16)
    b = b_ref[...].astype(jnp.bfloat16)
    b_wide = b.astype(jnp.float32)
    w = w_ref[0]
    rows = u_ref.shape[0]

    @pl.when(j < kv_tiles[1])
    def _():
        both = dot_f32(jnp.concatenate([u_ref[...], a], axis=0), w)
        norm, cross = column_norms(w, a, b_wide, both[rows:])
        n_ref[...] = norm
        cross_ref[...] = cross
        inner = dot_nt(u_ref[...], a).astype(jnp.bfloat16)
        before = both[:rows] + SCALE * dot_f32(inner, b)
        before_ref[...] = before
        y = before * (m_ref[...] / norm)

        @pl.when(j < q_tiles)
        def _():
            q_ref[...] = turn(y, cos_ref[...], sin_ref[...]).astype(jnp.bfloat16)

        @pl.when(j == q_tiles)
        def _():
            kv_ref[...] = turn(y, cos_ref[...], sin_ref[...]).astype(jnp.bfloat16)

        @pl.when(j > q_tiles)
        def _():
            kv_ref[...] = y.astype(jnp.bfloat16)

    @pl.when(j >= kv_tiles[1])
    def _():
        norm, cross = column_norms(w, a, b_wide, dot_f32(a, w))
        n_ref[...] = norm
        cross_ref[...] = cross


def project_qkv(x, gain, a, weights, b, m, cosine, sine):
    rows, width = x.shape
    cols = b.shape[1]
    per_half = weights.shape[2] // TILE
    q_tiles = width // TILE
    k_cols = weights.shape[2] - width
    kv_tiles = (q_tiles, q_tiles + 2 * k_cols // TILE)
    last = kv_tiles[1] - 1
    full = lambda shape: pl.BlockSpec(shape, lambda j: (0,) * len(shape))
    col = lambda height: pl.BlockSpec((height, TILE), lambda j: (0, j))
    which = lambda j: jnp.where(j < q_tiles, 0, jnp.where(j > last, 3, 1 + j - q_tiles))
    f32, low = jnp.float32, jnp.bfloat16
    return pl.pallas_call(
        functools.partial(project_kernel, kv_tiles),
        out_shape=(
            jax.ShapeDtypeStruct((rows, width), low),
            jax.ShapeDtypeStruct((rows, width + 2 * k_cols), f32),
            jax.ShapeDtypeStruct((rows, width), low),
            jax.ShapeDtypeStruct((rows, 2 * k_cols), low),
            jax.ShapeDtypeStruct((1, cols), f32),
            jax.ShapeDtypeStruct((16, cols), f32),
        ),
        grid=(cols // TILE,),
        in_specs=[
            full((rows, width)),
            full((1, width)),
            pl.BlockSpec((1, 16, width), lambda j: (which(j), 0, 0)),
            pl.BlockSpec((1, width, TILE), lambda j: (j // per_half, 0, j % per_half)),
            col(16),
            col(1),
            full(cosine.shape),
            full(sine.shape),
        ],
        out_specs=(
            full((rows, width)),
            pl.BlockSpec((rows, TILE), lambda j: (0, jnp.minimum(j, last))),
            pl.BlockSpec((rows, TILE), lambda j: (0, jnp.minimum(j, q_tiles - 1))),
            pl.BlockSpec((rows, TILE), lambda j: (0, jnp.clip(j - q_tiles, 0, last - q_tiles))),
            col(1),
            col(16),
        ),
        compiler_params=pltpu.CompilerParams(vmem_limit_bytes=40 << 20),
        cost_estimate=pl.CostEstimate(
            flops=2 * rows * width * cols, transcendentals=0, bytes_accessed=2 * width * cols
        ),
        name="project_qkv",
    )(x, gain, a, weights, b, m, cosine, sine)


def out_kernel(att_ref, a_ref, w_ref, b_ref, m_ref, n_ref, x_ref, gain_ref, before_ref, x1_ref, u2_ref):
    t = pl.program_id(0)
    a = a_ref[...].astype(jnp.bfloat16)
    b = b_ref[...].astype(jnp.bfloat16)
    inner = dot_nt(att_ref[...], a).astype(jnp.bfloat16)
    before = dot_f32(att_ref[...], w_ref[0]) + SCALE * dot_f32(inner, b)
    before_ref[...] = before
    x1_ref[:, pl.ds(pl.multiple_of(t * TILE, TILE), TILE)] = (
        x_ref[...].astype(jnp.float32) + before * (m_ref[...] / n_ref[...])
    )

    @pl.when(t == pl.num_programs(0) - 1)
    def _():
        v = x1_ref[...]
        u2_ref[...] = (v * unit_rms(v) * gain_ref[...]).astype(jnp.bfloat16)


def project_out(att, a, weights, b, m, norms, x, gain):
    rows, width = att.shape
    tiles = width // TILE
    skip = (weights.shape[2] - width) // TILE
    full = lambda shape: pl.BlockSpec(shape, lambda t: (0,) * len(shape))
    col = lambda height: pl.BlockSpec((height, TILE), lambda t: (0, t))
    f32 = jnp.float32
    return pl.pallas_call(
        out_kernel,
        out_shape=(
            jax.ShapeDtypeStruct((rows, width), f32),
            jax.ShapeDtypeStruct((rows, width), f32),
            jax.ShapeDtypeStruct((rows, width), jnp.bfloat16),
        ),
        grid=(tiles,),
        in_specs=[
            full((rows, width)),
            full((16, width)),
            pl.BlockSpec((1, width, TILE), lambda t: (1, 0, skip + t)),
            col(16),
            col(1),
            col(1),
            col(rows),
            full((1, width)),
        ],
        out_specs=(col(rows), full((rows, width)), full((rows, width))),
        compiler_params=pltpu.CompilerParams(vmem_limit_bytes=40 << 20),
        cost_estimate=pl.CostEstimate(
            flops=2 * rows * width * width, transcendentals=0, bytes_accessed=2 * width * width
        ),
        name="project_out",
    )(att, a, weights, b, m, norms, x, gain)


def out_back_kernel(in_ref, x1_ref, gain_ref, gy_ref, before_ref, att_ref, a_ref, b_ref, m_ref, n_ref, cross_ref,
                    w_ref, gx_ref, gatt_ref, ga_ref, gb_ref, gm_ref, lhs, gi, tail):
    t = pl.program_id(0)
    rows, width = gx_ref.shape
    low = jnp.bfloat16
    a = a_ref[...].astype(low)

    @pl.when(t == 0)
    def _():
        gx = gy_ref[...].astype(jnp.float32) + rms_back(x1_ref[...], gain_ref[...], in_ref[...])
        gx_ref[...] = gx
        norm = n_ref[...]
        gb = (gx * (m_ref[...] / norm)).astype(low)
        lhs[:rows] = gb
        b = b_ref[...].astype(low)
        b_wide = b.astype(jnp.float32)
        gi[...] = (SCALE * dot_nt(gb, b)).astype(low)
        gm = jnp.sum(gx * before_ref[...], axis=0, keepdims=True) / norm
        gm_ref[...] = gm
        c = -gm * m_ref[...] / (norm * norm)
        weighted = b_wide * c
        lhs[rows:] = weighted.astype(low)
        tail[...] = lax.dot_general(
            weighted, b_wide, last_last, precision=highest, preferred_element_type=jnp.float32
        )
        inner = dot_nt(att_ref[...], a).astype(low)
        gb_ref[...] = SCALE * dot_tn(inner, gb) + SCALE * c * cross_ref[...]

    span = pl.ds(pl.multiple_of(t * TILE, TILE), TILE)
    a_tile = a_ref[:, span].astype(low)
    gi_low = gi[...]
    back = dot_nt(lhs[...], w_ref[0, :, w_ref.shape[2] - width :])
    gatt_ref[...] = (back[:rows] + dot_f32(gi_low, a_tile)).astype(low)
    spread = back[rows:] + SCALE * jnp.dot(
        tail[...], a_tile.astype(jnp.float32), precision=highest, preferred_element_type=jnp.float32
    )
    ga_ref[...] = dot_tn(gi_low, att_ref[:, span]) + SCALE * spread


def out_back(in_grad, x1, gain, gy, before, att, a, b, m, norms, cross, weights):
    rows, width = x1.shape
    tiles = width // TILE
    full = lambda shape: pl.BlockSpec(shape, lambda t: (0,) * len(shape))
    col = lambda height: pl.BlockSpec((height, TILE), lambda t: (0, t))
    f32, low = jnp.float32, jnp.bfloat16
    wide = full((rows, width))
    return pl.pallas_call(
        out_back_kernel,
        out_shape=(
            jax.ShapeDtypeStruct((rows, width), f32),
            jax.ShapeDtypeStruct((rows, width), low),
            jax.ShapeDtypeStruct((16, width), f32),
            jax.ShapeDtypeStruct((16, width), f32),
            jax.ShapeDtypeStruct((1, width), f32),
        ),
        grid=(tiles,),
        in_specs=[wide, wide, full((1, width)), wide, wide, wide, full((16, width)), full((16, width)),
                  full((1, width)), full((1, width)), full((16, width)),
                  pl.BlockSpec((1, TILE, weights.shape[2]), lambda t: (1, t, 0))],
        out_specs=(wide, col(rows), col(16), full((16, width)), full((1, width))),
        scratch_shapes=[
            pltpu.VMEM((rows + 16, width), low),
            pltpu.VMEM((rows, 16), low),
            pltpu.VMEM((16, 16), f32),
        ],
        compiler_params=pltpu.CompilerParams(vmem_limit_bytes=48 << 20),
        cost_estimate=pl.CostEstimate(
            flops=2 * rows * width * width, transcendentals=0, bytes_accessed=2 * width * width
        ),
        name="out_back",
    )(in_grad, x1, gain, gy, before, att, a, b, m, norms, cross, weights)


def qkv_back_kernel(gq_ref, gkv_ref, cos_ref, sin_ref, before_ref, u_ref, a_ref, b_ref, m_ref, n_ref, cross_ref,
                    x_ref, gain_ref, gx_ref, w0_ref, w1_ref,
                    out_ref, ga_ref, gb_ref, gm_ref, lhs0, lhs1, gi, tail):
    t = pl.program_id(0)
    rows, width = gx_ref.shape
    low = jnp.bfloat16
    k_cols = w1_ref.shape[2]
    bounds = [(0, width), (width, width + k_cols), (width + k_cols, width + 2 * k_cols)]

    @pl.when(t == 0)
    def _():
        cosine, sine = cos_ref[...], -sin_ref[...]
        k_parts = [gkv_ref[:, 256 * j : 256 * j + 128] for j in range(k_cols // 128)]
        v_parts = [gkv_ref[:, 256 * j + 128 : 256 * j + 256] for j in range(k_cols // 128)]
        rounded = lambda z: z.astype(low).astype(jnp.float32)
        ups = [
            turn(gq_ref[...].astype(jnp.float32), cosine, sine),
            turn(rounded(jnp.concatenate(k_parts, axis=1)), cosine, sine),
            rounded(jnp.concatenate(v_parts, axis=1)),
        ]
        lhs0[rows:] = jnp.zeros_like(lhs0[rows:])
        lhs1[rows:] = jnp.zeros_like(lhs1[rows:])
        for p, (start, stop) in enumerate(bounds):
            g, norm, m = ups[p], n_ref[:, start:stop], m_ref[:, start:stop]
            a = a_ref[p].astype(low)
            b = b_ref[:, start:stop].astype(low)
            b_wide = b.astype(jnp.float32)
            gb = (g * (m / norm)).astype(low)
            gm = jnp.sum(g * before_ref[:, start:stop], axis=0, keepdims=True) / norm
            gm_ref[:, start:stop] = gm
            c = -gm * m / (norm * norm)
            weighted = b_wide * c
            gi[:, 16 * p : 16 * p + 16] = (SCALE * dot_nt(gb, b)).astype(low)
            tail[16 * p : 16 * p + 16] = lax.dot_general(
                weighted, b_wide, last_last, precision=highest, preferred_element_type=jnp.float32
            )
            inner = dot_nt(u_ref[...], a).astype(low)
            gb_ref[:, start:stop] = SCALE * dot_tn(inner, gb) + SCALE * c * cross_ref[:, start:stop]
            lhs, at = (lhs1, 0) if p == 2 else (lhs0, start)
            lhs[:rows, at : at + stop - start] = gb
            lhs[rows + 16 * p : rows + 16 * p + 16, at : at + stop - start] = weighted.astype(low)

    span = pl.ds(pl.multiple_of(t * TILE, TILE), TILE)
    back = dot_nt(lhs0[...], w0_ref[0]) + dot_nt(lhs1[...], w1_ref[0])
    grad_in = back[:rows]
    for p in range(3):
        a_tile = a_ref[p, :, span].astype(low)
        gi_p = gi[:, 16 * p : 16 * p + 16]
        grad_in = grad_in + dot_f32(gi_p, a_tile)
        spread = back[rows + 16 * p : rows + 16 * p + 16] + SCALE * jnp.dot(
            tail[16 * p : 16 * p + 16], a_tile.astype(jnp.float32), precision=highest,
            preferred_element_type=jnp.float32,
        )
        ga_ref[p] = dot_tn(gi_p, u_ref[:, span]) + SCALE * spread
    out_ref[:, span] = grad_in

    @pl.when(t == pl.num_programs(0) - 1)
    def _():
        v = x_ref[...].astype(jnp.float32)
        out_ref[...] = gx_ref[...] + rms_back(v, gain_ref[...], out_ref[...])


def qkv_back(gq, gkv, cosine, sine, before, u, a, b, m, norms, cross, x, gain, gx, weights):
    rows, width = gx.shape
    cols = before.shape[1]
    k_cols = (cols - width) // 2
    tiles = width // TILE
    full = lambda shape: pl.BlockSpec(shape, lambda t: (0,) * len(shape))
    f32, low = jnp.float32, jnp.bfloat16
    wide = full((rows, width))
    return pl.pallas_call(
        qkv_back_kernel,
        out_shape=(
            jax.ShapeDtypeStruct((rows, width), f32),
            jax.ShapeDtypeStruct((3, 16, width), f32),
            jax.ShapeDtypeStruct((16, cols), f32),
            jax.ShapeDtypeStruct((1, cols), f32),
        ),
        grid=(tiles,),
        in_specs=[wide, full(gkv.shape), full(cosine.shape), full(sine.shape), full((rows, cols)), wide,
                  full((3, 16, width)), full((16, cols)), full((1, cols)), full((1, cols)), full((16, cols)),
                  wide, full((1, width)), wide,
                  pl.BlockSpec((1, TILE, width + k_cols), lambda t: (0, t, 0)),
                  pl.BlockSpec((1, TILE, k_cols), lambda t: (1, t, 0))],
        out_specs=(wide, pl.BlockSpec((3, 16, TILE), lambda t: (0, 0, t)), full((16, cols)), full((1, cols))),
        scratch_shapes=[
            pltpu.VMEM((rows + 48, width + k_cols), low),
            pltpu.VMEM((rows + 48, k_cols), low),
            pltpu.VMEM((rows, 48), low),
            pltpu.VMEM((48, 16), f32),
        ],
        compiler_params=pltpu.CompilerParams(vmem_limit_bytes=48 << 20),
        cost_estimate=pl.CostEstimate(
            flops=2 * rows * width * cols, transcendentals=0, bytes_accessed=2 * width * cols
        ),
        name="qkv_back",
    )(gq, gkv, cosine, sine, before, u, a, b, m, norms, cross, x, gain, gx, weights, weights)

MESH = pl.DeviceIdType.MESH


def place_in_seq():
    s = lax.axis_index("seq")
    return s, s // 2, lax.rem(s, 2)


def greet(nc, q, s):
    barrier = pltpu.get_barrier_semaphore()

    def signal(target):
        pl.semaphore_signal(barrier, inc=1, device_id={"seq": target}, device_id_type=MESH)

    sibling = s + 1 - 2 * lax.rem(s, 2)
    signal(sibling)
    pl.when(q > 0)(lambda: signal(s - 2))
    pl.when(q < nc - 1)(lambda: signal(s + 2))
    pl.semaphore_wait(barrier, 1 + jnp.where(q > 0, 1, 0) + jnp.where(q < nc - 1, 1, 0))
    return sibling


def gather_kernel(n, count, *refs):
    nc = n // 2
    xs, outs = refs[:count], refs[count : 2 * count]
    local_sem, to_sib, to_left, to_right, recv = refs[2 * count :]
    s, q, c = place_in_seq()
    sibling = greet(nc, q, s)
    locals_ = [
        pltpu.make_async_copy(xs[k], outs[k].at[s], local_sem.at[k]) for k in range(count)
    ]
    for cp in locals_:
        cp.start()

    def copy(k, src, slot, sems, target):
        return pltpu.make_async_remote_copy(
            src_ref=src,
            dst_ref=outs[k].at[slot],
            send_sem=sems.at[k, slot],
            recv_sem=recv.at[k, slot],
            device_id={"seq": target},
            device_id_type=MESH,
        )

    for k in range(count):
        pl.when(q > 0)(lambda k=k: copy(k, xs[k], s, to_left, s - 2).start())
        pl.when(q < nc - 1)(lambda k=k: copy(k, xs[k], s, to_right, s + 2).start())
        copy(k, xs[k], s, to_sib, sibling).start()
    for t in range(1, nc):

        @pl.when(q - t >= 0)
        def _(t=t):
            slot = s - 2 * t
            for k in range(count):
                src = outs[k].at[slot]
                copy(k, src, slot, to_right, s).wait_recv()
                pl.when(q < nc - 1)(
                    lambda k=k: copy(k, src, slot, to_right, s + 2).start()
                )
                copy(k, src, slot, to_sib, sibling).start()

        @pl.when(q + t < nc)
        def _(t=t):
            slot = s + 2 * t
            for k in range(count):
                src = outs[k].at[slot]
                copy(k, src, slot, to_left, s).wait_recv()
                pl.when(q > 0)(lambda k=k: copy(k, src, slot, to_left, s - 2).start())
                copy(k, src, slot, to_sib, sibling).start()

    for cp in locals_:
        cp.wait()
    other = 1 - 2 * c
    for p in range(nc):
        mine, theirs = 2 * p + c, 2 * p + c + other
        for k in range(count):
            copy(k, outs[k].at[theirs], theirs, to_sib, sibling).wait_recv()
            copy(k, outs[k].at[mine], mine, to_sib, sibling).wait_send()
            pl.when((q < nc - 1) & (p <= q))(
                lambda k=k: copy(k, outs[k].at[mine], mine, to_right, sibling).wait_send()
            )
            pl.when((q > 0) & (p >= q))(
                lambda k=k: copy(k, outs[k].at[mine], mine, to_left, sibling).wait_send()
            )


def gather_seq(n, arrays, collective_id):
    count = len(arrays)
    nbytes = sum(a.size * a.dtype.itemsize for a in arrays)
    dma = pltpu.SemaphoreType.DMA
    return pl.pallas_call(
        functools.partial(gather_kernel, n, count),
        out_shape=tuple(jax.ShapeDtypeStruct((n, *a.shape), a.dtype) for a in arrays),
        in_specs=[pl.BlockSpec(memory_space=pl.ANY)] * count,
        out_specs=tuple([pl.BlockSpec(memory_space=pl.ANY)] * count),
        scratch_shapes=[dma((count,))] + [dma((count, n))] * 4,
        compiler_params=pltpu.CompilerParams(collective_id=collective_id, has_side_effects=True),
        cost_estimate=pl.CostEstimate(flops=0, transcendentals=0, bytes_accessed=nbytes * n * 20),
        name="gather_seq",
    )(*arrays)


def scatter_kernel(n, x_ref, e_ref, o_ref, all_ref, own, sib, from_left, from_right,
                   load_sem, to_sib, sib_in, to_right, right_in, to_left, left_in, e_out, e_in):
    nc = n // 2
    s, q, c = place_in_seq()
    sibling = s + 1 - 2 * c
    theirs = 1 - c
    barrier = pltpu.get_barrier_semaphore()
    for t in range(1, n):
        pl.semaphore_signal(
            barrier, inc=1, device_id={"seq": lax.rem(s + t, n)}, device_id_type=MESH
        )
    pl.semaphore_wait(barrier, n - 1)

    def small(t, slot):
        return pltpu.make_async_remote_copy(
            src_ref=e_ref,
            dst_ref=all_ref.at[slot],
            send_sem=e_out.at[t],
            recv_sem=e_in.at[t],
            device_id={"seq": lax.rem(s + t, n)},
            device_id_type=MESH,
        )

    for t in range(1, n):
        small(t, s).start()
    all_ref[s] = e_ref[...]

    def load(p):
        return pltpu.make_async_copy(x_ref.at[2 * p + c], own.at[p], load_sem.at[p])

    def to_sibling(p):
        return pltpu.make_async_remote_copy(
            src_ref=x_ref.at[2 * p + theirs],
            dst_ref=sib.at[p],
            send_sem=to_sib.at[p],
            recv_sem=sib_in.at[p],
            device_id={"seq": sibling},
            device_id_type=MESH,
        )

    def rightward(p, target):
        return pltpu.make_async_remote_copy(
            src_ref=own.at[p],
            dst_ref=from_left.at[p],
            send_sem=to_right.at[p],
            recv_sem=right_in.at[p],
            device_id={"seq": target},
            device_id_type=MESH,
        )

    def leftward(p, target):
        return pltpu.make_async_remote_copy(
            src_ref=own.at[p],
            dst_ref=from_right.at[p],
            send_sem=to_left.at[p],
            recv_sem=left_in.at[p],
            device_id={"seq": target},
            device_id_type=MESH,
        )

    order = []
    for t in range(nc):
        for p in (nc - 1 - t, t):
            if p not in order:
                order.append(p)
    for p in order:
        to_sibling(p).start()
        load(p).start()

    f32 = jnp.float32
    for p in order:
        load(p).wait()
        to_sibling(p).wait_recv()

        @pl.when(p > q)
        def _(p=p):
            @pl.when(q > 0)
            def _():
                rightward(p, s).wait_recv()
                total = own[p].astype(f32) + sib[p].astype(f32) + from_left[p].astype(f32)
                own[p] = total.astype(own.dtype)

            @pl.when(q == 0)
            def _():
                own[p] = (own[p].astype(f32) + sib[p].astype(f32)).astype(own.dtype)

            rightward(p, s + 2).start()

        @pl.when(p < q)
        def _(p=p):
            @pl.when(q < nc - 1)
            def _():
                leftward(p, s).wait_recv()
                total = own[p].astype(f32) + sib[p].astype(f32) + from_right[p].astype(f32)
                own[p] = total.astype(own.dtype)

            @pl.when(q == nc - 1)
            def _():
                own[p] = (own[p].astype(f32) + sib[p].astype(f32)).astype(own.dtype)

            leftward(p, s - 2).start()

    o_ref[...] = own[q].astype(f32) + sib[q].astype(f32)

    @pl.when(q > 0)
    def _():
        rightward(q, s).wait_recv()
        o_ref[...] += from_left[q].astype(f32)

    @pl.when(q < nc - 1)
    def _():
        leftward(q, s).wait_recv()
        o_ref[...] += from_right[q].astype(f32)

    for t in range(1, n):
        small(t, lax.rem(s - t + n, n)).wait_recv()
        small(t, s).wait_send()
    for p in range(nc):
        to_sibling(p).wait_send()
        pl.when(p > q)(lambda p=p: rightward(p, s).wait_send())
        pl.when(p < q)(lambda p=p: leftward(p, s).wait_send())


def scatter_seq(n, x, extra, collective_id):
    nc = n // 2
    _, rows, cols = x.shape
    dma = pltpu.SemaphoreType.DMA
    buf = pltpu.VMEM((nc, rows, cols), x.dtype)
    return pl.pallas_call(
        functools.partial(scatter_kernel, n),
        out_shape=(
            jax.ShapeDtypeStruct((rows, cols), jnp.float32),
            jax.ShapeDtypeStruct((n, *extra.shape), extra.dtype),
        ),
        in_specs=[pl.BlockSpec(memory_space=pl.ANY), pl.BlockSpec(memory_space=pltpu.VMEM)],
        out_specs=(pl.BlockSpec(memory_space=pltpu.VMEM),) * 2,
        scratch_shapes=[buf] * 4 + [dma((nc,))] * 7 + [dma((n,))] * 2,
        compiler_params=pltpu.CompilerParams(
            collective_id=collective_id, has_side_effects=True, vmem_limit_bytes=32 << 20
        ),
        cost_estimate=pl.CostEstimate(flops=0, transcendentals=0, bytes_accessed=x.size * 2 * 20),
        name="scatter_seq",
    )(x, extra)

def near_first(i, q, nc):
    short = jnp.where(q <= nc - 1 - q, q, nc - 1 - q)
    far = jnp.where(q <= nc - 1 - q, i, nc - 1 - i)
    step = (i + 1) // 2
    near = q - step if i % 2 else q + step
    return jnp.where(i <= 2 * short, near, far)


def weights_kernel(n, rows, xa, wa, local, edge, a_in, a_sib_in, a_out, a_sib_out):
    nc, half = n // 2, rows // 2
    others = half - 1
    s, q, c = place_in_seq()
    sibling = s + 1 - 2 * c
    r = lax.axis_index("rows")
    a, b = r // 2, lax.rem(r, 2)
    b_row = r + 1 - 2 * b

    def a_row(k):
        return lax.rem(a + k + half, half) * 2 + b

    def diagonal(k):
        return lax.rem(a + k + half, half) * 2 + 1 - b

    barrier = pltpu.get_barrier_semaphore()
    for t in range(1, n):
        pl.semaphore_signal(
            barrier, inc=1, device_id=(r, lax.rem(s + t, n)), device_id_type=MESH
        )
    pl.semaphore_signal(barrier, inc=1, device_id=(b_row, s), device_id_type=MESH)
    for k in range(1, half):
        pl.semaphore_signal(barrier, inc=1, device_id=(a_row(k), s), device_id_type=MESH)
    pl.semaphore_wait(barrier, n - 1 + half)

    def remote(src, dst, send, recv, row, seq):
        return pltpu.make_async_remote_copy(
            src_ref=src, dst_ref=dst, send_sem=send, recv_sem=recv,
            device_id=(row, seq), device_id_type=MESH,
        )

    both, first, second = pl.ds(0, 2), pl.ds(0, 1), pl.ds(1, 1)
    LINE, FROM_B = 0, 1

    def from_a(k):
        return 1 + k

    def relay_b(k):
        return 1 + others + k

    def relay_a(k):
        return 1 + 2 * others + k

    def a_view(p, core, parts, row):
        return wa.at[parts, 2 * p + core, row]

    def content(kind):
        if kind == LINE:
            return both, r
        if kind == FROM_B:
            return both, b_row
        for k in range(1, half):
            if kind == from_a(k):
                return both, a_row(-k)
            if kind == relay_b(k):
                return second, diagonal(-k)
            if kind == relay_a(k):
                return first, diagonal(-k)

    kinds = 2 + 3 * others

    def a_send(p, parts, row, kind, target_row):
        return remote(
            a_view(p, c, parts, row), a_view(p, c, parts, row),
            a_out.at[p, kind], a_in.at[p, kind], target_row, s,
        )

    def a_arrival(p, kind):
        parts, row = content(kind)
        return a_send(p, parts, row, kind, r)

    def a_to_sibling(p, kind, core):
        parts, row = content(kind)
        return remote(
            a_view(p, core, parts, row), a_view(p, core, parts, row),
            a_sib_out.at[p, kind], a_sib_in.at[p, kind], r, sibling,
        )

    def line_send(p, src, sem, target):
        return remote(src, a_view(p, c, both, r), sem, a_in.at[p, LINE], r, target)

    own = xa.at[both, r]
    to_left = lambda: line_send(q, own, edge.at[0], s - 2)
    to_right = lambda: line_send(q, own, edge.at[1], s + 2)
    pl.when(q > 0)(lambda: to_left().start())
    pl.when(q < nc - 1)(lambda: to_right().start())
    order = [near_first(i, q, nc) for i in range(nc)]
    sib_a = lambda: remote(xa, wa.at[:, s], edge.at[2], edge.at[3], r, sibling)
    keep_a = pltpu.make_async_copy(xa, wa.at[:, s], local.at[0])
    sib_a().start()
    keep_a.start()

    def spread_a(p):
        a_send(p, both, r, FROM_B, b_row).start()
        for k in range(1, half):
            a_send(p, both, r, from_a(k), a_row(k)).start()

    for p in order[1:]:
        a_arrival(p, LINE).wait_recv()
        pl.when((p < q) & (q < nc - 1))(
            lambda p=p: line_send(p, a_view(p, c, both, r), a_out.at[p, LINE], s + 2).start()
        )
        pl.when((p > q) & (q > 0))(
            lambda p=p: line_send(p, a_view(p, c, both, r), a_out.at[p, LINE], s - 2).start()
        )
        spread_a(p)
        a_to_sibling(p, LINE, c).start()
    for p in order[1:]:
        a_arrival(p, FROM_B).wait_recv()
        for k in range(1, half):
            a_send(p, first, b_row, relay_a(k), a_row(k)).start()
        a_to_sibling(p, FROM_B, c).start()
        for k in range(1, half):
            a_arrival(p, from_a(k)).wait_recv()
            a_send(p, second, a_row(-k), relay_b(k), b_row).start()
            a_to_sibling(p, from_a(k), c).start()
    for p in order[1:]:
        for k in range(1, half):
            for kind in (relay_b(k), relay_a(k)):
                a_arrival(p, kind).wait_recv()
                a_to_sibling(p, kind, c).start()
    keep_a.wait()
    sib_a().wait()
    pl.when(q > 0)(lambda: to_left().wait_send())
    pl.when(q < nc - 1)(lambda: to_right().wait_send())
    for p in order[1:]:
        pl.when(((p < q) & (q < nc - 1)) | ((p > q) & (q > 0)))(
            lambda p=p: line_send(p, a_view(p, c, both, r), a_out.at[p, LINE], s).wait_send()
        )
        for kind in range(kinds):
            a_to_sibling(p, kind, c).wait_send()
            a_to_sibling(p, kind, 1 - c).wait_recv()
        a_send(p, both, r, FROM_B, b_row).wait_send()
        for k in range(1, half):
            a_send(p, both, r, from_a(k), r).wait_send()
            a_send(p, first, b_row, relay_a(k), r).wait_send()
            a_send(p, second, a_row(-k), relay_b(k), r).wait_send()


def gather_weights(n, rows, xa, collective_id):
    nc = n // 2
    block = xa.shape[1]
    part = block // rows
    xa = xa.reshape(2, rows, part, xa.shape[2])
    kinds = 2 + 3 * (rows // 2 - 1)
    dma = pltpu.SemaphoreType.DMA
    anywhere = pl.BlockSpec(memory_space=pl.ANY)
    wa = pl.pallas_call(
        functools.partial(weights_kernel, n, rows),
        out_shape=jax.ShapeDtypeStruct((2, n, rows, part, xa.shape[3]), xa.dtype),
        in_specs=[anywhere],
        out_specs=anywhere,
        scratch_shapes=[dma((1,)), dma((4,))] + [dma((nc, kinds))] * 4,
        compiler_params=pltpu.CompilerParams(collective_id=collective_id, has_side_effects=True),
        cost_estimate=pl.CostEstimate(
            flops=0, transcendentals=0, bytes_accessed=250 * 1024 * 1024
        ),
        name="gather_weights",
    )(xa)
    return wa.reshape(2, n * block, -1)

def swap_halves(x):
    return pltpu.roll(x.astype(jnp.float32), HEAD_DIM, 1)


def stack_heads(block):
    lane = lax.broadcasted_iota(jnp.int32, (block.shape[0], 128), 1)
    rows = []
    for h in range(8):
        pair = block[:, (h // 2) * 128 : (h // 2 + 1) * 128].astype(jnp.float32)
        if h % 2 != h // 4:
            pair = swap_halves(pair)
        keep = lane < HEAD_DIM if h // 4 == 0 else lane >= HEAD_DIM
        rows.append(jnp.where(keep, pair, 0.0).astype(jnp.bfloat16))
    return jnp.concatenate(rows, axis=0)


def unstack_heads(stacked, span):
    lane = lax.broadcasted_iota(jnp.int32, (span, 128), 1)
    pairs = []
    for t in range(4):
        first = stacked[2 * t * span : (2 * t + 1) * span]
        second = stacked[(2 * t + 1) * span : (2 * t + 2) * span]
        if t < 2:
            second = swap_halves(second)
        else:
            first = swap_halves(first)
        pairs.append(jnp.where(lane < HEAD_DIM, first, second))
    return jnp.concatenate(pairs, axis=1)


def attend_kernel(valid_ref, q_ref, k_ref, v_ref, o_ref, p_ref):
    span = q_ref.shape[1]
    keys = k_ref.shape[0] * span
    q8 = stack_heads(q_ref[0])
    k2 = k_ref[:, 0].reshape(keys, 128)
    v2 = v_ref[:, 0].reshape(keys, 128)
    scores = lax.dot_general(q8, k2, last_last, preferred_element_type=jnp.float32)
    scores = scores * HEAD_DIM**-0.5
    first_pos = lax.axis_index("seq") * span
    q_pos = first_pos + lax.broadcasted_iota(jnp.int32, (8, span, keys), 1).reshape(8 * span, keys)
    k_pos = lax.broadcasted_iota(jnp.int32, (8 * span, keys), 1)
    allowed = (k_pos <= q_pos) & (k_pos < valid_ref[pl.program_id(0)])
    scores = jnp.where(allowed, scores, -1e30)
    unscaled = jnp.exp(scores - jnp.max(scores, axis=1, keepdims=True))
    shares = unscaled * (1.0 / jnp.sum(unscaled, axis=1, keepdims=True))
    shares = shares.astype(jnp.bfloat16)
    p_ref[0, 0] = shares
    mixed = jnp.dot(shares, v2, preferred_element_type=jnp.float32)
    o_ref[0] = unstack_heads(mixed, span).astype(jnp.bfloat16)


def attend(q, kv, valid):
    pair, span, width = q.shape
    n, kv_width = kv.shape[0], kv.shape[3] // 2
    groups = kv_width // 128
    keys = n * span
    q_spec = pl.BlockSpec((1, span, 512), lambda p, j, *_: (p, 0, j))
    flops = 4 * pair * groups * 8 * span * keys * 128
    return pl.pallas_call(
        attend_kernel,
        out_shape=(
            jax.ShapeDtypeStruct(q.shape, jnp.bfloat16),
            jax.ShapeDtypeStruct((pair, groups, 8 * span, keys), jnp.bfloat16),
        ),
        grid_spec=pltpu.PrefetchScalarGridSpec(
            num_scalar_prefetch=1,
            grid=(pair, groups),
            in_specs=[
                q_spec,
                pl.BlockSpec((n, 1, span, 128), lambda p, j, *_: (0, p, 0, j)),
                pl.BlockSpec((n, 1, span, 128), lambda p, j, *_: (0, p, 0, groups + j)),
            ],
            out_specs=(
                q_spec,
                pl.BlockSpec((1, 1, 8 * span, keys), lambda p, j, *_: (p, j, 0, 0)),
            ),
        ),
        compiler_params=pltpu.CompilerParams(vmem_limit_bytes=40 << 20),
        cost_estimate=pl.CostEstimate(
            flops=flops, transcendentals=flops // 512, bytes_accessed=8 << 20
        ),
        name="attend",
    )(valid, q, kv, kv)


def attend_back_kernel(q_ref, k_ref, v_ref, p_ref, g_ref, gq_ref, gkv_ref):
    span = q_ref.shape[1]
    keys = k_ref.shape[0] * span
    q8 = stack_heads(q_ref[0])
    g8 = stack_heads(g_ref[0])
    k2 = k_ref[:, 0].reshape(keys, 128)
    v2 = v_ref[:, 0].reshape(keys, 128)
    low = p_ref[0, 0]
    shares = low.astype(jnp.float32)
    grad_shares = lax.dot_general(g8, v2, last_last, preferred_element_type=jnp.float32)
    weighted = shares * grad_shares
    centre = jnp.sum(weighted, axis=1, keepdims=True)
    grad_scores = (weighted - shares * centre).astype(jnp.bfloat16)
    gq = jnp.dot(grad_scores, k2, preferred_element_type=jnp.float32) * HEAD_DIM**-0.5
    gq_ref[0] = unstack_heads(gq, span).astype(jnp.bfloat16)
    gk = lax.dot_general(grad_scores, q8, first_first, preferred_element_type=jnp.float32)
    gv = lax.dot_general(low, g8, first_first, preferred_element_type=jnp.float32)
    both = jnp.concatenate([gk * HEAD_DIM**-0.5, gv], axis=1).astype(jnp.bfloat16)
    gkv_ref[:, 0] = both.reshape(gkv_ref.shape[0], span, 256)


def attend_back(q, kv, shares, g):
    pair, span, _ = q.shape
    n, kv_width = kv.shape[0], kv.shape[3] // 2
    groups = kv_width // 128
    keys = n * span
    q_spec = pl.BlockSpec((1, span, 512), lambda p, j: (p, 0, j))
    flops = 10 * pair * groups * 8 * span * keys * 128
    return pl.pallas_call(
        attend_back_kernel,
        out_shape=(
            jax.ShapeDtypeStruct(q.shape, jnp.bfloat16),
            jax.ShapeDtypeStruct(kv.shape, jnp.bfloat16),
        ),
        grid=(pair, groups),
        in_specs=[
            q_spec,
            pl.BlockSpec((n, 1, span, 128), lambda p, j: (0, p, 0, j)),
            pl.BlockSpec((n, 1, span, 128), lambda p, j: (0, p, 0, groups + j)),
            pl.BlockSpec((1, 1, 8 * span, keys), lambda p, j: (p, j, 0, 0)),
            q_spec,
        ],
        out_specs=(
            q_spec,
            pl.BlockSpec((n, 1, span, 256), lambda p, j: (0, p, 0, j)),
        ),
        compiler_params=pltpu.CompilerParams(vmem_limit_bytes=40 << 20),
        cost_estimate=pl.CostEstimate(flops=flops, transcendentals=0, bytes_accessed=8 << 20),
        name="attend_back",
    )(q, kv, kv, shares, g)

def by_distance(i, q, nc):
    room = nc - 1 - q
    left_half = q <= room
    short = jnp.where(left_half, q, room)
    far = jnp.where(left_half, i, nc - 1 - i)
    step = (i + 1) // 2
    near = jnp.where(lax.rem(i, 2) == 1, q - step, q + step)
    return jnp.where(i <= 2 * short, near, far)


def ffn_kernel(n, rows, pieces, u_hbm, gy_hbm, wd_hbm, a_ref, b_ref, m_ref, ad_ref, bd_ref, md_ref, nd_ref,
               in_ref, down_hbm, ga_ref, gb_ref, gm_ref, norm_ref, gad_ref, gbd_ref, gmd_ref,
               w_parts, wd, u, gy, down, own, theirs, sib, from_left, from_right, ratio, cross,
               w_sem, load_sem, down_sem, to_sib, sib_in, to_right, right_in, to_left, left_in):
    nc = n // 2
    f32, low = jnp.float32, jnp.bfloat16
    s, q, c = place_in_seq()
    tokens = own.shape[1]

    weights = [pltpu.make_async_copy(wd_hbm, wd, w_sem.at[0])]
    for src, g, hold in place_pieces(rows, pieces):
        weights.append(
            pltpu.make_async_copy(src, w_parts.at[g, :, hold], w_sem.at[len(weights)])
        )
    for cp in weights:
        cp.start()

    def loads(i):
        p = by_distance(nc - 1 - i, q, nc)
        slot = lax.rem(i, 2)
        pair = pl.ds(2 * p, 2)
        return (
            pltpu.make_async_copy(u_hbm.at[pair], u.at[slot], load_sem.at[0, slot]),
            pltpu.make_async_copy(gy_hbm.at[pair], gy.at[slot], load_sem.at[1, slot]),
        )

    for cp in loads(0):
        cp.start()
    sibling = greet(nc, q, s)

    def to_sibling(p):
        return pltpu.make_async_remote_copy(
            src_ref=theirs.at[p], dst_ref=sib.at[p], send_sem=to_sib.at[p], recv_sem=sib_in.at[p],
            device_id={"seq": sibling}, device_id_type=MESH,
        )

    def rightward(p, target):
        return pltpu.make_async_remote_copy(
            src_ref=own.at[p], dst_ref=from_left.at[p], send_sem=to_right.at[p], recv_sem=right_in.at[p],
            device_id={"seq": target}, device_id_type=MESH,
        )

    def leftward(p, target):
        return pltpu.make_async_remote_copy(
            src_ref=own.at[p], dst_ref=from_right.at[p], send_sem=to_left.at[p], recv_sem=left_in.at[p],
            device_id={"seq": target}, device_id_type=MESH,
        )

    def down_out(p):
        return pltpu.make_async_copy(
            down.at[lax.rem(p, 2)], down_hbm.at[pl.ds(2 * p, 2)], down_sem.at[lax.rem(p, 2)]
        )

    def pass_on(p):
        to_sibling(p).wait_recv()

        @pl.when(p > q)
        def _():
            @pl.when(q > 0)
            def _():
                rightward(p, s).wait_recv()
                own[p] = (own[p].astype(f32) + sib[p].astype(f32) + from_left[p].astype(f32)).astype(low)

            @pl.when(q == 0)
            def _():
                own[p] = (own[p].astype(f32) + sib[p].astype(f32)).astype(low)

            rightward(p, s + 2).start()

        @pl.when(p < q)
        def _():
            @pl.when(q < nc - 1)
            def _():
                leftward(p, s).wait_recv()
                own[p] = (own[p].astype(f32) + sib[p].astype(f32) + from_right[p].astype(f32)).astype(low)

            @pl.when(q == nc - 1)
            def _():
                own[p] = (own[p].astype(f32) + sib[p].astype(f32)).astype(low)

            leftward(p, s - 2).start()

    def starts_flow(p):
        return ((p > q) & (q == 0)) | ((p < q) & (q == nc - 1))

    w = [w_parts.at[g] for g in range(2)]
    width = u_hbm.shape[2]
    weight = lambda g: w[g][...].reshape(width, -1)
    bd = bd_ref[...].astype(low)
    ad = ad_ref[...].astype(low)
    a = [a_ref[g].astype(low) for g in range(2)]
    b = [b_ref[g].astype(low) for g in range(2)]
    for cp in weights:
        cp.wait()
    for g in range(2):
        norm, cr = column_norms(weight(g), a[g], b[g].astype(f32), dot_f32(a[g], weight(g)))
        norm_ref[g] = norm
        cross[g] = cr
        ratio[g] = m_ref[g] / norm
    for ref in (ga_ref, gb_ref, gm_ref, gad_ref, gbd_ref, gmd_ref):
        ref[...] = jnp.zeros_like(ref)
    ratio_d = md_ref[...] / nd_ref[...]

    def step(i, carry):
        p = by_distance(nc - 1 - i, q, nc)
        slot = lax.rem(i, 2)
        for cp in loads(i):
            cp.wait()

        @pl.when(i + 1 < nc)
        def _():
            for cp in loads(i + 1):
                cp.start()

        x = u[slot].reshape(2 * tokens, -1)
        upstream = gy[slot].reshape(2 * tokens, -1).astype(f32)
        gb_d = (upstream * ratio_d).astype(low)
        gi_d = (SCALE * dot_nt(gb_d, bd)).astype(low)
        gh = dot_nt(gb_d, wd[...]) + dot_f32(gi_d, ad)
        inner = [dot_nt(x, a[g]).astype(low) for g in range(2)]
        before = [dot_f32(x, weight(g)) + SCALE * dot_f32(inner[g], b[g]) for g in range(2)]
        gate = before[0] * ratio[0]
        lift = before[1] * ratio[1]
        sig = 1.0 / (1.0 + jnp.exp(-gate))
        silu = gate * sig
        hidden = (silu * lift).astype(low)
        grads = [gh * lift * sig * (1.0 + gate * (1.0 - sig)), gh * silu]
        gb = [(grads[g] * ratio[g]).astype(low) for g in range(2)]
        gi = [(SCALE * dot_nt(gb[g], b[g])).astype(low) for g in range(2)]
        back = dot_nt(gb[0], weight(0)) + dot_nt(gb[1], weight(1)) + dot_f32(gi[0], a[0]) + dot_f32(gi[1], a[1])
        back = back.astype(low).reshape(2, tokens, -1)
        first, second = back[0], back[1]

        @pl.when(c == 0)
        def _():
            own[p] = first
            theirs[p] = second

        @pl.when(c == 1)
        def _():
            own[p] = second
            theirs[p] = first

        to_sibling(p).start()
        inner_d = dot_nt(hidden, ad).astype(low)
        part = dot_f32(hidden, wd[...]) + SCALE * dot_f32(inner_d, bd)

        @pl.when(i >= 2)
        def _():
            down_out(slot).wait()

        down[slot] = part.astype(low).reshape(2, tokens, -1)
        pltpu.make_async_copy(down.at[slot], down_hbm.at[pl.ds(2 * p, 2)], down_sem.at[slot]).start()
        gmd_ref[...] += jnp.sum(upstream * part, axis=0, keepdims=True)
        gad_ref[...] += dot_tn(gi_d, hidden)
        gbd_ref[...] += SCALE * dot_tn(inner_d, gb_d)
        for g in range(2):
            gm_ref[g] += jnp.sum(grads[g] * before[g], axis=0, keepdims=True)
            ga_ref[g] += dot_tn(gi[g], x)
            gb_ref[g] += SCALE * dot_tn(inner[g], gb[g])

        pl.when(starts_flow(p))(lambda: pass_on(p))
        last = by_distance(nc - i, q, nc)
        pl.when((i > 0) & jnp.logical_not(starts_flow(last)))(lambda: pass_on(last))
        return carry

    lax.fori_loop(0, nc, step, 0)

    gmd_ref[...] = gmd_ref[...] / nd_ref[...]
    for g in range(2):
        norm = norm_ref[g]
        gm = gm_ref[g] / norm
        gm_ref[g] = gm
        col = -gm * m_ref[g] / (norm * norm)
        b_wide = b[g].astype(f32)
        weighted = b_wide * col
        tail = lax.dot_general(
            weighted, b_wide, (((1,), (1,)), ((), ())), precision=highest, preferred_element_type=f32
        )
        spread = dot_nt(weighted.astype(low), weight(g)) + SCALE * jnp.dot(
            tail, a[g].astype(f32), precision=highest, preferred_element_type=f32
        )
        ga_ref[g] += SCALE * spread
        gb_ref[g] += SCALE * col * cross[g]

    to_sibling(q).wait_recv()
    in_ref[...] = own[q].astype(f32) + sib[q].astype(f32)

    @pl.when(q > 0)
    def _():
        rightward(q, s).wait_recv()
        in_ref[...] += from_left[q].astype(f32)

    @pl.when(q < nc - 1)
    def _():
        leftward(q, s).wait_recv()
        in_ref[...] += from_right[q].astype(f32)

    for i in range(min(2, nc)):
        pltpu.make_async_copy(down.at[i], down_hbm.at[pl.ds(0, 2)], down_sem.at[i]).wait()
    for p in range(nc):
        to_sibling(p).wait_send()
        pl.when(p > q)(lambda p=p: rightward(p, s).wait_send())
        pl.when(p < q)(lambda p=p: leftward(p, s).wait_send())


def reshard_units(gate_up, n, rows):
    half = rows // 2
    _, block, units_all = gate_up.shape
    part, units = block // rows, units_all // n
    r = lax.axis_index("rows")
    mine = lax.dynamic_slice_in_dim(gate_up, r * part, part, 1)
    mine = mine.reshape(2, part, n, units).transpose(2, 0, 1, 3)
    mine = lax.all_to_all(mine, "seq", split_axis=0, concat_axis=0, tiled=True)
    swap = [(i, i ^ 1) for i in range(rows)]
    turns = [[(i, (i + 2 * k) % rows) for i in range(rows)] for k in range(1, half)]
    from_b = lax.ppermute(mine, "rows", swap)
    from_a = [lax.ppermute(mine, "rows", turn) for turn in turns]
    pieces = [mine, from_b, *from_a]
    for k in range(1, half):
        pieces.append(lax.ppermute(from_b[:, 0], "rows", turns[k - 1]))
        pieces.append(lax.ppermute(from_a[k - 1][:, 1], "rows", swap))
    return pieces


def place_pieces(rows, pieces):
    half = rows // 2
    r = lax.axis_index("rows")
    a, b = r // 2, lax.rem(r, 2)
    turned = lambda k: 2 * lax.rem(a - k + half, half)
    holds = [r, 2 * a + 1 - b] + [turned(k) + b for k in range(1, half)]
    out = [(pieces[i].at[:, g], g, hold) for i, hold in enumerate(holds) for g in range(2)]
    for k in range(1, half):
        for g in range(2):
            out.append((pieces[half + 1 + 2 * (k - 1) + g], g, turned(k) + 1 - b))
    return out


def feed_forward(n, rows, pieces, u, gy, wd, a, b, m, ad, bd, md, nd, collective_id):
    nc = n // 2
    _, tokens, width = u.shape
    units = wd.shape[0]
    f32, low = jnp.float32, jnp.bfloat16
    shape = jax.ShapeDtypeStruct
    vmem = pl.BlockSpec(memory_space=pltpu.VMEM)
    hbm = pl.BlockSpec(memory_space=pl.ANY)
    dma = pltpu.SemaphoreType.DMA
    line = pltpu.VMEM((nc, tokens, width), low)
    pair = pltpu.VMEM((2, 2, tokens, width), low)
    part = pieces[0].shape[2]
    count = len(pieces)

    def kernel(*refs):
        ffn_kernel(n, rows, refs[:count], *refs[count:])

    return pl.pallas_call(
        kernel,
        out_shape=(
            shape((tokens, width), f32),
            shape((n, tokens, width), low),
            shape((2, 16, width), f32),
            shape((2, 16, units), f32),
            shape((2, 1, units), f32),
            shape((2, 1, units), f32),
            shape((16, units), f32),
            shape((16, width), f32),
            shape((1, width), f32),
        ),
        in_specs=[hbm] * (count + 3) + [vmem] * 7,
        out_specs=(vmem, hbm) + (vmem,) * 7,
        scratch_shapes=[
            pltpu.VMEM((2, n, rows, part, units), low),
            pltpu.VMEM((units, width), low),
            pair, pair, pair,
            line, line, line, line, line,
            pltpu.VMEM((2, 1, units), f32),
            pltpu.VMEM((2, 16, units), f32),
            dma((1 + 2 * rows,)), dma((2, 2)), dma((2,)),
        ] + [dma((nc,))] * 6,
        compiler_params=pltpu.CompilerParams(
            collective_id=collective_id, has_side_effects=True, vmem_limit_bytes=60 << 20
        ),
        cost_estimate=pl.CostEstimate(
            flops=12 * n * tokens * width * units, transcendentals=n * tokens * units,
            bytes_accessed=32 << 20,
        ),
        name="feed_forward",
    )(*pieces, u, gy, wd, a, b, m, ad, bd, md, nd)

def square_terms(weight, a_low, b_low):
    cross = dot_f32(a_low, weight)
    squares = jnp.sum(jnp.square(weight.astype(jnp.float32)), axis=0, keepdims=True)
    return squares + 2.0 * SCALE * jnp.sum(b_low.astype(jnp.float32) * cross, axis=0, keepdims=True), cross


def drift_stats(magnitude_vector, norms):
    drift = jnp.sqrt(jnp.mean(jnp.square(magnitude_vector - norms))) / jnp.sqrt(
        jnp.mean(jnp.square(magnitude_vector)) + 1e-06
    )
    return jnp.stack([drift, jnp.mean(norms)])


def local(
    layer_input,
    output_gradient,
    norm_gain_vectors,
    query_output_frozen,
    key_value_frozen,
    gate_up_frozen,
    down_frozen_weight,
    attention_adapter_a,
    query_output_adapter_b,
    key_value_adapter_b,
    query_magnitude,
    key_value_magnitude,
    output_magnitude,
    gate_up_adapter_a,
    gate_up_adapter_b,
    gate_up_magnitude,
    down_adapter_a,
    down_adapter_b,
    down_magnitude,
    prompt_length_list,
    response_length_list,
):
    pair_rows, span_len, model_width = layer_input.shape
    token_count = pair_rows * span_len
    kv_width = KV_HEADS * HEAD_DIM
    qkv_width = model_width + 2 * kv_width
    seq_size = lax.axis_size("seq")
    rows_size = lax.axis_size("rows")
    seq_index = lax.axis_index("seq")
    first_member = (seq_index == 0).astype(jnp.float32)
    low, f32 = jnp.bfloat16, jnp.float32
    rank = ADAPTER_RANK
    slice_units = down_frozen_weight.shape[0]
    start = seq_index * slice_units

    pieces = reshard_units(gate_up_frozen, seq_size, rows_size)
    packed = jnp.stack(
        [
            jnp.concatenate([query_output_frozen[0], key_value_frozen[0]], axis=1),
            jnp.concatenate([key_value_frozen[1], query_output_frozen[1]], axis=1),
        ]
    )
    weights = gather_weights(seq_size, rows_size, packed, 1)
    weights, grad_out_rows = lax.optimization_barrier(
        (weights, output_gradient.reshape(token_count, model_width))
    )
    gy_all = lax.all_gather(grad_out_rows, "seq", axis=0, tiled=False)

    b_attn = jnp.concatenate(
        [
            query_output_adapter_b[0],
            key_value_adapter_b[0],
            key_value_adapter_b[1],
            query_output_adapter_b[1],
        ],
        axis=1,
    )
    m_attn = jnp.concatenate(
        [query_magnitude, key_value_magnitude[0], key_value_magnitude[1], output_magnitude]
    )[None]
    b_gu = lax.dynamic_slice_in_dim(gate_up_adapter_b, start, slice_units, 2)
    m_gu = lax.dynamic_slice_in_dim(gate_up_magnitude, start, slice_units, 1)[:, None]
    a_d = lax.dynamic_slice_in_dim(down_adapter_a, start, slice_units, 1)
    b_d = down_adapter_b.astype(low)
    m_d = down_magnitude[None]
    sq_d, cross_d = square_terms(down_frozen_weight, a_d.astype(low), b_d)

    positions = seq_index * span_len + jnp.arange(span_len, dtype=jnp.int32)
    half_dim = HEAD_DIM // 2
    frequency = 500000.0 ** (-(jnp.arange(half_dim, dtype=f32) * 2.0) / HEAD_DIM)
    angles = positions.astype(f32)[:, None] * frequency[None, :]
    cosine = jnp.tile(jnp.cos(angles), (pair_rows, 4))
    sine = jnp.tile(jnp.sin(angles), (pair_rows, 4))
    valid_len = prompt_length_list[0] + response_length_list

    x = layer_input.reshape(token_count, model_width)
    gain_attn, gain_ffn = norm_gain_vectors[:1], norm_gain_vectors[1:]
    u1, before_qkv, q, kv, n_attn, cross_attn = project_qkv(
        x, gain_attn, attention_adapter_a, weights, b_attn, m_attn, cosine, sine
    )
    kv_all, sq_all = gather_seq(seq_size, [kv, sq_d], 2)
    kv_all = kv_all.reshape(seq_size, pair_rows, span_len, 2 * kv_width)
    q = q.reshape(pair_rows, span_len, model_width)
    att, shares = attend(q, kv_all, valid_len)
    att = att.reshape(token_count, model_width)
    b_o, m_o, n_o = b_attn[:, qkv_width:], m_attn[:, qkv_width:], n_attn[:, qkv_width:]
    a_o = attention_adapter_a[3]
    before_o, x1, u2 = project_out(att, a_o, weights, b_o, m_o, n_o, x, gain_ffn)

    (u2_all,) = gather_seq(seq_size, [u2], 3)
    a_d_wide, b_d_wide = down_adapter_a.astype(low).astype(f32), b_d.astype(f32)
    gram_d = jnp.dot(
        jnp.dot(a_d_wide, a_d_wide.T, precision=highest), b_d_wide, precision=highest
    )
    sq_d = jnp.sum(sq_all, axis=0) + SCALE * SCALE * jnp.sum(
        b_d_wide * gram_d, axis=0, keepdims=True
    )
    n_d = jnp.sqrt(sq_d + 1e-06)
    in_grad, down_parts, ga_gu, gb_gu, gm_gu, n_gu, ga_d, gb_d, gm_d = feed_forward(
        seq_size, rows_size, pieces, u2_all, gy_all, down_frozen_weight, gate_up_adapter_a, b_gu,
        m_gu, a_d, down_adapter_b, m_d, n_d, 4,
    )
    before_d = lax.psum_scatter(
        down_parts.reshape(seq_size * token_count, model_width), "seq", scatter_dimension=0,
        tiled=True,
    )
    layer_result = (x1 + before_d.astype(f32) * (m_d / n_d)).astype(low)

    gx1, grad_att, ga_o, gb_o, gm_o = out_back(
        in_grad, x1, gain_ffn, grad_out_rows, before_o, att, a_o, b_o, m_o, n_o,
        cross_attn[:, qkv_width:], weights,
    )
    gq, gkv = attend_back(q, kv_all, shares, grad_att.reshape(q.shape))
    gkv, gm_d_all = scatter_seq(
        seq_size, gkv.reshape(seq_size, token_count, 2 * kv_width), gm_d, 5
    )
    grad_inputs, ga_qkv, gb_qkv, gm_qkv = qkv_back(
        gq.reshape(token_count, model_width), gkv, cosine, sine, before_qkv, u1,
        attention_adapter_a[:3], b_attn[:, :qkv_width], m_attn[:, :qkv_width],
        n_attn[:, :qkv_width], cross_attn[:, :qkv_width], x, gain_attn, gx1, weights,
    )

    c_d = -jnp.sum(gm_d_all, axis=0) * m_d / (n_d * n_d)
    weighted = b_d_wide * c_d
    tail = lax.dot_general(weighted, b_d_wide, last_last, precision=highest)
    spread = dot_nt(weighted.astype(low), down_frozen_weight) + SCALE * jnp.dot(
        tail, a_d.astype(low).astype(f32), precision=highest
    )
    ga_d = ga_d + SCALE * spread
    gb_d = gb_d + SCALE * c_d * (cross_d + first_member * SCALE * gram_d)

    k_end = model_width + kv_width
    full_units = gate_up_magnitude.shape[1]

    def place(piece, axis):
        shape = list(piece.shape)
        shape[axis] = full_units
        return lax.dynamic_update_slice_in_dim(jnp.zeros(shape, piece.dtype), piece, start, axis)

    summed = lax.psum(
        (
            jnp.concatenate([ga_qkv, ga_o[None]], axis=0),
            jnp.stack([gb_qkv[:, :model_width], gb_o]),
            jnp.stack([gb_qkv[:, model_width:k_end], gb_qkv[:, k_end:]]),
            gm_qkv[0, :model_width],
            gm_qkv[0, model_width:].reshape(2, kv_width),
            gm_o[0],
            ga_gu,
            place(gb_gu, 2),
            place(gm_gu[:, 0], 1),
            place(ga_d, 1),
            gb_d,
            gm_d[0],
        ),
        ("rows", "seq"),
    )
    norms_gu = lax.all_gather(n_gu[:, 0], "seq", axis=1, tiled=True)
    stats = jnp.stack(
        [
            drift_stats(query_magnitude, n_attn[0, :model_width]),
            drift_stats(key_value_magnitude[0], n_attn[0, model_width:k_end]),
            drift_stats(key_value_magnitude[1], n_attn[0, k_end:qkv_width]),
            drift_stats(output_magnitude, n_o[0]),
            drift_stats(gate_up_magnitude[0], norms_gu[0]),
            drift_stats(gate_up_magnitude[1], norms_gu[1]),
            drift_stats(down_magnitude, n_d[0]),
        ]
    )
    shape = (pair_rows, span_len, model_width)
    return (layer_result.reshape(shape), grad_inputs.reshape(shape), *summed, stats)

def solution(mesh):
    return jax.shard_map(
        local,
        mesh=mesh,
        in_specs=(
            P("rows", "seq", None),
            P("rows", "seq", None),
            P(),
            P(None, "seq", None),
            P(None, "seq", None),
            P(None, "seq", None),
            P("seq", None),
            P(),
            P(),
            P(),
            P(),
            P(),
            P(),
            P(),
            P(),
            P(),
            P(),
            P(),
            P(),
            P("rows"),
            P("rows"),
        ),
        out_specs=(
            P("rows", "seq", None),
            P("rows", "seq", None),
            P(),
            P(),
            P(),
            P(),
            P(),
            P(),
            P(),
            P(),
            P(),
            P(),
            P(),
            P(),
            P(),
        ),
        check_vma=False,
    )
```

time: 1070 us -> 700 us (0.65)
  matrix products: 242 us -> 6.13 us
  local copies, waits for them, and re-layouts: 134 us -> 45.9 us
  other arithmetic: 75.8 us -> 20.3 us
  Pallas kernels: 333 us -> 366 us
  blocking collectives: 84.8 us -> 52.6 us
    dot_general x87 -> x4, matrix products: 99.5 us -> 1.99 us  [the longest x1 1.46 us: local(): jnp.dot(jnp.dot(a_d_wide, a_d_wide.T, precision=highest), b_d_wide, preci...]
    dot_general x20 -> x1, matrix products: 73.3 us -> 0.66 us  [dot_f32(): return jnp.dot(a, b, preferred_element_type=jnp.float32)]
    psum x1, waiting for transfers between devices: 131 us -> 64.3 us  [local(): lax.psum((jnp.concatenate([ga_qkv, ga_o[None]], axis=0), jnp.stack([gb_qk...]
    dot_general x20 -> x1, matrix products: 68.8 us -> 3.49 us  [dot_nt(): return lax.dot_general(a, b, last_last, preferred_element_type=jnp.float32)]
    pallas_call x2 -> x8, Pallas kernels: 115 us -> 169 us  [the longest x1 72.7 us: feed_forward(): pl.pallas_call(kernel, out_shape=(shape((tokens, width), f32), shape((n,...]
    reduce_scatter x2 -> x1, waiting for transfers between devices: 0.01 us -> 51.7 us  [local(): lax.psum_scatter(down_parts.reshape(seq_size * token_count, model_width),...]
    psum x3 -> x1, blocking collectives: 70.9 us -> 38.5 us  [local(): lax.psum((jnp.concatenate([ga_qkv, ga_o[None]], axis=0), jnp.stack([gb_qk...]
    convert_element_type x13 -> x0, local copies, waits for them, and re-layouts: 26.4 us -> none  [the longest x3 9.64 us: local(): attended = from_heads(mixed_heads, pair_rows, span_len, group_count, rati...]
  transfers between devices with their start and end apart: 9 -> 8, of which waited for: 3 -> 4; matrix products, arithmetic and copies ran while one was open for 25% -> 5% of each run, Pallas kernels for 29% -> 34%
where the time goes in v3:
time: 700 us; the launch traced here: 688 us
  Pallas kernels  366 us (52%)
  waiting for transfers between devices  156 us (22%)
  blocking collectives  52.6 us (8%)
  local copies, waits for them, and re-layouts  45.9 us (7%)
  between operations  29.8 us (4%)
  other arithmetic  20.3 us (3%)
  starting transfers between devices  11.4 us (2%)
    pallas_call x1, Pallas kernels, gather_weights(): pl.pallas_call(functools.partial(weights_kernel, n, rows), out_shape=jax....  131 us
    pallas_call x1, Pallas kernels, feed_forward(): pl.pallas_call(kernel, out_shape=(shape((tokens, width), f32), shape((n,...  72.7 us
    pallas_call x2, Pallas kernels, gather_seq(): pl.pallas_call(functools.partial(gather_kernel, n, count), out_shape=tupl...  66.5 us
    psum x1, waiting for transfers between devices, local(): lax.psum((jnp.concatenate([ga_qkv, ga_o[None]], axis=0), jnp.stack([gb_qk...  64.3 us
    reduce_scatter x1, waiting for transfers between devices, local(): lax.psum_scatter(down_parts.reshape(seq_size * token_count, model_width),...  51.7 us
    psum x1, blocking collectives, local(): lax.psum((jnp.concatenate([ga_qkv, ga_o[None]], axis=0), jnp.stack([gb_qk...  38.5 us
    pallas_call x1, Pallas kernels, scatter_seq(): pl.pallas_call(functools.partial(scatter_kernel, n), out_shape=(jax.Shape...  31 us
    ppermute x1, waiting for transfers between devices, reshard_units(): from_b = lax.ppermute(mine, 'rows', swap)  22.4 us
  transfers between devices with their start and end apart: 8, of which 4 were waited for; matrix products, arithmetic and copies ran while one was open for 5% of the time, Pallas kernels for 34%

profile of v3, /device:TPU:0, one launch (start us, length us, event | category | flops | bytes accessed | tf_op | source)
XLA Modules:
  0.0 687.8 jit_solution(5627939379467815748)
XLA Ops:
  7.2 1.8 constant_dynamic-slice_fusion.2
  9.0 1.4 copy.66
  10.6 2.5 copy.51
  13.1 6.5 all-to-all-start
  19.8 0.9 copy-done.56
  20.7 1.6 maximum_maximum_fusion.xa
  22.4 130.8 %gather_weights.1 = bf16[2,8,4,64,2560]{4,3,2,1,0:T(8,128)(2,1)} custom-call(bf16[2,4,64,2560]{3,2,1,0:T(8,128)(2,1)} %maximum_maximum_fusion.xa), custom_call_target="tpu_custom_call" | custom-call | bytes 262144000 | tf_op jit(solution)/shard_map/gather_weights/pallas_call | solution.py:782
  155.2 3.3 copy.52
  158.5 1.1 collective-permute-start
  160.9 17.3 %project_qkv.1 = (bf16[128,2048]{1,0:T(8,128)(2,1)S(1)}, f32[128,3072]{1,0:T(8,128)S(1)}, bf16[128,2048]{1,0:T(8,128)(2,1)S(1)}, bf16[128,1024]{1,0:T(8,128)(2,1...) custom-call(bf16[128,2048]{1,0:T(8,128)(2,1)S(1)} %bitcast.116, f32[1,2048]{1,0:T(1,128)S(1)} %get-tuple-element.175.gain_ref, ...), custom_call_target="tpu_custom_call" | custom-call | flops 2684354560 | bytes 20971520 | tf_op jit(solution)/shard_map/project_qkv/pallas_call | solution.py:122
  178.3 1.1 collective-permute-start.1
  179.3 1.3 slice_reduce_fusion.6
  181.3 1.5 fusion.7
  184.3 22.4 %collective-permute-done = bf16[8,2,64,1024]{3,2,0,1:T(8,128)(2,1)} collective-permute-done((bf16[8,2,64,1024]{3,2,0,1:T(8,128)(2,1)}, bf16[8,2,64,1024]{3,2,0,1:T(8,128)(2,1)}, u32[]{:S(2)}, u32[]{:S(2)}) %collective-permute-start) | collective-permute-done | bytes 2097184 | tf_op jit(solution)/shard_map/ppermute | solution.py:1158
  206.7 2.3 slice_bitcast_fusion.1
  209.0 1.5 collective-permute-start.2
  210.5 16.6 %collective-permute-done.1 = bf16[8,2,64,1024]{3,2,0,1:T(8,128)(2,1)S(1)} collective-permute-done((bf16[8,2,64,1024]{3,2,0,1:T(8,128)(2,1)}, bf16[8,2,64,1024]{3,2,0,1:T(8,128)(2,1)S(1)}, u32[]{:S(2)}, u32[]{:S(2)}) %collective-permute-start.1) | collective-permute-done | bytes 2097184 | tf_op jit(solution)/shard_map/ppermute | solution.py:1159
  227.1 1.1 slice_bitcast_fusion
  228.2 1.0 collective-permute-start.3
  233.0 24.0 %gather_seq.2 = (bf16[8,128,1024]{2,1,0:T(8,128)(2,1)}, f32[8,1,2048]{2,1,0:T(1,128)}) custom-call(bf16[128,1024]{1,0:T(8,128)(2,1)} %copy-done.25, f32[1,2048]{1,0:T(1,128)} %bitcast.149), custom_call_target="tpu_custom_call" | custom-call | bytes 43253760 | tf_op jit(solution)/shard_map/gather_seq/pallas_call | solution.py:471
  257.0 1.6 copy-done.2
  259.3 9.6 %attend.1 = (bf16[2,64,2048]{2,1,0:T(8,128)(2,1)S(1)}, bf16[2,4,512,512]{3,2,1,0:T(8,128)(2,1)S(1)}) custom-call(s32[2]{0:T(128)S(1)} %copy-done.38, bf16[2,64,2048]{2,1,0:T(8,128)(2,1)S(1)} %bitcast.125, bf16[8,2,64,1024]{3,2,1,0:T(8,128)(2,1)S(1)} %bitcast.112, bf16[8,2,64,1024]{3,2,1,0:T(8,128)(2,1)S(1)} %bitcast.113), custom_call_target="tpu_custom_call" | custom-call | flops 1073741824 | bytes 8388608 | tf_op jit(solution)/shard_map/attend/pallas_call | solution.py:854
  269.6 6.6 project_out.1
  276.3 1.0 copy-done.9
  278.1 42.5 %gather_seq.3.refs_5_ = bf16[8,128,2048]{2,1,0:T(8,128)(2,1)} custom-call(bf16[128,2048]{1,0:T(8,128)(2,1)} %copy-done.24), custom_call_target="tpu_custom_call" | custom-call | bytes 83886080 | tf_op jit(solution)/shard_map/gather_seq/pallas_call | solution.py:471
  321.9 1.5 reduce_sum.236
  324.1 2.0 multiply_reduce_fusion.3
  326.1 1.0 pad_maximum_fusion.3.b_ref
  327.1 3.2 copy.54.refs_1_
  330.3 1.5 copy.55.refs_2_
  331.8 72.7 %feed_forward.1 = (f32[128,2048]{1,0:T(8,128)}, bf16[8,128,2048]{2,1,0:T(8,128)(2,1)}, f32[2,16,2048]{2,1,0:T(8,128)}, f32[2,16,1024]{2,1,0:T(8,128)}, f32[2,1,1...) custom-call(bf16[8,2,64,1024]{3,2,1,0:T(8,128)(2,1)} %all-to-all-done., ...), custom_call_target="tpu_custom_call" | custom-call | flops 25769803776 | bytes 33554432 | tf_op jit(solution)/shard_map/feed_forward/pallas_call | solution.py:1197
  404.6 1.2 copy-done.12
  405.8 8.4 %out_back.1 = (f32[128,2048]{1,0:T(8,128)S(1)}, bf16[128,2048]{1,0:T(8,128)(2,1)S(1)}, f32[16,2048]{1,0:T(8,128)S(1)}, f32[16,2048]{1,0:T(8,128)S(1)}, f32[1,2048]{1,0:T(1,128)S(1)}) custom-call(f32[128,2048]{1,0:T(8,128)S(1)} %copy-done.12, f32[128,2048]{1,0:T(8,128)S(1)} %get-tuple-element.58.x1_ref, f32[1,2048]{1,0:T(1,128)S(1)} %copy-done.33, ...), custom_call_target="tpu_custom_call" | custom-call | flops 1073741824 | bytes 8388608 | tf_op jit(solution)/shard_map/out_back/pallas_call | solution.py:256
  414.4 9.8 %attend_back.1 = (bf16[2,64,2048]{2,1,0:T(8,128)(2,1)S(1)}, bf16[8,2,64,1024]{3,2,1,0:T(8,128)(2,1)S(1)}) custom-call(bf16[2,64,2048]{2,1,0:T(8,128)(2,1)S(1)} %bitcast.126, bf16[8,2,64,1024]{3,2,1,0:T(8,128)(2,1)S(1)} %bitcast.114, bf16[8,2,64,1024]{3,2,1,0:T(8,128)(2,1)S(1)} %bitcast.115, bf16[2,4,512,512]{3,2,1,0:T(8,128)(2,1)S(1)} %copy-done.40, ...), custom_call_target="tpu_custom_call" | custom-call | flops 2684354560 | bytes 8388608 | tf_op jit(solution)/shard_map/attend_back/pallas_call | solution.py:909
  424.9 31.0 %scatter_seq.1 = (f32[128,1024]{1,0:T(8,128)S(1)}, f32[8,1,2048]{2,1,0:T(1,128)S(1)}) custom-call(bf16[8,128,1024]{2,1,0:T(8,128)(2,1)S(1)} %bitcast.123, f32[1,2048]{1,0:T(1,128)S(1)} %copy-done.37), custom_call_target="tpu_custom_call" | custom-call | bytes 41943040 | tf_op jit(solution)/shard_map/scatter_seq/pallas_call | solution.py:611
  456.9 3.5 fusion.8
  460.7 1.2 copy-done.11
  461.9 1.0 copy-done.17
  463.0 13.2 %qkv_back.1 = (f32[128,2048]{1,0:T(8,128)}, f32[3,16,2048]{2,1,0:T(8,128)S(1)}, f32[16,3072]{1,0:T(8,128)S(1)}, f32[1,3072]{1,0:T(1,128)S(1)}) custom-call(bf16[128,2048]{1,0:T(8,128)(2,1)S(1)} %bitcast.124, f32[128,1024]{1,0:T(8,128)S(1)} %copy-done.19, f32[128,128]{1,0:T(8,128)S(1)} %copy.49.cos_ref, f32[128,128]{1,0:T(8,128)S(1)} %copy.50.sin_ref, ...), custom_call_target="tpu_custom_call" | custom-call | flops 1610612736 | bytes 12582912 | tf_op jit(solution)/shard_map/qkv_back/pallas_call | solution.py:353
  478.6 1.0 broadcast_in_dim.30
  487.1 1.3 slice_reduce_fusion.3
  496.7 14.1 %all-gather.1 = f32[2,1,8192]{2,1,0:T(1,128)S(1)} all-gather(f32[2,1,1024]{2,1,0:T(1,128)S(1)} %copy-done.84), channel_id=3, replica_groups=mesh['rows'=4,'seq'=8] {'seq'}, dimensions={2}, use_global_device_ids=true | all-gather | bytes 73728 | tf_op jit(solution)/shard_map/all_gather | solution.py:1401
  517.3 38.5 %all-reduce = (f32[2048]{0:T(1024)}, f32[2,512]{1,0:T(2,128)}, f32[2048]{0:T(1024)}, f32[2048]{0:T(1024)}) all-reduce(f32[2048]{0:T(1024)S(1)} %bitcast.150, f32[2,512]{1,0:T(2,128)S(1)} %reshape_squeeze.3, f32[2048]{0:T(1024)S(1)} %bitcast.134, f32[2048]{0:T(1024)S(1)} %bitcast.133), channel_id=1, replica_groups=mesh['rows'=4,'seq'=8] {'rows','seq'}, use_global_device_ids=true, to_apply=%region_8.0 | all-reduce | flops 7168 | bytes 57344 | tf_op jit(solution)/shard_map/psum | solution.py:1384
  555.8 64.3 %all-reduce.4.cloned.1.call-done = (f32[4,16,2048]{2,1,0:T(8,128)}, f32[2,16,2048]{2,1,0:T(8,128)}, f32[2,16,512]{2,1,0:T(8,128)}, f32[2,16,2048]{2,1,0:T(8,128)...) async-done(((f32[4,16,2048]{2,1,0:T(8,128)}, f32[2,16,2048]{2,1,0:T(8,128)}, f32[2,16,512]{2,1,0:T(8,128)}, ...) | async-done | bytes 2883600 | tf_op jit(solution)/shard_map/psum | solution.py:1384
  620.2 51.7 %reduce-scatter.2.cloned.1.call-done = bf16[128,2048]{1,0:T(8,128)(2,1)} async-done(((bf16[1024,2048]{1,0:T(8,128)(2,1)}), bf16[128,2048]{1,0:T(8,128)(2,1)}) %reduce-scatter.2.cloned.1.call-update) | async-done | bytes 524304 | tf_op jit(solution)/shard_map/reduce_scatter | solution.py:1347
  671.9 2.1 add_convert_fusion
  674.0 2.0 copy.81
  678.0 1.0 copy.85
  (259 shorter events, 29.5 us)
Async XLA Ops:
  7.2 316.2 %copy-start = (f32[2,16,8192]{2,1,0:T(8,128)S(1)}, f32[2,16,8192]{2,1,0:T(8,128)}, u32[]{:S(2)}) copy-start(f32[2,16,8192]{2,1,0:T(8,128)} %param.35) | copy-start | bytes 3145732
  13.1 142.1 %all-to-all-start = ((bf16[8,2,64,1024]{3,2,1,0:T(8,128)(2,1)}), bf16[8,2,64,1024]{3,2,1,0:T(8,128)(2,1)}, u32[]{:S(2)}, u32[]{:S(2)}) async-start(bf16[8,2,64,1024]{3,2,1,0:T(8,128)(2,1)} %copy.51), calls=%async_computation | async-start | bytes 4194304 | tf_op jit(solution)/shard_map/all_to_all | solution.py:1155
  19.6 312.2 %all-gather.4.cloned.1.call-start = ((), (), s32[]{:S(2)}) async-start(), calls=%async_computation.3 | async-start | bytes 4718592 | tf_op jit(solution)/shard_map/all_gather | solution.py:1291
  22.4 131.0 %copy-start.52 = (f32[16,8192]{1,0:T(8,128)S(1)}, f32[16,8192]{1,0:T(8,128)}, u32[]{:S(2)}) copy-start(f32[16,8192]{1,0:T(8,128)} %param.37) | copy-start | bytes 1572868
  22.4 131.6 %copy-start.86 = (f32[2,512]{1,0:T(2,128)S(1)}, f32[2,512]{1,0:T(2,128)}, u32[]{:S(2)}) copy-start(f32[2,512]{1,0:T(2,128)} %param.32) | copy-start | bytes 12292
  22.4 131.8 %copy-start.69 = (f32[2,16,512]{2,1,0:T(8,128)S(1)}, f32[2,16,512]{2,1,0:T(8,128)}, u32[]{:S(2)}) copy-start(f32[2,16,512]{2,1,0:T(8,128)} %param.30) | copy-start | bytes 196612
  22.4 132.1 %copy-start.83 = (f32[2,2048]{1,0:T(2,128)S(1)}, f32[2,2048]{1,0:T(2,128)}, u32[]{:S(2)}) copy-start(f32[2,2048]{1,0:T(2,128)} %param.23) | copy-start | bytes 49156
  22.4 132.7 %copy-start.61 = (f32[2,16,2048]{2,1,0:T(8,128)S(1)}, f32[2,16,2048]{2,1,0:T(8,128)}, u32[]{:S(2)}) copy-start(f32[2,16,2048]{2,1,0:T(8,128)} %param.29) | copy-start | bytes 786436
  153.3 466.9 %all-reduce.4.cloned.1.call-start = ((), (), s32[]{:S(2)}) async-start(), calls=%async_computation.4 | async-start | bytes 5767168 | tf_op jit(solution)/shard_map/psum | solution.py:1384
  154.2 24.0 %copy-start.58 = (f32[16,512]{1,0:T(8,128)}, f32[16,512]{1,0:T(8,128)S(1)}, u32[]{:S(2)}) copy-start(f32[16,512]{1,0:T(8,128)S(1)} %get-tuple-element.167) | copy-start | bytes 98308
  155.1 23.1 %copy-start.50 = (f32[16,2048]{1,0:T(8,128)}, f32[16,2048]{1,0:T(8,128)S(1)}, u32[]{:S(2)}) copy-start(f32[16,2048]{1,0:T(8,128)S(1)} %get-tuple-element.163) | copy-start | bytes 393220
  158.5 48.2 %collective-permute-start = (bf16[8,2,64,1024]{3,2,0,1:T(8,128)(2,1)}, bf16[8,2,64,1024]{3,2,0,1:T(8,128)(2,1)}, u32[]{:S(2)}, u32[]{:S(2)}) collective-permute-start(bf16[8,2,64,1024]{3,2,0,1:T(8,128)(2,1)} %copy.52), channel_id=1, source_target_pairs={{0,8},{8,0},{16,24},{24,16},{1,9},{9,1},{17,25},{25,17},{2,10},{10... | collective-permute-start | bytes 6291464 | tf_op jit(solution)/shard_map/ppermute | solution.py:1158
  160.8 19.8 %copy-start.41 = (bf16[1024,2048]{1,0:T(8,128)(2,1)S(1)}, bf16[1024,2048]{1,0:T(8,128)(2,1)}, u32[]{:S(2)}) copy-start(bf16[1024,2048]{1,0:T(8,128)(2,1)} %refs_7_.1) | copy-start | bytes 12582916
  160.9 19.7 %copy-start.53 = (f32[16,1024]{1,0:T(8,128)S(1)}, f32[16,1024]{1,0:T(8,128)}, u32[]{:S(2)}) copy-start(f32[16,1024]{1,0:T(8,128)} %constant_dynamic-slice_fusion.3.refs_11_) | copy-start | bytes 196612
  178.3 51.4 %copy-start.34 = (f32[1,5120]{1,0:T(1,128)}, f32[1,5120]{1,0:T(1,128)S(1)}, u32[]{:S(2)}) copy-start(f32[1,5120]{1,0:T(1,128)S(1)} %get-tuple-element.57) | copy-start | bytes 61444
  178.3 48.8 %collective-permute-start.1 = (bf16[8,2,64,1024]{3,2,0,1:T(8,128)(2,1)}, bf16[8,2,64,1024]{3,2,0,1:T(8,128)(2,1)S(1)}, u32[]{:S(2)}, u32[]{:S(2)}) collective-permute-start(bf16[8,2,64,1024]{3,2,0,1:T(8,128)(2,1)} %copy.52), channel_id=1, source_target_pairs={{0,16},{8,24},{16,0},{24,8},{1,17},{9,25},{17,1},{25,9},{2,18},{10... | collective-permute-start | bytes 6291464 | tf_op jit(solution)/shard_map/ppermute | solution.py:1159
  183.6 45.5 %copy-start.87 = (s32[2]{0:T(128)S(1)}, s32[2]{0:T(128)}, u32[]{:S(2)}) copy-start(s32[2]{0:T(128)} %param.41) | copy-start | bytes 28
  184.3 72.7 %copy-start.22 = (bf16[128,2048]{1,0:T(8,128)(2,1)S(1)}, bf16[128,2048]{1,0:T(8,128)(2,1)}, u32[]{:S(2)}) copy-start(bf16[128,2048]{1,0:T(8,128)(2,1)} %copy-done.21) | copy-start | bytes 1572868
  209.0 122.8 %collective-permute-start.2 = (bf16[8,64,1024]{2,1,0:T(8,128)(2,1)}, bf16[8,64,1024]{2,1,0:T(8,128)(2,1)}, u32[]{:S(2)}, u32[]{:S(2)}) collective-permute-start(bf16[8,64,1024]{2,1,0:T(8,128)(2,1)} %slice_bitcast_fusion.1), channel_id=1, source_target_pairs={{0,16},{8,24},{16,0},{24,8},{1,17},{9,25},{17,1},{25,9},{2,18},{10... | collective-permute-start | bytes 3145736 | tf_op jit(solution)/shard_map/ppermute | solution.py:1162
  228.2 103.6 %collective-permute-start.3 = (bf16[8,64,1024]{2,1,0:T(8,128)(2,1)}, bf16[8,64,1024]{2,1,0:T(8,128)(2,1)}, u32[]{:S(2)}, u32[]{:S(2)}) collective-permute-start(bf16[8,64,1024]{2,1,0:T(8,128)(2,1)} %slice_bitcast_fusion), channel_id=1, source_target_pairs={{0,8},{8,0},{16,24},{24,16},{1,9},{9,1},{17,25},{25,17},{2,10},{10... | collective-permute-start | bytes 3145736 | tf_op jit(solution)/shard_map/ppermute | solution.py:1163
  268.9 7.4 %copy-start.39 = (bf16[2,4,512,512]{3,2,1,0:T(8,128)(2,1)}, bf16[2,4,512,512]{3,2,1,0:T(8,128)(2,1)S(1)}, u32[]{:S(2)}) copy-start(bf16[2,4,512,512]{3,2,1,0:T(8,128)(2,1)S(1)} %get-tuple-element.63.p_ref) | copy-start | bytes 12582916
  331.8 72.8 %copy-start.6 = (bf16[2,64,2048]{2,1,0:T(8,128)(2,1)S(1)}, bf16[2,64,2048]{2,1,0:T(8,128)(2,1)}, u32[]{:S(2)}) copy-start(bf16[2,64,2048]{2,1,0:T(8,128)(2,1)} %param.22) | copy-start | bytes 1572868
  331.8 72.8 %copy-start.20 = (f32[16,2048]{1,0:T(8,128)S(1)}, f32[16,2048]{1,0:T(8,128)}, u32[]{:S(2)}) copy-start(f32[16,2048]{1,0:T(8,128)} %slice.123.cross_ref) | copy-start | bytes 393220
  331.8 72.8 %copy-start.33 = (f32[1,2048]{1,0:T(1,128)S(1)}, f32[1,2048]{1,0:T(1,128)}, u32[]{:S(2)}) copy-start(f32[1,2048]{1,0:T(1,128)} %get-tuple-element.174.gain_ref) | copy-start | bytes 24580
  405.8 8.5 %copy-start.3 = (bf16[8,128,1024]{2,1,0:T(8,128)(2,1)S(1)}, bf16[8,128,1024]{2,1,0:T(8,128)(2,1)}, u32[]{:S(2)}) copy-start(bf16[8,128,1024]{2,1,0:T(8,128)(2,1)} %get-tuple-element.55) | copy-start | bytes 6291460
  405.8 8.5 %copy-start.23 = (bf16[128,2048]{1,0:T(8,128)(2,1)S(1)}, bf16[128,2048]{1,0:T(8,128)(2,1)}, u32[]{:S(2)}) copy-start(bf16[128,2048]{1,0:T(8,128)(2,1)} %copy-done.21) | copy-start | bytes 1572868
  405.8 8.5 %copy-start.40 = (bf16[2,4,512,512]{3,2,1,0:T(8,128)(2,1)S(1)}, bf16[2,4,512,512]{3,2,1,0:T(8,128)(2,1)}, u32[]{:S(2)}) copy-start(bf16[2,4,512,512]{3,2,1,0:T(8,128)(2,1)} %copy-done.39) | copy-start | bytes 12582916
  414.2 9.9 %copy-start.10 = (f32[128,2048]{1,0:T(8,128)}, f32[128,2048]{1,0:T(8,128)S(1)}, u32[]{:S(2)}) copy-start(f32[128,2048]{1,0:T(8,128)S(1)} %get-tuple-element.74.gx_ref) | copy-start | bytes 3145732
  414.3 9.9 %copy-start.26 = (f32[16,2048]{1,0:T(8,128)}, f32[16,2048]{1,0:T(8,128)S(1)}, u32[]{:S(2)}) copy-start(f32[16,2048]{1,0:T(8,128)S(1)} %get-tuple-element.79) | copy-start | bytes 393220
  414.3 9.9 %copy-start.28 = (f32[16,2048]{1,0:T(8,128)}, f32[16,2048]{1,0:T(8,128)S(1)}, u32[]{:S(2)}) copy-start(f32[16,2048]{1,0:T(8,128)S(1)} %get-tuple-element.77) | copy-start | bytes 393220
  414.3 10.6 %copy-start.37 = (f32[1,2048]{1,0:T(1,128)S(1)}, f32[1,2048]{1,0:T(1,128)}, u32[]{:S(2)}) copy-start(f32[1,2048]{1,0:T(1,128)} %get-tuple-element.70.e_ref) | copy-start | bytes 24580
  414.3 42.5 %copy-start.77 = (f32[2048]{0:T(1024)S(1)}, f32[2048]{0:T(1024)}, u32[]{:S(2)}) copy-start(f32[2048]{0:T(1024)} %param.39) | copy-start | bytes 24580
  414.3 42.5 %copy-start.78 = (f32[2048]{0:T(1024)S(1)}, f32[2048]{0:T(1024)}, u32[]{:S(2)}) copy-start(f32[2048]{0:T(1024)} %get-tuple-element.156) | copy-start | bytes 24580
  414.3 42.6 %copy-start.45 = (f32[16,2048]{1,0:T(8,128)S(1)}, f32[16,2048]{1,0:T(8,128)}, u32[]{:S(2)}) copy-start(f32[16,2048]{1,0:T(8,128)} %refs_12_.1) | copy-start | bytes 393220
  463.0 13.3 %copy-start.54 = (f32[16,1024]{1,0:T(8,128)S(1)}, f32[16,1024]{1,0:T(8,128)}, u32[]{:S(2)}) copy-start(f32[16,1024]{1,0:T(8,128)} %constant_dynamic-slice_fusion.3.refs_11_) | copy-start | bytes 196612
  463.0 14.1 %copy-start.27 = (f32[16,2048]{1,0:T(8,128)S(1)}, f32[16,2048]{1,0:T(8,128)}, u32[]{:S(2)}) copy-start(f32[16,2048]{1,0:T(8,128)} %copy-done.26) | copy-start | bytes 393220
  463.0 14.8 %copy-start.29 = (f32[16,2048]{1,0:T(8,128)S(1)}, f32[16,2048]{1,0:T(8,128)}, u32[]{:S(2)}) copy-start(f32[16,2048]{1,0:T(8,128)} %copy-done.28) | copy-start | bytes 393220
  481.4 7.0 %copy-start.82 = (f32[1,512]{1,0:T(1,128)S(1)}, f32[1,512]{1,0:T(1,128)}, u32[]{:S(2)}) copy-start(f32[1,512]{1,0:T(1,128)} %copy-done.81) | copy-start | bytes 6148
  481.4 9.8 %copy-start.80 = (f32[1,512]{1,0:T(1,128)S(1)}, f32[1,512]{1,0:T(1,128)}, u32[]{:S(2)}) copy-start(f32[1,512]{1,0:T(1,128)} %copy-done.79) | copy-start | bytes 6148
  481.4 12.6 %copy-start.75 = (f32[2048]{0:T(1024)S(1)}, f32[2048]{0:T(1024)}, u32[]{:S(2)}) copy-start(f32[2048]{0:T(1024)} %param.31) | copy-start | bytes 24580
  481.4 12.6 %copy-start.76 = (f32[1,2048]{1,0:T(1,128)S(1)}, f32[1,2048]{1,0:T(1,128)}, u32[]{:S(2)}) copy-start(f32[1,2048]{1,0:T(1,128)} %get-tuple-element.171) | copy-start | bytes 24580
  481.4 15.3 %copy-start.84 = (f32[2,1,1024]{2,1,0:T(1,128)S(1)}, f32[2,1,1024]{2,1,0:T(1,128)}, u32[]{:S(2)}) copy-start(f32[2,1,1024]{2,1,0:T(1,128)} %get-tuple-element.88) | copy-start | bytes 24580
  481.4 29.3 %copy-start.67 = (f32[2,8192]{1,0:T(2,128)S(1)}, f32[2,8192]{1,0:T(2,128)}, u32[]{:S(2)}) copy-start(f32[2,8192]{1,0:T(2,128)} %param.36) | copy-start | bytes 196612
  481.4 190.4 %reduce-scatter.2.cloned.1.call-start = ((), (), s32[]{:S(2)}) async-start(), calls=%async_computation.2 | async-start | bytes 4718592 | tf_op jit(solution)/shard_map/reduce_scatter | solution.py:1347
  620.1 55.8 %copy-start.63 = (f32[2,16,2048]{2,1,0:T(8,128)S(1)}, f32[2,16,2048]{2,1,0:T(8,128)}, u32[]{:S(2)}) copy-start(f32[2,16,2048]{2,1,0:T(8,128)} %get-tuple-element.199) | copy-start | bytes 786436
  620.1 56.5 %copy-start.71 = (f32[2,16,512]{2,1,0:T(8,128)S(1)}, f32[2,16,512]{2,1,0:T(8,128)}, u32[]{:S(2)}) copy-start(f32[2,16,512]{2,1,0:T(8,128)} %get-tuple-element.200) | copy-start | bytes 196612
  620.2 57.1 %copy-start.62 = (f32[2,16,2048]{2,1,0:T(8,128)S(1)}, f32[2,16,2048]{2,1,0:T(8,128)}, u32[]{:S(2)}) copy-start(f32[2,16,2048]{2,1,0:T(8,128)} %get-tuple-element.204) | copy-start | bytes 786436
  674.0 7.1 %copy-start.1 = (f32[2,16,8192]{2,1,0:T(8,128)S(1)}, f32[2,16,8192]{2,1,0:T(8,128)}, u32[]{:S(2)}) copy-start(f32[2,16,8192]{2,1,0:T(8,128)} %param.35) | copy-start | bytes 3145732
  (48 other events, 171.1 us)
Sparse Core Ops, SparseCore 0:
  153.4 44.7 all-gather.3
  481.5 138.6 all-reduce.3
  622.4 49.3 reduce-scatter.1

commit v4 on v3

--- a/solution.py
+++ b/solution.py
@@ -399,231 +399,6 @@
     pl.semaphore_wait(barrier, 1 + jnp.where(q > 0, 1, 0) + jnp.where(q < nc - 1, 1, 0))
     return sibling
 
-
-def gather_kernel(n, count, *refs):
-    nc = n // 2
-    xs, outs = refs[:count], refs[count : 2 * count]
-    local_sem, to_sib, to_left, to_right, recv = refs[2 * count :]
-    s, q, c = place_in_seq()
-    sibling = greet(nc, q, s)
-    locals_ = [
-        pltpu.make_async_copy(xs[k], outs[k].at[s], local_sem.at[k]) for k in range(count)
-    ]
-    for cp in locals_:
-        cp.start()
-
-    def copy(k, src, slot, sems, target):
-        return pltpu.make_async_remote_copy(
-            src_ref=src,
-            dst_ref=outs[k].at[slot],
-            send_sem=sems.at[k, slot],
-            recv_sem=recv.at[k, slot],
-            device_id={"seq": target},
-            device_id_type=MESH,
-        )
-
-    for k in range(count):
-        pl.when(q > 0)(lambda k=k: copy(k, xs[k], s, to_left, s - 2).start())
-        pl.when(q < nc - 1)(lambda k=k: copy(k, xs[k], s, to_right, s + 2).start())
-        copy(k, xs[k], s, to_sib, sibling).start()
-    for t in range(1, nc):
-
-        @pl.when(q - t >= 0)
-        def _(t=t):
-            slot = s - 2 * t
-            for k in range(count):
-                src = outs[k].at[slot]
-                copy(k, src, slot, to_right, s).wait_recv()
-                pl.when(q < nc - 1)(
-                    lambda k=k: copy(k, src, slot, to_right, s + 2).start()
-                )
-                copy(k, src, slot, to_sib, sibling).start()
-
-        @pl.when(q + t < nc)
-        def _(t=t):
-            slot = s + 2 * t
-            for k in range(count):
-                src = outs[k].at[slot]
-                copy(k, src, slot, to_left, s).wait_recv()
-                pl.when(q > 0)(lambda k=k: copy(k, src, slot, to_left, s - 2).start())
-                copy(k, src, slot, to_sib, sibling).start()
-
-    for cp in locals_:
-        cp.wait()
-    other = 1 - 2 * c
-    for p in range(nc):
-        mine, theirs = 2 * p + c, 2 * p + c + other
-        for k in range(count):
-            copy(k, outs[k].at[theirs], theirs, to_sib, sibling).wait_recv()
-            copy(k, outs[k].at[mine], mine, to_sib, sibling).wait_send()
-            pl.when((q < nc - 1) & (p <= q))(
-                lambda k=k: copy(k, outs[k].at[mine], mine, to_right, sibling).wait_send()
-            )
-            pl.when((q > 0) & (p >= q))(
-                lambda k=k: copy(k, outs[k].at[mine], mine, to_left, sibling).wait_send()
-            )
-
-
-def gather_seq(n, arrays, collective_id):
-    count = len(arrays)
-    nbytes = sum(a.size * a.dtype.itemsize for a in arrays)
-    dma = pltpu.SemaphoreType.DMA
-    return pl.pallas_call(
-        functools.partial(gather_kernel, n, count),
-        out_shape=tuple(jax.ShapeDtypeStruct((n, *a.shape), a.dtype) for a in arrays),
-        in_specs=[pl.BlockSpec(memory_space=pl.ANY)] * count,
-        out_specs=tuple([pl.BlockSpec(memory_space=pl.ANY)] * count),
-        scratch_shapes=[dma((count,))] + [dma((count, n))] * 4,
-        compiler_params=pltpu.CompilerParams(collective_id=collective_id, has_side_effects=True),
-        cost_estimate=pl.CostEstimate(flops=0, transcendentals=0, bytes_accessed=nbytes * n * 20),
-        name="gather_seq",
-    )(*arrays)
-
-
-def scatter_kernel(n, x_ref, e_ref, o_ref, all_ref, own, sib, from_left, from_right,
-                   load_sem, to_sib, sib_in, to_right, right_in, to_left, left_in, e_out, e_in):
-    nc = n // 2
-    s, q, c = place_in_seq()
-    sibling = s + 1 - 2 * c
-    theirs = 1 - c
-    barrier = pltpu.get_barrier_semaphore()
-    for t in range(1, n):
-        pl.semaphore_signal(
-            barrier, inc=1, device_id={"seq": lax.rem(s + t, n)}, device_id_type=MESH
-        )
-    pl.semaphore_wait(barrier, n - 1)
-
-    def small(t, slot):
-        return pltpu.make_async_remote_copy(
-            src_ref=e_ref,
-            dst_ref=all_ref.at[slot],
-            send_sem=e_out.at[t],
-            recv_sem=e_in.at[t],
-            device_id={"seq": lax.rem(s + t, n)},
-            device_id_type=MESH,
-        )
-
-    for t in range(1, n):
-        small(t, s).start()
-    all_ref[s] = e_ref[...]
-
-    def load(p):
-        return pltpu.make_async_copy(x_ref.at[2 * p + c], own.at[p], load_sem.at[p])
-
-    def to_sibling(p):
-        return pltpu.make_async_remote_copy(
-            src_ref=x_ref.at[2 * p + theirs],
-            dst_ref=sib.at[p],
-            send_sem=to_sib.at[p],
-            recv_sem=sib_in.at[p],
-            device_id={"seq": sibling},
-            device_id_type=MESH,
-        )
-
-    def rightward(p, target):
-        return pltpu.make_async_remote_copy(
-            src_ref=own.at[p],
-            dst_ref=from_left.at[p],
-            send_sem=to_right.at[p],
-            recv_sem=right_in.at[p],
-            device_id={"seq": target},
-            device_id_type=MESH,
-        )
-
-    def leftward(p, target):
-        return pltpu.make_async_remote_copy(
-            src_ref=own.at[p],
-            dst_ref=from_right.at[p],
-            send_sem=to_left.at[p],
-            recv_sem=left_in.at[p],
-            device_id={"seq": target},
-            device_id_type=MESH,
-        )
-
-    order = []
-    for t in range(nc):
-        for p in (nc - 1 - t, t):
-            if p not in order:
-                order.append(p)
-    for p in order:
-        to_sibling(p).start()
-        load(p).start()
-
-    f32 = jnp.float32
-    for p in order:
-        load(p).wait()
-        to_sibling(p).wait_recv()
-
-        @pl.when(p > q)
-        def _(p=p):
-            @pl.when(q > 0)
-            def _():
-                rightward(p, s).wait_recv()
-                total = own[p].astype(f32) + sib[p].astype(f32) + from_left[p].astype(f32)
-                own[p] = total.astype(own.dtype)
-
-            @pl.when(q == 0)
-            def _():
-                own[p] = (own[p].astype(f32) + sib[p].astype(f32)).astype(own.dtype)
-
-            rightward(p, s + 2).start()
-
-        @pl.when(p < q)
-        def _(p=p):
-            @pl.when(q < nc - 1)
-            def _():
-                leftward(p, s).wait_recv()
-                total = own[p].astype(f32) + sib[p].astype(f32) + from_right[p].astype(f32)
-                own[p] = total.astype(own.dtype)
-
-            @pl.when(q == nc - 1)
-            def _():
-                own[p] = (own[p].astype(f32) + sib[p].astype(f32)).astype(own.dtype)
-
-            leftward(p, s - 2).start()
-
-    o_ref[...] = own[q].astype(f32) + sib[q].astype(f32)
-
-    @pl.when(q > 0)
-    def _():
-        rightward(q, s).wait_recv()
-        o_ref[...] += from_left[q].astype(f32)
-
-    @pl.when(q < nc - 1)
-    def _():
-        leftward(q, s).wait_recv()
-        o_ref[...] += from_right[q].astype(f32)
-
-    for t in range(1, n):
-        small(t, lax.rem(s - t + n, n)).wait_recv()
-        small(t, s).wait_send()
-    for p in range(nc):
-        to_sibling(p).wait_send()
-        pl.when(p > q)(lambda p=p: rightward(p, s).wait_send())
-        pl.when(p < q)(lambda p=p: leftward(p, s).wait_send())
-
-
-def scatter_seq(n, x, extra, collective_id):
-    nc = n // 2
-    _, rows, cols = x.shape
-    dma = pltpu.SemaphoreType.DMA
-    buf = pltpu.VMEM((nc, rows, cols), x.dtype)
-    return pl.pallas_call(
-        functools.partial(scatter_kernel, n),
-        out_shape=(
-            jax.ShapeDtypeStruct((rows, cols), jnp.float32),
-            jax.ShapeDtypeStruct((n, *extra.shape), extra.dtype),
-        ),
-        in_specs=[pl.BlockSpec(memory_space=pl.ANY), pl.BlockSpec(memory_space=pltpu.VMEM)],
-        out_specs=(pl.BlockSpec(memory_space=pltpu.VMEM),) * 2,
-        scratch_shapes=[buf] * 4 + [dma((nc,))] * 7 + [dma((n,))] * 2,
-        compiler_params=pltpu.CompilerParams(
-            collective_id=collective_id, has_side_effects=True, vmem_limit_bytes=32 << 20
-        ),
-        cost_estimate=pl.CostEstimate(flops=0, transcendentals=0, bytes_accessed=x.size * 2 * 20),
-        name="scatter_seq",
-    )(x, extra)
-
 def near_first(i, q, nc):
     short = jnp.where(q <= nc - 1 - q, q, nc - 1 - q)
     far = jnp.where(q <= nc - 1 - q, i, nc - 1 - i)
@@ -632,36 +407,43 @@
     return jnp.where(i <= 2 * short, near, far)
 
 
-def weights_kernel(n, rows, xa, wa, local, edge, a_in, a_sib_in, a_out, a_sib_out):
-    nc, half = n // 2, rows // 2
-    others = half - 1
-    s, q, c = place_in_seq()
-    sibling = s + 1 - 2 * c
+def place_in_rows(rows):
+    half = rows // 2
     r = lax.axis_index("rows")
     a, b = r // 2, lax.rem(r, 2)
-    b_row = r + 1 - 2 * b
-
-    def a_row(k):
-        return lax.rem(a + k + half, half) * 2 + b
-
-    def diagonal(k):
-        return lax.rem(a + k + half, half) * 2 + 1 - b
-
+    turned = lambda k: 2 * lax.rem(a + k + half, half)
+    return r, 2 * a + 1 - b, lambda k: turned(k) + b, lambda k: turned(k) + 1 - b
+
+
+def greet_all(n, rows):
+    s = lax.axis_index("seq")
+    r, b_row, a_row, _ = place_in_rows(rows)
     barrier = pltpu.get_barrier_semaphore()
     for t in range(1, n):
         pl.semaphore_signal(
             barrier, inc=1, device_id=(r, lax.rem(s + t, n)), device_id_type=MESH
         )
     pl.semaphore_signal(barrier, inc=1, device_id=(b_row, s), device_id_type=MESH)
-    for k in range(1, half):
+    for k in range(1, rows // 2):
         pl.semaphore_signal(barrier, inc=1, device_id=(a_row(k), s), device_id_type=MESH)
-    pl.semaphore_wait(barrier, n - 1 + half)
-
-    def remote(src, dst, send, recv, row, seq):
-        return pltpu.make_async_remote_copy(
-            src_ref=src, dst_ref=dst, send_sem=send, recv_sem=recv,
-            device_id=(row, seq), device_id_type=MESH,
-        )
+    pl.semaphore_wait(barrier, n - 1 + rows // 2)
+
+
+def remote(src, dst, send, recv, row, seq):
+    return pltpu.make_async_remote_copy(
+        src_ref=src, dst_ref=dst, send_sem=send, recv_sem=recv,
+        device_id=(row, seq), device_id_type=MESH,
+    )
+
+
+def weights_kernel(n, rows, xa, xg, wa, gz, near, local, edge, a_in, a_sib_in, a_out, a_sib_out, z_in, z_out):
+    nc, half = n // 2, rows // 2
+    others = half - 1
+    units = gz.shape[-1]
+    s, q, c = place_in_seq()
+    sibling = s + 1 - 2 * c
+    r, b_row, a_row, diagonal = place_in_rows(rows)
+    greet_all(n, rows)
 
     both, first, second = pl.ds(0, 2), pl.ds(0, 1), pl.ds(1, 1)
     LINE, FROM_B = 0, 1
@@ -710,6 +492,19 @@
             a_sib_out.at[p, kind], a_sib_in.at[p, kind], r, sibling,
         )
 
+    def columns(device):
+        return pl.ds(pl.multiple_of(device * units, units), units)
+
+    def z_send(p, core):
+        return remote(
+            xg.at[:, r, :, columns(2 * p + core)], gz.at[:, s],
+            z_out.at[p, core], z_in.at[q, c], r, 2 * p + core,
+        )
+
+    def z_arrival(p, core):
+        slot = gz.at[:, 2 * p + core]
+        return remote(slot, slot, z_out.at[p, core], z_in.at[p, core], r, s)
+
     def line_send(p, src, sem, target):
         return remote(src, a_view(p, c, both, r), sem, a_in.at[p, LINE], r, target)
 
@@ -720,15 +515,13 @@
     pl.when(q < nc - 1)(lambda: to_right().start())
     order = [near_first(i, q, nc) for i in range(nc)]
     sib_a = lambda: remote(xa, wa.at[:, s], edge.at[2], edge.at[3], r, sibling)
+    sib_g = lambda: remote(
+        xg.at[:, :, :, columns(sibling)], near.at[:, c], edge.at[4], edge.at[5], r, sibling
+    )
     keep_a = pltpu.make_async_copy(xa, wa.at[:, s], local.at[0])
+    keep_g = pltpu.make_async_copy(xg.at[:, :, :, columns(s)], near.at[:, c], local.at[1])
     sib_a().start()
     keep_a.start()
-
-    def spread_a(p):
-        a_send(p, both, r, FROM_B, b_row).start()
-        for k in range(1, half):
-            a_send(p, both, r, from_a(k), a_row(k)).start()
-
     for p in order[1:]:
         a_arrival(p, LINE).wait_recv()
         pl.when((p < q) & (q < nc - 1))(
@@ -737,8 +530,14 @@
         pl.when((p > q) & (q > 0))(
             lambda p=p: line_send(p, a_view(p, c, both, r), a_out.at[p, LINE], s - 2).start()
         )
-        spread_a(p)
+        a_send(p, both, r, FROM_B, b_row).start()
+        for k in range(1, half):
+            a_send(p, both, r, from_a(k), a_row(k)).start()
         a_to_sibling(p, LINE, c).start()
+        for core in range(2):
+            z_send(p, core).start()
+    sib_g().start()
+    keep_g.start()
     for p in order[1:]:
         a_arrival(p, FROM_B).wait_recv()
         for k in range(1, half):
@@ -754,7 +553,9 @@
                 a_arrival(p, kind).wait_recv()
                 a_to_sibling(p, kind, c).start()
     keep_a.wait()
+    keep_g.wait()
     sib_a().wait()
+    sib_g().wait()
     pl.when(q > 0)(lambda: to_left().wait_send())
     pl.when(q < nc - 1)(lambda: to_right().wait_send())
     for p in order[1:]:
@@ -769,29 +570,245 @@
             a_send(p, both, r, from_a(k), r).wait_send()
             a_send(p, first, b_row, relay_a(k), r).wait_send()
             a_send(p, second, a_row(-k), relay_b(k), r).wait_send()
-
-
-def gather_weights(n, rows, xa, collective_id):
+        for core in range(2):
+            z_send(p, core).wait_send()
+            z_arrival(p, core).wait_recv()
+
+
+def gather_weights(n, rows, xa, xg, collective_id):
     nc = n // 2
     block = xa.shape[1]
     part = block // rows
     xa = xa.reshape(2, rows, part, xa.shape[2])
+    xg = xg.reshape(2, rows, part, xg.shape[2])
+    units = xg.shape[3] // n
     kinds = 2 + 3 * (rows // 2 - 1)
     dma = pltpu.SemaphoreType.DMA
     anywhere = pl.BlockSpec(memory_space=pl.ANY)
-    wa = pl.pallas_call(
+    shape = jax.ShapeDtypeStruct
+    wa, gz, near = pl.pallas_call(
         functools.partial(weights_kernel, n, rows),
-        out_shape=jax.ShapeDtypeStruct((2, n, rows, part, xa.shape[3]), xa.dtype),
-        in_specs=[anywhere],
-        out_specs=anywhere,
-        scratch_shapes=[dma((1,)), dma((4,))] + [dma((nc, kinds))] * 4,
+        out_shape=(
+            shape((2, n, rows, part, xa.shape[3]), xa.dtype),
+            shape((2, n, part, units), xg.dtype),
+            shape((2, 2, rows, part, units), xg.dtype),
+        ),
+        in_specs=[anywhere] * 2,
+        out_specs=(anywhere,) * 3,
+        scratch_shapes=[dma((2,)), dma((6,))] + [dma((nc, kinds))] * 4 + [dma((nc, 2))] * 2,
         compiler_params=pltpu.CompilerParams(collective_id=collective_id, has_side_effects=True),
         cost_estimate=pl.CostEstimate(
             flops=0, transcendentals=0, bytes_accessed=250 * 1024 * 1024
         ),
         name="gather_weights",
-    )(xa)
-    return wa.reshape(2, n * block, -1)
+    )(xa, xg)
+    return wa.reshape(2, n * block, -1), gz, near
+
+
+def gather_kernel(n, rows, count, shared, *refs):
+    nc = n // 2
+    sources = refs[: count + len(shared[0])]
+    outs = refs[len(sources) : 2 * len(sources) - len(shared[0]) + len(shared[1])]
+    local_sem, to_sib, to_left, to_right, recv, share_out, share_in = refs[len(sources) + len(outs) :]
+    xs, held, swapped = sources[:count], sources[count:], outs[count:]
+    s, q, c = place_in_seq()
+    sibling = s + 1 - 2 * c
+    r, b_row, a_row, _ = place_in_rows(rows)
+    greet_all(n, rows)
+    locals_ = [
+        pltpu.make_async_copy(xs[k], outs[k].at[s], local_sem.at[k]) for k in range(count)
+    ]
+    for cp in locals_:
+        cp.start()
+
+    def copy(k, src, slot, sems, target):
+        return remote(src, outs[k].at[slot], sems.at[k, slot], recv.at[k, slot], r, target)
+
+    def share(i, p):
+        source, piece, turn, _ = shared[1][i]
+        pair = pl.ds(2 * p, 2)
+        src = held[source].at[pair] if piece is None else held[source].at[piece, pair]
+        target = b_row if turn == 0 else a_row(turn)
+        return remote(src, swapped[i].at[pair], share_out.at[i, p], share_in.at[i, p], target, s)
+
+    for k in range(count):
+        pl.when(q > 0)(lambda k=k: copy(k, xs[k], s, to_left, s - 2).start())
+        pl.when(q < nc - 1)(lambda k=k: copy(k, xs[k], s, to_right, s + 2).start())
+        copy(k, xs[k], s, to_sib, sibling).start()
+    order = [near_first(i, q, nc) for i in range(nc)]
+    for p in order[1:]:
+        for i in range(len(shared[1])):
+            share(i, p).start()
+    for p in order[1:]:
+        slot = 2 * p + c
+        for k in range(count):
+            src = outs[k].at[slot]
+            copy(k, src, slot, to_right, s).wait_recv()
+            pl.when((p < q) & (q < nc - 1))(
+                lambda k=k, src=src, slot=slot: copy(k, src, slot, to_right, s + 2).start()
+            )
+            pl.when((p > q) & (q > 0))(
+                lambda k=k, src=src, slot=slot: copy(k, src, slot, to_left, s - 2).start()
+            )
+            copy(k, src, slot, to_sib, sibling).start()
+    for cp in locals_:
+        cp.wait()
+    for p in range(nc):
+        mine, theirs = 2 * p + c, 2 * p + 1 - c
+        for k in range(count):
+            copy(k, outs[k].at[theirs], theirs, to_sib, sibling).wait_recv()
+            copy(k, outs[k].at[mine], mine, to_sib, sibling).wait_send()
+            pl.when((q < nc - 1) & (p <= q))(
+                lambda k=k, mine=mine: copy(k, outs[k].at[mine], mine, to_right, s).wait_send()
+            )
+            pl.when((q > 0) & (p >= q))(
+                lambda k=k, mine=mine: copy(k, outs[k].at[mine], mine, to_left, s).wait_send()
+            )
+    for p in order[1:]:
+        for i in range(len(shared[1])):
+            share(i, p).wait_send()
+            share(i, p).wait_recv()
+
+
+def gather_seq(n, rows, arrays, collective_id, held=(), shares=()):
+    nc, count = n // 2, len(arrays)
+    nbytes = sum(a.size * a.dtype.itemsize for a in arrays)
+    dma = pltpu.SemaphoreType.DMA
+    shape = jax.ShapeDtypeStruct
+    outs = [shape((n, *a.shape), a.dtype) for a in arrays]
+    outs += [shape(held[source].shape[-3:], held[source].dtype) for source, _, _ in shares]
+    anywhere = pl.BlockSpec(memory_space=pl.ANY)
+    listed = (tuple(held), [(source, piece, turn, None) for source, piece, turn in shares])
+    sems = dma((max(1, len(shares)), nc))
+    got = pl.pallas_call(
+        functools.partial(gather_kernel, n, rows, count, (range(len(held)), listed[1])),
+        out_shape=tuple(outs),
+        in_specs=[anywhere] * (count + len(held)),
+        out_specs=(anywhere,) * len(outs),
+        scratch_shapes=[dma((count,))] + [dma((count, n))] * 4 + [sems] * 2,
+        compiler_params=pltpu.CompilerParams(collective_id=collective_id, has_side_effects=True),
+        cost_estimate=pl.CostEstimate(flops=0, transcendentals=0, bytes_accessed=nbytes * n * 20),
+        name="gather_seq",
+    )(*arrays, *held)
+    return got[:count], got[count:]
+
+def scatter_kernel(n, x_ref, o_ref, own, sib, from_left, from_right,
+                   load_sem, to_sib, sib_in, to_right, right_in, to_left, left_in):
+    nc = n // 2
+    s, q, c = place_in_seq()
+    sibling = greet(nc, q, s)
+    theirs = 1 - c
+
+    def load(p):
+        return pltpu.make_async_copy(x_ref.at[2 * p + c], own.at[p], load_sem.at[p])
+
+    def to_sibling(p):
+        return pltpu.make_async_remote_copy(
+            src_ref=x_ref.at[2 * p + theirs],
+            dst_ref=sib.at[p],
+            send_sem=to_sib.at[p],
+            recv_sem=sib_in.at[p],
+            device_id={"seq": sibling},
+            device_id_type=MESH,
+        )
+
+    def rightward(p, target):
+        return pltpu.make_async_remote_copy(
+            src_ref=own.at[p],
+            dst_ref=from_left.at[p],
+            send_sem=to_right.at[p],
+            recv_sem=right_in.at[p],
+            device_id={"seq": target},
+            device_id_type=MESH,
+        )
+
+    def leftward(p, target):
+        return pltpu.make_async_remote_copy(
+            src_ref=own.at[p],
+            dst_ref=from_right.at[p],
+            send_sem=to_left.at[p],
+            recv_sem=left_in.at[p],
+            device_id={"seq": target},
+            device_id_type=MESH,
+        )
+
+    order = []
+    for t in range(nc):
+        for p in (nc - 1 - t, t):
+            if p not in order:
+                order.append(p)
+    for p in order:
+        to_sibling(p).start()
+        load(p).start()
+
+    f32 = jnp.float32
+    for p in order:
+        load(p).wait()
+        to_sibling(p).wait_recv()
+
+        @pl.when(p > q)
+        def _(p=p):
+            @pl.when(q > 0)
+            def _():
+                rightward(p, s).wait_recv()
+                total = own[p].astype(f32) + sib[p].astype(f32) + from_left[p].astype(f32)
+                own[p] = total.astype(own.dtype)
+
+            @pl.when(q == 0)
+            def _():
+                own[p] = (own[p].astype(f32) + sib[p].astype(f32)).astype(own.dtype)
+
+            rightward(p, s + 2).start()
+
+        @pl.when(p < q)
+        def _(p=p):
+            @pl.when(q < nc - 1)
+            def _():
+                leftward(p, s).wait_recv()
+                total = own[p].astype(f32) + sib[p].astype(f32) + from_right[p].astype(f32)
+                own[p] = total.astype(own.dtype)
+
+            @pl.when(q == nc - 1)
+            def _():
+                own[p] = (own[p].astype(f32) + sib[p].astype(f32)).astype(own.dtype)
+
+            leftward(p, s - 2).start()
+
+    o_ref[...] = own[q].astype(f32) + sib[q].astype(f32)
+
+    @pl.when(q > 0)
+    def _():
+        rightward(q, s).wait_recv()
+        o_ref[...] += from_left[q].astype(f32)
+
+    @pl.when(q < nc - 1)
+    def _():
+        leftward(q, s).wait_recv()
+        o_ref[...] += from_right[q].astype(f32)
+
+    for p in range(nc):
+        to_sibling(p).wait_send()
+        pl.when(p > q)(lambda p=p: rightward(p, s).wait_send())
+        pl.when(p < q)(lambda p=p: leftward(p, s).wait_send())
+
+
+def scatter_seq(n, x, collective_id):
+    nc = n // 2
+    _, rows, cols = x.shape
+    dma = pltpu.SemaphoreType.DMA
+    buf = pltpu.VMEM((nc, rows, cols), x.dtype)
+    return pl.pallas_call(
+        functools.partial(scatter_kernel, n),
+        out_shape=jax.ShapeDtypeStruct((rows, cols), jnp.float32),
+        in_specs=[pl.BlockSpec(memory_space=pl.ANY)],
+        out_specs=pl.BlockSpec(memory_space=pltpu.VMEM),
+        scratch_shapes=[buf] * 4 + [dma((nc,))] * 7,
+        compiler_params=pltpu.CompilerParams(
+            collective_id=collective_id, has_side_effects=True, vmem_limit_bytes=32 << 20
+        ),
+        cost_estimate=pl.CostEstimate(flops=0, transcendentals=0, bytes_accessed=x.size * 2 * 20),
+        name="scatter_seq",
+    )(x)
 
 def swap_halves(x):
     return pltpu.roll(x.astype(jnp.float32), HEAD_DIM, 1)
@@ -939,20 +956,18 @@
     return jnp.where(i <= 2 * short, near, far)
 
 
-def ffn_kernel(n, rows, pieces, u_hbm, gy_hbm, wd_hbm, a_ref, b_ref, m_ref, ad_ref, bd_ref, md_ref, nd_ref,
-               in_ref, down_hbm, ga_ref, gb_ref, gm_ref, norm_ref, gad_ref, gbd_ref, gmd_ref,
-               w_parts, wd, u, gy, down, own, theirs, sib, from_left, from_right, ratio, cross,
-               w_sem, load_sem, down_sem, to_sib, sib_in, to_right, right_in, to_left, left_in):
+def ffn_kernel(n, rows, pieces, u_hbm, gy_hbm, wd_hbm, a_ref, b_ref, m_ref, ad_ref, bd_ref, md_ref, sq_ref, gram_ref,
+               in_ref, down_hbm, ga_ref, gb_ref, gm_ref, norm_ref, gad_ref, gbd_ref, gmd_ref, nd_ref,
+               w_parts, wd, u, gy, down, own, theirs, sib, from_left, from_right, ratio, cross, gm_all,
+               w_sem, load_sem, down_sem, small_out, small_in, to_sib, sib_in, to_right, right_in, to_left, left_in):
     nc = n // 2
     f32, low = jnp.float32, jnp.bfloat16
     s, q, c = place_in_seq()
     tokens = own.shape[1]
 
     weights = [pltpu.make_async_copy(wd_hbm, wd, w_sem.at[0])]
-    for src, g, hold in place_pieces(rows, pieces):
-        weights.append(
-            pltpu.make_async_copy(src, w_parts.at[g, :, hold], w_sem.at[len(weights)])
-        )
+    for src, dst in place_pieces(n, rows, pieces, w_parts):
+        weights.append(pltpu.make_async_copy(src, dst, w_sem.at[len(weights)]))
     for cp in weights:
         cp.start()
 
@@ -967,7 +982,12 @@
 
     for cp in loads(0):
         cp.start()
-    sibling = greet(nc, q, s)
+    sibling = s + 1 - 2 * c
+    barrier = pltpu.get_barrier_semaphore()
+    for t in range(1, n):
+        pl.semaphore_signal(
+            barrier, inc=1, device_id={"seq": lax.rem(s + t, n)}, device_id_type=MESH
+        )
 
     def to_sibling(p):
         return pltpu.make_async_remote_copy(
@@ -1040,7 +1060,14 @@
         ratio[g] = m_ref[g] / norm
     for ref in (ga_ref, gb_ref, gm_ref, gad_ref, gbd_ref, gmd_ref):
         ref[...] = jnp.zeros_like(ref)
+    bd_wide = bd.astype(f32)
+    gram_b = jnp.dot(gram_ref[...], bd_wide, precision=highest, preferred_element_type=f32)
+    squares = jnp.sum(sq_ref[...], axis=0) + SCALE * SCALE * jnp.sum(
+        bd_wide * gram_b, axis=0, keepdims=True
+    )
+    nd_ref[...] = jnp.sqrt(squares + 1e-06)
     ratio_d = md_ref[...] / nd_ref[...]
+    pl.semaphore_wait(barrier, n - 1)
 
     def step(i, carry):
         p = by_distance(nc - 1 - i, q, nc)
@@ -1108,6 +1135,19 @@
     lax.fori_loop(0, nc, step, 0)
 
     gmd_ref[...] = gmd_ref[...] / nd_ref[...]
+
+    def small(t, slot):
+        return pltpu.make_async_remote_copy(
+            src_ref=gmd_ref,
+            dst_ref=gm_all.at[slot],
+            send_sem=small_out.at[t],
+            recv_sem=small_in.at[t],
+            device_id={"seq": lax.rem(s + t, n)},
+            device_id_type=MESH,
+        )
+
+    for t in range(1, n):
+        small(t, s).start()
     for g in range(2):
         norm = norm_ref[g]
         gm = gm_ref[g] / norm
@@ -1116,13 +1156,30 @@
         b_wide = b[g].astype(f32)
         weighted = b_wide * col
         tail = lax.dot_general(
-            weighted, b_wide, (((1,), (1,)), ((), ())), precision=highest, preferred_element_type=f32
+            weighted, b_wide, last_last, precision=highest, preferred_element_type=f32
         )
         spread = dot_nt(weighted.astype(low), weight(g)) + SCALE * jnp.dot(
             tail, a[g].astype(f32), precision=highest, preferred_element_type=f32
         )
         ga_ref[g] += SCALE * spread
         gb_ref[g] += SCALE * col * cross[g]
+
+    gm_line = gmd_ref[...]
+    for t in range(1, n):
+        slot = lax.rem(s - t + n, n)
+        small(t, slot).wait_recv()
+        gm_line = gm_line + gm_all[slot]
+    col = -gm_line * md_ref[...] / (nd_ref[...] * nd_ref[...])
+    weighted = bd_wide * col
+    tail = lax.dot_general(
+        weighted, bd_wide, last_last, precision=highest, preferred_element_type=f32
+    )
+    gad_ref[...] += SCALE * (
+        dot_nt(weighted.astype(low), wd[...])
+        + SCALE * jnp.dot(tail, ad.astype(f32), precision=highest, preferred_element_type=f32)
+    )
+    own_gram = jnp.where(s == 0, SCALE, 0.0) * gram_b
+    gbd_ref[...] += SCALE * col * (dot_f32(ad, wd[...]) + own_gram)
 
     to_sibling(q).wait_recv()
     in_ref[...] = own[q].astype(f32) + sib[q].astype(f32)
@@ -1139,45 +1196,41 @@
 
     for i in range(min(2, nc)):
         pltpu.make_async_copy(down.at[i], down_hbm.at[pl.ds(0, 2)], down_sem.at[i]).wait()
+    for t in range(1, n):
+        small(t, s).wait_send()
     for p in range(nc):
         to_sibling(p).wait_send()
         pl.when(p > q)(lambda p=p: rightward(p, s).wait_send())
         pl.when(p < q)(lambda p=p: leftward(p, s).wait_send())
 
 
-def reshard_units(gate_up, n, rows):
-    half = rows // 2
-    _, block, units_all = gate_up.shape
-    part, units = block // rows, units_all // n
-    r = lax.axis_index("rows")
-    mine = lax.dynamic_slice_in_dim(gate_up, r * part, part, 1)
-    mine = mine.reshape(2, part, n, units).transpose(2, 0, 1, 3)
-    mine = lax.all_to_all(mine, "seq", split_axis=0, concat_axis=0, tiled=True)
-    swap = [(i, i ^ 1) for i in range(rows)]
-    turns = [[(i, (i + 2 * k) % rows) for i in range(rows)] for k in range(1, half)]
-    from_b = lax.ppermute(mine, "rows", swap)
-    from_a = [lax.ppermute(mine, "rows", turn) for turn in turns]
-    pieces = [mine, from_b, *from_a]
-    for k in range(1, half):
-        pieces.append(lax.ppermute(from_b[:, 0], "rows", turns[k - 1]))
-        pieces.append(lax.ppermute(from_a[k - 1][:, 1], "rows", swap))
-    return pieces
-
-
-def place_pieces(rows, pieces):
-    half = rows // 2
-    r = lax.axis_index("rows")
-    a, b = r // 2, lax.rem(r, 2)
-    turned = lambda k: 2 * lax.rem(a - k + half, half)
-    holds = [r, 2 * a + 1 - b] + [turned(k) + b for k in range(1, half)]
-    out = [(pieces[i].at[:, g], g, hold) for i, hold in enumerate(holds) for g in range(2)]
-    for k in range(1, half):
-        for g in range(2):
-            out.append((pieces[half + 1 + 2 * (k - 1) + g], g, turned(k) + 1 - b))
+def share_plan(rows):
+    turns = range(1, rows // 2)
+    first = [(0, 0, k) for k in turns] + [(0, 1, 0)]
+    second = [(0, 0, 0)] + [(0, 1, k) for k in turns]
+    second += [(k, None, 0) for k in turns] + [(rows // 2, None, k) for k in turns]
+    return first, second
+
+
+def place_pieces(n, rows, pieces, w_parts):
+    nc, half = n // 2, rows // 2
+    _, q, _ = place_in_seq()
+    r, b_row, a_row, diagonal = place_in_rows(rows)
+    own, near = pieces[:2]
+    turns = range(1, half)
+    held = [(own.at[g], g, r) for g in range(2)]
+    kinds = [(0, a_row(-k)) for k in turns] + [(1, b_row)]
+    kinds += [(0, b_row)] + [(1, a_row(-k)) for k in turns]
+    kinds += [(0, diagonal(-k)) for k in turns] + [(1, diagonal(-k)) for k in turns]
+    held += [(piece, g, hold) for piece, (g, hold) in zip(pieces[2:], kinds)]
+    out = [(near, w_parts.at[:, pl.ds(2 * q, 2)])]
+    for i in range(1, nc):
+        pair = pl.ds(2 * near_first(i, q, nc), 2)
+        out += [(src.at[pair], w_parts.at[g, pair, hold]) for src, g, hold in held]
     return out
 
 
-def feed_forward(n, rows, pieces, u, gy, wd, a, b, m, ad, bd, md, nd, collective_id):
+def feed_forward(n, rows, pieces, u, gy, wd, a, b, m, ad, bd, md, sq, gram, collective_id):
     nc = n // 2
     _, tokens, width = u.shape
     units = wd.shape[0]
@@ -1189,6 +1242,7 @@
     line = pltpu.VMEM((nc, tokens, width), low)
     pair = pltpu.VMEM((2, 2, tokens, width), low)
     part = pieces[0].shape[2]
+    copies = 2 + (n // 2 - 1) * (2 + 2 * rows - 2)
     count = len(pieces)
 
     def kernel(*refs):
@@ -1206,9 +1260,10 @@
             shape((16, units), f32),
             shape((16, width), f32),
             shape((1, width), f32),
-        ),
-        in_specs=[hbm] * (count + 3) + [vmem] * 7,
-        out_specs=(vmem, hbm) + (vmem,) * 7,
+            shape((1, width), f32),
+        ),
+        in_specs=[hbm] * (count + 3) + [vmem] * 8,
+        out_specs=(vmem, hbm) + (vmem,) * 8,
         scratch_shapes=[
             pltpu.VMEM((2, n, rows, part, units), low),
             pltpu.VMEM((units, width), low),
@@ -1216,7 +1271,8 @@
             line, line, line, line, line,
             pltpu.VMEM((2, 1, units), f32),
             pltpu.VMEM((2, 16, units), f32),
-            dma((1 + 2 * rows,)), dma((2, 2)), dma((2,)),
+            pltpu.VMEM((n, 1, width), f32),
+            dma((copies,)), dma((2, 2)), dma((2,)), dma((n,)), dma((n,)),
         ] + [dma((nc,))] * 6,
         compiler_params=pltpu.CompilerParams(
             collective_id=collective_id, has_side_effects=True, vmem_limit_bytes=60 << 20
@@ -1226,12 +1282,245 @@
             bytes_accessed=32 << 20,
         ),
         name="feed_forward",
-    )(*pieces, u, gy, wd, a, b, m, ad, bd, md, nd)
+    )(*pieces, u, gy, wd, a, b, m, ad, bd, md, sq, gram)
+
+def reduce_kernel(n, rows, ga_qkv, ga_o, gb_qkv, gb_o, ga_gu, gb_d, gm_qkv, gm_o, gm_d, gb_gu, gm_gu, n_gu, ga_d,
+                  o_ga, o_gb_qo, o_gb_kv, o_gm_q, o_gm_kv, o_gm_o, o_ga_gu, o_gb_gu, o_gm_gu, o_ga_d, o_gb_d, o_gm_d, o_n,
+                  part, from_sib, mid, from_rows, from_line, line_out, units, units_in, whole, units_all,
+                  sib_out, sib_in, row_out, row_in, line_send, line_in, back_send, back_in, wide_send, wide_in,
+                  pass_send, pass_in):
+    nc = n // 2
+    f32, low = jnp.float32, jnp.bfloat16
+    s, q, c = place_in_seq()
+    sibling = s + 1 - 2 * c
+    r = lax.axis_index("rows")
+    width = ga_o.shape[1]
+    cols = width // (2 * rows)
+    kv = (gb_qkv.shape[1] - width) // 2
+    height = part.shape[2]
+    piece = height // nc
+    unit_rows = units.shape[1]
+    size = units.shape[2]
+
+    barrier = pltpu.get_barrier_semaphore()
+    for t in range(1, n):
+        pl.semaphore_signal(barrier, inc=1, device_id=(r, lax.rem(s + t, n)), device_id_type=MESH)
+    for t in range(1, rows):
+        pl.semaphore_signal(barrier, inc=1, device_id=(lax.rem(r + t, rows), s), device_id_type=MESH)
+
+    gb_k, gb_v = gb_qkv[:, width : width + kv], gb_qkv[:, width + kv :]
+    small = jnp.concatenate(
+        [
+            jnp.concatenate([gb_k[:8], gb_k[8:], gb_v[:8], gb_v[8:]], axis=1),
+            gm_qkv[:, :width],
+            gm_o[...],
+            gm_d[...],
+            jnp.concatenate([gm_qkv[:, width:], jnp.zeros((1, width - 2 * kv), f32)], axis=1),
+            jnp.zeros((4, width), f32),
+        ],
+        axis=0,
+    )
+    groups = [ga_qkv[0], ga_qkv[1], ga_qkv[2], ga_o[...], gb_qkv[:, :width], gb_o[...], ga_gu[0], ga_gu[1], gb_d[...], small]
+    for j in range(2 * rows):
+        for g, value in enumerate(groups):
+            part[j % 2, j // 2, 16 * g : 16 * g + 16] = value[:, cols * j : cols * (j + 1)].astype(low)
+        if height > 160:
+            part[j % 2, j // 2, 160:] = jnp.zeros((height - 160, cols), low)
+    n_high = [n_gu[g].astype(low).astype(f32) for g in range(2)]
+    n_rest = [n_gu[g] - n_high[g] for g in range(2)]
+    tops = jnp.concatenate(
+        [gm_gu[0], gm_gu[1]]
+        + [v * (1.0 / rows) for v in (n_high[0], n_rest[0], n_high[1], n_rest[1])]
+        + [jnp.zeros((2, size), f32)],
+        axis=0,
+    )
+    blocks = [gb_gu[0][:8], gb_gu[0][8:], gb_gu[1][:8], gb_gu[1][8:], ga_d[:8], ga_d[8:], tops, jnp.zeros((8, size), f32)]
+    per = unit_rows // 8
+    for j in range(rows):
+        units[j] = jnp.concatenate(blocks[per * j : per * (j + 1)], axis=0).astype(low)
+    pl.semaphore_wait(barrier, n - 1 + rows - 1)
+
+    def to_sibling():
+        return remote(part.at[1 - c], from_sib, sib_out.at[0], sib_in.at[0], r, sibling)
+
+    def member(t):
+        return lax.rem(r + t + rows, rows)
+
+    def row_send(t):
+        return remote(mid.at[member(t)], from_rows.at[t], row_out.at[0, t], row_in.at[0, t], member(t), s)
+
+    def unit_send(t):
+        return remote(units.at[member(t)], units_in.at[t], row_out.at[1, t], row_in.at[1, t], member(t), s)
+
+    def chip(t):
+        return lax.rem(q + t + nc, nc)
+
+    def line_part(t):
+        return remote(line_out.at[chip(t)], from_line.at[t], line_send.at[t], line_in.at[t], r, 2 * chip(t) + c)
+
+    def back(t, slot):
+        return remote(whole.at[r, c, slot], whole.at[r, c, slot], back_send.at[0, t], back_in.at[0, t], r, 2 * chip(t) + c)
+
+    def unit_back(t, slot):
+        return remote(
+            units_all.at[r, c, slot], units_all.at[r, c, slot], back_send.at[1, t], back_in.at[1, t], r, 2 * chip(t) + c
+        )
+
+    def wide(t, row):
+        return remote(whole.at[row, c], whole.at[row, c], wide_send.at[0, t], wide_in.at[0, t], member(t), s)
+
+    def unit_wide(t, row):
+        return remote(units_all.at[row, c], units_all.at[row, c], wide_send.at[1, t], wide_in.at[1, t], member(t), s)
+
+    def hand(t, row, core):
+        return remote(whole.at[row, core], whole.at[row, core], pass_send.at[0, t], pass_in.at[0, t], r, sibling)
+
+    def unit_hand(t, row, core):
+        return remote(units_all.at[row, core], units_all.at[row, core], pass_send.at[1, t], pass_in.at[1, t], r, sibling)
+
+    to_sibling().start()
+    for t in range(1, rows):
+        unit_send(t).start()
+    to_sibling().wait_recv()
+    for t in range(rows):
+        mid[member(t)] = (part[c, member(t)].astype(f32) + from_sib[member(t)].astype(f32)).astype(low)
+        if t:
+            row_send(t).start()
+    unit_sum = units[r].astype(f32)
+    for t in range(1, rows):
+        unit_send(t).wait_recv()
+        unit_sum = unit_sum + units_in[t].astype(f32)
+    units_all[r, c, q] = unit_sum.astype(low)
+    for t in range(1, nc):
+        unit_back(t, q).start()
+    total = mid[r].astype(f32)
+    for t in range(1, rows):
+        row_send(t).wait_recv()
+        total = total + from_rows[t].astype(f32)
+    for p in range(nc):
+        line_out[p] = total[piece * p : piece * (p + 1)].astype(low)
+    for t in range(1, nc):
+        line_part(t).start()
+    own = line_out[q].astype(f32)
+    for t in range(1, nc):
+        line_part(t).wait_recv()
+        own = own + from_line[t].astype(f32)
+    whole[r, c, q] = own.astype(low)
+    for t in range(1, nc):
+        back(t, q).start()
+    for t in range(1, nc):
+        back(t, chip(-t)).wait_recv()
+        unit_back(t, chip(-t)).wait_recv()
+    for t in range(1, rows):
+        wide(t, r).start()
+        unit_wide(t, r).start()
+    hand(0, r, c).start()
+    unit_hand(0, r, c).start()
+    for t in range(1, rows):
+        wide(t, member(-t)).wait_recv()
+        hand(t, member(-t), c).start()
+        unit_wide(t, member(-t)).wait_recv()
+        unit_hand(t, member(-t), c).start()
+    for t in range(rows):
+        hand(t, member(-t), 1 - c).wait_recv()
+        unit_hand(t, member(-t), 1 - c).wait_recv()
+
+    for j in range(2 * rows):
+        block = jnp.concatenate([whole[j // 2, j % 2, p].astype(f32) for p in range(nc)], axis=0)
+        at = slice(cols * j, cols * (j + 1))
+        for g in range(4):
+            o_ga[g, :, at] = block[16 * g : 16 * g + 16]
+        o_gb_qo[0, :, at] = block[64:80]
+        o_gb_qo[1, :, at] = block[80:96]
+        o_ga_gu[0, :, at] = block[96:112]
+        o_ga_gu[1, :, at] = block[112:128]
+        o_gb_d[:, at] = block[128:144]
+        which, start = divmod(cols * j, kv)
+        o_gb_kv[which // 2, 8 * (which % 2) : 8 * (which % 2) + 8, start : start + cols] = block[144:152]
+        o_gm_q[:, at] = block[152:153]
+        o_gm_o[:, at] = block[153:154]
+        o_gm_d[:, at] = block[154:155]
+        if which < 2:
+            o_gm_kv[which : which + 1, start : start + cols] = block[155:156]
+    for j in range(rows):
+        for dev in range(n):
+            block = units_all[j, dev % 2, dev // 2].astype(f32)
+            at = slice(size * dev, size * (dev + 1))
+            for t in range(per):
+                rows8, place = block[8 * t : 8 * t + 8], per * j + t
+                half = slice(8 * (place % 2), 8 * (place % 2) + 8)
+                if place < 4:
+                    o_gb_gu[place // 2, half, at] = rows8
+                elif place < 6:
+                    o_ga_d[half, at] = rows8
+                elif place == 6:
+                    o_gm_gu[:, at] = rows8[:2]
+                    o_n[0:1, at] = rows8[2:3] + rows8[3:4]
+                    o_n[1:2, at] = rows8[4:5] + rows8[5:6]
+
+    to_sibling().wait_send()
+    for t in range(1, rows):
+        row_send(t).wait_send()
+        unit_send(t).wait_send()
+        wide(t, r).wait_send()
+        unit_wide(t, r).wait_send()
+    for t in range(1, nc):
+        line_part(t).wait_send()
+        back(t, q).wait_send()
+        unit_back(t, q).wait_send()
+    for t in range(rows):
+        hand(t, member(-t), c).wait_send()
+        unit_hand(t, member(-t), c).wait_send()
+
+
+def sum_gradients(n, rows, full, own_units, collective_id):
+    nc = n // 2
+    width, size = full[1].shape[1], own_units[3].shape[1]
+    kv = (full[2].shape[1] - width) // 2
+    wide_units = size * n
+    cols = width // (2 * rows)
+    height = -(-160 // (8 * nc)) * 8 * nc
+    unit_rows = 64 // rows
+    f32, low = jnp.float32, jnp.bfloat16
+    shape = lambda *dims: jax.ShapeDtypeStruct(dims, f32)
+    vmem = pl.BlockSpec(memory_space=pltpu.VMEM)
+    dma = pltpu.SemaphoreType.DMA
+    outs = (
+        shape(4, 16, width), shape(2, 16, width), shape(2, 16, kv), shape(1, width), shape(2, kv), shape(1, width),
+        shape(2, 16, width), shape(2, 16, wide_units), shape(2, wide_units), shape(16, wide_units), shape(16, width),
+        shape(1, width), shape(2, wide_units),
+    )
+    block = (rows, height, cols)
+    return pl.pallas_call(
+        functools.partial(reduce_kernel, n, rows),
+        out_shape=outs,
+        in_specs=[vmem] * 13,
+        out_specs=(vmem,) * 13,
+        scratch_shapes=[
+            pltpu.VMEM((2, *block), low),
+            pltpu.VMEM(block, low),
+            pltpu.VMEM(block, low),
+            pltpu.VMEM(block, low),
+            pltpu.VMEM((nc, height // nc, cols), low),
+            pltpu.VMEM((nc, height // nc, cols), low),
+            pltpu.VMEM((rows, unit_rows, size), low),
+            pltpu.VMEM((rows, unit_rows, size), low),
+            pltpu.VMEM((rows, 2, nc, height // nc, cols), low),
+            pltpu.VMEM((rows, 2, nc, unit_rows, size), low),
+            dma((1,)), dma((1,)), dma((2, rows)), dma((2, rows)), dma((nc,)), dma((nc,)),
+            dma((2, nc)), dma((2, nc)), dma((2, rows)), dma((2, rows)), dma((2, rows)), dma((2, rows)),
+        ],
+        compiler_params=pltpu.CompilerParams(
+            collective_id=collective_id, has_side_effects=True, vmem_limit_bytes=48 << 20
+        ),
+        cost_estimate=pl.CostEstimate(flops=0, transcendentals=0, bytes_accessed=64 << 20),
+        name="sum_gradients",
+    )(*full, *own_units)
 
 def square_terms(weight, a_low, b_low):
     cross = dot_f32(a_low, weight)
     squares = jnp.sum(jnp.square(weight.astype(jnp.float32)), axis=0, keepdims=True)
-    return squares + 2.0 * SCALE * jnp.sum(b_low.astype(jnp.float32) * cross, axis=0, keepdims=True), cross
+    return squares + 2.0 * SCALE * jnp.sum(b_low.astype(jnp.float32) * cross, axis=0, keepdims=True)
 
 
 def drift_stats(magnitude_vector, norms):
@@ -1271,20 +1560,18 @@
     seq_size = lax.axis_size("seq")
     rows_size = lax.axis_size("rows")
     seq_index = lax.axis_index("seq")
-    first_member = (seq_index == 0).astype(jnp.float32)
     low, f32 = jnp.bfloat16, jnp.float32
-    rank = ADAPTER_RANK
     slice_units = down_frozen_weight.shape[0]
     start = seq_index * slice_units
 
-    pieces = reshard_units(gate_up_frozen, seq_size, rows_size)
     packed = jnp.stack(
         [
             jnp.concatenate([query_output_frozen[0], key_value_frozen[0]], axis=1),
             jnp.concatenate([key_value_frozen[1], query_output_frozen[1]], axis=1),
         ]
     )
-    weights = gather_weights(seq_size, rows_size, packed, 1)
+    weights, gu_own, gu_near = gather_weights(seq_size, rows_size, packed, gate_up_frozen, 1)
+    shares_1, shares_2 = share_plan(rows_size)
     weights, grad_out_rows = lax.optimization_barrier(
         (weights, output_gradient.reshape(token_count, model_width))
     )
@@ -1307,7 +1594,7 @@
     a_d = lax.dynamic_slice_in_dim(down_adapter_a, start, slice_units, 1)
     b_d = down_adapter_b.astype(low)
     m_d = down_magnitude[None]
-    sq_d, cross_d = square_terms(down_frozen_weight, a_d.astype(low), b_d)
+    sq_d = square_terms(down_frozen_weight, a_d.astype(low), b_d)
 
     positions = seq_index * span_len + jnp.arange(span_len, dtype=jnp.int32)
     half_dim = HEAD_DIM // 2
@@ -1322,7 +1609,9 @@
     u1, before_qkv, q, kv, n_attn, cross_attn = project_qkv(
         x, gain_attn, attention_adapter_a, weights, b_attn, m_attn, cosine, sine
     )
-    kv_all, sq_all = gather_seq(seq_size, [kv, sq_d], 2)
+    (kv_all, sq_all), gu_1 = gather_seq(
+        seq_size, rows_size, [kv, sq_d], 2, (gu_own,), shares_1
+    )
     kv_all = kv_all.reshape(seq_size, pair_rows, span_len, 2 * kv_width)
     q = q.reshape(pair_rows, span_len, model_width)
     att, shares = attend(q, kv_all, valid_len)
@@ -1331,18 +1620,14 @@
     a_o = attention_adapter_a[3]
     before_o, x1, u2 = project_out(att, a_o, weights, b_o, m_o, n_o, x, gain_ffn)
 
-    (u2_all,) = gather_seq(seq_size, [u2], 3)
-    a_d_wide, b_d_wide = down_adapter_a.astype(low).astype(f32), b_d.astype(f32)
-    gram_d = jnp.dot(
-        jnp.dot(a_d_wide, a_d_wide.T, precision=highest), b_d_wide, precision=highest
-    )
-    sq_d = jnp.sum(sq_all, axis=0) + SCALE * SCALE * jnp.sum(
-        b_d_wide * gram_d, axis=0, keepdims=True
-    )
-    n_d = jnp.sqrt(sq_d + 1e-06)
-    in_grad, down_parts, ga_gu, gb_gu, gm_gu, n_gu, ga_d, gb_d, gm_d = feed_forward(
-        seq_size, rows_size, pieces, u2_all, gy_all, down_frozen_weight, gate_up_adapter_a, b_gu,
-        m_gu, a_d, down_adapter_b, m_d, n_d, 4,
+    (u2_all,), gu_2 = gather_seq(
+        seq_size, rows_size, [u2], 3, (gu_own, *gu_1), shares_2
+    )
+    a_d_wide = down_adapter_a.astype(low).astype(f32)
+    gram_d = jnp.dot(a_d_wide, a_d_wide.T, precision=highest)
+    in_grad, down_parts, ga_gu, gb_gu, gm_gu, n_gu, ga_d, gb_d, gm_d, n_d = feed_forward(
+        seq_size, rows_size, (gu_own, gu_near, *gu_1, *gu_2), u2_all, gy_all, down_frozen_weight,
+        gate_up_adapter_a, b_gu, m_gu, a_d, down_adapter_b, m_d, sq_all, gram_d, 4,
     )
     before_d = lax.psum_scatter(
         down_parts.reshape(seq_size * token_count, model_width), "seq", scatter_dimension=0,
@@ -1355,50 +1640,22 @@
         cross_attn[:, qkv_width:], weights,
     )
     gq, gkv = attend_back(q, kv_all, shares, grad_att.reshape(q.shape))
-    gkv, gm_d_all = scatter_seq(
-        seq_size, gkv.reshape(seq_size, token_count, 2 * kv_width), gm_d, 5
-    )
+    gkv = scatter_seq(seq_size, gkv.reshape(seq_size, token_count, 2 * kv_width), 5)
     grad_inputs, ga_qkv, gb_qkv, gm_qkv = qkv_back(
         gq.reshape(token_count, model_width), gkv, cosine, sine, before_qkv, u1,
         attention_adapter_a[:3], b_attn[:, :qkv_width], m_attn[:, :qkv_width],
         n_attn[:, :qkv_width], cross_attn[:, :qkv_width], x, gain_attn, gx1, weights,
     )
 
-    c_d = -jnp.sum(gm_d_all, axis=0) * m_d / (n_d * n_d)
-    weighted = b_d_wide * c_d
-    tail = lax.dot_general(weighted, b_d_wide, last_last, precision=highest)
-    spread = dot_nt(weighted.astype(low), down_frozen_weight) + SCALE * jnp.dot(
-        tail, a_d.astype(low).astype(f32), precision=highest
-    )
-    ga_d = ga_d + SCALE * spread
-    gb_d = gb_d + SCALE * c_d * (cross_d + first_member * SCALE * gram_d)
-
+    sums = sum_gradients(
+        seq_size, rows_size,
+        (ga_qkv, ga_o, gb_qkv, gb_o, ga_gu, gb_d, gm_qkv, gm_o, gm_d),
+        (gb_gu, gm_gu, n_gu, ga_d),
+        6,
+    )
+    norms_gu = sums[12]
+    summed = (*sums[:3], sums[3][0], sums[4], sums[5][0], *sums[6:11], sums[11][0])
     k_end = model_width + kv_width
-    full_units = gate_up_magnitude.shape[1]
-
-    def place(piece, axis):
-        shape = list(piece.shape)
-        shape[axis] = full_units
-        return lax.dynamic_update_slice_in_dim(jnp.zeros(shape, piece.dtype), piece, start, axis)
-
-    summed = lax.psum(
-        (
-            jnp.concatenate([ga_qkv, ga_o[None]], axis=0),
-            jnp.stack([gb_qkv[:, :model_width], gb_o]),
-            jnp.stack([gb_qkv[:, model_width:k_end], gb_qkv[:, k_end:]]),
-            gm_qkv[0, :model_width],
-            gm_qkv[0, model_width:].reshape(2, kv_width),
-            gm_o[0],
-            ga_gu,
-            place(gb_gu, 2),
-            place(gm_gu[:, 0], 1),
-            place(ga_d, 1),
-            gb_d,
-            gm_d[0],
-        ),
-        ("rows", "seq"),
-    )
-    norms_gu = lax.all_gather(n_gu[:, 0], "seq", axis=1, tiled=True)
     stats = jnp.stack(
         [
             drift_stats(query_magnitude, n_attn[0, :model_width]),

time: 700 us -> 531 us (0.76)
  waiting for transfers between devices: 156 us -> 0.04 us
  blocking collectives: 52.6 us -> 0 us
  Pallas kernels: 366 us -> 417 us
  starting transfers between devices: 11.4 us -> 0.08 us
    psum x1 -> x0, waiting for transfers between devices: 64.3 us -> none  [local(): lax.psum((jnp.concatenate([ga_qkv, ga_o[None]], axis=0), jnp.stack([gb_qk...]
    reduce_scatter x1, waiting for transfers between devices: 51.7 us -> 0.01 us  [local(): lax.psum_scatter(down_parts.reshape(seq_size * token_count, model_width),...]
    pallas_call x4 -> x5, Pallas kernels: 228 us -> 275 us  [the longest x1 137 us: gather_weights(): pl.pallas_call(functools.partial(weights_kernel, n, rows), out_shape=(sha...]
    ppermute x4 -> x0, waiting for transfers between devices: 39 us -> none  [the longest x1 22.4 us: reshard_units(): from_b = lax.ppermute(mine, 'rows', swap)]
    psum x1 -> x0, blocking collectives: 38.5 us -> none  [local(): lax.psum((jnp.concatenate([ga_qkv, ga_o[None]], axis=0), jnp.stack([gb_qk...]
    all_gather x1 -> x0, blocking collectives: 14.1 us -> none  [local(): norms_gu = lax.all_gather(n_gu[:, 0], 'seq', axis=1, tiled=True)]
    unnamed x185 -> x140, local copies, waits for them, and re-layouts: 19.6 us -> 28.5 us
  transfers between devices with their start and end apart: 8 -> 2, of which waited for: 4 -> 0; matrix products, arithmetic and copies ran while one was open for 5% -> 8% of each run, Pallas kernels for 34% -> 39%
where the time goes in v4:
time: 531 us; the launch traced here: 520 us
  Pallas kernels  417 us (79%)
  local copies, waits for them, and re-layouts  48.3 us (9%)
  between operations  30.1 us (6%)
  other arithmetic  19.7 us (4%)
  matrix products  5.38 us (1%)
    pallas_call x1, Pallas kernels, gather_weights(): pl.pallas_call(functools.partial(weights_kernel, n, rows), out_shape=(sha...  137 us
    pallas_call x2, Pallas kernels, gather_seq(): pl.pallas_call(functools.partial(gather_kernel, n, rows, count, (range(le...  78 us
    pallas_call x1, Pallas kernels, feed_forward(): pl.pallas_call(kernel, out_shape=(shape((tokens, width), f32), shape((n,...  77.2 us
    pallas_call x1, Pallas kernels, scatter_seq(): pl.pallas_call(functools.partial(scatter_kernel, n), out_shape=jax.ShapeD...  31.8 us
    unnamed x140, local copies, waits for them, and re-layouts  28.5 us
    pallas_call x1, Pallas kernels, sum_gradients(): pl.pallas_call(functools.partial(reduce_kernel, n, rows), out_shape=outs,...  28.4 us
    pallas_call x1, Pallas kernels, project_qkv(): pl.pallas_call(functools.partial(project_kernel, kv_tiles), out_shape=(ja...  17.2 us
    pallas_call x1, Pallas kernels, qkv_back(): pl.pallas_call(qkv_back_kernel, out_shape=(jax.ShapeDtypeStruct((rows, wi...  13.5 us
  transfers between devices with their start and end apart: 2, of which 0 were waited for; matrix products, arithmetic and copies ran while one was open for 8% of the time, Pallas kernels for 39%

profile of v4, /device:TPU:0, one launch (start us, length us, event | category | flops | bytes accessed | tf_op | source)
XLA Modules:
  0.0 520.4 jit_solution(15901601653752158009)
XLA Ops:
  7.3 1.8 fusion.4
  9.2 1.6 maximum_maximum_fusion.xa
  10.8 136.9 %gather_weights.1 = (bf16[2,8,4,64,2560]{4,3,2,1,0:T(8,128)(2,1)}, bf16[2,8,64,1024]{3,2,1,0:T(8,128)(2,1)}, bf16[2,2,4,64,1024]{4,3,2,1,0:T(8,128)(2,1)}) custom-call(bf16[2,4,64,2560]{3,2,1,0:T(8,128)(2,1)} %maximum_maximum_fusion.xa, bf16[2,4,64,8192]{3,2,1,0:T(8,128)(2,1)} %bitcast.105), custom_call_target="tpu_custom_call" | custom-call | bytes 262144000 | tf_op jit(solution)/shard_map/gather_weights/pallas_call | solution.py:589
  149.3 0.9 constant_dynamic-slice_fusion
  151.6 3.3 fusion
  155.0 0.9 multiply_reduce_fusion
  157.9 17.2 %project_qkv.1 = (bf16[128,2048]{1,0:T(8,128)(2,1)S(1)}, f32[128,3072]{1,0:T(8,128)S(1)}, bf16[128,2048]{1,0:T(8,128)(2,1)S(1)}, bf16[128,1024]{1,0:T(8,128)(2,1...) custom-call(bf16[128,2048]{1,0:T(8,128)(2,1)S(1)} %bitcast.81, f32[1,2048]{1,0:T(1,128)S(1)} %get-tuple-element.198.gain_ref, ...), custom_call_target="tpu_custom_call" | custom-call | flops 2684354560 | bytes 20971520 | tf_op jit(solution)/shard_map/project_qkv/pallas_call | solution.py:122
  175.1 1.1 copy-done.9
  178.5 34.6 %gather_seq.2 = (bf16[8,128,1024]{2,1,0:T(8,128)(2,1)}, f32[8,1,2048]{2,1,0:T(1,128)}, bf16[8,64,1024]{2,1,0:T(8,128)(2,1)}, bf16[8,64,1024]{2,1,0:T(8,128)(2,1)}) custom-call(bf16[128,1024]{1,0:T(8,128)(2,1)} %copy-done.23, f32[1,2048]{1,0:T(1,128)} %bitcast.113, bf16[2,8,64,1024]{3,2,1,0:T(8,128)(2,1)} %get-tuple-element.78.refs_2_.refs_1_.refs_0_), custom_call_target="tpu_custom_call" | custom-call | bytes 43253760 | tf_op jit(solution)/shard_map/gather_seq/pallas_call | solution.py:683
  213.1 1.6 copy-done.2
  214.7 1.0 copy-done.19
  215.7 9.6 %attend.1 = (bf16[2,64,2048]{2,1,0:T(8,128)(2,1)S(1)}, bf16[2,4,512,512]{3,2,1,0:T(8,128)(2,1)S(1)}) custom-call(s32[2]{0:T(128)S(1)} %broadcast_add_fusion.valid_ref, bf16[2,64,2048]{2,1,0:T(8,128)(2,1)S(1)} %bitcast.90, bf16[8,2,64,1024]{3,2,1,0:T(8,128)(2,1)S(1)} %bitcast.77, bf16[8,2,64,1024]{3,2,1,0:T(8,128)(2,1)S(1)} %bitcast.78), custom_call_target="tpu_custom_call" | custom-call | flops 1073741824 | bytes 8388608 | tf_op jit(solution)/shard_map/attend/pallas_call | solution.py:871
  225.3 2.0 copy-done.45
  227.3 1.2 slice_reduce_fusion.5
  229.3 5.9 %project_out.1 = (f32[128,2048]{1,0:T(8,128)S(1)}, f32[128,2048]{1,0:T(8,128)S(1)}, bf16[128,2048]{1,0:T(8,128)(2,1)S(1)}) custom-call(bf16[128,2048]{1,0:T(8,128)(2,1)S(1)} %bitcast.84, f32[16,2048]{1,0:T(8,128)S(1)} %slice_bitcast_fusion.a_ref, bf16[2,2048,2560]{2,1,0:T(8,128)(2,1)} %bitcast.101, f32[16,2048]{1,0:T(8,128)S(1)} %get-tuple-element.190.b_ref, ...), custom_call_target="tpu_custom_call" | custom-call | flops 1073741824 | bytes 8388608 | tf_op jit(solution)/shard_map/project_out/pallas_call | solution.py:183
  235.2 1.0 copy-done.10
  236.9 43.5 %gather_seq.3 = (bf16[8,128,2048]{2,1,0:T(8,128)(2,1)}, bf16[8,64,1024]{2,1,0:T(8,128)(2,1)}, bf16[8,64,1024]{2,1,0:T(8,128)(2,1)}, bf16[8,64,1024]{2,1,0:T(8,128)(2,1)}, bf16[8,64,1024]{2,1,0:T(8,128)(2,1)}) custom-call(bf16[128,2048]{1,0:T(8,128)(2,1)} %copy-done.21, bf16[2,8,64,1024]{3,2,1,0:T(8,128)(2,1)} %get-tuple-element.78.refs_2_.refs_1_.refs_0_, ...), custom_call_target="tpu_custom_call" | custom-call | bytes 83886080 | tf_op jit(solution)/shard_map/gather_seq/pallas_call | solution.py:683
  281.1 2.0 fusion.1.refs_18_
  283.1 77.2 %feed_forward.1 = (f32[128,2048]{1,0:T(8,128)}, bf16[8,128,2048]{2,1,0:T(8,128)(2,1)}, f32[2,16,2048]{2,1,0:T(8,128)}, f32[2,16,1024]{2,1,0:T(8,128)}, f32[2,1,1...) custom-call(bf16[2,8,64,1024]{3,2,1,0:T(8,128)(2,1)} %get-tuple-elem, ...), custom_call_target="tpu_custom_call" | custom-call | flops 25769803776 | bytes 33554432 | tf_op jit(solution)/shard_map/feed_forward/pallas_call | solution.py:1251
  360.4 1.4 slice.103.n_ref
  361.8 1.6 slice.100.cross_ref
  363.3 1.6 slice.104.cross_ref
  364.9 1.3 slice.113.m_ref
  367.0 1.3 multiply_reduce_fusion.7
  371.1 1.3 slice_reduce_fusion.2
  372.4 1.3 multiply_reduce_fusion.11
  376.3 1.3 multiply_reduce_fusion.13
  380.4 1.3 multiply_reduce_fusion.9
  384.4 1.0 pad_maximum_fusion.1.b_ref
  385.4 1.3 multiply_reduce_fusion.5
  388.1 1.9 fusion.7
  391.5 1.2 copy-done.11
  392.7 0.9 copy-done.17
  394.3 8.5 %out_back.1 = (f32[128,2048]{1,0:T(8,128)S(1)}, bf16[128,2048]{1,0:T(8,128)(2,1)S(1)}, f32[16,2048]{1,0:T(8,128)S(1)}, f32[16,2048]{1,0:T(8,128)S(1)}, f32[1,2048]{1,0:T(1,128)S(1)}) custom-call(f32[128,2048]{1,0:T(8,128)S(1)} %copy-done.11, f32[128,2048]{1,0:T(8,128)S(1)} %get-tuple-element.82.x1_ref, f32[1,2048]{1,0:T(1,128)S(1)} %copy-done.32, ...), custom_call_target="tpu_custom_call" | custom-call | flops 1073741824 | bytes 8388608 | tf_op jit(solution)/shard_map/out_back/pallas_call | solution.py:256
  402.9 9.9 %attend_back.1 = (bf16[2,64,2048]{2,1,0:T(8,128)(2,1)S(1)}, bf16[8,2,64,1024]{3,2,1,0:T(8,128)(2,1)S(1)}) custom-call(bf16[2,64,2048]{2,1,0:T(8,128)(2,1)S(1)} %bitcast.91, bf16[8,2,64,1024]{3,2,1,0:T(8,128)(2,1)S(1)} %bitcast.79, bf16[8,2,64,1024]{3,2,1,0:T(8,128)(2,1)S(1)} %bitcast.80, bf16[2,4,512,512]{3,2,1,0:T(8,128)(2,1)S(1)} %copy-done.46, ...), custom_call_target="tpu_custom_call" | custom-call | flops 2684354560 | bytes 8388608 | tf_op jit(solution)/shard_map/attend_back/pallas_call | solution.py:926
  412.8 31.8 %scatter_seq.1.gkv_ref = f32[128,1024]{1,0:T(8,128)S(1)} custom-call(bf16[8,128,1024]{2,1,0:T(8,128)(2,1)S(1)} %bitcast.86), custom_call_target="tpu_custom_call" | custom-call | bytes 41943040 | tf_op jit(solution)/shard_map/scatter_seq/pallas_call | solution.py:800
  444.7 13.5 %qkv_back.1 = (f32[128,2048]{1,0:T(8,128)}, f32[3,16,2048]{2,1,0:T(8,128)S(1)}, f32[16,3072]{1,0:T(8,128)S(1)}, f32[1,3072]{1,0:T(1,128)S(1)}) custom-call(bf16[128,2048]{1,0:T(8,128)(2,1)S(1)} %bitcast.89, f32[128,1024]{1,0:T(8,128)S(1)} %scatter_seq.1.gkv_ref, f32[128,128]{1,0:T(8,128)S(1)} %copy.42.cos_ref, f32[128,128]{1,0:T(8,128)S(1)} %copy.43.sin_ref, ...), custom_call_target="tpu_custom_call" | custom-call | flops 1610612736 | bytes 12582912 | tf_op jit(solution)/shard_map/qkv_back/pallas_call | solution.py:353
  458.2 28.4 %sum_gradients.1 = (f32[4,16,2048]{2,1,0:T(8,128)S(1)}, f32[2,16,2048]{2,1,0:T(8,128)S(1)}, f32[2,16,512]{2,1,0:T(8,128)S(1)}, f32[1,2048]{1,0:T(1,128)S(1)}, f3...) custom-call(f32[3,16,2048]{2,1,0:T(8,128)S(1)} %get-tuple-element.10, ...), custom_call_target="tpu_custom_call" | custom-call | bytes 67108864 | tf_op jit(solution)/shard_map/sum_gradients/pallas_call | solution.py:1494
  486.6 1.0 copy-done.12
  493.0 1.3 copy.51
  496.9 1.3 copy.50
  498.2 1.4 stack.121
  499.6 2.1 add_convert_fusion
  502.4 1.7 copy.67
  504.1 1.5 copy.68
  505.6 1.3 copy.69
  506.9 1.3 copy.70
  509.5 1.0 copy.73
  (170 shorter events, 22.6 us)
Async XLA Ops:
  7.2 273.2 %copy-start = (f32[2,16,8192]{2,1,0:T(8,128)S(1)}, f32[2,16,8192]{2,1,0:T(8,128)}, u32[]{:S(2)}) copy-start(f32[2,16,8192]{2,1,0:T(8,128)} %param.35) | copy-start | bytes 3145732
  7.2 1.9 copy-start.49
  7.2 275.9 %all-gather.3.cloned.1.call-start = ((), (), s32[]{:S(2)}) async-start(), calls=%async_computation.2 | async-start | bytes 4718592 | tf_op jit(solution)/shard_map/all_gather | solution.py:1578
  10.8 138.4 %copy-start.62 = (f32[2,512]{1,0:T(2,128)S(1)}, f32[2,512]{1,0:T(2,128)}, u32[]{:S(2)}) copy-start(f32[2,512]{1,0:T(2,128)} %param.32) | copy-start | bytes 12292
  10.8 138.4 %copy-start.57 = (f32[2048]{0:T(1024)S(1)}, f32[2048]{0:T(1024)}, u32[]{:S(2)}) copy-start(f32[2048]{0:T(1024)} %param.33) | copy-start | bytes 24580
  10.8 138.4 %copy-start.58 = (f32[2048]{0:T(1024)S(1)}, f32[2048]{0:T(1024)}, u32[]{:S(2)}) copy-start(f32[2048]{0:T(1024)} %param.31) | copy-start | bytes 24580
  10.8 140.8 %copy-start.54 = (f32[16,2048]{1,0:T(8,128)S(1)}, f32[16,2048]{1,0:T(8,128)}, u32[]{:S(2)}) copy-start(f32[16,2048]{1,0:T(8,128)} %refs_15_.1) | copy-start | bytes 393220
  147.7 351.9 %reduce-scatter.2.cloned.1.call-start = ((), (), s32[]{:S(2)}) async-start(), calls=%async_computation.1 | async-start | bytes 4718592 | tf_op jit(solution)/shard_map/reduce_scatter | solution.py:1632
  149.2 6.7 %copy-start.59 = (f32[1,512]{1,0:T(1,128)}, f32[1,512]{1,0:T(1,128)S(1)}, u32[]{:S(2)}) copy-start(f32[1,512]{1,0:T(1,128)S(1)} %get-tuple-element.201) | copy-start | bytes 6148
  149.2 6.7 %copy-start.60 = (f32[1,512]{1,0:T(1,128)}, f32[1,512]{1,0:T(1,128)S(1)}, u32[]{:S(2)}) copy-start(f32[1,512]{1,0:T(1,128)S(1)} %get-tuple-element.202) | copy-start | bytes 6148
  149.2 8.6 %copy-start.26 = (f32[5120]{0:T(1024)}, f32[5120]{0:T(1024)S(1)}, u32[]{:S(2)}) copy-start(f32[5120]{0:T(1024)S(1)} %pad_maximum_fusion.2) | copy-start | bytes 61444
  149.2 5.8 %copy-start.47 = (bf16[1024,2048]{1,0:T(8,128)(2,1)S(1)}, bf16[1024,2048]{1,0:T(8,128)(2,1)}, u32[]{:S(2)}) copy-start(bf16[1024,2048]{1,0:T(8,128)(2,1)} %refs_10_.1) | copy-start | bytes 12582916
  151.6 4.3 copy-start.52
  151.6 4.9 copy-start.56
  151.6 4.9 copy-start.61
  151.6 5.6 %copy-start.53 = (f32[2,16,2048]{2,1,0:T(8,128)S(1)}, f32[2,16,2048]{2,1,0:T(8,128)}, u32[]{:S(2)}) copy-start(f32[2,16,2048]{2,1,0:T(8,128)} %param.29) | copy-start | bytes 786436
  151.6 6.2 %copy-start.4 = (bf16[2,64,2048]{2,1,0:T(8,128)(2,1)S(1)}, bf16[2,64,2048]{2,1,0:T(8,128)(2,1)}, u32[]{:S(2)}) copy-start(bf16[2,64,2048]{2,1,0:T(8,128)(2,1)} %param.21) | copy-start | bytes 1572868
  151.6 6.2 %copy-start.5 = (f32[4,16,2048]{2,1,0:T(8,128)S(1)}, f32[4,16,2048]{2,1,0:T(8,128)}, u32[]{:S(2)}) copy-start(f32[4,16,2048]{2,1,0:T(8,128)} %a_ref.1) | copy-start | bytes 1572868
  157.2 17.9 %copy-start.29 = (f32[1,2048]{1,0:T(1,128)}, f32[1,2048]{1,0:T(1,128)S(1)}, u32[]{:S(2)}) copy-start(f32[1,2048]{1,0:T(1,128)S(1)} %get-tuple-element.198.gain_ref) | copy-start | bytes 24580
  157.9 55.2 %copy-start.63 = (s32[2]{0:T(128)S(1)}, s32[2]{0:T(128)}, u32[]{:S(2)}) copy-start(s32[2]{0:T(128)} %param.41) | copy-start | bytes 28
  175.1 1.1 copy-start.9
  178.5 48.8 %copy-start.37 = (f32[1,5120]{1,0:T(1,128)}, f32[1,5120]{1,0:T(1,128)S(1)}, u32[]{:S(2)}) copy-start(f32[1,5120]{1,0:T(1,128)S(1)} %get-tuple-element.81) | copy-start | bytes 61444
  178.5 50.1 %copy-start.15 = (bf16[128,2048]{1,0:T(8,128)(2,1)}, bf16[128,2048]{1,0:T(8,128)(2,1)S(1)}, u32[]{:S(2)}) copy-start(bf16[128,2048]{1,0:T(8,128)(2,1)S(1)} %get-tuple-element.104.u_ref) | copy-start | bytes 1572868
  213.1 1.6 copy-start.2
  225.3 2.0 copy-start.45
  360.3 5.9 %copy-start.6 = (f32[4,16,2048]{2,1,0:T(8,128)S(1)}, f32[4,16,2048]{2,1,0:T(8,128)}, u32[]{:S(2)}) copy-start(f32[4,16,2048]{2,1,0:T(8,128)} %a_ref.1) | copy-start | bytes 1572868
  360.3 31.1 %copy-start.7 = (bf16[2,64,2048]{2,1,0:T(8,128)(2,1)S(1)}, bf16[2,64,2048]{2,1,0:T(8,128)(2,1)}, u32[]{:S(2)}) copy-start(bf16[2,64,2048]{2,1,0:T(8,128)(2,1)} %param.22) | copy-start | bytes 1572868
  391.5 1.2 copy-start.11
  394.3 8.5 %copy-start.3 = (bf16[8,128,1024]{2,1,0:T(8,128)(2,1)S(1)}, bf16[8,128,1024]{2,1,0:T(8,128)(2,1)}, u32[]{:S(2)}) copy-start(bf16[8,128,1024]{2,1,0:T(8,128)(2,1)} %get-tuple-element.79) | copy-start | bytes 6291460
  394.3 8.5 %copy-start.20 = (bf16[128,2048]{1,0:T(8,128)(2,1)S(1)}, bf16[128,2048]{1,0:T(8,128)(2,1)}, u32[]{:S(2)}) copy-start(bf16[128,2048]{1,0:T(8,128)(2,1)} %copy-done.18) | copy-start | bytes 1572868
  394.3 8.5 %copy-start.46 = (bf16[2,4,512,512]{3,2,1,0:T(8,128)(2,1)S(1)}, bf16[2,4,512,512]{3,2,1,0:T(8,128)(2,1)}, u32[]{:S(2)}) copy-start(bf16[2,4,512,512]{3,2,1,0:T(8,128)(2,1)} %copy-done.45) | copy-start | bytes 12582916
  402.8 41.7 %copy-start.8 = (f32[3,16,2048]{2,1,0:T(8,128)S(1)}, f32[3,16,2048]{2,1,0:T(8,128)}, u32[]{:S(2)}) copy-start(f32[3,16,2048]{2,1,0:T(8,128)} %slice.101.a_ref) | copy-start | bytes 1179652
  402.9 41.7 %copy-start.14 = (f32[16,3072]{1,0:T(8,128)S(1)}, f32[16,3072]{1,0:T(8,128)}, u32[]{:S(2)}) copy-start(f32[16,3072]{1,0:T(8,128)} %slice.104.cross_ref) | copy-start | bytes 589828
  402.9 41.7 %copy-start.16 = (bf16[128,2048]{1,0:T(8,128)(2,1)S(1)}, bf16[128,2048]{1,0:T(8,128)(2,1)}, u32[]{:S(2)}) copy-start(bf16[128,2048]{1,0:T(8,128)(2,1)} %copy-done.15) | copy-start | bytes 1572868
  402.9 41.7 %copy-start.30 = (f32[1,2048]{1,0:T(1,128)S(1)}, f32[1,2048]{1,0:T(1,128)}, u32[]{:S(2)}) copy-start(f32[1,2048]{1,0:T(1,128)} %copy-done.29) | copy-start | bytes 24580
  402.9 41.7 %copy-start.38 = (f32[1,3072]{1,0:T(1,128)S(1)}, f32[1,3072]{1,0:T(1,128)}, u32[]{:S(2)}) copy-start(f32[1,3072]{1,0:T(1,128)} %slice.103.n_ref) | copy-start | bytes 36868
  402.9 41.7 %copy-start.39 = (f32[1,3072]{1,0:T(1,128)S(1)}, f32[1,3072]{1,0:T(1,128)}, u32[]{:S(2)}) copy-start(f32[1,3072]{1,0:T(1,128)} %slice.113.m_ref) | copy-start | bytes 36868
  444.6 13.6 %copy-start.25 = (f32[2,16,2048]{2,1,0:T(8,128)S(1)}, f32[2,16,2048]{2,1,0:T(8,128)}, u32[]{:S(2)}) copy-start(f32[2,16,2048]{2,1,0:T(8,128)} %get-tuple-element.111.ga_gu) | copy-start | bytes 786436
  444.6 13.5 %copy-start.27 = (f32[2,16,1024]{2,1,0:T(8,128)S(1)}, f32[2,16,1024]{2,1,0:T(8,128)}, u32[]{:S(2)}) copy-start(f32[2,16,1024]{2,1,0:T(8,128)} %get-tuple-element.116.gb_gu) | copy-start | bytes 393220
  444.6 13.5 %copy-start.28 = (f32[16,2048]{1,0:T(8,128)S(1)}, f32[16,2048]{1,0:T(8,128)}, u32[]{:S(2)}) copy-start(f32[16,2048]{1,0:T(8,128)} %get-tuple-element.112.gb_d) | copy-start | bytes 393220
  444.7 13.5 %copy-start.33 = (f32[16,1024]{1,0:T(8,128)S(1)}, f32[16,1024]{1,0:T(8,128)}, u32[]{:S(2)}) copy-start(f32[16,1024]{1,0:T(8,128)} %get-tuple-element.119.ga_d) | copy-start | bytes 196612
  444.7 13.5 %copy-start.40 = (f32[2,1,1024]{2,1,0:T(1,128)S(1)}, f32[2,1,1024]{2,1,0:T(1,128)}, u32[]{:S(2)}) copy-start(f32[2,1,1024]{2,1,0:T(1,128)} %get-tuple-element.117.gm_gu) | copy-start | bytes 24580
  444.7 13.5 %copy-start.41 = (f32[2,1,1024]{2,1,0:T(1,128)S(1)}, f32[2,1,1024]{2,1,0:T(1,128)}, u32[]{:S(2)}) copy-start(f32[2,1,1024]{2,1,0:T(1,128)} %get-tuple-element.118.n_gu) | copy-start | bytes 24580
  444.7 13.5 %copy-start.42 = (f32[1,2048]{1,0:T(1,128)S(1)}, f32[1,2048]{1,0:T(1,128)}, u32[]{:S(2)}) copy-start(f32[1,2048]{1,0:T(1,128)} %get-tuple-element.115.gm_d) | copy-start | bytes 24580
  444.7 44.9 %copy-start.55 = (f32[2,8192]{1,0:T(2,128)S(1)}, f32[2,8192]{1,0:T(2,128)}, u32[]{:S(2)}) copy-start(f32[2,8192]{1,0:T(2,128)} %param.36) | copy-start | bytes 196612
  458.2 54.9 %copy-start.1 = (f32[2,16,8192]{2,1,0:T(8,128)S(1)}, f32[2,16,8192]{2,1,0:T(8,128)}, u32[]{:S(2)}) copy-start(f32[2,16,8192]{2,1,0:T(8,128)} %param.35) | copy-start | bytes 3145732
  499.6 9.9 %copy-start.13 = (f32[2,16,8192]{2,1,0:T(8,128)S(1)}, f32[2,16,8192]{2,1,0:T(8,128)}, u32[]{:S(2)}) copy-start(f32[2,16,8192]{2,1,0:T(8,128)} %copy-done.12) | copy-start | bytes 3145732
  499.6 10.9 %copy-start.35 = (f32[2,8192]{1,0:T(2,128)S(1)}, f32[2,8192]{1,0:T(2,128)}, u32[]{:S(2)}) copy-start(f32[2,8192]{1,0:T(2,128)} %copy-done.34) | copy-start | bytes 196612
  (18 other events, 14.0 us)
Sparse Core Ops, SparseCore 0:
  147.8 47.3 all-gather.2
  360.5 48.1 reduce-scatter.1

commit v5 on v4

--- a/solution.py
+++ b/solution.py
@@ -52,11 +52,13 @@
     return z * jnp.tile(cosine, (1, copies)) + other * jnp.tile(sine, (1, copies))
 
 
+def column_squares(w):
+    return jnp.sum(jnp.square(w.astype(jnp.float32)), axis=0, keepdims=True)
+
+
 def column_norms(w, a, b_wide, cross):
-    ones = jnp.ones((16, w.shape[0]), jnp.bfloat16)
-    squares = dot_f32(ones, w * w)[:1]
     gram_b = jnp.dot(dot_nt(a, a), b_wide, precision=highest, preferred_element_type=jnp.float32)
-    squares = squares + 2.0 * SCALE * jnp.sum(b_wide * cross, axis=0, keepdims=True)
+    squares = column_squares(w) + 2.0 * SCALE * jnp.sum(b_wide * cross, axis=0, keepdims=True)
     squares = squares + SCALE * SCALE * jnp.sum(b_wide * gram_b, axis=0, keepdims=True)
     return jnp.sqrt(squares + 1e-06), cross + SCALE * gram_b
 
@@ -122,12 +124,12 @@
     return pl.pallas_call(
         functools.partial(project_kernel, kv_tiles),
         out_shape=(
-            jax.ShapeDtypeStruct((rows, width), low),
-            jax.ShapeDtypeStruct((rows, width + 2 * k_cols), f32),
-            jax.ShapeDtypeStruct((rows, width), low),
-            jax.ShapeDtypeStruct((rows, 2 * k_cols), low),
-            jax.ShapeDtypeStruct((1, cols), f32),
-            jax.ShapeDtypeStruct((16, cols), f32),
+            pltpu.HBM((rows, width), low),
+            pltpu.HBM((rows, width + 2 * k_cols), f32),
+            pltpu.HBM((rows, width), low),
+            pltpu.HBM((rows, 2 * k_cols), low),
+            pltpu.HBM((1, cols), f32),
+            pltpu.HBM((16, cols), f32),
         ),
         grid=(cols // TILE,),
         in_specs=[
@@ -158,7 +160,7 @@
 
 def out_kernel(att_ref, a_ref, w_ref, b_ref, m_ref, n_ref, x_ref, gain_ref, before_ref, x1_ref, u2_ref):
     t = pl.program_id(0)
-    a = a_ref[...].astype(jnp.bfloat16)
+    a = a_ref[0].astype(jnp.bfloat16)
     b = b_ref[...].astype(jnp.bfloat16)
     inner = dot_nt(att_ref[...], a).astype(jnp.bfloat16)
     before = dot_f32(att_ref[...], w_ref[0]) + SCALE * dot_f32(inner, b)
@@ -179,22 +181,24 @@
     skip = (weights.shape[2] - width) // TILE
     full = lambda shape: pl.BlockSpec(shape, lambda t: (0,) * len(shape))
     col = lambda height: pl.BlockSpec((height, TILE), lambda t: (0, t))
+    ahead = b.shape[1] // TILE - tiles
+    later = lambda height: pl.BlockSpec((height, TILE), lambda t: (0, ahead + t))
     f32 = jnp.float32
     return pl.pallas_call(
         out_kernel,
         out_shape=(
-            jax.ShapeDtypeStruct((rows, width), f32),
-            jax.ShapeDtypeStruct((rows, width), f32),
-            jax.ShapeDtypeStruct((rows, width), jnp.bfloat16),
+            pltpu.HBM((rows, width), f32),
+            pltpu.HBM((rows, width), f32),
+            pltpu.HBM((rows, width), jnp.bfloat16),
         ),
         grid=(tiles,),
         in_specs=[
             full((rows, width)),
-            full((16, width)),
+            pl.BlockSpec((1, 16, width), lambda t: (3, 0, 0)),
             pl.BlockSpec((1, width, TILE), lambda t: (1, 0, skip + t)),
-            col(16),
-            col(1),
-            col(1),
+            later(16),
+            later(1),
+            later(1),
             col(rows),
             full((1, width)),
         ],
@@ -212,31 +216,32 @@
     t = pl.program_id(0)
     rows, width = gx_ref.shape
     low = jnp.bfloat16
-    a = a_ref[...].astype(low)
+    a = a_ref[0].astype(low)
+    o_cols = slice(b_ref.shape[1] - width, b_ref.shape[1])
 
     @pl.when(t == 0)
     def _():
         gx = gy_ref[...].astype(jnp.float32) + rms_back(x1_ref[...], gain_ref[...], in_ref[...])
         gx_ref[...] = gx
-        norm = n_ref[...]
-        gb = (gx * (m_ref[...] / norm)).astype(low)
+        norm, m = n_ref[:, o_cols], m_ref[:, o_cols]
+        gb = (gx * (m / norm)).astype(low)
         lhs[:rows] = gb
-        b = b_ref[...].astype(low)
+        b = b_ref[:, o_cols].astype(low)
         b_wide = b.astype(jnp.float32)
         gi[...] = (SCALE * dot_nt(gb, b)).astype(low)
         gm = jnp.sum(gx * before_ref[...], axis=0, keepdims=True) / norm
         gm_ref[...] = gm
-        c = -gm * m_ref[...] / (norm * norm)
+        c = -gm * m / (norm * norm)
         weighted = b_wide * c
         lhs[rows:] = weighted.astype(low)
         tail[...] = lax.dot_general(
             weighted, b_wide, last_last, precision=highest, preferred_element_type=jnp.float32
         )
         inner = dot_nt(att_ref[...], a).astype(low)
-        gb_ref[...] = SCALE * dot_tn(inner, gb) + SCALE * c * cross_ref[...]
+        gb_ref[...] = SCALE * dot_tn(inner, gb) + SCALE * c * cross_ref[:, o_cols]
 
     span = pl.ds(pl.multiple_of(t * TILE, TILE), TILE)
-    a_tile = a_ref[:, span].astype(low)
+    a_tile = a_ref[0, :, span].astype(low)
     gi_low = gi[...]
     back = dot_nt(lhs[...], w_ref[0, :, w_ref.shape[2] - width :])
     gatt_ref[...] = (back[:rows] + dot_f32(gi_low, a_tile)).astype(low)
@@ -256,15 +261,16 @@
     return pl.pallas_call(
         out_back_kernel,
         out_shape=(
-            jax.ShapeDtypeStruct((rows, width), f32),
-            jax.ShapeDtypeStruct((rows, width), low),
+            pltpu.HBM((rows, width), f32),
+            pltpu.HBM((rows, width), low),
             jax.ShapeDtypeStruct((16, width), f32),
             jax.ShapeDtypeStruct((16, width), f32),
             jax.ShapeDtypeStruct((1, width), f32),
         ),
         grid=(tiles,),
-        in_specs=[wide, wide, full((1, width)), wide, wide, wide, full((16, width)), full((16, width)),
-                  full((1, width)), full((1, width)), full((16, width)),
+        in_specs=[wide, wide, full((1, width)), wide, wide, wide,
+                  pl.BlockSpec((1, 16, width), lambda t: (3, 0, 0)),
+                  full(b.shape), full(m.shape), full(norms.shape), full(cross.shape),
                   pl.BlockSpec((1, TILE, weights.shape[2]), lambda t: (1, t, 0))],
         out_specs=(wide, col(rows), col(16), full((16, width)), full((1, width))),
         scratch_shapes=[
@@ -353,14 +359,14 @@
     return pl.pallas_call(
         qkv_back_kernel,
         out_shape=(
-            jax.ShapeDtypeStruct((rows, width), f32),
+            pltpu.HBM((rows, width), f32),
             jax.ShapeDtypeStruct((3, 16, width), f32),
             jax.ShapeDtypeStruct((16, cols), f32),
             jax.ShapeDtypeStruct((1, cols), f32),
         ),
         grid=(tiles,),
         in_specs=[wide, full(gkv.shape), full(cosine.shape), full(sine.shape), full((rows, cols)), wide,
-                  full((3, 16, width)), full((16, cols)), full((1, cols)), full((1, cols)), full((16, cols)),
+                  full(a.shape), full(b.shape), full(m.shape), full(norms.shape), full(cross.shape),
                   wide, full((1, width)), wide,
                   pl.BlockSpec((1, TILE, width + k_cols), lambda t: (0, t, 0)),
                   pl.BlockSpec((1, TILE, k_cols), lambda t: (1, t, 0))],
@@ -436,7 +442,7 @@
     )
 
 
-def weights_kernel(n, rows, xa, xg, wa, gz, near, local, edge, a_in, a_sib_in, a_out, a_sib_out, z_in, z_out):
+def weights_kernel(n, rows, xa, xg, wd_hbm, ad_ref, bd_ref, wa, gz, near, sq_ref, gram_ref, wd, local, edge, a_in, a_sib_in, a_out, a_sib_out, z_in, z_out):
     nc, half = n // 2, rows // 2
     others = half - 1
     units = gz.shape[-1]
@@ -522,6 +528,15 @@
     keep_g = pltpu.make_async_copy(xg.at[:, :, :, columns(s)], near.at[:, c], local.at[1])
     sib_a().start()
     keep_a.start()
+    take_d = pltpu.make_async_copy(wd_hbm, wd, local.at[2])
+    take_d.start()
+    a_low = ad_ref[...].astype(jnp.bfloat16)
+    gram_ref[...] = dot_nt(a_low, a_low)
+    mine = pl.ds(pl.multiple_of(s * wd.shape[0], wd.shape[0]), wd.shape[0])
+    b_wide = bd_ref[...].astype(jnp.bfloat16).astype(jnp.float32)
+    take_d.wait()
+    cross = dot_f32(ad_ref[:, mine].astype(jnp.bfloat16), wd[...])
+    sq_ref[...] = column_squares(wd[...]) + 2.0 * SCALE * jnp.sum(b_wide * cross, axis=0, keepdims=True)
     for p in order[1:]:
         a_arrival(p, LINE).wait_recv()
         pl.when((p < q) & (q < nc - 1))(
@@ -534,6 +549,7 @@
         for k in range(1, half):
             a_send(p, both, r, from_a(k), a_row(k)).start()
         a_to_sibling(p, LINE, c).start()
+    for p in order[1:]:
         for core in range(2):
             z_send(p, core).start()
     sib_g().start()
@@ -575,7 +591,7 @@
             z_arrival(p, core).wait_recv()
 
 
-def gather_weights(n, rows, xa, xg, collective_id):
+def gather_weights(n, rows, xa, xg, wd, ad, bd, collective_id):
     nc = n // 2
     block = xa.shape[1]
     part = block // rows
@@ -586,23 +602,28 @@
     dma = pltpu.SemaphoreType.DMA
     anywhere = pl.BlockSpec(memory_space=pl.ANY)
     shape = jax.ShapeDtypeStruct
-    wa, gz, near = pl.pallas_call(
+    vmem = pl.BlockSpec(memory_space=pltpu.VMEM)
+    wa, gz, near, sq, gram = pl.pallas_call(
         functools.partial(weights_kernel, n, rows),
         out_shape=(
             shape((2, n, rows, part, xa.shape[3]), xa.dtype),
             shape((2, n, part, units), xg.dtype),
             shape((2, 2, rows, part, units), xg.dtype),
-        ),
-        in_specs=[anywhere] * 2,
-        out_specs=(anywhere,) * 3,
-        scratch_shapes=[dma((2,)), dma((6,))] + [dma((nc, kinds))] * 4 + [dma((nc, 2))] * 2,
-        compiler_params=pltpu.CompilerParams(collective_id=collective_id, has_side_effects=True),
+            shape((1, wd.shape[1]), jnp.float32),
+            shape((16, 16), jnp.float32),
+        ),
+        in_specs=[anywhere] * 3 + [vmem] * 2,
+        out_specs=(anywhere,) * 3 + (vmem,) * 2,
+        scratch_shapes=[pltpu.VMEM(wd.shape, wd.dtype), dma((3,)), dma((6,))] + [dma((nc, kinds))] * 4 + [dma((nc, 2))] * 2,
+        compiler_params=pltpu.CompilerParams(
+            collective_id=collective_id, has_side_effects=True, vmem_limit_bytes=32 << 20
+        ),
         cost_estimate=pl.CostEstimate(
             flops=0, transcendentals=0, bytes_accessed=250 * 1024 * 1024
         ),
         name="gather_weights",
-    )(xa, xg)
-    return wa.reshape(2, n * block, -1), gz, near
+    )(xa, xg, wd, ad, bd)
+    return wa.reshape(2, n * block, -1), gz, near, sq, gram
 
 
 def gather_kernel(n, rows, count, shared, *refs):
@@ -871,8 +892,8 @@
     return pl.pallas_call(
         attend_kernel,
         out_shape=(
-            jax.ShapeDtypeStruct(q.shape, jnp.bfloat16),
-            jax.ShapeDtypeStruct((pair, groups, 8 * span, keys), jnp.bfloat16),
+            pltpu.HBM(q.shape, jnp.bfloat16),
+            pltpu.HBM((pair, groups, 8 * span, keys), jnp.bfloat16),
         ),
         grid_spec=pltpu.PrefetchScalarGridSpec(
             num_scalar_prefetch=1,
@@ -926,8 +947,8 @@
     return pl.pallas_call(
         attend_back_kernel,
         out_shape=(
-            jax.ShapeDtypeStruct(q.shape, jnp.bfloat16),
-            jax.ShapeDtypeStruct(kv.shape, jnp.bfloat16),
+            pltpu.HBM(q.shape, jnp.bfloat16),
+            pltpu.HBM(kv.shape, jnp.bfloat16),
         ),
         grid=(pair, groups),
         in_specs=[
@@ -956,7 +977,7 @@
     return jnp.where(i <= 2 * short, near, far)
 
 
-def ffn_kernel(n, rows, pieces, u_hbm, gy_hbm, wd_hbm, a_ref, b_ref, m_ref, ad_ref, bd_ref, md_ref, sq_ref, gram_ref,
+def ffn_kernel(n, rows, pieces, u_hbm, gy0_hbm, gy1_hbm, wd_hbm, a_ref, b_ref, m_ref, ad_ref, bd_ref, md_ref, sq_ref, gram_ref,
                in_ref, down_hbm, ga_ref, gb_ref, gm_ref, norm_ref, gad_ref, gbd_ref, gmd_ref, nd_ref,
                w_parts, wd, u, gy, down, own, theirs, sib, from_left, from_right, ratio, cross, gm_all,
                w_sem, load_sem, down_sem, small_out, small_in, to_sib, sib_in, to_right, right_in, to_left, left_in):
@@ -977,7 +998,12 @@
         pair = pl.ds(2 * p, 2)
         return (
             pltpu.make_async_copy(u_hbm.at[pair], u.at[slot], load_sem.at[0, slot]),
-            pltpu.make_async_copy(gy_hbm.at[pair], gy.at[slot], load_sem.at[1, slot]),
+            pltpu.make_async_copy(
+                gy0_hbm.at[pair], gy.at[slot, :, : tokens // 2], load_sem.at[1, slot]
+            ),
+            pltpu.make_async_copy(
+                gy1_hbm.at[pair], gy.at[slot, :, tokens // 2 :], load_sem.at[2, slot]
+            ),
         )
 
     for cp in loads(0):
@@ -1047,17 +1073,20 @@
     w = [w_parts.at[g] for g in range(2)]
     width = u_hbm.shape[2]
     weight = lambda g: w[g][...].reshape(width, -1)
+    units = wd.shape[0]
+    mine = pl.ds(pl.multiple_of(s * units, units), units)
     bd = bd_ref[...].astype(low)
-    ad = ad_ref[...].astype(low)
+    ad = ad_ref[:, mine].astype(low)
     a = [a_ref[g].astype(low) for g in range(2)]
-    b = [b_ref[g].astype(low) for g in range(2)]
+    b = [b_ref[g, :, mine].astype(low) for g in range(2)]
+    m = [m_ref[g : g + 1, mine] for g in range(2)]
     for cp in weights:
         cp.wait()
     for g in range(2):
         norm, cr = column_norms(weight(g), a[g], b[g].astype(f32), dot_f32(a[g], weight(g)))
         norm_ref[g] = norm
         cross[g] = cr
-        ratio[g] = m_ref[g] / norm
+        ratio[g] = m[g] / norm
     for ref in (ga_ref, gb_ref, gm_ref, gad_ref, gbd_ref, gmd_ref):
         ref[...] = jnp.zeros_like(ref)
     bd_wide = bd.astype(f32)
@@ -1152,7 +1181,7 @@
         norm = norm_ref[g]
         gm = gm_ref[g] / norm
         gm_ref[g] = gm
-        col = -gm * m_ref[g] / (norm * norm)
+        col = -gm * m[g] / (norm * norm)
         b_wide = b[g].astype(f32)
         weighted = b_wide * col
         tail = lax.dot_general(
@@ -1230,7 +1259,7 @@
     return out
 
 
-def feed_forward(n, rows, pieces, u, gy, wd, a, b, m, ad, bd, md, sq, gram, collective_id):
+def feed_forward(n, rows, pieces, u, gy0, gy1, wd, a, b, m, ad, bd, md, sq, gram, collective_id):
     nc = n // 2
     _, tokens, width = u.shape
     units = wd.shape[0]
@@ -1262,7 +1291,7 @@
             shape((1, width), f32),
             shape((1, width), f32),
         ),
-        in_specs=[hbm] * (count + 3) + [vmem] * 8,
+        in_specs=[hbm] * (count + 4) + [vmem] * 8,
         out_specs=(vmem, hbm) + (vmem,) * 8,
         scratch_shapes=[
             pltpu.VMEM((2, n, rows, part, units), low),
@@ -1272,7 +1301,7 @@
             pltpu.VMEM((2, 1, units), f32),
             pltpu.VMEM((2, 16, units), f32),
             pltpu.VMEM((n, 1, width), f32),
-            dma((copies,)), dma((2, 2)), dma((2,)), dma((n,)), dma((n,)),
+            dma((copies,)), dma((3, 2)), dma((2,)), dma((n,)), dma((n,)),
         ] + [dma((nc,))] * 6,
         compiler_params=pltpu.CompilerParams(
             collective_id=collective_id, has_side_effects=True, vmem_limit_bytes=60 << 20
@@ -1282,11 +1311,10 @@
             bytes_accessed=32 << 20,
         ),
         name="feed_forward",
-    )(*pieces, u, gy, wd, a, b, m, ad, bd, md, sq, gram)
+    )(*pieces, u, gy0, gy1, wd, a, b, m, ad, bd, md, sq, gram)
 
 def reduce_kernel(n, rows, ga_qkv, ga_o, gb_qkv, gb_o, ga_gu, gb_d, gm_qkv, gm_o, gm_d, gb_gu, gm_gu, n_gu, ga_d,
-                  o_ga, o_gb_qo, o_gb_kv, o_gm_q, o_gm_kv, o_gm_o, o_ga_gu, o_gb_gu, o_gm_gu, o_ga_d, o_gb_d, o_gm_d, o_n,
-                  part, from_sib, mid, from_rows, from_line, line_out, units, units_in, whole, units_all,
+                  whole, units_all, part, from_sib, mid, from_rows, from_line, line_out, units, units_in,
                   sib_out, sib_in, row_out, row_in, line_send, line_in, back_send, back_in, wide_send, wide_in,
                   pass_send, pass_in):
     nc = n // 2
@@ -1425,6 +1453,70 @@
         hand(t, member(-t), 1 - c).wait_recv()
         unit_hand(t, member(-t), 1 - c).wait_recv()
 
+    to_sibling().wait_send()
+    for t in range(1, rows):
+        row_send(t).wait_send()
+        unit_send(t).wait_send()
+        wide(t, r).wait_send()
+        unit_wide(t, r).wait_send()
+    for t in range(1, nc):
+        line_part(t).wait_send()
+        back(t, q).wait_send()
+        unit_back(t, q).wait_send()
+    for t in range(rows):
+        hand(t, member(-t), c).wait_send()
+        unit_hand(t, member(-t), c).wait_send()
+
+
+def sum_gradients(n, rows, full, own_units, collective_id):
+    nc = n // 2
+    width, size = full[1].shape[1], own_units[3].shape[1]
+    cols = width // (2 * rows)
+    height = -(-160 // (8 * nc)) * 8 * nc
+    unit_rows = 64 // rows
+    low = jnp.bfloat16
+    vmem = pl.BlockSpec(memory_space=pltpu.VMEM)
+    dma = pltpu.SemaphoreType.DMA
+    block = (rows, height, cols)
+    return pl.pallas_call(
+        functools.partial(reduce_kernel, n, rows),
+        out_shape=(
+            jax.ShapeDtypeStruct((rows, 2, nc, height // nc, cols), low),
+            jax.ShapeDtypeStruct((rows, 2, nc, unit_rows, size), low),
+        ),
+        in_specs=[vmem] * 13,
+        out_specs=(vmem,) * 2,
+        scratch_shapes=[
+            pltpu.VMEM((2, *block), low),
+            pltpu.VMEM(block, low),
+            pltpu.VMEM(block, low),
+            pltpu.VMEM(block, low),
+            pltpu.VMEM((nc, height // nc, cols), low),
+            pltpu.VMEM((nc, height // nc, cols), low),
+            pltpu.VMEM((rows, unit_rows, size), low),
+            pltpu.VMEM((rows, unit_rows, size), low),
+            dma((1,)), dma((1,)), dma((2, rows)), dma((2, rows)), dma((nc,)), dma((nc,)),
+            dma((2, nc)), dma((2, nc)), dma((2, rows)), dma((2, rows)), dma((2, rows)), dma((2, rows)),
+        ],
+        compiler_params=pltpu.CompilerParams(
+            collective_id=collective_id, has_side_effects=True, vmem_limit_bytes=48 << 20
+        ),
+        cost_estimate=pl.CostEstimate(flops=0, transcendentals=0, bytes_accessed=64 << 20),
+        name="sum_gradients",
+    )(*full, *own_units)
+
+
+def finish_kernel(n, rows, whole, units_all, x1, before, m_attn, n_attn, m_d, n_d, m_gu,
+                  o_out, o_ga, o_gb_qo, o_gb_kv, o_gm_q, o_gm_kv, o_gm_o, o_ga_gu, o_gb_gu, o_gm_gu, o_ga_d, o_gb_d,
+                  o_gm_d, o_stats, n_gu):
+    f32 = jnp.float32
+    nc = n // 2
+    width = o_gb_d.shape[1]
+    kv = o_gb_kv.shape[2]
+    cols = width // (2 * rows)
+    size = units_all.shape[4]
+    per = units_all.shape[3] // 8
+    o_out[...] = (x1[...] + before[...].astype(f32) * (m_d[...] / n_d[...])).astype(o_out.dtype)
     for j in range(2 * rows):
         block = jnp.concatenate([whole[j // 2, j % 2, p].astype(f32) for p in range(nc)], axis=0)
         at = slice(cols * j, cols * (j + 1))
@@ -1437,9 +1529,9 @@
         o_gb_d[:, at] = block[128:144]
         which, start = divmod(cols * j, kv)
         o_gb_kv[which // 2, 8 * (which % 2) : 8 * (which % 2) + 8, start : start + cols] = block[144:152]
-        o_gm_q[:, at] = block[152:153]
-        o_gm_o[:, at] = block[153:154]
-        o_gm_d[:, at] = block[154:155]
+        o_gm_q[at] = block[152]
+        o_gm_o[at] = block[153]
+        o_gm_d[at] = block[154]
         if which < 2:
             o_gm_kv[which : which + 1, start : start + cols] = block[155:156]
     for j in range(rows):
@@ -1455,80 +1547,43 @@
                     o_ga_d[half, at] = rows8
                 elif place == 6:
                     o_gm_gu[:, at] = rows8[:2]
-                    o_n[0:1, at] = rows8[2:3] + rows8[3:4]
-                    o_n[1:2, at] = rows8[4:5] + rows8[5:6]
-
-    to_sibling().wait_send()
-    for t in range(1, rows):
-        row_send(t).wait_send()
-        unit_send(t).wait_send()
-        wide(t, r).wait_send()
-        unit_wide(t, r).wait_send()
-    for t in range(1, nc):
-        line_part(t).wait_send()
-        back(t, q).wait_send()
-        unit_back(t, q).wait_send()
-    for t in range(rows):
-        hand(t, member(-t), c).wait_send()
-        unit_hand(t, member(-t), c).wait_send()
-
-
-def sum_gradients(n, rows, full, own_units, collective_id):
-    nc = n // 2
-    width, size = full[1].shape[1], own_units[3].shape[1]
-    kv = (full[2].shape[1] - width) // 2
-    wide_units = size * n
-    cols = width // (2 * rows)
-    height = -(-160 // (8 * nc)) * 8 * nc
-    unit_rows = 64 // rows
-    f32, low = jnp.float32, jnp.bfloat16
-    shape = lambda *dims: jax.ShapeDtypeStruct(dims, f32)
+                    n_gu[0:1, at] = rows8[2:3] + rows8[3:4]
+                    n_gu[1:2, at] = rows8[4:5] + rows8[5:6]
+
+
+    row = lax.broadcasted_iota(jnp.int32, o_stats.shape, 0)
+    col = lax.broadcasted_iota(jnp.int32, o_stats.shape, 1)
+    bounds = [(0, width), (width, width + kv), (width + kv, width + 2 * kv), (width + 2 * kv, 2 * width + 2 * kv)]
+    both = [(m_attn[:, i:j], n_attn[:, i:j]) for i, j in bounds]
+    both += [(m_gu[g : g + 1, :], n_gu[g : g + 1, :]) for g in range(2)] + [(m_d[...], n_d[...])]
+    stats = jnp.zeros(o_stats.shape, f32)
+    for p, (m, norm) in enumerate(both):
+        drift = jnp.mean(jnp.square(m - norm), axis=1, keepdims=True)
+        drift = jnp.sqrt(drift) / jnp.sqrt(jnp.mean(jnp.square(m), axis=1, keepdims=True) + 1e-06)
+        stats = jnp.where((row == p) & (col == 0), drift, stats)
+        stats = jnp.where((row == p) & (col == 1), jnp.mean(norm, axis=1, keepdims=True), stats)
+    o_stats[...] = stats
+
+
+def finish(n, rows, sums, x1, before, m_attn, n_attn, m_d, n_d, m_gu):
+    tokens, width = x1.shape
+    kv = (m_attn.shape[1] - 2 * width) // 2
+    units = m_gu.shape[1]
+    shape = lambda *dims: pltpu.HBM(dims, jnp.float32)
     vmem = pl.BlockSpec(memory_space=pltpu.VMEM)
-    dma = pltpu.SemaphoreType.DMA
-    outs = (
-        shape(4, 16, width), shape(2, 16, width), shape(2, 16, kv), shape(1, width), shape(2, kv), shape(1, width),
-        shape(2, 16, width), shape(2, 16, wide_units), shape(2, wide_units), shape(16, wide_units), shape(16, width),
-        shape(1, width), shape(2, wide_units),
-    )
-    block = (rows, height, cols)
     return pl.pallas_call(
-        functools.partial(reduce_kernel, n, rows),
-        out_shape=outs,
-        in_specs=[vmem] * 13,
-        out_specs=(vmem,) * 13,
-        scratch_shapes=[
-            pltpu.VMEM((2, *block), low),
-            pltpu.VMEM(block, low),
-            pltpu.VMEM(block, low),
-            pltpu.VMEM(block, low),
-            pltpu.VMEM((nc, height // nc, cols), low),
-            pltpu.VMEM((nc, height // nc, cols), low),
-            pltpu.VMEM((rows, unit_rows, size), low),
-            pltpu.VMEM((rows, unit_rows, size), low),
-            pltpu.VMEM((rows, 2, nc, height // nc, cols), low),
-            pltpu.VMEM((rows, 2, nc, unit_rows, size), low),
-            dma((1,)), dma((1,)), dma((2, rows)), dma((2, rows)), dma((nc,)), dma((nc,)),
-            dma((2, nc)), dma((2, nc)), dma((2, rows)), dma((2, rows)), dma((2, rows)), dma((2, rows)),
-        ],
-        compiler_params=pltpu.CompilerParams(
-            collective_id=collective_id, has_side_effects=True, vmem_limit_bytes=48 << 20
-        ),
-        cost_estimate=pl.CostEstimate(flops=0, transcendentals=0, bytes_accessed=64 << 20),
-        name="sum_gradients",
-    )(*full, *own_units)
-
-def square_terms(weight, a_low, b_low):
-    cross = dot_f32(a_low, weight)
-    squares = jnp.sum(jnp.square(weight.astype(jnp.float32)), axis=0, keepdims=True)
-    return squares + 2.0 * SCALE * jnp.sum(b_low.astype(jnp.float32) * cross, axis=0, keepdims=True)
-
-
-def drift_stats(magnitude_vector, norms):
-    drift = jnp.sqrt(jnp.mean(jnp.square(magnitude_vector - norms))) / jnp.sqrt(
-        jnp.mean(jnp.square(magnitude_vector)) + 1e-06
-    )
-    return jnp.stack([drift, jnp.mean(norms)])
-
+        functools.partial(finish_kernel, n, rows),
+        out_shape=(
+            pltpu.HBM((tokens, width), jnp.bfloat16), shape(4, 16, width), shape(2, 16, width), shape(2, 16, kv),
+            shape(width), shape(2, kv), shape(width), shape(2, 16, width), shape(2, 16, units), shape(2, units),
+            shape(16, units), shape(16, width), shape(width), shape(7, 2),
+        ),
+        in_specs=[vmem] * 2 + [pl.BlockSpec()] * 7,
+        scratch_shapes=[pltpu.VMEM((2, units), jnp.float32)],
+        compiler_params=pltpu.CompilerParams(vmem_limit_bytes=40 << 20),
+        cost_estimate=pl.CostEstimate(flops=0, transcendentals=0, bytes_accessed=8 << 20),
+        name="finish",
+    )(*sums, x1, before, m_attn, n_attn, m_d, n_d, m_gu)
 
 def local(
     layer_input,
@@ -1556,13 +1611,10 @@
     pair_rows, span_len, model_width = layer_input.shape
     token_count = pair_rows * span_len
     kv_width = KV_HEADS * HEAD_DIM
-    qkv_width = model_width + 2 * kv_width
     seq_size = lax.axis_size("seq")
     rows_size = lax.axis_size("rows")
     seq_index = lax.axis_index("seq")
-    low, f32 = jnp.bfloat16, jnp.float32
-    slice_units = down_frozen_weight.shape[0]
-    start = seq_index * slice_units
+    f32 = jnp.float32
 
     packed = jnp.stack(
         [
@@ -1570,12 +1622,15 @@
             jnp.concatenate([key_value_frozen[1], query_output_frozen[1]], axis=1),
         ]
     )
-    weights, gu_own, gu_near = gather_weights(seq_size, rows_size, packed, gate_up_frozen, 1)
+    weights, gu_own, gu_near, sq_d, gram_d = gather_weights(
+        seq_size, rows_size, packed, gate_up_frozen, down_frozen_weight, down_adapter_a,
+        down_adapter_b, 1,
+    )
     shares_1, shares_2 = share_plan(rows_size)
-    weights, grad_out_rows = lax.optimization_barrier(
-        (weights, output_gradient.reshape(token_count, model_width))
-    )
-    gy_all = lax.all_gather(grad_out_rows, "seq", axis=0, tiled=False)
+    grad_out_rows = output_gradient.reshape(token_count, model_width)
+    half_0, half_1 = jnp.split(grad_out_rows, 2)
+    weights, half_0 = lax.optimization_barrier((weights, half_0))
+    gy_0 = lax.all_gather(half_0, "seq", axis=0, tiled=False)
 
     b_attn = jnp.concatenate(
         [
@@ -1589,12 +1644,7 @@
     m_attn = jnp.concatenate(
         [query_magnitude, key_value_magnitude[0], key_value_magnitude[1], output_magnitude]
     )[None]
-    b_gu = lax.dynamic_slice_in_dim(gate_up_adapter_b, start, slice_units, 2)
-    m_gu = lax.dynamic_slice_in_dim(gate_up_magnitude, start, slice_units, 1)[:, None]
-    a_d = lax.dynamic_slice_in_dim(down_adapter_a, start, slice_units, 1)
-    b_d = down_adapter_b.astype(low)
     m_d = down_magnitude[None]
-    sq_d = square_terms(down_frozen_weight, a_d.astype(low), b_d)
 
     positions = seq_index * span_len + jnp.arange(span_len, dtype=jnp.int32)
     half_dim = HEAD_DIM // 2
@@ -1612,39 +1662,38 @@
     (kv_all, sq_all), gu_1 = gather_seq(
         seq_size, rows_size, [kv, sq_d], 2, (gu_own,), shares_1
     )
+    kv_all, half_1 = lax.optimization_barrier((kv_all, half_1))
+    gy_1 = lax.all_gather(half_1, "seq", axis=0, tiled=False)
     kv_all = kv_all.reshape(seq_size, pair_rows, span_len, 2 * kv_width)
     q = q.reshape(pair_rows, span_len, model_width)
     att, shares = attend(q, kv_all, valid_len)
     att = att.reshape(token_count, model_width)
-    b_o, m_o, n_o = b_attn[:, qkv_width:], m_attn[:, qkv_width:], n_attn[:, qkv_width:]
-    a_o = attention_adapter_a[3]
-    before_o, x1, u2 = project_out(att, a_o, weights, b_o, m_o, n_o, x, gain_ffn)
+    before_o, x1, u2 = project_out(
+        att, attention_adapter_a, weights, b_attn, m_attn, n_attn, x, gain_ffn
+    )
 
     (u2_all,), gu_2 = gather_seq(
         seq_size, rows_size, [u2], 3, (gu_own, *gu_1), shares_2
     )
-    a_d_wide = down_adapter_a.astype(low).astype(f32)
-    gram_d = jnp.dot(a_d_wide, a_d_wide.T, precision=highest)
     in_grad, down_parts, ga_gu, gb_gu, gm_gu, n_gu, ga_d, gb_d, gm_d, n_d = feed_forward(
-        seq_size, rows_size, (gu_own, gu_near, *gu_1, *gu_2), u2_all, gy_all, down_frozen_weight,
-        gate_up_adapter_a, b_gu, m_gu, a_d, down_adapter_b, m_d, sq_all, gram_d, 4,
+        seq_size, rows_size, (gu_own, gu_near, *gu_1, *gu_2), u2_all, gy_0, gy_1,
+        down_frozen_weight, gate_up_adapter_a, gate_up_adapter_b, gate_up_magnitude, down_adapter_a,
+        down_adapter_b, m_d, sq_all, gram_d, 4,
     )
     before_d = lax.psum_scatter(
         down_parts.reshape(seq_size * token_count, model_width), "seq", scatter_dimension=0,
         tiled=True,
     )
-    layer_result = (x1 + before_d.astype(f32) * (m_d / n_d)).astype(low)
 
     gx1, grad_att, ga_o, gb_o, gm_o = out_back(
-        in_grad, x1, gain_ffn, grad_out_rows, before_o, att, a_o, b_o, m_o, n_o,
-        cross_attn[:, qkv_width:], weights,
+        in_grad, x1, gain_ffn, grad_out_rows, before_o, att, attention_adapter_a, b_attn, m_attn,
+        n_attn, cross_attn, weights,
     )
     gq, gkv = attend_back(q, kv_all, shares, grad_att.reshape(q.shape))
     gkv = scatter_seq(seq_size, gkv.reshape(seq_size, token_count, 2 * kv_width), 5)
     grad_inputs, ga_qkv, gb_qkv, gm_qkv = qkv_back(
         gq.reshape(token_count, model_width), gkv, cosine, sine, before_qkv, u1,
-        attention_adapter_a[:3], b_attn[:, :qkv_width], m_attn[:, :qkv_width],
-        n_attn[:, :qkv_width], cross_attn[:, :qkv_width], x, gain_attn, gx1, weights,
+        attention_adapter_a, b_attn, m_attn, n_attn, cross_attn, x, gain_attn, gx1, weights,
     )
 
     sums = sum_gradients(
@@ -1653,19 +1702,8 @@
         (gb_gu, gm_gu, n_gu, ga_d),
         6,
     )
-    norms_gu = sums[12]
-    summed = (*sums[:3], sums[3][0], sums[4], sums[5][0], *sums[6:11], sums[11][0])
-    k_end = model_width + kv_width
-    stats = jnp.stack(
-        [
-            drift_stats(query_magnitude, n_attn[0, :model_width]),
-            drift_stats(key_value_magnitude[0], n_attn[0, model_width:k_end]),
-            drift_stats(key_value_magnitude[1], n_attn[0, k_end:qkv_width]),
-            drift_stats(output_magnitude, n_o[0]),
-            drift_stats(gate_up_magnitude[0], norms_gu[0]),
-            drift_stats(gate_up_magnitude[1], norms_gu[1]),
-            drift_stats(down_magnitude, n_d[0]),
-        ]
+    layer_result, *summed, stats = finish(
+        seq_size, rows_size, sums, x1, before_d, m_attn, n_attn, m_d, n_d, gate_up_magnitude
     )
     shape = (pair_rows, span_len, model_width)
     return (layer_result.reshape(shape), grad_inputs.reshape(shape), *summed, stats)

time: 531 us -> 441 us (0.83); the launches traced: 520 us -> 440 us
  local copies, waits for them, and re-layouts: 48.3 us -> 27.5 us
  Pallas kernels: 417 us -> 397 us
  other arithmetic: 19.7 us -> 0.42 us
  between operations: 30.1 us -> 15 us
  matrix products: 5.38 us -> 0 us
    pallas_call x1, Pallas kernels: 137 us -> 102 us  [gather_weights(): pl.pallas_call(functools.partial(weights_kernel, n, rows), out_shape=(sha...]
    reduce_sum x10 -> x0, other arithmetic: 12.7 us -> none  [the longest x6 7.37 us: drift_stats(): jnp.mean(jnp.square(magnitude_vector)) + 1e-06]
    pallas_call x1, Pallas kernels: 31.8 us -> 42.3 us  [scatter_seq(): pl.pallas_call(functools.partial(scatter_kernel, n), out_shape=jax.ShapeD...]
    another operation x8 -> x0, local copies, waits for them, and re-layouts: 7.19 us -> none  [local(): jnp.stack([drift_stats(query_magnitude, n_attn[0, :model_width]), drift_s...]
    slice x6 -> x0, local copies, waits for them, and re-layouts: 6.65 us -> none  [the longest x1 1.62 us: local(): cross_attn[:, :qkv_width]]
    unnamed x140 -> x103, local copies, waits for them, and re-layouts: 28.5 us -> 22.2 us
    dot_general x2 -> x0, matrix products: 5.38 us -> none  [the longest x1 3.35 us: dot_f32(): return jnp.dot(a, b, preferred_element_type=jnp.float32)]
    pallas_call x7 -> x8, Pallas kernels: 92.9 us -> 97.7 us  [the longest x1 28.7 us: sum_gradients(): pl.pallas_call(functools.partial(reduce_kernel, n, rows), out_shape=(jax....]
  transfers between devices with their start and end apart: 2 -> 3, of which waited for: 0 -> 0; matrix products, arithmetic and copies ran while one was open for 8% -> 0% of each run, Pallas kernels for 39% -> 49%
where the time goes in v5:
time: 441 us; the launch traced here: 440 us
  Pallas kernels  397 us (90%)
  local copies, waits for them, and re-layouts  27.5 us (6%)
  between operations  15 us (3%)
    pallas_call x1, Pallas kernels, gather_weights(): pl.pallas_call(functools.partial(weights_kernel, n, rows), out_shape=(sha...  102 us
    pallas_call x2, Pallas kernels, gather_seq(): pl.pallas_call(functools.partial(gather_kernel, n, rows, count, (range(le...  77.6 us
    pallas_call x1, Pallas kernels, feed_forward(): pl.pallas_call(kernel, out_shape=(shape((tokens, width), f32), shape((n,...  77.2 us
    pallas_call x1, Pallas kernels, scatter_seq(): pl.pallas_call(functools.partial(scatter_kernel, n), out_shape=jax.ShapeD...  42.3 us
    pallas_call x1, Pallas kernels, sum_gradients(): pl.pallas_call(functools.partial(reduce_kernel, n, rows), out_shape=(jax....  28.7 us
    unnamed x103, local copies, waits for them, and re-layouts  22.2 us
    pallas_call x1, Pallas kernels, project_qkv(): pl.pallas_call(functools.partial(project_kernel, kv_tiles), out_shape=(pl...  16.7 us
    pallas_call x1, Pallas kernels, qkv_back(): pl.pallas_call(qkv_back_kernel, out_shape=(pltpu.HBM((rows, width), f32),...  13.5 us
  transfers between devices with their start and end apart: 3, of which 0 were waited for; matrix products, arithmetic and copies ran while one was open for 0% of the time, Pallas kernels for 49%

profile of v5, /device:TPU:0, one launch (start us, length us, event | category | flops | bytes accessed | tf_op | source)
XLA Modules:
  0.0 440.2 jit_solution(13919032028030088030)
XLA Ops:
  7.2 0.0 all-gather.5.cloned.1.call-start
  7.2 1.1 fusion.1
  8.3 1.9 slice_bitcast_fusion
  10.2 1.8 fusion
  12.0 0.2 maximum_maximum_fusion.xa
  12.2 1.9 copy-done.4
  14.2 0.3 copy-done.23
  14.4 2.2 copy-done.7
  16.7 102.4 %gather_weights.1 = (bf16[2,8,4,64,2560]{4,3,2,1,0:T(8,128)(2,1)}, bf16[2,8,64,1024]{3,2,1,0:T(8,128)(2,1)S(1)}, bf16[2,2,4,64,1024]{4,3,2,1,0:T(8,128)(2,1)S(1)}, f32[1,2048]{1,0:T(1,128)S(1)}, f32[16,16]{1,0:T(8,128)S(1)}) custom-call(bf16[2,4,64,2560]{3,2,1,0:T(8,128)(2,1)S(1)} %maximum_maximum_fusion.xa, bf16[2,4,64,8192]{3,2,1,0:T(8,128)(2,1)S(1)} %bitcast.45, ...), custom_call_target="tpu_custom_call" | custom-call | bytes 262144000 | tf_op jit(solution)/shard_map/gather_weights/pallas_call | solution.py:606
  119.1 1.3 copy-done.3
  120.4 0.6 copy-done.36
  121.0 1.3 copy-done.41
  122.3 0.6 copy-done.43
  123.0 0.0 all-gather.7.cloned.1.call-start
  123.1 0.1 multiply_sine_fusion
  123.2 0.1 tile.21
  123.4 0.1 copy.38.sin_ref
  123.5 0.1 tile.9
  123.7 0.1 copy.37.cos_ref
  123.9 0.0 copy-done
  124.0 0.2 copy-done.5
  124.1 16.7 %project_qkv.1 = (bf16[128,2048]{1,0:T(8,128)(2,1)}, f32[128,3072]{1,0:T(8,128)}, bf16[128,2048]{1,0:T(8,128)(2,1)}, bf16[128,1024]{1,0:T(8,128)(2,1)}, f32[1,5120]{1,0:T(1,128)}, /*index=5*/f32[16,5120]{1,0:T(8,128)}) custom-call(bf16[128,2048]{1,0:T(8,128)(2,1)S(1)} %bitcast.46, f32[1,2048]{1,0:T(1,128)S(1)} %get-tuple-element.188.gain_ref, ...), custom_call_target="tpu_custom_call" | custom-call | flops 2684354560 | bytes 20971520 | tf_op jit(solution)/shard_map/project_qkv/pallas_call | solution.py:124
  140.8 32.2 %gather_seq.2 = (bf16[8,128,1024]{2,1,0:T(8,128)(2,1)}, f32[8,1,2048]{2,1,0:T(1,128)}, bf16[8,64,1024]{2,1,0:T(8,128)(2,1)}, bf16[8,64,1024]{2,1,0:T(8,128)(2,1)}) custom-call(bf16[128,1024]{1,0:T(8,128)(2,1)} %get-tuple-element.84.refs_0_, f32[1,2048]{1,0:T(1,128)} %copy-done.36, bf16[2,8,64,1024]{3,2,1,0:T(8,128)(2,1)} %copy-done.3), custom_call_target="tpu_custom_call" | custom-call | bytes 43253760 | tf_op jit(solution)/shard_map/gather_seq/pallas_call | solution.py:704
  173.1 0.0 reduce-scatter.2.cloned.1.call-start
  173.8 1.6 copy-done.1
  175.4 10.4 %attend.1 = (bf16[2,64,2048]{2,1,0:T(8,128)(2,1)}, bf16[2,4,512,512]{3,2,1,0:T(8,128)(2,1)}) custom-call(s32[2]{0:T(128)S(1)} %broadcast_add_fusion.valid_ref, bf16[2,64,2048]{2,1,0:T(8,128)(2,1)S(1)} %bitcast.59, bf16[8,2,64,1024]{3,2,1,0:T(8,128)(2,1)S(1)} %bitcast.41, bf16[8,2,64,1024]{3,2,1,0:T(8,128)(2,1)S(1)} %bitcast.42), custom_call_target="tpu_custom_call" | custom-call | flops 1073741824 | bytes 8388608 | tf_op jit(solution)/shard_map/attend/pallas_call | solution.py:892
  185.8 1.0 copy-done.8
  186.9 7.2 %project_out.1 = (f32[128,2048]{1,0:T(8,128)}, f32[128,2048]{1,0:T(8,128)}, bf16[128,2048]{1,0:T(8,128)(2,1)}) custom-call(bf16[128,2048]{1,0:T(8,128)(2,1)S(1)} %bitcast.49, f32[4,16,2048]{2,1,0:T(8,128)S(1)} %copy-done, bf16[2,2048,2560]{2,1,0:T(8,128)(2,1)} %bitcast.65, f32[16,5120]{1,0:T(8,128)S(1)} %pad_maximum_fusion.b_ref, f32[1,5120]{1,0:T(1,128)S(1)} %bitcast.54, ...), custom_call_target="tpu_custom_call" | custom-call | flops 1073741824 | bytes 8388608 | tf_op jit(solution)/shard_map/project_out/pallas_call | solution.py:187
  194.1 45.4 %gather_seq.3 = (bf16[8,128,2048]{2,1,0:T(8,128)(2,1)}, bf16[8,64,1024]{2,1,0:T(8,128)(2,1)}, bf16[8,64,1024]{2,1,0:T(8,128)(2,1)}, bf16[8,64,1024]{2,1,0:T(8,128)(2,1)}, bf16[8,64,1024]{2,1,0:T(8,128)(2,1)}) custom-call(bf16[128,2048]{1,0:T(8,128)(2,1)} %get-tuple-element.95.refs_0_, bf16[2,8,64,1024]{3,2,1,0:T(8,128)(2,1)} %copy-done.3, ...), custom_call_target="tpu_custom_call" | custom-call | bytes 83886080 | tf_op jit(solution)/shard_map/gather_seq/pallas_call | solution.py:704
  239.5 77.2 %feed_forward.1 = (f32[128,2048]{1,0:T(8,128)}, bf16[8,128,2048]{2,1,0:T(8,128)(2,1)}, f32[2,16,2048]{2,1,0:T(8,128)}, f32[2,16,1024]{2,1,0:T(8,128)}, f32[2,1,1...) custom-call(bf16[2,8,64,1024]{3,2,1,0:T(8,128)(2,1)} %copy-done.3, ...), custom_call_target="tpu_custom_call" | custom-call | flops 25769803776 | bytes 33554432 | tf_op jit(solution)/shard_map/feed_forward/pallas_call | solution.py:1280
  316.8 1.2 copy-done.6
  317.9 0.1 copy-done.9
  318.1 0.2 copy-done.11
  318.2 1.0 copy-done.12
  319.2 1.2 copy-done.14
  320.4 1.4 copy-done.15
  321.9 8.8 %out_back.1 = (f32[128,2048]{1,0:T(8,128)}, bf16[128,2048]{1,0:T(8,128)(2,1)}, f32[16,2048]{1,0:T(8,128)S(1)}, f32[16,2048]{1,0:T(8,128)S(1)}, f32[1,2048]{1,0:T(1,128)S(1)}) custom-call(f32[128,2048]{1,0:T(8,128)S(1)} %copy-done.15, f32[128,2048]{1,0:T(8,128)S(1)} %copy-done.6, f32[1,2048]{1,0:T(1,128)S(1)} %get-tuple-element.187.gain_ref, ...), custom_call_target="tpu_custom_call" | custom-call | flops 1073741824 | bytes 8388608 | tf_op jit(solution)/shard_map/out_back/pallas_call | solution.py:261
  330.6 1.0 copy-done.42
  331.7 10.4 %attend_back.1 = (bf16[2,64,2048]{2,1,0:T(8,128)(2,1)}, bf16[8,2,64,1024]{3,2,1,0:T(8,128)(2,1)}) custom-call(bf16[2,64,2048]{2,1,0:T(8,128)(2,1)S(1)} %bitcast.60, bf16[8,2,64,1024]{3,2,1,0:T(8,128)(2,1)S(1)} %bitcast.43, bf16[8,2,64,1024]{3,2,1,0:T(8,128)(2,1)S(1)} %bitcast.44, bf16[2,4,512,512]{3,2,1,0:T(8,128)(2,1)S(1)} %copy-done.40, ...), custom_call_target="tpu_custom_call" | custom-call | flops 2684354560 | bytes 8388608 | tf_op jit(solution)/shard_map/attend_back/pallas_call | solution.py:947
  342.1 1.6 copy-done.10
  343.7 42.3 %scatter_seq.1.gkv_ref = f32[128,1024]{1,0:T(8,128)S(1)} custom-call(bf16[8,128,1024]{2,1,0:T(8,128)(2,1)S(1)} %bitcast.51), custom_call_target="tpu_custom_call" | custom-call | bytes 41943040 | tf_op jit(solution)/shard_map/scatter_seq/pallas_call | solution.py:821
  386.2 13.5 %qkv_back.1 = (f32[128,2048]{1,0:T(8,128)}, f32[3,16,2048]{2,1,0:T(8,128)S(1)}, f32[16,3072]{1,0:T(8,128)S(1)}, f32[1,3072]{1,0:T(1,128)S(1)}) custom-call(bf16[128,2048]{1,0:T(8,128)(2,1)S(1)} %bitcast.58, f32[128,1024]{1,0:T(8,128)S(1)} %scatter_seq.1.gkv_ref, f32[128,128]{1,0:T(8,128)S(1)} %copy-done.20, f32[128,128]{1,0:T(8,128)S(1)} %copy-done.18, ...), custom_call_target="tpu_custom_call" | custom-call | flops 1610612736 | bytes 12582912 | tf_op jit(solution)/shard_map/qkv_back/pallas_call | solution.py:359
  399.7 28.7 %sum_gradients.1 = (bf16[4,2,4,40,256]{4,3,2,1,0:T(8,128)(2,1)S(1)}, bf16[4,2,4,16,1024]{4,3,2,1,0:T(8,128)(2,1)S(1)}) custom-call(f32[3,16,2048]{2,1,0:T(8,128)S(1)} %get-tuple-element.115.ga_qkv, f32[16,2048]{1,0:T(8,128)S(1)} %get-tuple-element.116.ga_o, f32[16,3072]{1,0:T(8,128)S(1)} %get-tuple-element.117.gb_qkv, ...), custom_call_target="tpu_custom_call" | custom-call | bytes 67108864 | tf_op jit(solution)/shard_map/sum_gradients/pallas_call | solution.py:1481
  428.4 0.0 reduce-scatter.2.cloned.1.call-done.before
  428.5 1.0 copy-done.26
  429.5 0.8 copy-done.32
  430.3 2.1 finish.1
  432.4 1.3 copy.41
  (97 shorter events, 0.5 us)
Async XLA Ops:
  7.2 232.3 %all-gather.5.cloned.1.call-start = ((), (), s32[]{:S(2)}) async-start(), calls=%async_computation.2 | async-start | bytes 2359296 | tf_op jit(solution)/shard_map/all_gather | solution.py:1633
  10.2 4.0 copy-start.4
  12.0 2.4 copy-start.23
  12.0 2.4 copy-start.29
  14.4 2.2 copy-start.7
  16.6 107.1 %copy-start.49 = (f32[2,512]{1,0:T(2,128)S(1)}, f32[2,512]{1,0:T(2,128)}, u32[]{:S(2)}) copy-start(f32[2,512]{1,0:T(2,128)} %param.32) | copy-start | bytes 12292
  16.6 107.2 %copy-start.47 = (f32[2048]{0:T(1024)S(1)}, f32[2048]{0:T(1024)}, u32[]{:S(2)}) copy-start(f32[2048]{0:T(1024)} %param.33) | copy-start | bytes 24580
  16.6 107.2 %copy-start.48 = (f32[2048]{0:T(1024)S(1)}, f32[2048]{0:T(1024)}, u32[]{:S(2)}) copy-start(f32[2048]{0:T(1024)} %param.31) | copy-start | bytes 24580
  16.6 107.2 %copy-start.45 = (f32[2,16,512]{2,1,0:T(8,128)S(1)}, f32[2,16,512]{2,1,0:T(8,128)}, u32[]{:S(2)}) copy-start(f32[2,16,512]{2,1,0:T(8,128)} %param.30) | copy-start | bytes 196612
  16.6 107.2 %copy-start.46 = (f32[2,2048]{1,0:T(2,128)S(1)}, f32[2,2048]{1,0:T(2,128)}, u32[]{:S(2)}) copy-start(f32[2,2048]{1,0:T(2,128)} %param.23) | copy-start | bytes 49156
  16.7 107.2 %copy-start.44 = (f32[2,16,2048]{2,1,0:T(8,128)S(1)}, f32[2,16,2048]{2,1,0:T(8,128)}, u32[]{:S(2)}) copy-start(f32[2,16,2048]{2,1,0:T(8,128)} %param.29) | copy-start | bytes 786436
  119.1 1.3 copy-start.3
  121.0 1.3 copy-start.41
  122.9 1.2 copy-start.5
  123.0 116.5 %all-gather.7.cloned.1.call-start = ((), (), s32[]{:S(2)}) async-start(), calls=%async_computation.3 | async-start | bytes 2359296 | tf_op jit(solution)/shard_map/all_gather | solution.py:1666
  123.5 17.3 %copy-start.17 = (f32[128,128]{1,0:T(8,128)}, f32[128,128]{1,0:T(8,128)S(1)}, u32[]{:S(2)}) copy-start(f32[128,128]{1,0:T(8,128)S(1)} %copy.38.sin_ref) | copy-start | bytes 196612
  123.8 17.0 %copy-start.19 = (f32[128,128]{1,0:T(8,128)}, f32[128,128]{1,0:T(8,128)S(1)}, u32[]{:S(2)}) copy-start(f32[128,128]{1,0:T(8,128)S(1)} %copy.37.cos_ref) | copy-start | bytes 196612
  140.8 33.0 %copy-start.50 = (s32[2]{0:T(128)S(1)}, s32[2]{0:T(128)}, u32[]{:S(2)}) copy-start(s32[2]{0:T(128)} %param.41) | copy-start | bytes 28
  140.8 33.0 %copy-start.24 = (bf16[128,2048]{1,0:T(8,128)(2,1)S(1)}, bf16[128,2048]{1,0:T(8,128)(2,1)}, u32[]{:S(2)}) copy-start(bf16[128,2048]{1,0:T(8,128)(2,1)} %get-tuple-element.83) | copy-start | bytes 1572868
  173.1 12.7 %copy-start.27 = (f32[1,5120]{1,0:T(1,128)S(1)}, f32[1,5120]{1,0:T(1,128)}, u32[]{:S(2)}) copy-start(f32[1,5120]{1,0:T(1,128)} %get-tuple-element.94.n_ref.n_attn) | copy-start | bytes 61444
  173.1 255.3 %reduce-scatter.2.cloned.1.call-start = ((), (), s32[]{:S(2)}) async-start(), calls=%async_computation.1 | async-start | bytes 4718592 | tf_op jit(solution)/shard_map/reduce_scatter | solution.py:1683
  173.8 1.6 copy-start.1
  316.7 1.2 copy-start.6
  316.7 1.3 copy-start.9
  316.7 1.5 copy-start.11
  319.2 1.2 copy-start.14
  320.4 1.4 copy-start.15
  321.9 8.8 %copy-start.2 = (bf16[8,128,1024]{2,1,0:T(8,128)(2,1)S(1)}, bf16[8,128,1024]{2,1,0:T(8,128)(2,1)}, u32[]{:S(2)}) copy-start(bf16[8,128,1024]{2,1,0:T(8,128)(2,1)} %get-tuple-element.88) | copy-start | bytes 6291460
  321.9 8.8 %copy-start.25 = (bf16[128,2048]{1,0:T(8,128)(2,1)S(1)}, bf16[128,2048]{1,0:T(8,128)(2,1)}, u32[]{:S(2)}) copy-start(bf16[128,2048]{1,0:T(8,128)(2,1)} %get-tuple-element.83) | copy-start | bytes 1572868
  321.9 8.8 %copy-start.40 = (bf16[2,4,512,512]{3,2,1,0:T(8,128)(2,1)S(1)}, bf16[2,4,512,512]{3,2,1,0:T(8,128)(2,1)}, u32[]{:S(2)}) copy-start(bf16[2,4,512,512]{3,2,1,0:T(8,128)(2,1)} %get-tuple-element.89.p_ref) | copy-start | bytes 12582916
  330.6 1.0 copy-start.42
  331.7 54.3 %copy-start.13 = (f32[16,5120]{1,0:T(8,128)S(1)}, f32[16,5120]{1,0:T(8,128)}, u32[]{:S(2)}) copy-start(f32[16,5120]{1,0:T(8,128)} %get-tuple-element.108.cross_ref) | copy-start | bytes 983044
  331.7 54.3 %copy-start.16 = (f32[128,2048]{1,0:T(8,128)S(1)}, f32[128,2048]{1,0:T(8,128)}, u32[]{:S(2)}) copy-start(f32[128,2048]{1,0:T(8,128)} %get-tuple-element.114.gx_ref) | copy-start | bytes 3145732
  331.7 54.3 %copy-start.18 = (f32[128,128]{1,0:T(8,128)S(1)}, f32[128,128]{1,0:T(8,128)}, u32[]{:S(2)}) copy-start(f32[128,128]{1,0:T(8,128)} %copy-done.17) | copy-start | bytes 196612
  331.7 54.4 %copy-start.20 = (f32[128,128]{1,0:T(8,128)S(1)}, f32[128,128]{1,0:T(8,128)}, u32[]{:S(2)}) copy-start(f32[128,128]{1,0:T(8,128)} %copy-done.19) | copy-start | bytes 196612
  331.7 54.4 %copy-start.21 = (bf16[128,2048]{1,0:T(8,128)(2,1)S(1)}, bf16[128,2048]{1,0:T(8,128)(2,1)}, u32[]{:S(2)}) copy-start(bf16[128,2048]{1,0:T(8,128)(2,1)} %get-tuple-element.113.u_ref) | copy-start | bytes 1572868
  342.1 1.6 copy-start.10
  343.7 42.3 %copy-start.22 = (bf16[2,64,2048]{2,1,0:T(8,128)(2,1)S(1)}, bf16[2,64,2048]{2,1,0:T(8,128)(2,1)}, u32[]{:S(2)}) copy-start(bf16[2,64,2048]{2,1,0:T(8,128)(2,1)} %get-tuple-element.110) | copy-start | bytes 1572868
  386.1 13.6 %copy-start.28 = (f32[2,16,2048]{2,1,0:T(8,128)S(1)}, f32[2,16,2048]{2,1,0:T(8,128)}, u32[]{:S(2)}) copy-start(f32[2,16,2048]{2,1,0:T(8,128)} %get-tuple-element.119.ga_gu) | copy-start | bytes 786436
  386.1 13.6 %copy-start.30 = (f32[2,16,1024]{2,1,0:T(8,128)S(1)}, f32[2,16,1024]{2,1,0:T(8,128)}, u32[]{:S(2)}) copy-start(f32[2,16,1024]{2,1,0:T(8,128)} %get-tuple-element.124.gb_gu) | copy-start | bytes 393220
  386.1 13.6 %copy-start.31 = (f32[16,2048]{1,0:T(8,128)S(1)}, f32[16,2048]{1,0:T(8,128)}, u32[]{:S(2)}) copy-start(f32[16,2048]{1,0:T(8,128)} %get-tuple-element.120.gb_d) | copy-start | bytes 393220
  386.1 13.6 %copy-start.33 = (f32[16,1024]{1,0:T(8,128)S(1)}, f32[16,1024]{1,0:T(8,128)}, u32[]{:S(2)}) copy-start(f32[16,1024]{1,0:T(8,128)} %get-tuple-element.127.ga_d) | copy-start | bytes 196612
  386.1 13.6 %copy-start.37 = (f32[2,1,1024]{2,1,0:T(1,128)S(1)}, f32[2,1,1024]{2,1,0:T(1,128)}, u32[]{:S(2)}) copy-start(f32[2,1,1024]{2,1,0:T(1,128)} %get-tuple-element.125.gm_gu) | copy-start | bytes 24580
  386.1 13.6 %copy-start.38 = (f32[2,1,1024]{2,1,0:T(1,128)S(1)}, f32[2,1,1024]{2,1,0:T(1,128)}, u32[]{:S(2)}) copy-start(f32[2,1,1024]{2,1,0:T(1,128)} %get-tuple-element.126.n_gu) | copy-start | bytes 24580
  386.1 13.6 %copy-start.39 = (f32[1,2048]{1,0:T(1,128)S(1)}, f32[1,2048]{1,0:T(1,128)}, u32[]{:S(2)}) copy-start(f32[1,2048]{1,0:T(1,128)} %get-tuple-element.123.gm_d) | copy-start | bytes 24580
  386.1 42.3 %copy-start.34 = (f32[2048]{0:T(1024)S(1)}, f32[2048]{0:T(1024)}, u32[]{:S(2)}) copy-start(f32[2048]{0:T(1024)} %param.39) | copy-start | bytes 24580
  386.1 42.3 %copy-start.35 = (f32[1,2048]{1,0:T(1,128)S(1)}, f32[1,2048]{1,0:T(1,128)}, u32[]{:S(2)}) copy-start(f32[1,2048]{1,0:T(1,128)} %get-tuple-element.131.n_d) | copy-start | bytes 24580
  428.4 1.0 copy-start.26
  (6 other events, 5.1 us)
Sparse Core Ops, SparseCore 0:
  123.1 30.4 all-gather.4
  173.2 28.5 all-gather.6
  316.9 65.2 reduce-scatter.1

commit v6 on v5

--- a/solution.py
+++ b/solution.py
@@ -56,37 +56,41 @@
     return jnp.sum(jnp.square(w.astype(jnp.float32)), axis=0, keepdims=True)
 
 
-def column_norms(w, a, b_wide, cross):
-    gram_b = jnp.dot(dot_nt(a, a), b_wide, precision=highest, preferred_element_type=jnp.float32)
+def two_terms(value):
+    high = value.astype(jnp.bfloat16)
+    return jnp.concatenate([high, (value - high.astype(jnp.float32)).astype(jnp.bfloat16)], axis=0)
+
+
+def dot_two(terms, b):
+    both = dot_f32(terms, b)
+    half = both.shape[0] // 2
+    return both[:half] + both[half:]
+
+
+def column_norms(w, gram, b, cross):
+    b_wide = b.astype(jnp.float32)
+    gram_b = dot_two(gram, b)
     squares = column_squares(w) + 2.0 * SCALE * jnp.sum(b_wide * cross, axis=0, keepdims=True)
     squares = squares + SCALE * SCALE * jnp.sum(b_wide * gram_b, axis=0, keepdims=True)
     return jnp.sqrt(squares + 1e-06), cross + SCALE * gram_b
 
 
-def project_kernel(kv_tiles, x_ref, gain_ref, a_ref, w_ref, b_ref, m_ref, cos_ref, sin_ref,
-                   u_ref, before_ref, q_ref, kv_ref, n_ref, cross_ref):
+def project_kernel(kv_tiles, u_ref, inner_ref, gram_ref, a_ref, w_ref, b_ref, m_ref, cos_ref, sin_ref,
+                   before_ref, q_ref, kv_ref, n_ref, cross_ref):
     j = pl.program_id(0)
-    q_tiles = kv_tiles[0]
-
-    @pl.when(j == 0)
-    def _():
-        v = x_ref[...].astype(jnp.float32)
-        u_ref[...] = (v * unit_rms(v) * gain_ref[...]).astype(jnp.bfloat16)
-
+    q_tiles, last = kv_tiles
     a = a_ref[0].astype(jnp.bfloat16)
     b = b_ref[...].astype(jnp.bfloat16)
-    b_wide = b.astype(jnp.float32)
     w = w_ref[0]
     rows = u_ref.shape[0]
 
-    @pl.when(j < kv_tiles[1])
+    @pl.when(j <= last)
     def _():
         both = dot_f32(jnp.concatenate([u_ref[...], a], axis=0), w)
-        norm, cross = column_norms(w, a, b_wide, both[rows:])
+        norm, cross = column_norms(w, gram_ref[0], b, both[rows:])
         n_ref[...] = norm
         cross_ref[...] = cross
-        inner = dot_nt(u_ref[...], a).astype(jnp.bfloat16)
-        before = both[:rows] + SCALE * dot_f32(inner, b)
+        before = both[:rows] + SCALE * dot_f32(inner_ref[0], b)
         before_ref[...] = before
         y = before * (m_ref[...] / norm)
 
@@ -102,29 +106,27 @@
         def _():
             kv_ref[...] = y.astype(jnp.bfloat16)
 
-    @pl.when(j >= kv_tiles[1])
+    @pl.when(j > last)
     def _():
-        norm, cross = column_norms(w, a, b_wide, dot_f32(a, w))
+        norm, cross = column_norms(w, gram_ref[0], b, dot_f32(a, w))
         n_ref[...] = norm
         cross_ref[...] = cross
 
 
-def project_qkv(x, gain, a, weights, b, m, cosine, sine):
-    rows, width = x.shape
+def project_qkv(u, inner, grams, a, weights, b, m, cosine, sine):
+    rows, width = u.shape
     cols = b.shape[1]
     per_half = weights.shape[2] // TILE
     q_tiles = width // TILE
     k_cols = weights.shape[2] - width
-    kv_tiles = (q_tiles, q_tiles + 2 * k_cols // TILE)
-    last = kv_tiles[1] - 1
+    last = q_tiles + 2 * k_cols // TILE - 1
     full = lambda shape: pl.BlockSpec(shape, lambda j: (0,) * len(shape))
     col = lambda height: pl.BlockSpec((height, TILE), lambda j: (0, j))
     which = lambda j: jnp.where(j < q_tiles, 0, jnp.where(j > last, 3, 1 + j - q_tiles))
     f32, low = jnp.float32, jnp.bfloat16
     return pl.pallas_call(
-        functools.partial(project_kernel, kv_tiles),
+        functools.partial(project_kernel, (q_tiles, last)),
         out_shape=(
-            pltpu.HBM((rows, width), low),
             pltpu.HBM((rows, width + 2 * k_cols), f32),
             pltpu.HBM((rows, width), low),
             pltpu.HBM((rows, 2 * k_cols), low),
@@ -134,7 +136,8 @@
         grid=(cols // TILE,),
         in_specs=[
             full((rows, width)),
-            full((1, width)),
+            pl.BlockSpec((1, rows, 16), lambda j: (jnp.minimum(which(j), 2), 0, 0)),
+            pl.BlockSpec((1, 32, 16), lambda j: (which(j), 0, 0)),
             pl.BlockSpec((1, 16, width), lambda j: (which(j), 0, 0)),
             pl.BlockSpec((1, width, TILE), lambda j: (j // per_half, 0, j % per_half)),
             col(16),
@@ -143,7 +146,6 @@
             full(sine.shape),
         ],
         out_specs=(
-            full((rows, width)),
             pl.BlockSpec((rows, TILE), lambda j: (0, jnp.minimum(j, last))),
             pl.BlockSpec((rows, TILE), lambda j: (0, jnp.minimum(j, q_tiles - 1))),
             pl.BlockSpec((rows, TILE), lambda j: (0, jnp.clip(j - q_tiles, 0, last - q_tiles))),
@@ -155,10 +157,11 @@
             flops=2 * rows * width * cols, transcendentals=0, bytes_accessed=2 * width * cols
         ),
         name="project_qkv",
-    )(x, gain, a, weights, b, m, cosine, sine)
-
-
-def out_kernel(att_ref, a_ref, w_ref, b_ref, m_ref, n_ref, x_ref, gain_ref, before_ref, x1_ref, u2_ref):
+    )(u, inner, grams, a, weights, b, m, cosine, sine)
+
+
+def out_kernel(att_ref, a_ref, w_ref, b_ref, m_ref, n_ref, x_ref, gain_ref, next_ref,
+               before_ref, x1_ref, u2_ref, inner_ref):
     t = pl.program_id(0)
     a = a_ref[0].astype(jnp.bfloat16)
     b = b_ref[...].astype(jnp.bfloat16)
@@ -172,10 +175,14 @@
     @pl.when(t == pl.num_programs(0) - 1)
     def _():
         v = x1_ref[...]
-        u2_ref[...] = (v * unit_rms(v) * gain_ref[...]).astype(jnp.bfloat16)
-
-
-def project_out(att, a, weights, b, m, norms, x, gain):
+        u2 = (v * unit_rms(v) * gain_ref[...]).astype(jnp.bfloat16)
+        u2_ref[...] = u2
+        following = next_ref[...].reshape(-1, u2.shape[1]).astype(jnp.bfloat16)
+        inner_ref[...] = jnp.zeros_like(inner_ref)
+        inner_ref[:, : following.shape[0]] = dot_nt(u2, following).astype(jnp.bfloat16)
+
+
+def project_out(att, a, weights, b, m, norms, x, gain, following):
     rows, width = att.shape
     tiles = width // TILE
     skip = (weights.shape[2] - width) // TILE
@@ -190,6 +197,7 @@
             pltpu.HBM((rows, width), f32),
             pltpu.HBM((rows, width), f32),
             pltpu.HBM((rows, width), jnp.bfloat16),
+            pltpu.HBM((rows, 128), jnp.bfloat16),
         ),
         grid=(tiles,),
         in_specs=[
@@ -201,14 +209,15 @@
             later(1),
             col(rows),
             full((1, width)),
+            full(following.shape),
         ],
-        out_specs=(col(rows), full((rows, width)), full((rows, width))),
+        out_specs=(col(rows), full((rows, width)), full((rows, width)), full((rows, 128))),
         compiler_params=pltpu.CompilerParams(vmem_limit_bytes=40 << 20),
         cost_estimate=pl.CostEstimate(
             flops=2 * rows * width * width, transcendentals=0, bytes_accessed=2 * width * width
         ),
         name="project_out",
-    )(att, a, weights, b, m, norms, x, gain)
+    )(att, a, weights, b, m, norms, x, gain, following)
 
 
 def out_back_kernel(in_ref, x1_ref, gain_ref, gy_ref, before_ref, att_ref, a_ref, b_ref, m_ref, n_ref, cross_ref,
@@ -227,16 +236,13 @@
         gb = (gx * (m / norm)).astype(low)
         lhs[:rows] = gb
         b = b_ref[:, o_cols].astype(low)
-        b_wide = b.astype(jnp.float32)
         gi[...] = (SCALE * dot_nt(gb, b)).astype(low)
         gm = jnp.sum(gx * before_ref[...], axis=0, keepdims=True) / norm
         gm_ref[...] = gm
         c = -gm * m / (norm * norm)
-        weighted = b_wide * c
-        lhs[rows:] = weighted.astype(low)
-        tail[...] = lax.dot_general(
-            weighted, b_wide, last_last, precision=highest, preferred_element_type=jnp.float32
-        )
+        weighted = (b.astype(jnp.float32) * c).astype(low)
+        lhs[rows:] = weighted
+        tail[...] = two_terms(dot_nt(weighted, b))
         inner = dot_nt(att_ref[...], a).astype(low)
         gb_ref[...] = SCALE * dot_tn(inner, gb) + SCALE * c * cross_ref[:, o_cols]
 
@@ -245,9 +251,7 @@
     gi_low = gi[...]
     back = dot_nt(lhs[...], w_ref[0, :, w_ref.shape[2] - width :])
     gatt_ref[...] = (back[:rows] + dot_f32(gi_low, a_tile)).astype(low)
-    spread = back[rows:] + SCALE * jnp.dot(
-        tail[...], a_tile.astype(jnp.float32), precision=highest, preferred_element_type=jnp.float32
-    )
+    spread = back[rows:] + SCALE * dot_two(tail[...], a_tile)
     ga_ref[...] = dot_tn(gi_low, att_ref[:, span]) + SCALE * spread
 
 
@@ -276,7 +280,7 @@
         scratch_shapes=[
             pltpu.VMEM((rows + 16, width), low),
             pltpu.VMEM((rows, 16), low),
-            pltpu.VMEM((16, 16), f32),
+            pltpu.VMEM((32, 16), low),
         ],
         compiler_params=pltpu.CompilerParams(vmem_limit_bytes=48 << 20),
         cost_estimate=pl.CostEstimate(
@@ -286,7 +290,7 @@
     )(in_grad, x1, gain, gy, before, att, a, b, m, norms, cross, weights)
 
 
-def qkv_back_kernel(gq_ref, gkv_ref, cos_ref, sin_ref, before_ref, u_ref, a_ref, b_ref, m_ref, n_ref, cross_ref,
+def qkv_back_kernel(gq_ref, gkv_ref, cos_ref, sin_ref, before_ref, u_ref, inner_ref, a_ref, b_ref, m_ref, n_ref, cross_ref,
                     x_ref, gain_ref, gx_ref, w0_ref, w1_ref,
                     out_ref, ga_ref, gb_ref, gm_ref, lhs0, lhs1, gi, tail):
     t = pl.program_id(0)
@@ -310,23 +314,18 @@
         lhs1[rows:] = jnp.zeros_like(lhs1[rows:])
         for p, (start, stop) in enumerate(bounds):
             g, norm, m = ups[p], n_ref[:, start:stop], m_ref[:, start:stop]
-            a = a_ref[p].astype(low)
             b = b_ref[:, start:stop].astype(low)
-            b_wide = b.astype(jnp.float32)
             gb = (g * (m / norm)).astype(low)
             gm = jnp.sum(g * before_ref[:, start:stop], axis=0, keepdims=True) / norm
             gm_ref[:, start:stop] = gm
             c = -gm * m / (norm * norm)
-            weighted = b_wide * c
+            weighted = (b.astype(jnp.float32) * c).astype(low)
             gi[:, 16 * p : 16 * p + 16] = (SCALE * dot_nt(gb, b)).astype(low)
-            tail[16 * p : 16 * p + 16] = lax.dot_general(
-                weighted, b_wide, last_last, precision=highest, preferred_element_type=jnp.float32
-            )
-            inner = dot_nt(u_ref[...], a).astype(low)
-            gb_ref[:, start:stop] = SCALE * dot_tn(inner, gb) + SCALE * c * cross_ref[:, start:stop]
+            tail[p] = two_terms(dot_nt(weighted, b))
+            gb_ref[:, start:stop] = SCALE * dot_tn(inner_ref[p], gb) + SCALE * c * cross_ref[:, start:stop]
             lhs, at = (lhs1, 0) if p == 2 else (lhs0, start)
             lhs[:rows, at : at + stop - start] = gb
-            lhs[rows + 16 * p : rows + 16 * p + 16, at : at + stop - start] = weighted.astype(low)
+            lhs[rows + 16 * p : rows + 16 * p + 16, at : at + stop - start] = weighted
 
     span = pl.ds(pl.multiple_of(t * TILE, TILE), TILE)
     back = dot_nt(lhs0[...], w0_ref[0]) + dot_nt(lhs1[...], w1_ref[0])
@@ -335,10 +334,7 @@
         a_tile = a_ref[p, :, span].astype(low)
         gi_p = gi[:, 16 * p : 16 * p + 16]
         grad_in = grad_in + dot_f32(gi_p, a_tile)
-        spread = back[rows + 16 * p : rows + 16 * p + 16] + SCALE * jnp.dot(
-            tail[16 * p : 16 * p + 16], a_tile.astype(jnp.float32), precision=highest,
-            preferred_element_type=jnp.float32,
-        )
+        spread = back[rows + 16 * p : rows + 16 * p + 16] + SCALE * dot_two(tail[p], a_tile)
         ga_ref[p] = dot_tn(gi_p, u_ref[:, span]) + SCALE * spread
     out_ref[:, span] = grad_in
 
@@ -348,7 +344,7 @@
         out_ref[...] = gx_ref[...] + rms_back(v, gain_ref[...], out_ref[...])
 
 
-def qkv_back(gq, gkv, cosine, sine, before, u, a, b, m, norms, cross, x, gain, gx, weights):
+def qkv_back(gq, gkv, cosine, sine, before, u, inner, a, b, m, norms, cross, x, gain, gx, weights):
     rows, width = gx.shape
     cols = before.shape[1]
     k_cols = (cols - width) // 2
@@ -365,7 +361,7 @@
             jax.ShapeDtypeStruct((1, cols), f32),
         ),
         grid=(tiles,),
-        in_specs=[wide, full(gkv.shape), full(cosine.shape), full(sine.shape), full((rows, cols)), wide,
+        in_specs=[wide, full(gkv.shape), full(cosine.shape), full(sine.shape), full((rows, cols)), wide, full(inner.shape),
                   full(a.shape), full(b.shape), full(m.shape), full(norms.shape), full(cross.shape),
                   wide, full((1, width)), wide,
                   pl.BlockSpec((1, TILE, width + k_cols), lambda t: (0, t, 0)),
@@ -375,14 +371,14 @@
             pltpu.VMEM((rows + 48, width + k_cols), low),
             pltpu.VMEM((rows + 48, k_cols), low),
             pltpu.VMEM((rows, 48), low),
-            pltpu.VMEM((48, 16), f32),
+            pltpu.VMEM((3, 32, 16), low),
         ],
         compiler_params=pltpu.CompilerParams(vmem_limit_bytes=48 << 20),
         cost_estimate=pl.CostEstimate(
             flops=2 * rows * width * cols, transcendentals=0, bytes_accessed=2 * width * cols
         ),
         name="qkv_back",
-    )(gq, gkv, cosine, sine, before, u, a, b, m, norms, cross, x, gain, gx, weights, weights)
+    )(gq, gkv, cosine, sine, before, u, inner, a, b, m, norms, cross, x, gain, gx, weights, weights)
 
 MESH = pl.DeviceIdType.MESH
 
@@ -442,7 +438,9 @@
     )
 
 
-def weights_kernel(n, rows, xa, xg, wd_hbm, ad_ref, bd_ref, wa, gz, near, sq_ref, gram_ref, wd, local, edge, a_in, a_sib_in, a_out, a_sib_out, z_in, z_out):
+def weights_kernel(n, rows, qo, kv, xg, wd_hbm, ad_hbm, bd_hbm, x_hbm, gain_ref, aa_hbm, ag_hbm,
+                   wa, gz, near, sq_ref, gram_ref, u_hbm, inner_ref,
+                   wd, ad_ref, bd_ref, x_ref, aa_ref, ag_ref, local, edge, a_in, a_sib_in, a_out, a_sib_out, z_in, z_out):
     nc, half = n // 2, rows // 2
     others = half - 1
     units = gz.shape[-1]
@@ -511,39 +509,76 @@
         slot = gz.at[:, 2 * p + core]
         return remote(slot, slot, z_out.at[p, core], z_in.at[p, core], r, s)
 
-    def line_send(p, src, sem, target):
-        return remote(src, a_view(p, c, both, r), sem, a_in.at[p, LINE], r, target)
-
-    own = xa.at[both, r]
-    to_left = lambda: line_send(q, own, edge.at[0], s - 2)
-    to_right = lambda: line_send(q, own, edge.at[1], s + 2)
-    pl.when(q > 0)(lambda: to_left().start())
-    pl.when(q < nc - 1)(lambda: to_right().start())
+    def line_send(p, sem, target):
+        view = a_view(p, c, both, r)
+        return remote(view, view, sem, a_in.at[p, LINE], r, target)
+
+    wide, k_cols = qo.shape[-1], kv.shape[-1]
+    blocks = [(qo, 0, 0), (kv, 0, wide), (kv, 1, 0), (qo, 1, k_cols)]
+
+    def own_blocks(part, out):
+        for source, i, start in blocks:
+            columns_of = pl.ds(start, source.shape[-1])
+            out(source.at[i, part], wa.at[i, s, part, :, columns_of])
+
+    def own_line(sem, target):
+        own_blocks(
+            r, lambda src, dst: remote(src, dst, sem, a_in.at[q, LINE], r, target).start()
+        )
+
+    pl.when(q > 0)(lambda: own_line(edge.at[0], s - 2))
+    pl.when(q < nc - 1)(lambda: own_line(edge.at[1], s + 2))
     order = [near_first(i, q, nc) for i in range(nc)]
-    sib_a = lambda: remote(xa, wa.at[:, s], edge.at[2], edge.at[3], r, sibling)
+    whole_block = wa.at[:, s]
+    sib_a = lambda: remote(whole_block, whole_block, edge.at[2], edge.at[3], r, sibling)
     sib_g = lambda: remote(
         xg.at[:, :, :, columns(sibling)], near.at[:, c], edge.at[4], edge.at[5], r, sibling
     )
-    keep_a = pltpu.make_async_copy(xa, wa.at[:, s], local.at[0])
+    keep_a = pltpu.make_async_copy(whole_block, whole_block, local.at[0])
     keep_g = pltpu.make_async_copy(xg.at[:, :, :, columns(s)], near.at[:, c], local.at[1])
-    sib_a().start()
-    keep_a.start()
-    take_d = pltpu.make_async_copy(wd_hbm, wd, local.at[2])
-    take_d.start()
-    a_low = ad_ref[...].astype(jnp.bfloat16)
-    gram_ref[...] = dot_nt(a_low, a_low)
-    mine = pl.ds(pl.multiple_of(s * wd.shape[0], wd.shape[0]), wd.shape[0])
-    b_wide = bd_ref[...].astype(jnp.bfloat16).astype(jnp.float32)
-    take_d.wait()
-    cross = dot_f32(ad_ref[:, mine].astype(jnp.bfloat16), wd[...])
-    sq_ref[...] = column_squares(wd[...]) + 2.0 * SCALE * jnp.sum(b_wide * cross, axis=0, keepdims=True)
+    all_parts = pl.ds(0, rows)
+    own_blocks(all_parts, lambda src, dst: remote(src, dst, edge.at[2], edge.at[3], r, sibling).start())
+    own_blocks(all_parts, lambda src, dst: pltpu.make_async_copy(src, dst, local.at[0]).start())
+    takes = [
+        pltpu.make_async_copy(src, dst, local.at[3 + i])
+        for i, (src, dst) in enumerate(
+            [(x_hbm, x_ref), (aa_hbm, aa_ref), (ag_hbm, ag_ref), (ad_hbm, ad_ref), (bd_hbm, bd_ref), (wd_hbm, wd)]
+        )
+    ]
+    for cp in takes:
+        cp.start()
+    for cp in takes:
+        cp.wait()
+    low = jnp.bfloat16
+    v = x_ref[...].astype(jnp.float32)
+    u = (v * unit_rms(v) * gain_ref[...]).astype(low)
+    x_ref[...] = u
+    keep_u = pltpu.make_async_copy(x_ref, u_hbm, local.at[2])
+    keep_u.start()
+    for g in range(4):
+        a = aa_ref[g].astype(low)
+        gram_ref[g] = two_terms(dot_nt(a, a))
+        if g < 3:
+            inner_ref[g] = dot_nt(u, a).astype(low)
+    for g in range(2):
+        a = ag_ref[g].astype(low)
+        gram_ref[4 + g] = two_terms(dot_nt(a, a))
+
+    def down_squares():
+        a = ad_ref[...].astype(low)
+        gram_ref[6] = two_terms(dot_nt(a, a))
+        mine = pl.ds(pl.multiple_of(s * wd.shape[0], wd.shape[0]), wd.shape[0])
+        cross = dot_f32(ad_ref[:, mine].astype(low), wd[...])
+        b_wide = bd_ref[...].astype(low).astype(jnp.float32)
+        sq_ref[...] = column_squares(wd[...]) + 2.0 * SCALE * jnp.sum(b_wide * cross, axis=0, keepdims=True)
+
     for p in order[1:]:
         a_arrival(p, LINE).wait_recv()
         pl.when((p < q) & (q < nc - 1))(
-            lambda p=p: line_send(p, a_view(p, c, both, r), a_out.at[p, LINE], s + 2).start()
+            lambda p=p: line_send(p, a_out.at[p, LINE], s + 2).start()
         )
         pl.when((p > q) & (q > 0))(
-            lambda p=p: line_send(p, a_view(p, c, both, r), a_out.at[p, LINE], s - 2).start()
+            lambda p=p: line_send(p, a_out.at[p, LINE], s - 2).start()
         )
         a_send(p, both, r, FROM_B, b_row).start()
         for k in range(1, half):
@@ -554,6 +589,8 @@
             z_send(p, core).start()
     sib_g().start()
     keep_g.start()
+    down_squares()
+    keep_u.wait()
     for p in order[1:]:
         a_arrival(p, FROM_B).wait_recv()
         for k in range(1, half):
@@ -572,11 +609,11 @@
     keep_g.wait()
     sib_a().wait()
     sib_g().wait()
-    pl.when(q > 0)(lambda: to_left().wait_send())
-    pl.when(q < nc - 1)(lambda: to_right().wait_send())
+    pl.when(q > 0)(lambda: line_send(q, edge.at[0], s).wait_send())
+    pl.when(q < nc - 1)(lambda: line_send(q, edge.at[1], s).wait_send())
     for p in order[1:]:
         pl.when(((p < q) & (q < nc - 1)) | ((p > q) & (q > 0)))(
-            lambda p=p: line_send(p, a_view(p, c, both, r), a_out.at[p, LINE], s).wait_send()
+            lambda p=p: line_send(p, a_out.at[p, LINE], s).wait_send()
         )
         for kind in range(kinds):
             a_to_sibling(p, kind, c).wait_send()
@@ -591,30 +628,37 @@
             z_arrival(p, core).wait_recv()
 
 
-def gather_weights(n, rows, xa, xg, wd, ad, bd, collective_id):
+def gather_weights(n, rows, qo, kv, xg, wd, ad, bd, x, gain, aa, ag, collective_id):
     nc = n // 2
-    block = xa.shape[1]
+    _, block, width = qo.shape
     part = block // rows
-    xa = xa.reshape(2, rows, part, xa.shape[2])
+    cols = width + kv.shape[2]
+    qo = qo.reshape(2, rows, part, width)
+    kv = kv.reshape(2, rows, part, kv.shape[2])
     xg = xg.reshape(2, rows, part, xg.shape[2])
     units = xg.shape[3] // n
     kinds = 2 + 3 * (rows // 2 - 1)
     dma = pltpu.SemaphoreType.DMA
     anywhere = pl.BlockSpec(memory_space=pl.ANY)
-    shape = jax.ShapeDtypeStruct
     vmem = pl.BlockSpec(memory_space=pltpu.VMEM)
-    wa, gz, near, sq, gram = pl.pallas_call(
+    low = qo.dtype
+    wa, gz, near, sq, grams, u, inner = pl.pallas_call(
         functools.partial(weights_kernel, n, rows),
         out_shape=(
-            shape((2, n, rows, part, xa.shape[3]), xa.dtype),
-            shape((2, n, part, units), xg.dtype),
-            shape((2, 2, rows, part, units), xg.dtype),
-            shape((1, wd.shape[1]), jnp.float32),
-            shape((16, 16), jnp.float32),
-        ),
-        in_specs=[anywhere] * 3 + [vmem] * 2,
-        out_specs=(anywhere,) * 3 + (vmem,) * 2,
-        scratch_shapes=[pltpu.VMEM(wd.shape, wd.dtype), dma((3,)), dma((6,))] + [dma((nc, kinds))] * 4 + [dma((nc, 2))] * 2,
+            pltpu.HBM((2, n, rows, part, cols), low),
+            pltpu.HBM((2, n, part, units), low),
+            pltpu.HBM((2, 2, rows, part, units), low),
+            jax.ShapeDtypeStruct((1, width), jnp.float32),
+            jax.ShapeDtypeStruct((7, 32, 16), low),
+            pltpu.HBM(x.shape, low),
+            jax.ShapeDtypeStruct((3, x.shape[0], 16), low),
+        ),
+        in_specs=[anywhere] * 7 + [vmem] + [anywhere] * 2,
+        out_specs=(anywhere,) * 3 + (vmem,) * 2 + (anywhere, vmem),
+        scratch_shapes=[pltpu.VMEM(v.shape, v.dtype) for v in (wd, ad, bd, x, aa, ag)]
+        + [dma((9,)), dma((6,))]
+        + [dma((nc, kinds))] * 4
+        + [dma((nc, 2))] * 2,
         compiler_params=pltpu.CompilerParams(
             collective_id=collective_id, has_side_effects=True, vmem_limit_bytes=32 << 20
         ),
@@ -622,8 +666,8 @@
             flops=0, transcendentals=0, bytes_accessed=250 * 1024 * 1024
         ),
         name="gather_weights",
-    )(xa, xg, wd, ad, bd)
-    return wa.reshape(2, n * block, -1), gz, near, sq, gram
+    )(qo, kv, xg, wd, ad, bd, x, gain, aa, ag)
+    return wa.reshape(2, n * block, cols), gz, near, sq, grams, u, inner
 
 
 def gather_kernel(n, rows, count, shared, *refs):
@@ -977,9 +1021,9 @@
     return jnp.where(i <= 2 * short, near, far)
 
 
-def ffn_kernel(n, rows, pieces, u_hbm, gy0_hbm, gy1_hbm, wd_hbm, a_ref, b_ref, m_ref, ad_ref, bd_ref, md_ref, sq_ref, gram_ref,
-               in_ref, down_hbm, ga_ref, gb_ref, gm_ref, norm_ref, gad_ref, gbd_ref, gmd_ref, nd_ref,
-               w_parts, wd, u, gy, down, own, theirs, sib, from_left, from_right, ratio, cross, gm_all,
+def ffn_kernel(n, rows, pieces, u_hbm, inner_hbm, gy0_hbm, gy1_hbm, wd_hbm, a_ref, b_ref, m_ref, ad_ref, bd_ref, md_ref, sq_ref, gram_ref,
+               in_ref, down0_hbm, down1_hbm, ga_ref, gb_ref, gm_ref, norm_ref, gad_ref, gbd_ref, gmd_ref, nd_ref,
+               w_parts, wd, u, side, gy, down, own, theirs, sib, from_left, from_right, ratio, cross, gm_all,
                w_sem, load_sem, down_sem, small_out, small_in, to_sib, sib_in, to_right, right_in, to_left, left_in):
     nc = n // 2
     f32, low = jnp.float32, jnp.bfloat16
@@ -1004,6 +1048,7 @@
             pltpu.make_async_copy(
                 gy1_hbm.at[pair], gy.at[slot, :, tokens // 2 :], load_sem.at[2, slot]
             ),
+            pltpu.make_async_copy(inner_hbm.at[pair], side.at[slot], load_sem.at[3, slot]),
         )
 
     for cp in loads(0):
@@ -1033,10 +1078,14 @@
             device_id={"seq": target}, device_id_type=MESH,
         )
 
-    def down_out(p):
-        return pltpu.make_async_copy(
-            down.at[lax.rem(p, 2)], down_hbm.at[pl.ds(2 * p, 2)], down_sem.at[lax.rem(p, 2)]
-        )
+    def down_out(slot, p):
+        half = tokens // 2
+        return [
+            pltpu.make_async_copy(
+                down.at[slot, :, half * k : half * (k + 1)], out.at[pl.ds(2 * p, 2)], down_sem.at[k, slot]
+            )
+            for k, out in enumerate((down0_hbm, down1_hbm))
+        ]
 
     def pass_on(p):
         to_sibling(p).wait_recv()
@@ -1082,15 +1131,16 @@
     m = [m_ref[g : g + 1, mine] for g in range(2)]
     for cp in weights:
         cp.wait()
+    a_both = jnp.concatenate(a, axis=0)
     for g in range(2):
-        norm, cr = column_norms(weight(g), a[g], b[g].astype(f32), dot_f32(a[g], weight(g)))
+        norm, cr = column_norms(weight(g), gram_ref[4 + g], b[g], dot_f32(a[g], weight(g)))
         norm_ref[g] = norm
         cross[g] = cr
         ratio[g] = m[g] / norm
     for ref in (ga_ref, gb_ref, gm_ref, gad_ref, gbd_ref, gmd_ref):
         ref[...] = jnp.zeros_like(ref)
     bd_wide = bd.astype(f32)
-    gram_b = jnp.dot(gram_ref[...], bd_wide, precision=highest, preferred_element_type=f32)
+    gram_b = dot_two(gram_ref[6], bd)
     squares = jnp.sum(sq_ref[...], axis=0) + SCALE * SCALE * jnp.sum(
         bd_wide * gram_b, axis=0, keepdims=True
     )
@@ -1114,7 +1164,8 @@
         gb_d = (upstream * ratio_d).astype(low)
         gi_d = (SCALE * dot_nt(gb_d, bd)).astype(low)
         gh = dot_nt(gb_d, wd[...]) + dot_f32(gi_d, ad)
-        inner = [dot_nt(x, a[g]).astype(low) for g in range(2)]
+        sides = side[slot].reshape(2 * tokens, -1)
+        inner = [sides[:, 16 * g : 16 * g + 16] for g in range(2)]
         before = [dot_f32(x, weight(g)) + SCALE * dot_f32(inner[g], b[g]) for g in range(2)]
         gate = before[0] * ratio[0]
         lift = before[1] * ratio[1]
@@ -1123,8 +1174,8 @@
         hidden = (silu * lift).astype(low)
         grads = [gh * lift * sig * (1.0 + gate * (1.0 - sig)), gh * silu]
         gb = [(grads[g] * ratio[g]).astype(low) for g in range(2)]
-        gi = [(SCALE * dot_nt(gb[g], b[g])).astype(low) for g in range(2)]
-        back = dot_nt(gb[0], weight(0)) + dot_nt(gb[1], weight(1)) + dot_f32(gi[0], a[0]) + dot_f32(gi[1], a[1])
+        gi = jnp.concatenate([(SCALE * dot_nt(gb[g], b[g])).astype(low) for g in range(2)], axis=1)
+        back = dot_nt(gb[0], weight(0)) + dot_nt(gb[1], weight(1)) + dot_f32(gi, a_both)
         back = back.astype(low).reshape(2, tokens, -1)
         first, second = back[0], back[1]
 
@@ -1144,16 +1195,18 @@
 
         @pl.when(i >= 2)
         def _():
-            down_out(slot).wait()
+            for cp in down_out(slot, p):
+                cp.wait()
 
         down[slot] = part.astype(low).reshape(2, tokens, -1)
-        pltpu.make_async_copy(down.at[slot], down_hbm.at[pl.ds(2 * p, 2)], down_sem.at[slot]).start()
+        for cp in down_out(slot, p):
+            cp.start()
         gmd_ref[...] += jnp.sum(upstream * part, axis=0, keepdims=True)
         gad_ref[...] += dot_tn(gi_d, hidden)
         gbd_ref[...] += SCALE * dot_tn(inner_d, gb_d)
+        ga_ref[...] += dot_tn(gi, x).reshape(ga_ref.shape)
         for g in range(2):
             gm_ref[g] += jnp.sum(grads[g] * before[g], axis=0, keepdims=True)
-            ga_ref[g] += dot_tn(gi[g], x)
             gb_ref[g] += SCALE * dot_tn(inner[g], gb[g])
 
         pl.when(starts_flow(p))(lambda: pass_on(p))
@@ -1182,15 +1235,9 @@
         gm = gm_ref[g] / norm
         gm_ref[g] = gm
         col = -gm * m[g] / (norm * norm)
-        b_wide = b[g].astype(f32)
-        weighted = b_wide * col
-        tail = lax.dot_general(
-            weighted, b_wide, last_last, precision=highest, preferred_element_type=f32
-        )
-        spread = dot_nt(weighted.astype(low), weight(g)) + SCALE * jnp.dot(
-            tail, a[g].astype(f32), precision=highest, preferred_element_type=f32
-        )
-        ga_ref[g] += SCALE * spread
+        weighted = (b[g].astype(f32) * col).astype(low)
+        tail = two_terms(dot_nt(weighted, b[g]))
+        ga_ref[g] += SCALE * (dot_nt(weighted, weight(g)) + SCALE * dot_two(tail, a[g]))
         gb_ref[g] += SCALE * col * cross[g]
 
     gm_line = gmd_ref[...]
@@ -1199,14 +1246,9 @@
         small(t, slot).wait_recv()
         gm_line = gm_line + gm_all[slot]
     col = -gm_line * md_ref[...] / (nd_ref[...] * nd_ref[...])
-    weighted = bd_wide * col
-    tail = lax.dot_general(
-        weighted, bd_wide, last_last, precision=highest, preferred_element_type=f32
-    )
-    gad_ref[...] += SCALE * (
-        dot_nt(weighted.astype(low), wd[...])
-        + SCALE * jnp.dot(tail, ad.astype(f32), precision=highest, preferred_element_type=f32)
-    )
+    weighted = (bd_wide * col).astype(low)
+    tail = two_terms(dot_nt(weighted, bd))
+    gad_ref[...] += SCALE * (dot_nt(weighted, wd[...]) + SCALE * dot_two(tail, ad))
     own_gram = jnp.where(s == 0, SCALE, 0.0) * gram_b
     gbd_ref[...] += SCALE * col * (dot_f32(ad, wd[...]) + own_gram)
 
@@ -1224,7 +1266,8 @@
         in_ref[...] += from_right[q].astype(f32)
 
     for i in range(min(2, nc)):
-        pltpu.make_async_copy(down.at[i], down_hbm.at[pl.ds(0, 2)], down_sem.at[i]).wait()
+        for cp in down_out(i, 0):
+            cp.wait()
     for t in range(1, n):
         small(t, s).wait_send()
     for p in range(nc):
@@ -1259,7 +1302,7 @@
     return out
 
 
-def feed_forward(n, rows, pieces, u, gy0, gy1, wd, a, b, m, ad, bd, md, sq, gram, collective_id):
+def feed_forward(n, rows, pieces, u, inner, gy0, gy1, wd, a, b, m, ad, bd, md, sq, gram, collective_id):
     nc = n // 2
     _, tokens, width = u.shape
     units = wd.shape[0]
@@ -1281,7 +1324,8 @@
         kernel,
         out_shape=(
             shape((tokens, width), f32),
-            shape((n, tokens, width), low),
+            pltpu.HBM((n, tokens // 2, width), low),
+            pltpu.HBM((n, tokens // 2, width), low),
             shape((2, 16, width), f32),
             shape((2, 16, units), f32),
             shape((2, 1, units), f32),
@@ -1291,17 +1335,20 @@
             shape((1, width), f32),
             shape((1, width), f32),
         ),
-        in_specs=[hbm] * (count + 4) + [vmem] * 8,
-        out_specs=(vmem, hbm) + (vmem,) * 8,
+        in_specs=[hbm] * (count + 5) + [vmem] * 8,
+        out_specs=(vmem, hbm, hbm) + (vmem,) * 8,
         scratch_shapes=[
             pltpu.VMEM((2, n, rows, part, units), low),
             pltpu.VMEM((units, width), low),
-            pair, pair, pair,
+            pair,
+            pltpu.VMEM((2, 2, tokens, 128), low),
+            pair,
+            pair,
             line, line, line, line, line,
             pltpu.VMEM((2, 1, units), f32),
             pltpu.VMEM((2, 16, units), f32),
             pltpu.VMEM((n, 1, width), f32),
-            dma((copies,)), dma((3, 2)), dma((2,)), dma((n,)), dma((n,)),
+            dma((copies,)), dma((4, 2)), dma((2, 2)), dma((n,)), dma((n,)),
         ] + [dma((nc,))] * 6,
         compiler_params=pltpu.CompilerParams(
             collective_id=collective_id, has_side_effects=True, vmem_limit_bytes=60 << 20
@@ -1311,7 +1358,7 @@
             bytes_accessed=32 << 20,
         ),
         name="feed_forward",
-    )(*pieces, u, gy0, gy1, wd, a, b, m, ad, bd, md, sq, gram)
+    )(*pieces, u, inner, gy0, gy1, wd, a, b, m, ad, bd, md, sq, gram)
 
 def reduce_kernel(n, rows, ga_qkv, ga_o, gb_qkv, gb_o, ga_gu, gb_d, gm_qkv, gm_o, gm_d, gb_gu, gm_gu, n_gu, ga_d,
                   whole, units_all, part, from_sib, mid, from_rows, from_line, line_out, units, units_in,
@@ -1506,7 +1553,7 @@
     )(*full, *own_units)
 
 
-def finish_kernel(n, rows, whole, units_all, x1, before, m_attn, n_attn, m_d, n_d, m_gu,
+def finish_kernel(n, rows, whole, units_all, x1, before_0, before_1, m_attn, n_attn, m_d, n_d, m_gu,
                   o_out, o_ga, o_gb_qo, o_gb_kv, o_gm_q, o_gm_kv, o_gm_o, o_ga_gu, o_gb_gu, o_gm_gu, o_ga_d, o_gb_d,
                   o_gm_d, o_stats, n_gu):
     f32 = jnp.float32
@@ -1516,7 +1563,10 @@
     cols = width // (2 * rows)
     size = units_all.shape[4]
     per = units_all.shape[3] // 8
-    o_out[...] = (x1[...] + before[...].astype(f32) * (m_d[...] / n_d[...])).astype(o_out.dtype)
+    half = x1.shape[0] // 2
+    for k, before in enumerate((before_0, before_1)):
+        own = slice(half * k, half * (k + 1))
+        o_out[own] = (x1[own] + before[...].astype(f32) * (m_d[...] / n_d[...])).astype(o_out.dtype)
     for j in range(2 * rows):
         block = jnp.concatenate([whole[j // 2, j % 2, p].astype(f32) for p in range(nc)], axis=0)
         at = slice(cols * j, cols * (j + 1))
@@ -1565,7 +1615,7 @@
     o_stats[...] = stats
 
 
-def finish(n, rows, sums, x1, before, m_attn, n_attn, m_d, n_d, m_gu):
+def finish(n, rows, sums, x1, before_0, before_1, m_attn, n_attn, m_d, n_d, m_gu):
     tokens, width = x1.shape
     kv = (m_attn.shape[1] - 2 * width) // 2
     units = m_gu.shape[1]
@@ -1578,12 +1628,12 @@
             shape(width), shape(2, kv), shape(width), shape(2, 16, width), shape(2, 16, units), shape(2, units),
             shape(16, units), shape(16, width), shape(width), shape(7, 2),
         ),
-        in_specs=[vmem] * 2 + [pl.BlockSpec()] * 7,
+        in_specs=[vmem] * 2 + [pl.BlockSpec()] * 8,
         scratch_shapes=[pltpu.VMEM((2, units), jnp.float32)],
         compiler_params=pltpu.CompilerParams(vmem_limit_bytes=40 << 20),
         cost_estimate=pl.CostEstimate(flops=0, transcendentals=0, bytes_accessed=8 << 20),
         name="finish",
-    )(*sums, x1, before, m_attn, n_attn, m_d, n_d, m_gu)
+    )(*sums, x1, before_0, before_1, m_attn, n_attn, m_d, n_d, m_gu)
 
 def local(
     layer_input,
@@ -1616,15 +1666,12 @@
     seq_index = lax.axis_index("seq")
     f32 = jnp.float32
 
-    packed = jnp.stack(
-        [
-            jnp.concatenate([query_output_frozen[0], key_value_frozen[0]], axis=1),
-            jnp.concatenate([key_value_frozen[1], query_output_frozen[1]], axis=1),
-        ]
-    )
-    weights, gu_own, gu_near, sq_d, gram_d = gather_weights(
-        seq_size, rows_size, packed, gate_up_frozen, down_frozen_weight, down_adapter_a,
-        down_adapter_b, 1,
+    x = layer_input.reshape(token_count, model_width)
+    gain_attn, gain_ffn = norm_gain_vectors[:1], norm_gain_vectors[1:]
+    weights, gu_own, gu_near, sq_d, grams, u1, inner_1 = gather_weights(
+        seq_size, rows_size, query_output_frozen, key_value_frozen, gate_up_frozen,
+        down_frozen_weight, down_adapter_a, down_adapter_b, x, gain_attn, attention_adapter_a,
+        gate_up_adapter_a, 1,
     )
     shares_1, shares_2 = share_plan(rows_size)
     grad_out_rows = output_gradient.reshape(token_count, model_width)
@@ -1654,10 +1701,8 @@
     sine = jnp.tile(jnp.sin(angles), (pair_rows, 4))
     valid_len = prompt_length_list[0] + response_length_list
 
-    x = layer_input.reshape(token_count, model_width)
-    gain_attn, gain_ffn = norm_gain_vectors[:1], norm_gain_vectors[1:]
-    u1, before_qkv, q, kv, n_attn, cross_attn = project_qkv(
-        x, gain_attn, attention_adapter_a, weights, b_attn, m_attn, cosine, sine
+    before_qkv, q, kv, n_attn, cross_attn = project_qkv(
+        u1, inner_1, grams, attention_adapter_a, weights, b_attn, m_attn, cosine, sine
     )
     (kv_all, sq_all), gu_1 = gather_seq(
         seq_size, rows_size, [kv, sq_d], 2, (gu_own,), shares_1
@@ -1668,22 +1713,20 @@
     q = q.reshape(pair_rows, span_len, model_width)
     att, shares = attend(q, kv_all, valid_len)
     att = att.reshape(token_count, model_width)
-    before_o, x1, u2 = project_out(
-        att, attention_adapter_a, weights, b_attn, m_attn, n_attn, x, gain_ffn
+    before_o, x1, u2, inner_2 = project_out(
+        att, attention_adapter_a, weights, b_attn, m_attn, n_attn, x, gain_ffn, gate_up_adapter_a
     )
 
-    (u2_all,), gu_2 = gather_seq(
-        seq_size, rows_size, [u2], 3, (gu_own, *gu_1), shares_2
+    (u2_all, inner_all), gu_2 = gather_seq(
+        seq_size, rows_size, [u2, inner_2], 3, (gu_own, *gu_1), shares_2
     )
-    in_grad, down_parts, ga_gu, gb_gu, gm_gu, n_gu, ga_d, gb_d, gm_d, n_d = feed_forward(
-        seq_size, rows_size, (gu_own, gu_near, *gu_1, *gu_2), u2_all, gy_0, gy_1,
+    in_grad, down_0, down_1, ga_gu, gb_gu, gm_gu, n_gu, ga_d, gb_d, gm_d, n_d = feed_forward(
+        seq_size, rows_size, (gu_own, gu_near, *gu_1, *gu_2), u2_all, inner_all, gy_0, gy_1,
         down_frozen_weight, gate_up_adapter_a, gate_up_adapter_b, gate_up_magnitude, down_adapter_a,
-        down_adapter_b, m_d, sq_all, gram_d, 4,
+        down_adapter_b, m_d, sq_all, grams, 4,
     )
-    before_d = lax.psum_scatter(
-        down_parts.reshape(seq_size * token_count, model_width), "seq", scatter_dimension=0,
-        tiled=True,
-    )
+    flat = lambda v: v.reshape(-1, model_width)
+    before_0 = lax.psum_scatter(flat(down_0), "seq", scatter_dimension=0, tiled=True)
 
     gx1, grad_att, ga_o, gb_o, gm_o = out_back(
         in_grad, x1, gain_ffn, grad_out_rows, before_o, att, attention_adapter_a, b_attn, m_attn,
@@ -1691,8 +1734,10 @@
     )
     gq, gkv = attend_back(q, kv_all, shares, grad_att.reshape(q.shape))
     gkv = scatter_seq(seq_size, gkv.reshape(seq_size, token_count, 2 * kv_width), 5)
+    gkv, down_1 = lax.optimization_barrier((gkv, down_1))
+    before_1 = lax.psum_scatter(flat(down_1), "seq", scatter_dimension=0, tiled=True)
     grad_inputs, ga_qkv, gb_qkv, gm_qkv = qkv_back(
-        gq.reshape(token_count, model_width), gkv, cosine, sine, before_qkv, u1,
+        gq.reshape(token_count, model_width), gkv, cosine, sine, before_qkv, u1, inner_1,
         attention_adapter_a, b_attn, m_attn, n_attn, cross_attn, x, gain_attn, gx1, weights,
     )
 
@@ -1703,7 +1748,7 @@
         6,
     )
     layer_result, *summed, stats = finish(
-        seq_size, rows_size, sums, x1, before_d, m_attn, n_attn, m_d, n_d, gate_up_magnitude
+        seq_size, rows_size, sums, x1, before_0, before_1, m_attn, n_attn, m_d, n_d, gate_up_magnitude
     )
     shape = (pair_rows, span_len, model_width)
     return (layer_result.reshape(shape), grad_inputs.reshape(shape), *summed, stats)

time: 441 us -> 464 us (1.052)
  waiting for transfers between devices: 0.11 us -> 25.9 us
  Pallas kernels: 397 us -> 385 us
  local copies, waits for them, and re-layouts: 27.5 us -> 36.1 us
    reduce_scatter x1 -> x2, waiting for transfers between devices: 0.02 us -> 25.3 us  [the longest x1 25.3 us: local(): lax.psum_scatter(flat(down_0), 'seq', scatter_dimension=0, tiled=True)]
    unnamed x103 -> x123, local copies, waits for them, and re-layouts: 22.2 us -> 32.9 us
    pallas_call x1, Pallas kernels: 42.3 us -> 31.7 us  [scatter_seq(): pl.pallas_call(functools.partial(scatter_kernel, n), out_shape=jax.ShapeD...]
  transfers between devices with their start and end apart: 3 -> 4, of which waited for: 0 -> 1; matrix products, arithmetic and copies ran while one was open for 0% -> 0% of each run, Pallas kernels for 49% -> 34%
where the time goes in v6:
time: 464 us; the launch traced here: 462 us
  Pallas kernels  385 us (83%)
  local copies, waits for them, and re-layouts  36.1 us (8%)
  waiting for transfers between devices  25.9 us (6%)
  between operations  15 us (3%)
    pallas_call x1, Pallas kernels, gather_weights(): pl.pallas_call(functools.partial(weights_kernel, n, rows), out_shape=(plt...  102 us
    pallas_call x2, Pallas kernels, gather_seq(): pl.pallas_call(functools.partial(gather_kernel, n, rows, count, (range(le...  79.5 us
    pallas_call x1, Pallas kernels, feed_forward(): pl.pallas_call(kernel, out_shape=(shape((tokens, width), f32), pltpu.HBM(...  74.5 us
    unnamed x123, local copies, waits for them, and re-layouts  32.9 us
    pallas_call x1, Pallas kernels, scatter_seq(): pl.pallas_call(functools.partial(scatter_kernel, n), out_shape=jax.ShapeD...  31.7 us
    pallas_call x1, Pallas kernels, sum_gradients(): pl.pallas_call(functools.partial(reduce_kernel, n, rows), out_shape=(jax....  31 us
    reduce_scatter x1, waiting for transfers between devices, local(): lax.psum_scatter(flat(down_0), 'seq', scatter_dimension=0, tiled=True)  25.3 us
    pallas_call x1, Pallas kernels, project_qkv(): pl.pallas_call(functools.partial(project_kernel, (q_tiles, last)), out_sh...  14.7 us
  transfers between devices with their start and end apart: 4, of which 1 were waited for; matrix products, arithmetic and copies ran while one was open for 0% of the time, Pallas kernels for 34%

profile of v6, /device:TPU:0, one launch (start us, length us, event | category | flops | bytes accessed | tf_op | source)
XLA Modules:
  0.0 462.3 jit_solution(9231563584010683900)
XLA Ops:
  7.2 0.8 fusion
  8.0 1.9 slice_bitcast_fusion
  9.9 1.0 copy-done
  11.0 3.4 copy-done.4
  14.3 1.0 copy-done.5
  15.4 2.2 copy-done.8
  17.6 1.6 copy-done.14
  19.2 0.9 copy-done.17
  20.1 1.0 copy-done.27
  21.2 1.0 copy-done.28
  22.2 0.9 copy-done.37
  23.1 102.5 %gather_weights.1 = (bf16[2,8,4,64,2560]{4,3,2,1,0:T(8,128)(2,1)}, bf16[2,8,64,1024]{3,2,1,0:T(8,128)(2,1)}, bf16[2,2,4,64,1024]{4,3,2,1,0:T(8,128)(2,1)}, f32[1...) custom-call(bf16[2,4,64,2048]{3,2,1,0:T(8,128)(2,1)S(1)} %bitcast.52, ...), custom_call_target="tpu_custom_call" | custom-call | bytes 262144000 | tf_op jit(solution)/shard_map/gather_weights/pallas_call | solution.py:645
  125.6 0.6 copy-done.52
  126.3 0.1 multiply_sine_fusion
  126.5 0.1 tile.21
  126.8 0.1 tile.9
  127.3 0.2 copy-done.9
  127.5 14.7 %project_qkv.1 = (f32[128,3072]{1,0:T(8,128)}, bf16[128,2048]{1,0:T(8,128)(2,1)}, bf16[128,1024]{1,0:T(8,128)(2,1)}, f32[1,5120]{1,0:T(1,128)}, f32[16,5120]{1,0:T(8,128)}) custom-call(bf16[128,2048]{1,0:T(8,128)(2,1)S(1)} %copy-done.9, bf16[3,128,16]{2,1,0:T(8,128)(2,1)S(1)} %get-tuple-element.88.inner_ref, ...), custom_call_target="tpu_custom_call" | custom-call | flops 2684354560 | bytes 20971520 | tf_op jit(solution)/shard_map/project_qkv/pallas_call | solution.py:127
  142.2 33.3 %gather_seq.2 = (bf16[8,128,1024]{2,1,0:T(8,128)(2,1)}, f32[8,1,2048]{2,1,0:T(1,128)}, bf16[8,64,1024]{2,1,0:T(8,128)(2,1)}, bf16[8,64,1024]{2,1,0:T(8,128)(2,1)}) custom-call(bf16[128,1024]{1,0:T(8,128)(2,1)} %get-tuple-element.93.refs_0_, f32[1,2048]{1,0:T(1,128)} %copy-done.52, bf16[2,8,64,1024]{3,2,1,0:T(8,128)(2,1)} %get-tuple-element.95.refs_2_.refs_0_), custom_call_target="tpu_custom_call" | custom-call | bytes 43253760 | tf_op jit(solution)/shard_map/gather_seq/pallas_call | solution.py:748
  176.3 1.6 copy-done.2
  177.9 10.4 %attend.1 = (bf16[2,64,2048]{2,1,0:T(8,128)(2,1)}, bf16[2,4,512,512]{3,2,1,0:T(8,128)(2,1)}) custom-call(s32[2]{0:T(128)S(1)} %broadcast_add_fusion.valid_ref, bf16[2,64,2048]{2,1,0:T(8,128)(2,1)S(1)} %bitcast.60, bf16[8,2,64,1024]{3,2,1,0:T(8,128)(2,1)S(1)} %bitcast.40, bf16[8,2,64,1024]{3,2,1,0:T(8,128)(2,1)S(1)} %bitcast.41), custom_call_target="tpu_custom_call" | custom-call | flops 1073741824 | bytes 8388608 | tf_op jit(solution)/shard_map/attend/pallas_call | solution.py:936
  188.3 1.0 copy-done.10
  189.3 7.4 %project_out.1 = (f32[128,2048]{1,0:T(8,128)}, f32[128,2048]{1,0:T(8,128)}, bf16[128,2048]{1,0:T(8,128)(2,1)}, bf16[128,128]{1,0:T(8,128)(2,1)}) custom-call(bf16[128,2048]{1,0:T(8,128)(2,1)S(1)} %bitcast.48, f32[4,16,2048]{2,1,0:T(8,128)S(1)} %copy-done.1, bf16[2,2048,2560]{2,1,0:T(8,128)(2,1)} %bitcast.66, f32[16,5120]{1,0:T(8,128)S(1)} %pad_maximum_fusion.b_ref, ...), custom_call_target="tpu_custom_call" | custom-call | flops 1073741824 | bytes 8388608 | tf_op jit(solution)/shard_map/project_out/pallas_call | solution.py:194
  196.7 46.2 %gather_seq.3 = (bf16[8,128,2048]{2,1,0:T(8,128)(2,1)}, bf16[8,128,128]{2,1,0:T(8,128)(2,1)}, bf16[8,64,1024]{2,1,0:T(8,128)(2,1)}, bf16[8,64,1024]{2,1,0:T(8,12...) custom-call(bf16[128,2048]{1,0:T(8,128)(2,1)} %get-tuple-element.104.refs_0_, ...), custom_call_target="tpu_custom_call" | custom-call | bytes 89128960 | tf_op jit(solution)/shard_map/gather_seq/pallas_call | solution.py:748
  243.0 74.5 %feed_forward.1 = (f32[128,2048]{1,0:T(8,128)}, bf16[8,64,2048]{2,1,0:T(8,128)(2,1)}, bf16[8,64,2048]{2,1,0:T(8,128)(2,1)}, f32[2,16,2048]{2,1,0:T(8,128)}, f32[...) custom-call(bf16[2,8,64,1024]{3,2,1,0:T(8,128)(2,1)} %get-tuple-elem, ...), custom_call_target="tpu_custom_call" | custom-call | flops 25769803776 | bytes 33554432 | tf_op jit(solution)/shard_map/feed_forward/pallas_call | solution.py:1323
  317.6 1.0 copy-done.15
  318.6 1.2 copy-done.19
  319.8 1.2 copy-done.21
  321.0 8.5 %out_back.1 = (f32[128,2048]{1,0:T(8,128)}, bf16[128,2048]{1,0:T(8,128)(2,1)}, f32[16,2048]{1,0:T(8,128)S(1)}, f32[16,2048]{1,0:T(8,128)S(1)}, f32[1,2048]{1,0:T(1,128)S(1)}) custom-call(f32[128,2048]{1,0:T(8,128)S(1)} %copy-done.21, f32[128,2048]{1,0:T(8,128)S(1)} %copy-done.7, f32[1,2048]{1,0:T(1,128)S(1)} %get-tuple-element.195.gain_ref, ...), custom_call_target="tpu_custom_call" | custom-call | flops 1073741824 | bytes 8388608 | tf_op jit(solution)/shard_map/out_back/pallas_call | solution.py:265
  329.6 1.1 copy-done.54
  330.7 10.4 %attend_back.1 = (bf16[2,64,2048]{2,1,0:T(8,128)(2,1)}, bf16[8,2,64,1024]{3,2,1,0:T(8,128)(2,1)}) custom-call(bf16[2,64,2048]{2,1,0:T(8,128)(2,1)S(1)} %bitcast.61, bf16[8,2,64,1024]{3,2,1,0:T(8,128)(2,1)S(1)} %bitcast.42, bf16[8,2,64,1024]{3,2,1,0:T(8,128)(2,1)S(1)} %bitcast.43, bf16[2,4,512,512]{3,2,1,0:T(8,128)(2,1)S(1)} %copy-done.53, ...), custom_call_target="tpu_custom_call" | custom-call | flops 2684354560 | bytes 8388608 | tf_op jit(solution)/shard_map/attend_back/pallas_call | solution.py:991
  341.1 1.6 copy-done.12
  342.7 31.7 %scatter_seq.1.gkv_ref = f32[128,1024]{1,0:T(8,128)S(1)} custom-call(bf16[8,128,1024]{2,1,0:T(8,128)(2,1)S(1)} %bitcast.50), custom_call_target="tpu_custom_call" | custom-call | bytes 41943040 | tf_op jit(solution)/shard_map/scatter_seq/pallas_call | solution.py:865
  374.5 0.5 reduce-scatter.3.cloned.1.call-update
  375.1 1.0 copy-done.16
  376.0 1.2 copy-done.20
  377.3 0.8 copy-done.23
  378.1 0.8 copy-done.25
  378.9 1.1 copy-done.26
  380.0 0.9 copy-done.32
  381.0 12.2 %qkv_back.1 = (f32[128,2048]{1,0:T(8,128)}, f32[3,16,2048]{2,1,0:T(8,128)S(1)}, f32[16,3072]{1,0:T(8,128)S(1)}, f32[1,3072]{1,0:T(1,128)S(1)}) custom-call(bf16[128,2048]{1,0:T(8,128)(2,1)S(1)} %bitcast.58, f32[128,1024]{1,0:T(8,128)S(1)} %scatter_seq.1.gkv_ref, f32[128,128]{1,0:T(8,128)S(1)} %copy-done.25, f32[128,128]{1,0:T(8,128)S(1)} %copy-done.23, ...), custom_call_target="tpu_custom_call" | custom-call | flops 1610612736 | bytes 12582912 | tf_op jit(solution)/shard_map/qkv_back/pallas_call | solution.py:355
  393.3 31.0 %sum_gradients.1 = (bf16[4,2,4,40,256]{4,3,2,1,0:T(8,128)(2,1)S(1)}, bf16[4,2,4,16,1024]{4,3,2,1,0:T(8,128)(2,1)S(1)}) custom-call(f32[3,16,2048]{2,1,0:T(8,128)S(1)} %get-tuple-element.126.ga_qkv, f32[16,2048]{1,0:T(8,128)S(1)} %copy-done.41, f32[16,3072]{1,0:T(8,128)S(1)} %get-tuple-element.128.gb_qkv, f32[16,2048]{1,0:T(8,128)S(1)} %copy-done.43, ...), custom_call_target="tpu_custom_call" | custom-call | bytes 67108864 | tf_op jit(solution)/shard_map/sum_gradients/pallas_call | solution.py:1528
  424.3 25.3 %reduce-scatter.3.cloned.1.call-done.before_0 = bf16[64,2048]{1,0:T(8,128)(2,1)} async-done(((bf16[512,2048]{1,0:T(8,128)(2,1)}), bf16[64,2048]{1,0:T(8,128)(2,1)}) %reduce-scatter.3.cloned.1.call-update) | async-done | bytes 262160 | tf_op jit(solution)/shard_map/reduce_scatter | solution.py:1729
  449.6 0.9 copy-done.34
  450.5 0.9 copy-done.35
  451.5 0.8 copy-done.44
  452.3 2.1 finish.1
  454.4 1.3 copy.41
  (117 shorter events, 0.9 us)
Async XLA Ops:
  7.2 235.8 %all-gather.5.cloned.1.call-start = ((), (), s32[]{:S(2)}) async-start(), calls=%async_computation.4 | async-start | bytes 2359296 | tf_op jit(solution)/shard_map/all_gather | solution.py:1680
  11.0 3.4 copy-start.4
  15.4 2.2 copy-start.8
  17.6 1.6 copy-start.14
  23.1 103.9 %copy-start.59 = (f32[2,512]{1,0:T(2,128)S(1)}, f32[2,512]{1,0:T(2,128)}, u32[]{:S(2)}) copy-start(f32[2,512]{1,0:T(2,128)} %param.32) | copy-start | bytes 12292
  23.1 104.0 %copy-start.57 = (f32[2048]{0:T(1024)S(1)}, f32[2048]{0:T(1024)}, u32[]{:S(2)}) copy-start(f32[2048]{0:T(1024)} %param.33) | copy-start | bytes 24580
  23.1 104.0 %copy-start.58 = (f32[2048]{0:T(1024)S(1)}, f32[2048]{0:T(1024)}, u32[]{:S(2)}) copy-start(f32[2048]{0:T(1024)} %param.31) | copy-start | bytes 24580
  23.1 104.0 %copy-start.56 = (f32[2,16,512]{2,1,0:T(8,128)S(1)}, f32[2,16,512]{2,1,0:T(8,128)}, u32[]{:S(2)}) copy-start(f32[2,16,512]{2,1,0:T(8,128)} %param.30) | copy-start | bytes 196612
  23.1 104.0 %copy-start.55 = (f32[2,16,2048]{2,1,0:T(8,128)S(1)}, f32[2,16,2048]{2,1,0:T(8,128)}, u32[]{:S(2)}) copy-start(f32[2,16,2048]{2,1,0:T(8,128)} %param.29) | copy-start | bytes 786436
  126.2 16.0 %copy-start.31 = (bf16[3,128,16]{2,1,0:T(8,128)(2,1)}, bf16[3,128,16]{2,1,0:T(8,128)(2,1)S(1)}, u32[]{:S(2)}) copy-start(bf16[3,128,16]{2,1,0:T(8,128)(2,1)S(1)} %get-tuple-element.88.inner_ref) | copy-start | bytes 36868
  126.2 16.0 %copy-start.46 = (bf16[7,32,16]{2,1,0:T(8,128)(2,1)}, bf16[7,32,16]{2,1,0:T(8,128)(2,1)S(1)}, u32[]{:S(2)}) copy-start(bf16[7,32,16]{2,1,0:T(8,128)(2,1)S(1)} %get-tuple-element.89.gram_ref.refs_20_) | copy-start | bytes 21508
  126.2 1.1 copy-start.1
  126.2 1.3 copy-start.9
  126.2 116.8 %all-gather.7.cloned.1.call-start = ((), (), s32[]{:S(2)}) async-start(), calls=%async_computation.5 | async-start | bytes 2359296 | tf_op jit(solution)/shard_map/all_gather | solution.py:1711
  126.7 15.4 %copy-start.22 = (f32[128,128]{1,0:T(8,128)}, f32[128,128]{1,0:T(8,128)S(1)}, u32[]{:S(2)}) copy-start(f32[128,128]{1,0:T(8,128)S(1)} %copy.38.sin_ref) | copy-start | bytes 196612
  127.0 15.2 %copy-start.24 = (f32[128,128]{1,0:T(8,128)}, f32[128,128]{1,0:T(8,128)S(1)}, u32[]{:S(2)}) copy-start(f32[128,128]{1,0:T(8,128)S(1)} %copy.37.cos_ref) | copy-start | bytes 196612
  142.2 34.0 %copy-start.60 = (s32[2]{0:T(128)S(1)}, s32[2]{0:T(128)}, u32[]{:S(2)}) copy-start(s32[2]{0:T(128)} %param.41) | copy-start | bytes 28
  142.2 34.0 %copy-start.29 = (bf16[128,2048]{1,0:T(8,128)(2,1)S(1)}, bf16[128,2048]{1,0:T(8,128)(2,1)}, u32[]{:S(2)}) copy-start(bf16[128,2048]{1,0:T(8,128)(2,1)} %get-tuple-element.92) | copy-start | bytes 1572868
  175.5 248.7 %reduce-scatter.5.cloned.1.call-start = ((), (), s32[]{:S(2)}) async-start(), calls=%async_computation.3 | async-start | bytes 2359296 | tf_op jit(solution)/shard_map/reduce_scatter | solution.py:1738
  176.3 1.6 copy-start.2
  177.9 10.4 %copy-start.6 = (bf16[2,64,2048]{2,1,0:T(8,128)(2,1)S(1)}, bf16[2,64,2048]{2,1,0:T(8,128)(2,1)}, u32[]{:S(2)}) copy-start(bf16[2,64,2048]{2,1,0:T(8,128)(2,1)} %param.21) | copy-start | bytes 1572868
  177.9 10.4 %copy-start.18 = (f32[2,16,2048]{2,1,0:T(8,128)S(1)}, f32[2,16,2048]{2,1,0:T(8,128)}, u32[]{:S(2)}) copy-start(f32[2,16,2048]{2,1,0:T(8,128)} %refs_13_.1) | copy-start | bytes 786436
  177.9 10.4 %copy-start.33 = (f32[1,5120]{1,0:T(1,128)S(1)}, f32[1,5120]{1,0:T(1,128)}, u32[]{:S(2)}) copy-start(f32[1,5120]{1,0:T(1,128)} %get-tuple-element.103.n_ref.n_attn) | copy-start | bytes 61444
  243.0 74.6 %copy-start.7 = (f32[128,2048]{1,0:T(8,128)S(1)}, f32[128,2048]{1,0:T(8,128)}, u32[]{:S(2)}) copy-start(f32[128,2048]{1,0:T(8,128)} %get-tuple-element.116.x1_ref.x1) | copy-start | bytes 3145732
  243.0 74.6 %copy-start.11 = (bf16[2,64,2048]{2,1,0:T(8,128)(2,1)S(1)}, bf16[2,64,2048]{2,1,0:T(8,128)(2,1)}, u32[]{:S(2)}) copy-start(bf16[2,64,2048]{2,1,0:T(8,128)(2,1)} %get-tuple-element.102) | copy-start | bytes 1572868
  243.0 74.6 %copy-start.13 = (bf16[2,64,2048]{2,1,0:T(8,128)(2,1)S(1)}, bf16[2,64,2048]{2,1,0:T(8,128)(2,1)}, u32[]{:S(2)}) copy-start(bf16[2,64,2048]{2,1,0:T(8,128)(2,1)} %param.22) | copy-start | bytes 1572868
  318.6 1.2 copy-start.19
  319.8 1.2 copy-start.21
  321.0 8.5 %copy-start.3 = (bf16[8,128,1024]{2,1,0:T(8,128)(2,1)S(1)}, bf16[8,128,1024]{2,1,0:T(8,128)(2,1)}, u32[]{:S(2)}) copy-start(bf16[8,128,1024]{2,1,0:T(8,128)(2,1)} %get-tuple-element.97) | copy-start | bytes 6291460
  321.0 8.6 %copy-start.30 = (bf16[128,2048]{1,0:T(8,128)(2,1)S(1)}, bf16[128,2048]{1,0:T(8,128)(2,1)}, u32[]{:S(2)}) copy-start(bf16[128,2048]{1,0:T(8,128)(2,1)} %get-tuple-element.92) | copy-start | bytes 1572868
  321.0 8.6 %copy-start.53 = (bf16[2,4,512,512]{3,2,1,0:T(8,128)(2,1)S(1)}, bf16[2,4,512,512]{3,2,1,0:T(8,128)(2,1)}, u32[]{:S(2)}) copy-start(bf16[2,4,512,512]{3,2,1,0:T(8,128)(2,1)} %get-tuple-element.98.p_ref) | copy-start | bytes 12582916
  329.6 11.5 %copy-start.40 = (f32[16,2048]{1,0:T(8,128)}, f32[16,2048]{1,0:T(8,128)S(1)}, u32[]{:S(2)}) copy-start(f32[16,2048]{1,0:T(8,128)S(1)} %get-tuple-element.127.ga_o) | copy-start | bytes 393220
  329.6 11.5 %copy-start.42 = (f32[16,2048]{1,0:T(8,128)}, f32[16,2048]{1,0:T(8,128)S(1)}, u32[]{:S(2)}) copy-start(f32[16,2048]{1,0:T(8,128)S(1)} %get-tuple-element.129.gb_o) | copy-start | bytes 393220
  329.6 1.1 copy-start.54
  341.1 1.6 copy-start.12
  374.5 75.1 %reduce-scatter.3.cloned.1.call-start = ((), (), s32[]{:S(2)}) async-start(), calls=%async_computation.2 | async-start | bytes 2359296 | tf_op jit(solution)/shard_map/reduce_scatter | solution.py:1729
  376.0 1.2 copy-start.20
  380.9 12.3 %copy-start.36 = (f32[2,16,2048]{2,1,0:T(8,128)S(1)}, f32[2,16,2048]{2,1,0:T(8,128)}, u32[]{:S(2)}) copy-start(f32[2,16,2048]{2,1,0:T(8,128)} %get-tuple-element.130.ga_gu) | copy-start | bytes 786436
  380.9 12.3 %copy-start.38 = (f32[2,16,1024]{2,1,0:T(8,128)S(1)}, f32[2,16,1024]{2,1,0:T(8,128)}, u32[]{:S(2)}) copy-start(f32[2,16,1024]{2,1,0:T(8,128)} %get-tuple-element.135.gb_gu) | copy-start | bytes 393220
  380.9 12.3 %copy-start.39 = (f32[16,2048]{1,0:T(8,128)S(1)}, f32[16,2048]{1,0:T(8,128)}, u32[]{:S(2)}) copy-start(f32[16,2048]{1,0:T(8,128)} %get-tuple-element.131.gb_d) | copy-start | bytes 393220
  380.9 12.3 %copy-start.41 = (f32[16,2048]{1,0:T(8,128)S(1)}, f32[16,2048]{1,0:T(8,128)}, u32[]{:S(2)}) copy-start(f32[16,2048]{1,0:T(8,128)} %copy-done.40) | copy-start | bytes 393220
  380.9 12.3 %copy-start.43 = (f32[16,2048]{1,0:T(8,128)S(1)}, f32[16,2048]{1,0:T(8,128)}, u32[]{:S(2)}) copy-start(f32[16,2048]{1,0:T(8,128)} %copy-done.42) | copy-start | bytes 393220
  381.0 12.3 %copy-start.45 = (f32[16,1024]{1,0:T(8,128)S(1)}, f32[16,1024]{1,0:T(8,128)}, u32[]{:S(2)}) copy-start(f32[16,1024]{1,0:T(8,128)} %get-tuple-element.138.ga_d) | copy-start | bytes 196612
  381.0 12.3 %copy-start.49 = (f32[2,1,1024]{2,1,0:T(1,128)S(1)}, f32[2,1,1024]{2,1,0:T(1,128)}, u32[]{:S(2)}) copy-start(f32[2,1,1024]{2,1,0:T(1,128)} %get-tuple-element.136.gm_gu) | copy-start | bytes 24580
  381.0 12.3 %copy-start.50 = (f32[2,1,1024]{2,1,0:T(1,128)S(1)}, f32[2,1,1024]{2,1,0:T(1,128)}, u32[]{:S(2)}) copy-start(f32[2,1,1024]{2,1,0:T(1,128)} %get-tuple-element.137.n_gu) | copy-start | bytes 24580
  381.0 12.3 %copy-start.51 = (f32[1,2048]{1,0:T(1,128)S(1)}, f32[1,2048]{1,0:T(1,128)}, u32[]{:S(2)}) copy-start(f32[1,2048]{1,0:T(1,128)} %get-tuple-element.134.gm_d) | copy-start | bytes 24580
  381.0 68.6 %copy-start.47 = (f32[2048]{0:T(1024)S(1)}, f32[2048]{0:T(1024)}, u32[]{:S(2)}) copy-start(f32[2048]{0:T(1024)} %param.39) | copy-start | bytes 24580
  381.0 68.6 %copy-start.48 = (f32[1,2048]{1,0:T(1,128)S(1)}, f32[1,2048]{1,0:T(1,128)}, u32[]{:S(2)}) copy-start(f32[1,2048]{1,0:T(1,128)} %get-tuple-element.143.n_d) | copy-start | bytes 24580
  (17 other events, 16.0 us)
Sparse Core Ops, SparseCore 0:
  126.4 31.0 all-gather.4
  175.7 28.6 all-gather.6
  374.6 36.1 reduce-scatter.4
  413.0 36.5 reduce-scatter.2

commit v7 on v6

--- a/solution.py
+++ b/solution.py
@@ -29,6 +29,10 @@
 
 def dot_tn(a, b):
     return lax.dot_general(a, b, first_first, preferred_element_type=jnp.float32)
+
+
+def in_hbm(*arrays):
+    return [pltpu.with_memory_space_constraint(v, pltpu.HBM) for v in arrays]
 
 
 def unit_rms(v):
@@ -157,7 +161,7 @@
             flops=2 * rows * width * cols, transcendentals=0, bytes_accessed=2 * width * cols
         ),
         name="project_qkv",
-    )(u, inner, grams, a, weights, b, m, cosine, sine)
+    )(*in_hbm(u), inner, grams, *in_hbm(a, weights, b), m, cosine, sine)
 
 
 def out_kernel(att_ref, a_ref, w_ref, b_ref, m_ref, n_ref, x_ref, gain_ref, next_ref,
@@ -217,7 +221,7 @@
             flops=2 * rows * width * width, transcendentals=0, bytes_accessed=2 * width * width
         ),
         name="project_out",
-    )(att, a, weights, b, m, norms, x, gain, following)
+    )(*in_hbm(att, a, weights, b), m, norms, *in_hbm(x), gain, *in_hbm(following))
 
 
 def out_back_kernel(in_ref, x1_ref, gain_ref, gy_ref, before_ref, att_ref, a_ref, b_ref, m_ref, n_ref, cross_ref,
@@ -283,11 +287,9 @@
             pltpu.VMEM((32, 16), low),
         ],
         compiler_params=pltpu.CompilerParams(vmem_limit_bytes=48 << 20),
-        cost_estimate=pl.CostEstimate(
-            flops=2 * rows * width * width, transcendentals=0, bytes_accessed=2 * width * width
-        ),
+        cost_estimate=pl.CostEstimate(flops=0, transcendentals=0, bytes_accessed=1 << 20),
         name="out_back",
-    )(in_grad, x1, gain, gy, before, att, a, b, m, norms, cross, weights)
+    )(in_grad, *in_hbm(x1), gain, *in_hbm(gy, before, att, a, b), m, norms, *in_hbm(cross, weights))
 
 
 def qkv_back_kernel(gq_ref, gkv_ref, cos_ref, sin_ref, before_ref, u_ref, inner_ref, a_ref, b_ref, m_ref, n_ref, cross_ref,
@@ -374,11 +376,10 @@
             pltpu.VMEM((3, 32, 16), low),
         ],
         compiler_params=pltpu.CompilerParams(vmem_limit_bytes=48 << 20),
-        cost_estimate=pl.CostEstimate(
-            flops=2 * rows * width * cols, transcendentals=0, bytes_accessed=2 * width * cols
-        ),
+        cost_estimate=pl.CostEstimate(flops=0, transcendentals=0, bytes_accessed=1 << 20),
         name="qkv_back",
-    )(gq, gkv, cosine, sine, before, u, inner, a, b, m, norms, cross, x, gain, gx, weights, weights)
+    )(*in_hbm(gq), gkv, cosine, sine, *in_hbm(before, u), inner, *in_hbm(a, b), m, norms, *in_hbm(cross, x), gain,
+      *in_hbm(gx, weights, weights))
 
 MESH = pl.DeviceIdType.MESH
 
@@ -639,7 +640,7 @@
     units = xg.shape[3] // n
     kinds = 2 + 3 * (rows // 2 - 1)
     dma = pltpu.SemaphoreType.DMA
-    anywhere = pl.BlockSpec(memory_space=pl.ANY)
+    anywhere = pl.BlockSpec(memory_space=pltpu.HBM)
     vmem = pl.BlockSpec(memory_space=pltpu.VMEM)
     low = qo.dtype
     wa, gz, near, sq, grams, u, inner = pl.pallas_call(
@@ -666,7 +667,7 @@
             flops=0, transcendentals=0, bytes_accessed=250 * 1024 * 1024
         ),
         name="gather_weights",
-    )(qo, kv, xg, wd, ad, bd, x, gain, aa, ag)
+    )(*in_hbm(qo, kv, xg, wd, ad, bd, x), gain, *in_hbm(aa, ag))
     return wa.reshape(2, n * block, cols), gz, near, sq, grams, u, inner
 
 
@@ -742,7 +743,7 @@
     shape = jax.ShapeDtypeStruct
     outs = [shape((n, *a.shape), a.dtype) for a in arrays]
     outs += [shape(held[source].shape[-3:], held[source].dtype) for source, _, _ in shares]
-    anywhere = pl.BlockSpec(memory_space=pl.ANY)
+    anywhere = pl.BlockSpec(memory_space=pltpu.HBM)
     listed = (tuple(held), [(source, piece, turn, None) for source, piece, turn in shares])
     sems = dma((max(1, len(shares)), nc))
     got = pl.pallas_call(
@@ -865,15 +866,15 @@
     return pl.pallas_call(
         functools.partial(scatter_kernel, n),
         out_shape=jax.ShapeDtypeStruct((rows, cols), jnp.float32),
-        in_specs=[pl.BlockSpec(memory_space=pl.ANY)],
+        in_specs=[pl.BlockSpec(memory_space=pltpu.HBM)],
         out_specs=pl.BlockSpec(memory_space=pltpu.VMEM),
         scratch_shapes=[buf] * 4 + [dma((nc,))] * 7,
         compiler_params=pltpu.CompilerParams(
             collective_id=collective_id, has_side_effects=True, vmem_limit_bytes=32 << 20
         ),
-        cost_estimate=pl.CostEstimate(flops=0, transcendentals=0, bytes_accessed=x.size * 2 * 20),
+        cost_estimate=pl.CostEstimate(flops=0, transcendentals=0, bytes_accessed=1 << 20),
         name="scatter_seq",
-    )(x)
+    )(*in_hbm(x))
 
 def swap_halves(x):
     return pltpu.roll(x.astype(jnp.float32), HEAD_DIM, 1)
@@ -957,7 +958,7 @@
             flops=flops, transcendentals=flops // 512, bytes_accessed=8 << 20
         ),
         name="attend",
-    )(valid, q, kv, kv)
+    )(valid, *in_hbm(q, kv, kv))
 
 
 def attend_back_kernel(q_ref, k_ref, v_ref, p_ref, g_ref, gq_ref, gkv_ref):
@@ -987,7 +988,6 @@
     groups = kv_width // 128
     keys = n * span
     q_spec = pl.BlockSpec((1, span, 512), lambda p, j: (p, 0, j))
-    flops = 10 * pair * groups * 8 * span * keys * 128
     return pl.pallas_call(
         attend_back_kernel,
         out_shape=(
@@ -1007,9 +1007,9 @@
             pl.BlockSpec((n, 1, span, 256), lambda p, j: (0, p, 0, j)),
         ),
         compiler_params=pltpu.CompilerParams(vmem_limit_bytes=40 << 20),
-        cost_estimate=pl.CostEstimate(flops=flops, transcendentals=0, bytes_accessed=8 << 20),
+        cost_estimate=pl.CostEstimate(flops=0, transcendentals=0, bytes_accessed=1 << 20),
         name="attend_back",
-    )(q, kv, kv, shares, g)
+    )(*in_hbm(q, kv, kv, shares, g))
 
 def by_distance(i, q, nc):
     room = nc - 1 - q
@@ -1309,7 +1309,7 @@
     f32, low = jnp.float32, jnp.bfloat16
     shape = jax.ShapeDtypeStruct
     vmem = pl.BlockSpec(memory_space=pltpu.VMEM)
-    hbm = pl.BlockSpec(memory_space=pl.ANY)
+    hbm = pl.BlockSpec(memory_space=pltpu.HBM)
     dma = pltpu.SemaphoreType.DMA
     line = pltpu.VMEM((nc, tokens, width), low)
     pair = pltpu.VMEM((2, 2, tokens, width), low)
@@ -1548,7 +1548,7 @@
         compiler_params=pltpu.CompilerParams(
             collective_id=collective_id, has_side_effects=True, vmem_limit_bytes=48 << 20
         ),
-        cost_estimate=pl.CostEstimate(flops=0, transcendentals=0, bytes_accessed=64 << 20),
+        cost_estimate=pl.CostEstimate(flops=0, transcendentals=0, bytes_accessed=1 << 20),
         name="sum_gradients",
     )(*full, *own_units)
 
@@ -1633,7 +1633,7 @@
         compiler_params=pltpu.CompilerParams(vmem_limit_bytes=40 << 20),
         cost_estimate=pl.CostEstimate(flops=0, transcendentals=0, bytes_accessed=8 << 20),
         name="finish",
-    )(*sums, x1, before_0, before_1, m_attn, n_attn, m_d, n_d, m_gu)
+    )(*sums, *in_hbm(x1, before_0, before_1), m_attn, n_attn, m_d, n_d, m_gu)
 
 def local(
     layer_input,
@@ -1734,7 +1734,7 @@
     )
     gq, gkv = attend_back(q, kv_all, shares, grad_att.reshape(q.shape))
     gkv = scatter_seq(seq_size, gkv.reshape(seq_size, token_count, 2 * kv_width), 5)
-    gkv, down_1 = lax.optimization_barrier((gkv, down_1))
+    gkv, down_1, before_0 = lax.optimization_barrier((gkv, down_1, before_0))
     before_1 = lax.psum_scatter(flat(down_1), "seq", scatter_dimension=0, tiled=True)
     grad_inputs, ga_qkv, gb_qkv, gm_qkv = qkv_back(
         gq.reshape(token_count, model_width), gkv, cosine, sine, before_qkv, u1, inner_1,

time: 464 us -> 434 us (0.935)
  local copies, waits for them, and re-layouts: 36.1 us -> 6.36 us
  Pallas kernels: 385 us -> 411 us
  waiting for transfers between devices: 25.9 us -> 0.15 us
    unnamed x123 -> x41, local copies, waits for them, and re-layouts: 32.9 us -> 3.15 us
    reduce_scatter x1, waiting for transfers between devices: 25.3 us -> 0.02 us  [local(): lax.psum_scatter(flat(down_0), 'seq', scatter_dimension=0, tiled=True)]
    pallas_call x1, Pallas kernels: 102 us -> 118 us  [gather_weights(): pl.pallas_call(functools.partial(weights_kernel, n, rows), out_shape=(plt...]
  transfers between devices with their start and end apart: 4 -> 4, of which waited for: 1 -> 0; matrix products, arithmetic and copies ran while one was open for 0% -> 0% of each run, Pallas kernels for 34% -> 50%
where the time goes in v7:
time: 434 us; the launch traced here: 433 us
  Pallas kernels  411 us (95%)
  between operations  14.8 us (3%)
  local copies, waits for them, and re-layouts  6.36 us (1%)
    pallas_call x1, Pallas kernels, gather_weights(): pl.pallas_call(functools.partial(weights_kernel, n, rows), out_shape=(plt...  118 us
    pallas_call x2, Pallas kernels, gather_seq(): pl.pallas_call(functools.partial(gather_kernel, n, rows, count, (range(le...  79.3 us
    pallas_call x1, Pallas kernels, feed_forward(): pl.pallas_call(kernel, out_shape=(shape((tokens, width), f32), pltpu.HBM(...  74.4 us
    pallas_call x1, Pallas kernels, scatter_seq(): pl.pallas_call(functools.partial(scatter_kernel, n), out_shape=jax.ShapeD...  35.6 us
    pallas_call x1, Pallas kernels, sum_gradients(): pl.pallas_call(functools.partial(reduce_kernel, n, rows), out_shape=(jax....  31.9 us
    pallas_call x1, Pallas kernels, project_qkv(): pl.pallas_call(functools.partial(project_kernel, (q_tiles, last)), out_sh...  15.5 us
    pallas_call x1, Pallas kernels, qkv_back(): pl.pallas_call(qkv_back_kernel, out_shape=(pltpu.HBM((rows, width), f32),...  12.3 us
    pallas_call x1, Pallas kernels, attend_back(): pl.pallas_call(attend_back_kernel, out_shape=(pltpu.HBM(q.shape, jnp.bflo...  11.3 us
  transfers between devices with their start and end apart: 4, of which 0 were waited for; matrix products, arithmetic and copies ran while one was open for 0% of the time, Pallas kernels for 50%

profile of v7, /device:TPU:0, one launch (start us, length us, event | category | flops | bytes accessed | tf_op | source)
XLA Modules:
  0.0 433.3 jit_solution(10175660948382106150)
XLA Ops:
  7.2 0.0 all-gather.5.cloned.1.call-start
  7.2 0.8 fusion
  8.0 1.9 slice_bitcast_fusion
  9.9 0.0 copy-start.14
  9.9 118.5 %gather_weights.1 = (bf16[2,8,4,64,2560]{4,3,2,1,0:T(8,128)(2,1)}, bf16[2,8,64,1024]{3,2,1,0:T(8,128)(2,1)}, bf16[2,2,4,64,1024]{4,3,2,1,0:T(8,128)(2,1)}, f32[1...) custom-call(bf16[2,4,64,2048]{3,2,1,0:T(8,128)(2,1)} %bitcast.68, ...), custom_call_target="tpu_custom_call" | custom-call | bytes 262144000 | tf_op jit(solution)/shard_map/gather_weights/pallas_call | solution.py:646
  128.4 0.0 copy-start.13
  128.4 0.6 copy-done.13
  129.0 0.0 all-gather.5.cloned.1.call-update
  129.0 0.0 all-gather.7.cloned.1.call-start
  129.1 0.1 multiply_sine_fusion
  129.3 0.1 tile.21
  129.5 0.1 copy.38.sin_ref
  129.6 0.1 tile.9
  129.7 0.1 copy.37.cos_ref
  129.8 0.0 copy-done.16
  129.9 0.0 copy-done.17
  129.9 0.0 copy-done.14
  129.9 0.8 pad_maximum_fusion.b_ref
  130.7 15.5 %project_qkv.1 = (f32[128,3072]{1,0:T(8,128)}, bf16[128,2048]{1,0:T(8,128)(2,1)}, bf16[128,1024]{1,0:T(8,128)(2,1)}, f32[1,5120]{1,0:T(1,128)}, f32[16,5120]{1,0:T(8,128)}) custom-call(bf16[128,2048]{1,0:T(8,128)(2,1)} %get-tuple-element.88.u_ref, bf16[3,128,16]{2,1,0:T(8,128)(2,1)S(1)} %get-tuple-element.89.inner_ref, ...), custom_call_target="tpu_custom_call" | custom-call | flops 2684354560 | bytes 20971520 | tf_op jit(solution)/shard_map/project_qkv/pallas_call | solution.py:131
  146.2 0.0 copy-start.19
  146.2 32.1 %gather_seq.2 = (bf16[8,128,1024]{2,1,0:T(8,128)(2,1)}, f32[8,1,2048]{2,1,0:T(1,128)}, bf16[8,64,1024]{2,1,0:T(8,128)(2,1)}, bf16[8,64,1024]{2,1,0:T(8,128)(2,1)}) custom-call(bf16[128,1024]{1,0:T(8,128)(2,1)} %get-tuple-element.94.refs_0_, f32[1,2048]{1,0:T(1,128)} %copy-done.13, bf16[2,8,64,1024]{3,2,1,0:T(8,128)(2,1)} %get-tuple-element.96.refs_2_.refs_0_), custom_call_target="tpu_custom_call" | custom-call | bytes 43253760 | tf_op jit(solution)/shard_map/gather_seq/pallas_call | solution.py:749
  178.4 0.0 all-gather.7.cloned.1.call-update
  178.4 0.0 reduce-scatter.3.cloned.1.call-start
  179.1 0.0 copy-start.1
  179.1 11.1 %attend.1 = (bf16[2,64,2048]{2,1,0:T(8,128)(2,1)}, bf16[2,4,512,512]{3,2,1,0:T(8,128)(2,1)}) custom-call(s32[2]{0:T(128)S(1)} %broadcast_add_fusion.valid_ref, bf16[2,64,2048]{2,1,0:T(8,128)(2,1)} %bitcast.60, bf16[8,2,64,1024]{3,2,1,0:T(8,128)(2,1)} %bitcast.52, bf16[8,2,64,1024]{3,2,1,0:T(8,128)(2,1)} %bitcast.53), custom_call_target="tpu_custom_call" | custom-call | flops 1073741824 | bytes 8388608 | tf_op jit(solution)/shard_map/attend/pallas_call | solution.py:937
  190.3 7.8 %project_out.1 = (f32[128,2048]{1,0:T(8,128)}, f32[128,2048]{1,0:T(8,128)}, bf16[128,2048]{1,0:T(8,128)(2,1)}, bf16[128,128]{1,0:T(8,128)(2,1)}) custom-call(bf16[128,2048]{1,0:T(8,128)(2,1)} %bitcast.62, f32[4,16,2048]{2,1,0:T(8,128)} %a_ref.7, bf16[2,2048,2560]{2,1,0:T(8,128)(2,1)} %bitcast.48, f32[16,5120]{1,0:T(8,128)} %pad_maximum_fusion.b_ref, ...), custom_call_target="tpu_custom_call" | custom-call | flops 1073741824 | bytes 8388608 | tf_op jit(solution)/shard_map/project_out/pallas_call | solution.py:198
  198.1 47.1 %gather_seq.3 = (bf16[8,128,2048]{2,1,0:T(8,128)(2,1)}, bf16[8,128,128]{2,1,0:T(8,128)(2,1)}, bf16[8,64,1024]{2,1,0:T(8,128)(2,1)}, bf16[8,64,1024]{2,1,0:T(8,12...) custom-call(bf16[128,2048]{1,0:T(8,128)(2,1)} %get-tuple-element.105.refs_0_, ...), custom_call_target="tpu_custom_call" | custom-call | bytes 89128960 | tf_op jit(solution)/shard_map/gather_seq/pallas_call | solution.py:749
  245.2 0.0 all-gather.5.cloned.1.call-done
  245.3 0.0 all-gather.7.cloned.1.call-done
  245.3 74.4 %feed_forward.1 = (f32[128,2048]{1,0:T(8,128)}, bf16[8,64,2048]{2,1,0:T(8,128)(2,1)}, bf16[8,64,2048]{2,1,0:T(8,128)(2,1)}, f32[2,16,2048]{2,1,0:T(8,128)}, f32[...) custom-call(bf16[2,8,64,1024]{3,2,1,0:T(8,128)(2,1)} %get-tuple-elem, ...), custom_call_target="tpu_custom_call" | custom-call | flops 25769803776 | bytes 33554432 | tf_op jit(solution)/shard_map/feed_forward/pallas_call | solution.py:1323
  319.7 0.0 reduce-scatter.3.cloned.1.call-update
  319.7 0.0 reduce-scatter.5.cloned.1.call-start
  319.8 1.1 copy-done
  320.9 9.6 %out_back.1 = (f32[128,2048]{1,0:T(8,128)}, bf16[128,2048]{1,0:T(8,128)(2,1)}, f32[16,2048]{1,0:T(8,128)S(1)}, f32[16,2048]{1,0:T(8,128)S(1)}, f32[1,2048]{1,0:T(1,128)S(1)}) custom-call(f32[128,2048]{1,0:T(8,128)S(1)} %copy-done, f32[128,2048]{1,0:T(8,128)} %get-tuple-element.117.x1_ref.x1, f32[1,2048]{1,0:T(1,128)S(1)} %get-tuple-element.197.gain_ref, ...), custom_call_target="tpu_custom_call" | custom-call | bytes 1048576 | tf_op jit(solution)/shard_map/out_back/pallas_call | solution.py:269
  330.6 11.3 %attend_back.1 = (bf16[2,64,2048]{2,1,0:T(8,128)(2,1)}, bf16[8,2,64,1024]{3,2,1,0:T(8,128)(2,1)}) custom-call(bf16[2,64,2048]{2,1,0:T(8,128)(2,1)} %bitcast.61, bf16[8,2,64,1024]{3,2,1,0:T(8,128)(2,1)} %bitcast.54, bf16[8,2,64,1024]{3,2,1,0:T(8,128)(2,1)} %bitcast.55, bf16[2,4,512,512]{3,2,1,0:T(8,128)(2,1)} %get-tuple-element.99.p_ref, ...), custom_call_target="tpu_custom_call" | custom-call | bytes 1048576 | tf_op jit(solution)/shard_map/attend_back/pallas_call | solution.py:991
  341.9 35.6 %scatter_seq.1.gkv_ref = f32[128,1024]{1,0:T(8,128)S(1)} custom-call(bf16[8,128,1024]{2,1,0:T(8,128)(2,1)} %bitcast.64), custom_call_target="tpu_custom_call" | custom-call | bytes 1048576 | tf_op jit(solution)/shard_map/scatter_seq/pallas_call | solution.py:866
  377.5 0.0 reduce-scatter.3.cloned.1.call-done.before_0
  377.6 0.0 reduce-scatter.5.cloned.1.call-update
  377.7 0.0 copy-start.5
  377.7 0.0 copy-start.8
  377.7 12.3 %qkv_back.1 = (f32[128,2048]{1,0:T(8,128)}, f32[3,16,2048]{2,1,0:T(8,128)S(1)}, f32[16,3072]{1,0:T(8,128)S(1)}, f32[1,3072]{1,0:T(1,128)S(1)}) custom-call(bf16[128,2048]{1,0:T(8,128)(2,1)} %bitcast.69, f32[128,1024]{1,0:T(8,128)S(1)} %scatter_seq.1.gkv_ref, f32[128,128]{1,0:T(8,128)S(1)} %copy.37.cos_ref, f32[128,128]{1,0:T(8,128)S(1)} %copy.38.sin_ref, ...), custom_call_target="tpu_custom_call" | custom-call | bytes 1048576 | tf_op jit(solution)/shard_map/qkv_back/pallas_call | solution.py:357
  390.0 0.0 copy-done.3
  390.0 0.0 copy-done.4
  390.1 0.0 copy-done.6
  390.1 31.9 %sum_gradients.1 = (bf16[4,2,4,40,256]{4,3,2,1,0:T(8,128)(2,1)S(1)}, bf16[4,2,4,16,1024]{4,3,2,1,0:T(8,128)(2,1)S(1)}) custom-call(f32[3,16,2048]{2,1,0:T(8,128)S(1)} %get-tuple-element.128.ga_qkv, f32[16,2048]{1,0:T(8,128)S(1)} %get-tuple-element.129.ga_o, f32[16,3072]{1,0:T(8,128)S(1)} %get-tuple-element.130.gb_qkv, ...), custom_call_target="tpu_custom_call" | custom-call | bytes 1048576 | tf_op jit(solution)/shard_map/sum_gradients/pallas_call | solution.py:1528
  422.0 0.0 reduce-scatter.5.cloned.1.call-done.before_1
  422.0 3.4 finish.1
  425.5 1.3 copy.41
  (35 shorter events, 0.2 us)
Async XLA Ops:
  7.2 238.1 %all-gather.5.cloned.1.call-start = ((), (), s32[]{:S(2)}) async-start(), calls=%async_computation.4 | async-start | bytes 2359296 | tf_op jit(solution)/shard_map/all_gather | solution.py:1680
  9.9 119.9 %copy-start.18 = (f32[2,512]{1,0:T(2,128)S(1)}, f32[2,512]{1,0:T(2,128)}, u32[]{:S(2)}) copy-start(f32[2,512]{1,0:T(2,128)} %param.32) | copy-start | bytes 12292
  9.9 119.9 %copy-start.16 = (f32[2048]{0:T(1024)S(1)}, f32[2048]{0:T(1024)}, u32[]{:S(2)}) copy-start(f32[2048]{0:T(1024)} %param.33) | copy-start | bytes 24580
  9.9 119.9 %copy-start.17 = (f32[2048]{0:T(1024)S(1)}, f32[2048]{0:T(1024)}, u32[]{:S(2)}) copy-start(f32[2048]{0:T(1024)} %param.31) | copy-start | bytes 24580
  9.9 120.0 %copy-start.15 = (f32[2,16,512]{2,1,0:T(8,128)S(1)}, f32[2,16,512]{2,1,0:T(8,128)}, u32[]{:S(2)}) copy-start(f32[2,16,512]{2,1,0:T(8,128)} %param.30) | copy-start | bytes 196612
  9.9 120.0 %copy-start.14 = (f32[2,16,2048]{2,1,0:T(8,128)S(1)}, f32[2,16,2048]{2,1,0:T(8,128)}, u32[]{:S(2)}) copy-start(f32[2,16,2048]{2,1,0:T(8,128)} %param.29) | copy-start | bytes 786436
  128.4 0.6 copy-start.13
  129.0 17.2 %copy-start.7 = (bf16[7,32,16]{2,1,0:T(8,128)(2,1)}, bf16[7,32,16]{2,1,0:T(8,128)(2,1)S(1)}, u32[]{:S(2)}) copy-start(bf16[7,32,16]{2,1,0:T(8,128)(2,1)S(1)} %get-tuple-element.90.gram_ref.refs_20_) | copy-start | bytes 21508
  129.0 116.2 %all-gather.7.cloned.1.call-start = ((), (), s32[]{:S(2)}) async-start(), calls=%async_computation.5 | async-start | bytes 2359296 | tf_op jit(solution)/shard_map/all_gather | solution.py:1711
  146.2 32.9 %copy-start.19 = (s32[2]{0:T(128)S(1)}, s32[2]{0:T(128)}, u32[]{:S(2)}) copy-start(s32[2]{0:T(128)} %param.41) | copy-start | bytes 28
  178.4 199.2 %reduce-scatter.3.cloned.1.call-start = ((), (), s32[]{:S(2)}) async-start(), calls=%async_computation.2 | async-start | bytes 2359296 | tf_op jit(solution)/shard_map/reduce_scatter | solution.py:1729
  179.1 11.2 %copy-start.1 = (f32[1,5120]{1,0:T(1,128)S(1)}, f32[1,5120]{1,0:T(1,128)}, u32[]{:S(2)}) copy-start(f32[1,5120]{1,0:T(1,128)} %get-tuple-element.104.n_ref.n_attn) | copy-start | bytes 61444
  319.7 1.2 copy-start
  319.7 102.3 %reduce-scatter.5.cloned.1.call-start = ((), (), s32[]{:S(2)}) async-start(), calls=%async_computation.3 | async-start | bytes 2359296 | tf_op jit(solution)/shard_map/reduce_scatter | solution.py:1738
  377.6 12.4 %copy-start.2 = (f32[2,16,2048]{2,1,0:T(8,128)S(1)}, f32[2,16,2048]{2,1,0:T(8,128)}, u32[]{:S(2)}) copy-start(f32[2,16,2048]{2,1,0:T(8,128)} %get-tuple-element.132.ga_gu) | copy-start | bytes 786436
  377.6 12.4 %copy-start.3 = (f32[2,16,1024]{2,1,0:T(8,128)S(1)}, f32[2,16,1024]{2,1,0:T(8,128)}, u32[]{:S(2)}) copy-start(f32[2,16,1024]{2,1,0:T(8,128)} %get-tuple-element.137.gb_gu) | copy-start | bytes 393220
  377.6 12.4 %copy-start.4 = (f32[16,2048]{1,0:T(8,128)S(1)}, f32[16,2048]{1,0:T(8,128)}, u32[]{:S(2)}) copy-start(f32[16,2048]{1,0:T(8,128)} %get-tuple-element.133.gb_d) | copy-start | bytes 393220
  377.6 12.4 %copy-start.6 = (f32[16,1024]{1,0:T(8,128)S(1)}, f32[16,1024]{1,0:T(8,128)}, u32[]{:S(2)}) copy-start(f32[16,1024]{1,0:T(8,128)} %get-tuple-element.140.ga_d) | copy-start | bytes 196612
  377.6 12.4 %copy-start.10 = (f32[2,1,1024]{2,1,0:T(1,128)S(1)}, f32[2,1,1024]{2,1,0:T(1,128)}, u32[]{:S(2)}) copy-start(f32[2,1,1024]{2,1,0:T(1,128)} %get-tuple-element.138.gm_gu) | copy-start | bytes 24580
  377.7 12.4 %copy-start.11 = (f32[2,1,1024]{2,1,0:T(1,128)S(1)}, f32[2,1,1024]{2,1,0:T(1,128)}, u32[]{:S(2)}) copy-start(f32[2,1,1024]{2,1,0:T(1,128)} %get-tuple-element.139.n_gu) | copy-start | bytes 24580
  377.7 12.4 %copy-start.12 = (f32[1,2048]{1,0:T(1,128)S(1)}, f32[1,2048]{1,0:T(1,128)}, u32[]{:S(2)}) copy-start(f32[1,2048]{1,0:T(1,128)} %get-tuple-element.136.gm_d) | copy-start | bytes 24580
  377.7 44.3 %copy-start.5 = (f32[2,8192]{1,0:T(2,128)S(1)}, f32[2,8192]{1,0:T(2,128)}, u32[]{:S(2)}) copy-start(f32[2,8192]{1,0:T(2,128)} %m_gu.1) | copy-start | bytes 196612
  377.7 44.3 %copy-start.8 = (f32[2048]{0:T(1024)S(1)}, f32[2048]{0:T(1024)}, u32[]{:S(2)}) copy-start(f32[2048]{0:T(1024)} %param.39) | copy-start | bytes 24580
  377.7 44.3 %copy-start.9 = (f32[1,2048]{1,0:T(1,128)S(1)}, f32[1,2048]{1,0:T(1,128)}, u32[]{:S(2)}) copy-start(f32[1,2048]{1,0:T(1,128)} %get-tuple-element.145.n_d) | copy-start | bytes 24580
Sparse Core Ops, SparseCore 0:
  129.2 29.6 all-gather.4
  178.5 28.5 all-gather.6
  319.9 39.1 reduce-scatter.2
  377.7 37.7 reduce-scatter.4

commit v8 on v7

--- a/solution.py
+++ b/solution.py
@@ -388,20 +388,6 @@
     s = lax.axis_index("seq")
     return s, s // 2, lax.rem(s, 2)
 
-
-def greet(nc, q, s):
-    barrier = pltpu.get_barrier_semaphore()
-
-    def signal(target):
-        pl.semaphore_signal(barrier, inc=1, device_id={"seq": target}, device_id_type=MESH)
-
-    sibling = s + 1 - 2 * lax.rem(s, 2)
-    signal(sibling)
-    pl.when(q > 0)(lambda: signal(s - 2))
-    pl.when(q < nc - 1)(lambda: signal(s + 2))
-    pl.semaphore_wait(barrier, 1 + jnp.where(q > 0, 1, 0) + jnp.where(q < nc - 1, 1, 0))
-    return sibling
-
 def near_first(i, q, nc):
     short = jnp.where(q <= nc - 1 - q, q, nc - 1 - q)
     far = jnp.where(q <= nc - 1 - q, i, nc - 1 - i)
@@ -441,7 +427,7 @@
 
 def weights_kernel(n, rows, qo, kv, xg, wd_hbm, ad_hbm, bd_hbm, x_hbm, gain_ref, aa_hbm, ag_hbm,
                    wa, gz, near, sq_ref, gram_ref, u_hbm, inner_ref,
-                   wd, ad_ref, bd_ref, x_ref, aa_ref, ag_ref, local, edge, a_in, a_sib_in, a_out, a_sib_out, z_in, z_out):
+                   wd, ad_ref, bd_ref, x_ref, aa_ref, ag_ref, own_ref, cols_ref, local, edge, a_in, a_sib_in, a_out, a_sib_out, z_in, z_out):
     nc, half = n // 2, rows // 2
     others = half - 1
     units = gz.shape[-1]
@@ -520,11 +506,14 @@
     def own_blocks(part, out):
         for source, i, start in blocks:
             columns_of = pl.ds(start, source.shape[-1])
-            out(source.at[i, part], wa.at[i, s, part, :, columns_of])
+            out(source.at[i, part], i, columns_of)
 
     def own_line(sem, target):
         own_blocks(
-            r, lambda src, dst: remote(src, dst, sem, a_in.at[q, LINE], r, target).start()
+            r,
+            lambda src, i, cols: remote(
+                src, wa.at[i, s, r, :, cols], sem, a_in.at[q, LINE], r, target
+            ).start(),
         )
 
     pl.when(q > 0)(lambda: own_line(edge.at[0], s - 2))
@@ -535,11 +524,23 @@
     sib_g = lambda: remote(
         xg.at[:, :, :, columns(sibling)], near.at[:, c], edge.at[4], edge.at[5], r, sibling
     )
-    keep_a = pltpu.make_async_copy(whole_block, whole_block, local.at[0])
-    keep_g = pltpu.make_async_copy(xg.at[:, :, :, columns(s)], near.at[:, c], local.at[1])
+    keep_a = pltpu.make_async_copy(own_ref, whole_block, local.at[0])
+    keep_g = pltpu.make_async_copy(cols_ref, near.at[:, c], local.at[1])
     all_parts = pl.ds(0, rows)
-    own_blocks(all_parts, lambda src, dst: remote(src, dst, edge.at[2], edge.at[3], r, sibling).start())
-    own_blocks(all_parts, lambda src, dst: pltpu.make_async_copy(src, dst, local.at[0]).start())
+    own_blocks(
+        all_parts,
+        lambda src, i, cols: remote(
+            src, wa.at[i, s, :, :, cols], edge.at[2], edge.at[3], r, sibling
+        ).start(),
+    )
+    own_blocks(
+        all_parts,
+        lambda src, i, cols: pltpu.make_async_copy(
+            src, own_ref.at[i, :, :, cols], local.at[9]
+        ).start(),
+    )
+    take_cols = pltpu.make_async_copy(xg.at[:, :, :, columns(s)], cols_ref, local.at[10])
+    take_cols.start()
     takes = [
         pltpu.make_async_copy(src, dst, local.at[3 + i])
         for i, (src, dst) in enumerate(
@@ -550,6 +551,10 @@
         cp.start()
     for cp in takes:
         cp.wait()
+    pltpu.make_async_copy(own_ref, own_ref, local.at[9]).wait()
+    keep_a.start()
+    take_cols.wait()
+    keep_g.start()
     low = jnp.bfloat16
     v = x_ref[...].astype(jnp.float32)
     u = (v * unit_rms(v) * gain_ref[...]).astype(low)
@@ -589,7 +594,6 @@
         for core in range(2):
             z_send(p, core).start()
     sib_g().start()
-    keep_g.start()
     down_squares()
     keep_u.wait()
     for p in order[1:]:
@@ -657,7 +661,8 @@
         in_specs=[anywhere] * 7 + [vmem] + [anywhere] * 2,
         out_specs=(anywhere,) * 3 + (vmem,) * 2 + (anywhere, vmem),
         scratch_shapes=[pltpu.VMEM(v.shape, v.dtype) for v in (wd, ad, bd, x, aa, ag)]
-        + [dma((9,)), dma((6,))]
+        + [pltpu.VMEM((2, rows, part, cols), low), pltpu.VMEM((2, rows, part, units), low)]
+        + [dma((11,)), dma((6,))]
         + [dma((nc, kinds))] * 4
         + [dma((nc, 2))] * 2,
         compiler_params=pltpu.CompilerParams(
@@ -675,16 +680,19 @@
     nc = n // 2
     sources = refs[: count + len(shared[0])]
     outs = refs[len(sources) : 2 * len(sources) - len(shared[0]) + len(shared[1])]
-    local_sem, to_sib, to_left, to_right, recv, share_out, share_in = refs[len(sources) + len(outs) :]
+    scratch = refs[len(sources) + len(outs) :]
+    held_here = scratch[:count]
+    local_sem, to_sib, to_left, to_right, recv, share_out, share_in = scratch[count:]
     xs, held, swapped = sources[:count], sources[count:], outs[count:]
     s, q, c = place_in_seq()
     sibling = s + 1 - 2 * c
     r, b_row, a_row, _ = place_in_rows(rows)
     greet_all(n, rows)
-    locals_ = [
-        pltpu.make_async_copy(xs[k], outs[k].at[s], local_sem.at[k]) for k in range(count)
+    takes = [pltpu.make_async_copy(xs[k], held_here[k], local_sem.at[0, k]) for k in range(count)]
+    keeps = [
+        pltpu.make_async_copy(held_here[k], outs[k].at[s], local_sem.at[1, k]) for k in range(count)
     ]
-    for cp in locals_:
+    for cp in takes:
         cp.start()
 
     def copy(k, src, slot, sems, target):
@@ -705,6 +713,9 @@
     for p in order[1:]:
         for i in range(len(shared[1])):
             share(i, p).start()
+    for take, keep in zip(takes, keeps):
+        take.wait()
+        keep.start()
     for p in order[1:]:
         slot = 2 * p + c
         for k in range(count):
@@ -717,7 +728,7 @@
                 lambda k=k, src=src, slot=slot: copy(k, src, slot, to_left, s - 2).start()
             )
             copy(k, src, slot, to_sib, sibling).start()
-    for cp in locals_:
+    for cp in keeps:
         cp.wait()
     for p in range(nc):
         mine, theirs = 2 * p + c, 2 * p + 1 - c
@@ -751,130 +762,15 @@
         out_shape=tuple(outs),
         in_specs=[anywhere] * (count + len(held)),
         out_specs=(anywhere,) * len(outs),
-        scratch_shapes=[dma((count,))] + [dma((count, n))] * 4 + [sems] * 2,
+        scratch_shapes=[pltpu.VMEM(a.shape, a.dtype) for a in arrays]
+        + [dma((2, count))]
+        + [dma((count, n))] * 4
+        + [sems] * 2,
         compiler_params=pltpu.CompilerParams(collective_id=collective_id, has_side_effects=True),
         cost_estimate=pl.CostEstimate(flops=0, transcendentals=0, bytes_accessed=nbytes * n * 20),
         name="gather_seq",
     )(*arrays, *held)
     return got[:count], got[count:]
-
-def scatter_kernel(n, x_ref, o_ref, own, sib, from_left, from_right,
-                   load_sem, to_sib, sib_in, to_right, right_in, to_left, left_in):
-    nc = n // 2
-    s, q, c = place_in_seq()
-    sibling = greet(nc, q, s)
-    theirs = 1 - c
-
-    def load(p):
-        return pltpu.make_async_copy(x_ref.at[2 * p + c], own.at[p], load_sem.at[p])
-
-    def to_sibling(p):
-        return pltpu.make_async_remote_copy(
-            src_ref=x_ref.at[2 * p + theirs],
-            dst_ref=sib.at[p],
-            send_sem=to_sib.at[p],
-            recv_sem=sib_in.at[p],
-            device_id={"seq": sibling},
-            device_id_type=MESH,
-        )
-
-    def rightward(p, target):
-        return pltpu.make_async_remote_copy(
-            src_ref=own.at[p],
-            dst_ref=from_left.at[p],
-            send_sem=to_right.at[p],
-            recv_sem=right_in.at[p],
-            device_id={"seq": target},
-            device_id_type=MESH,
-        )
-
-    def leftward(p, target):
-        return pltpu.make_async_remote_copy(
-            src_ref=own.at[p],
-            dst_ref=from_right.at[p],
-            send_sem=to_left.at[p],
-            recv_sem=left_in.at[p],
-            device_id={"seq": target},
-            device_id_type=MESH,
-        )
-
-    order = []
-    for t in range(nc):
-        for p in (nc - 1 - t, t):
-            if p not in order:
-                order.append(p)
-    for p in order:
-        to_sibling(p).start()
-        load(p).start()
-
-    f32 = jnp.float32
-    for p in order:
-        load(p).wait()
-        to_sibling(p).wait_recv()
-
-        @pl.when(p > q)
-        def _(p=p):
-            @pl.when(q > 0)
-            def _():
-                rightward(p, s).wait_recv()
-                total = own[p].astype(f32) + sib[p].astype(f32) + from_left[p].astype(f32)
-                own[p] = total.astype(own.dtype)
-
-            @pl.when(q == 0)
-            def _():
-                own[p] = (own[p].astype(f32) + sib[p].astype(f32)).astype(own.dtype)
-
-            rightward(p, s + 2).start()
-
-        @pl.when(p < q)
-        def _(p=p):
-            @pl.when(q < nc - 1)
-            def _():
-                leftward(p, s).wait_recv()
-                total = own[p].astype(f32) + sib[p].astype(f32) + from_right[p].astype(f32)
-                own[p] = total.astype(own.dtype)
-
-            @pl.when(q == nc - 1)
-            def _():
-                own[p] = (own[p].astype(f32) + sib[p].astype(f32)).astype(own.dtype)
-
-            leftward(p, s - 2).start()
-
-    o_ref[...] = own[q].astype(f32) + sib[q].astype(f32)
-
-    @pl.when(q > 0)
-    def _():
-        rightward(q, s).wait_recv()
-        o_ref[...] += from_left[q].astype(f32)
-
-    @pl.when(q < nc - 1)
-    def _():
-        leftward(q, s).wait_recv()
-        o_ref[...] += from_right[q].astype(f32)
-
-    for p in range(nc):
-        to_sibling(p).wait_send()
-        pl.when(p > q)(lambda p=p: rightward(p, s).wait_send())
-        pl.when(p < q)(lambda p=p: leftward(p, s).wait_send())
-
-
-def scatter_seq(n, x, collective_id):
-    nc = n // 2
-    _, rows, cols = x.shape
-    dma = pltpu.SemaphoreType.DMA
-    buf = pltpu.VMEM((nc, rows, cols), x.dtype)
-    return pl.pallas_call(
-        functools.partial(scatter_kernel, n),
-        out_shape=jax.ShapeDtypeStruct((rows, cols), jnp.float32),
-        in_specs=[pl.BlockSpec(memory_space=pltpu.HBM)],
-        out_specs=pl.BlockSpec(memory_space=pltpu.VMEM),
-        scratch_shapes=[buf] * 4 + [dma((nc,))] * 7,
-        compiler_params=pltpu.CompilerParams(
-            collective_id=collective_id, has_side_effects=True, vmem_limit_bytes=32 << 20
-        ),
-        cost_estimate=pl.CostEstimate(flops=0, transcendentals=0, bytes_accessed=1 << 20),
-        name="scatter_seq",
-    )(*in_hbm(x))
 
 def swap_halves(x):
     return pltpu.roll(x.astype(jnp.float32), HEAD_DIM, 1)
@@ -1209,9 +1105,9 @@
             gm_ref[g] += jnp.sum(grads[g] * before[g], axis=0, keepdims=True)
             gb_ref[g] += SCALE * dot_tn(inner[g], gb[g])
 
-        pl.when(starts_flow(p))(lambda: pass_on(p))
         last = by_distance(nc - i, q, nc)
-        pl.when((i > 0) & jnp.logical_not(starts_flow(last)))(lambda: pass_on(last))
+        pl.when((i > 0) & (i < nc - 1) & jnp.logical_not(starts_flow(last)))(lambda: pass_on(last))
+        pl.when(starts_flow(p) | (i == nc - 2))(lambda: pass_on(p))
         return carry
 
     lax.fori_loop(0, nc, step, 0)
@@ -1360,8 +1256,218 @@
         name="feed_forward",
     )(*pieces, u, inner, gy0, gy1, wd, a, b, m, ad, bd, md, sq, gram)
 
-def reduce_kernel(n, rows, ga_qkv, ga_o, gb_qkv, gb_o, ga_gu, gb_d, gm_qkv, gm_o, gm_d, gb_gu, gm_gu, n_gu, ga_d,
-                  whole, units_all, part, from_sib, mid, from_rows, from_line, line_out, units, units_in,
+def greet_cross(n, rows, wait=True):
+    s, r = lax.axis_index("seq"), lax.axis_index("rows")
+    barrier = pltpu.get_barrier_semaphore()
+    for t in range(1, n):
+        pl.semaphore_signal(barrier, inc=1, device_id=(r, lax.rem(s + t, n)), device_id_type=MESH)
+    for t in range(1, rows):
+        pl.semaphore_signal(barrier, inc=1, device_id=(lax.rem(r + t, rows), s), device_id_type=MESH)
+    if wait:
+        pl.semaphore_wait(barrier, n + rows - 2)
+
+
+def scatter_kernel(n, rows, x_ref, gb_gu, gm_gu, n_gu, ga_d, o_ref, units_all, own, sib, from_left, from_right,
+                   units, units_in, load_sem, to_sib, sib_in, to_right, right_in, to_left, left_in,
+                   row_out, row_in, back_send, back_in, wide_send, wide_in, pass_send, pass_in):
+    nc = n // 2
+    s, q, c = place_in_seq()
+    sibling = s + 1 - 2 * c
+    theirs = 1 - c
+    r = lax.axis_index("rows")
+    greet_cross(n, rows)
+    f32, low = jnp.float32, jnp.bfloat16
+    unit_rows, size = units.shape[1:]
+
+    def load(p):
+        return pltpu.make_async_copy(x_ref.at[2 * p + c], own.at[p], load_sem.at[p])
+
+    def to_sibling(p):
+        return pltpu.make_async_remote_copy(
+            src_ref=x_ref.at[2 * p + theirs],
+            dst_ref=sib.at[p],
+            send_sem=to_sib.at[p],
+            recv_sem=sib_in.at[p],
+            device_id={"seq": sibling},
+            device_id_type=MESH,
+        )
+
+    def rightward(p, target):
+        return pltpu.make_async_remote_copy(
+            src_ref=own.at[p],
+            dst_ref=from_left.at[p],
+            send_sem=to_right.at[p],
+            recv_sem=right_in.at[p],
+            device_id={"seq": target},
+            device_id_type=MESH,
+        )
+
+    def leftward(p, target):
+        return pltpu.make_async_remote_copy(
+            src_ref=own.at[p],
+            dst_ref=from_right.at[p],
+            send_sem=to_left.at[p],
+            recv_sem=left_in.at[p],
+            device_id={"seq": target},
+            device_id_type=MESH,
+        )
+
+    order = []
+    for t in range(nc):
+        for p in (nc - 1 - t, t):
+            if p not in order:
+                order.append(p)
+    for p in order:
+        to_sibling(p).start()
+        load(p).start()
+
+    n_high = [n_gu[g].astype(low).astype(f32) for g in range(2)]
+    n_rest = [n_gu[g] - n_high[g] for g in range(2)]
+    tops = jnp.concatenate(
+        [gm_gu[0], gm_gu[1]]
+        + [v * (1.0 / rows) for v in (n_high[0], n_rest[0], n_high[1], n_rest[1])]
+        + [jnp.zeros((2, size), f32)],
+        axis=0,
+    )
+    blocks = [gb_gu[0][:8], gb_gu[0][8:], gb_gu[1][:8], gb_gu[1][8:], ga_d[:8], ga_d[8:], tops, jnp.zeros((8, size), f32)]
+    per = unit_rows // 8
+    for j in range(rows):
+        units[j] = jnp.concatenate(blocks[per * j : per * (j + 1)], axis=0).astype(low)
+
+    def member(t):
+        return lax.rem(r + t + rows, rows)
+
+    def chip(t):
+        return lax.rem(q + t + nc, nc)
+
+    def unit_send(t):
+        return remote(units.at[member(t)], units_in.at[t], row_out.at[t], row_in.at[t], member(t), s)
+
+    def unit_back(t, slot):
+        place = units_all.at[r, c, slot]
+        return remote(place, place, back_send.at[t], back_in.at[t], r, 2 * chip(t) + c)
+
+    def unit_wide(t, row):
+        place = units_all.at[row, c]
+        return remote(place, place, wide_send.at[t], wide_in.at[t], member(t), s)
+
+    def unit_hand(t, row, core):
+        place = units_all.at[row, core]
+        return remote(place, place, pass_send.at[t], pass_in.at[t], r, sibling)
+
+    def sum_units():
+        total = units[r].astype(f32)
+        for t in range(1, rows):
+            unit_send(t).wait_recv()
+            total = total + units_in[t].astype(f32)
+        units_all[r, c, q] = total.astype(low)
+        for t in range(1, nc):
+            unit_back(t, q).start()
+
+    def spread_units():
+        for t in range(1, nc):
+            unit_back(t, chip(-t)).wait_recv()
+        for t in range(1, rows):
+            unit_wide(t, r).start()
+        unit_hand(0, r, c).start()
+
+    for t in range(1, rows):
+        unit_send(t).start()
+    for step, p in enumerate(order):
+        if step == 1:
+            sum_units()
+        if step == nc // 2:
+            spread_units()
+        load(p).wait()
+        to_sibling(p).wait_recv()
+
+        @pl.when(p > q)
+        def _(p=p):
+            @pl.when(q > 0)
+            def _():
+                rightward(p, s).wait_recv()
+                total = own[p].astype(f32) + sib[p].astype(f32) + from_left[p].astype(f32)
+                own[p] = total.astype(own.dtype)
+
+            @pl.when(q == 0)
+            def _():
+                own[p] = (own[p].astype(f32) + sib[p].astype(f32)).astype(own.dtype)
+
+            rightward(p, s + 2).start()
+
+        @pl.when(p < q)
+        def _(p=p):
+            @pl.when(q < nc - 1)
+            def _():
+                leftward(p, s).wait_recv()
+                total = own[p].astype(f32) + sib[p].astype(f32) + from_right[p].astype(f32)
+                own[p] = total.astype(own.dtype)
+
+            @pl.when(q == nc - 1)
+            def _():
+                own[p] = (own[p].astype(f32) + sib[p].astype(f32)).astype(own.dtype)
+
+            leftward(p, s - 2).start()
+
+    o_ref[...] = own[q].astype(f32) + sib[q].astype(f32)
+
+    @pl.when(q > 0)
+    def _():
+        rightward(q, s).wait_recv()
+        o_ref[...] += from_left[q].astype(f32)
+
+    @pl.when(q < nc - 1)
+    def _():
+        leftward(q, s).wait_recv()
+        o_ref[...] += from_right[q].astype(f32)
+
+    for t in range(1, rows):
+        unit_wide(t, member(-t)).wait_recv()
+        unit_hand(t, member(-t), c).start()
+    for t in range(rows):
+        unit_hand(t, member(-t), theirs).wait_recv()
+        unit_hand(t, member(-t), c).wait_send()
+    for t in range(1, rows):
+        unit_send(t).wait_send()
+        unit_wide(t, r).wait_send()
+    for t in range(1, nc):
+        unit_back(t, q).wait_send()
+    for p in range(nc):
+        to_sibling(p).wait_send()
+        pl.when(p > q)(lambda p=p: rightward(p, s).wait_send())
+        pl.when(p < q)(lambda p=p: leftward(p, s).wait_send())
+
+
+def scatter_seq(n, rows, x, own_units, collective_id):
+    nc = n // 2
+    _, height, cols = x.shape
+    size = own_units[3].shape[1]
+    unit_rows = 64 // rows
+    low = jnp.bfloat16
+    dma = pltpu.SemaphoreType.DMA
+    buf = pltpu.VMEM((nc, height, cols), x.dtype)
+    small = pltpu.VMEM((rows, unit_rows, size), low)
+    vmem = pl.BlockSpec(memory_space=pltpu.VMEM)
+    return pl.pallas_call(
+        functools.partial(scatter_kernel, n, rows),
+        out_shape=(
+            jax.ShapeDtypeStruct((height, cols), jnp.float32),
+            jax.ShapeDtypeStruct((rows, 2, nc, unit_rows, size), low),
+        ),
+        in_specs=[pl.BlockSpec(memory_space=pltpu.HBM)] + [vmem] * 4,
+        out_specs=(vmem,) * 2,
+        scratch_shapes=[buf] * 4 + [small] * 2 + [dma((nc,))] * 7
+        + [dma((rows,))] * 2 + [dma((nc,))] * 2 + [dma((rows,))] * 4,
+        compiler_params=pltpu.CompilerParams(
+            collective_id=collective_id, has_side_effects=True, vmem_limit_bytes=32 << 20
+        ),
+        cost_estimate=pl.CostEstimate(flops=0, transcendentals=0, bytes_accessed=1 << 20),
+        name="scatter_seq",
+    )(*in_hbm(x), *own_units)
+
+
+def reduce_kernel(n, rows, ga_qkv, ga_o, gb_qkv, gb_o, ga_gu, gb_d, gm_qkv, gm_o, gm_d,
+                  whole, part, from_sib, mid, from_rows, from_line, line_out,
                   sib_out, sib_in, row_out, row_in, line_send, line_in, back_send, back_in, wide_send, wide_in,
                   pass_send, pass_in):
     nc = n // 2
@@ -1374,15 +1480,8 @@
     kv = (gb_qkv.shape[1] - width) // 2
     height = part.shape[2]
     piece = height // nc
-    unit_rows = units.shape[1]
-    size = units.shape[2]
-
-    barrier = pltpu.get_barrier_semaphore()
-    for t in range(1, n):
-        pl.semaphore_signal(barrier, inc=1, device_id=(r, lax.rem(s + t, n)), device_id_type=MESH)
-    for t in range(1, rows):
-        pl.semaphore_signal(barrier, inc=1, device_id=(lax.rem(r + t, rows), s), device_id_type=MESH)
-
+
+    greet_cross(n, rows, wait=False)
     gb_k, gb_v = gb_qkv[:, width : width + kv], gb_qkv[:, width + kv :]
     small = jnp.concatenate(
         [
@@ -1401,19 +1500,7 @@
             part[j % 2, j // 2, 16 * g : 16 * g + 16] = value[:, cols * j : cols * (j + 1)].astype(low)
         if height > 160:
             part[j % 2, j // 2, 160:] = jnp.zeros((height - 160, cols), low)
-    n_high = [n_gu[g].astype(low).astype(f32) for g in range(2)]
-    n_rest = [n_gu[g] - n_high[g] for g in range(2)]
-    tops = jnp.concatenate(
-        [gm_gu[0], gm_gu[1]]
-        + [v * (1.0 / rows) for v in (n_high[0], n_rest[0], n_high[1], n_rest[1])]
-        + [jnp.zeros((2, size), f32)],
-        axis=0,
-    )
-    blocks = [gb_gu[0][:8], gb_gu[0][8:], gb_gu[1][:8], gb_gu[1][8:], ga_d[:8], ga_d[8:], tops, jnp.zeros((8, size), f32)]
-    per = unit_rows // 8
-    for j in range(rows):
-        units[j] = jnp.concatenate(blocks[per * j : per * (j + 1)], axis=0).astype(low)
-    pl.semaphore_wait(barrier, n - 1 + rows - 1)
+    pl.semaphore_wait(pltpu.get_barrier_semaphore(), n + rows - 2)
 
     def to_sibling():
         return remote(part.at[1 - c], from_sib, sib_out.at[0], sib_in.at[0], r, sibling)
@@ -1422,10 +1509,7 @@
         return lax.rem(r + t + rows, rows)
 
     def row_send(t):
-        return remote(mid.at[member(t)], from_rows.at[t], row_out.at[0, t], row_in.at[0, t], member(t), s)
-
-    def unit_send(t):
-        return remote(units.at[member(t)], units_in.at[t], row_out.at[1, t], row_in.at[1, t], member(t), s)
+        return remote(mid.at[member(t)], from_rows.at[t], row_out.at[t], row_in.at[t], member(t), s)
 
     def chip(t):
         return lax.rem(q + t + nc, nc)
@@ -1434,40 +1518,20 @@
         return remote(line_out.at[chip(t)], from_line.at[t], line_send.at[t], line_in.at[t], r, 2 * chip(t) + c)
 
     def back(t, slot):
-        return remote(whole.at[r, c, slot], whole.at[r, c, slot], back_send.at[0, t], back_in.at[0, t], r, 2 * chip(t) + c)
-
-    def unit_back(t, slot):
-        return remote(
-            units_all.at[r, c, slot], units_all.at[r, c, slot], back_send.at[1, t], back_in.at[1, t], r, 2 * chip(t) + c
-        )
+        return remote(whole.at[r, c, slot], whole.at[r, c, slot], back_send.at[t], back_in.at[t], r, 2 * chip(t) + c)
 
     def wide(t, row):
-        return remote(whole.at[row, c], whole.at[row, c], wide_send.at[0, t], wide_in.at[0, t], member(t), s)
-
-    def unit_wide(t, row):
-        return remote(units_all.at[row, c], units_all.at[row, c], wide_send.at[1, t], wide_in.at[1, t], member(t), s)
+        return remote(whole.at[row, c], whole.at[row, c], wide_send.at[t], wide_in.at[t], member(t), s)
 
     def hand(t, row, core):
-        return remote(whole.at[row, core], whole.at[row, core], pass_send.at[0, t], pass_in.at[0, t], r, sibling)
-
-    def unit_hand(t, row, core):
-        return remote(units_all.at[row, core], units_all.at[row, core], pass_send.at[1, t], pass_in.at[1, t], r, sibling)
+        return remote(whole.at[row, core], whole.at[row, core], pass_send.at[t], pass_in.at[t], r, sibling)
 
     to_sibling().start()
-    for t in range(1, rows):
-        unit_send(t).start()
     to_sibling().wait_recv()
     for t in range(rows):
         mid[member(t)] = (part[c, member(t)].astype(f32) + from_sib[member(t)].astype(f32)).astype(low)
         if t:
             row_send(t).start()
-    unit_sum = units[r].astype(f32)
-    for t in range(1, rows):
-        unit_send(t).wait_recv()
-        unit_sum = unit_sum + units_in[t].astype(f32)
-    units_all[r, c, q] = unit_sum.astype(low)
-    for t in range(1, nc):
-        unit_back(t, q).start()
     total = mid[r].astype(f32)
     for t in range(1, rows):
         row_send(t).wait_recv()
@@ -1485,54 +1549,40 @@
         back(t, q).start()
     for t in range(1, nc):
         back(t, chip(-t)).wait_recv()
-        unit_back(t, chip(-t)).wait_recv()
     for t in range(1, rows):
         wide(t, r).start()
-        unit_wide(t, r).start()
     hand(0, r, c).start()
-    unit_hand(0, r, c).start()
     for t in range(1, rows):
         wide(t, member(-t)).wait_recv()
         hand(t, member(-t), c).start()
-        unit_wide(t, member(-t)).wait_recv()
-        unit_hand(t, member(-t), c).start()
     for t in range(rows):
         hand(t, member(-t), 1 - c).wait_recv()
-        unit_hand(t, member(-t), 1 - c).wait_recv()
 
     to_sibling().wait_send()
     for t in range(1, rows):
         row_send(t).wait_send()
-        unit_send(t).wait_send()
         wide(t, r).wait_send()
-        unit_wide(t, r).wait_send()
     for t in range(1, nc):
         line_part(t).wait_send()
         back(t, q).wait_send()
-        unit_back(t, q).wait_send()
     for t in range(rows):
         hand(t, member(-t), c).wait_send()
-        unit_hand(t, member(-t), c).wait_send()
-
-
-def sum_gradients(n, rows, full, own_units, collective_id):
+
+
+def sum_gradients(n, rows, full, collective_id):
     nc = n // 2
-    width, size = full[1].shape[1], own_units[3].shape[1]
+    width = full[1].shape[1]
     cols = width // (2 * rows)
     height = -(-160 // (8 * nc)) * 8 * nc
-    unit_rows = 64 // rows
     low = jnp.bfloat16
     vmem = pl.BlockSpec(memory_space=pltpu.VMEM)
     dma = pltpu.SemaphoreType.DMA
     block = (rows, height, cols)
     return pl.pallas_call(
         functools.partial(reduce_kernel, n, rows),
-        out_shape=(
-            jax.ShapeDtypeStruct((rows, 2, nc, height // nc, cols), low),
-            jax.ShapeDtypeStruct((rows, 2, nc, unit_rows, size), low),
-        ),
-        in_specs=[vmem] * 13,
-        out_specs=(vmem,) * 2,
+        out_shape=jax.ShapeDtypeStruct((rows, 2, nc, height // nc, cols), low),
+        in_specs=[vmem] * 9,
+        out_specs=vmem,
         scratch_shapes=[
             pltpu.VMEM((2, *block), low),
             pltpu.VMEM(block, low),
@@ -1540,17 +1590,15 @@
             pltpu.VMEM(block, low),
             pltpu.VMEM((nc, height // nc, cols), low),
             pltpu.VMEM((nc, height // nc, cols), low),
-            pltpu.VMEM((rows, unit_rows, size), low),
-            pltpu.VMEM((rows, unit_rows, size), low),
-            dma((1,)), dma((1,)), dma((2, rows)), dma((2, rows)), dma((nc,)), dma((nc,)),
-            dma((2, nc)), dma((2, nc)), dma((2, rows)), dma((2, rows)), dma((2, rows)), dma((2, rows)),
+            dma((1,)), dma((1,)), dma((rows,)), dma((rows,)), dma((nc,)), dma((nc,)),
+            dma((nc,)), dma((nc,)), dma((rows,)), dma((rows,)), dma((rows,)), dma((rows,)),
         ],
         compiler_params=pltpu.CompilerParams(
             collective_id=collective_id, has_side_effects=True, vmem_limit_bytes=48 << 20
         ),
         cost_estimate=pl.CostEstimate(flops=0, transcendentals=0, bytes_accessed=1 << 20),
         name="sum_gradients",
-    )(*full, *own_units)
+    )(*full)
 
 
 def finish_kernel(n, rows, whole, units_all, x1, before_0, before_1, m_attn, n_attn, m_d, n_d, m_gu,
@@ -1615,25 +1663,25 @@
     o_stats[...] = stats
 
 
-def finish(n, rows, sums, x1, before_0, before_1, m_attn, n_attn, m_d, n_d, m_gu):
+def finish(n, rows, sums, units, x1, before_0, before_1, m_attn, n_attn, m_d, n_d, m_gu):
     tokens, width = x1.shape
     kv = (m_attn.shape[1] - 2 * width) // 2
-    units = m_gu.shape[1]
+    wide_units = m_gu.shape[1]
     shape = lambda *dims: pltpu.HBM(dims, jnp.float32)
     vmem = pl.BlockSpec(memory_space=pltpu.VMEM)
     return pl.pallas_call(
         functools.partial(finish_kernel, n, rows),
         out_shape=(
             pltpu.HBM((tokens, width), jnp.bfloat16), shape(4, 16, width), shape(2, 16, width), shape(2, 16, kv),
-            shape(width), shape(2, kv), shape(width), shape(2, 16, width), shape(2, 16, units), shape(2, units),
-            shape(16, units), shape(16, width), shape(width), shape(7, 2),
+            shape(width), shape(2, kv), shape(width), shape(2, 16, width), shape(2, 16, wide_units), shape(2, wide_units),
+            shape(16, wide_units), shape(16, width), shape(width), shape(7, 2),
         ),
         in_specs=[vmem] * 2 + [pl.BlockSpec()] * 8,
-        scratch_shapes=[pltpu.VMEM((2, units), jnp.float32)],
+        scratch_shapes=[pltpu.VMEM((2, wide_units), jnp.float32)],
         compiler_params=pltpu.CompilerParams(vmem_limit_bytes=40 << 20),
         cost_estimate=pl.CostEstimate(flops=0, transcendentals=0, bytes_accessed=8 << 20),
         name="finish",
-    )(*sums, *in_hbm(x1, before_0, before_1), m_attn, n_attn, m_d, n_d, m_gu)
+    )(sums, units, *in_hbm(x1, before_0, before_1), m_attn, n_attn, m_d, n_d, m_gu)
 
 def local(
     layer_input,
@@ -1733,7 +1781,10 @@
         n_attn, cross_attn, weights,
     )
     gq, gkv = attend_back(q, kv_all, shares, grad_att.reshape(q.shape))
-    gkv = scatter_seq(seq_size, gkv.reshape(seq_size, token_count, 2 * kv_width), 5)
+    gkv, units = scatter_seq(
+        seq_size, rows_size, gkv.reshape(seq_size, token_count, 2 * kv_width),
+        (gb_gu, gm_gu, n_gu, ga_d), 5,
+    )
     gkv, down_1, before_0 = lax.optimization_barrier((gkv, down_1, before_0))
     before_1 = lax.psum_scatter(flat(down_1), "seq", scatter_dimension=0, tiled=True)
     grad_inputs, ga_qkv, gb_qkv, gm_qkv = qkv_back(
@@ -1744,11 +1795,10 @@
     sums = sum_gradients(
         seq_size, rows_size,
         (ga_qkv, ga_o, gb_qkv, gb_o, ga_gu, gb_d, gm_qkv, gm_o, gm_d),
-        (gb_gu, gm_gu, n_gu, ga_d),
         6,
     )
     layer_result, *summed, stats = finish(
-        seq_size, rows_size, sums, x1, before_0, before_1, m_attn, n_attn, m_d, n_d, gate_up_magnitude
+        seq_size, rows_size, sums, units, x1, before_0, before_1, m_attn, n_attn, m_d, n_d, gate_up_magnitude
     )
     shape = (pair_rows, span_len, model_width)
     return (layer_result.reshape(shape), grad_inputs.reshape(shape), *summed, stats)

time: 434 us -> 419 us (0.965)
  Pallas kernels: 411 us -> 396 us
    pallas_call x1, Pallas kernels: 118 us -> 103 us  [gather_weights(): pl.pallas_call(functools.partial(weights_kernel, n, rows), out_shape=(plt...]
    pallas_call x2, Pallas kernels: 67.5 us -> 77.3 us  [the longest x1 41.1 us: scatter_seq(): pl.pallas_call(functools.partial(scatter_kernel, n, rows), out_shape=(jax...]
    pallas_call x1, Pallas kernels: 74.4 us -> 64.7 us  [feed_forward(): pl.pallas_call(kernel, out_shape=(shape((tokens, width), f32), pltpu.HBM(...]
  transfers between devices with their start and end apart: 4 -> 4, of which waited for: 0 -> 0; matrix products, arithmetic and copies ran while one was open for 0% -> 0% of each run, Pallas kernels for 50% -> 54%
where the time goes in v8:
time: 419 us; the launch traced here: 418 us
  Pallas kernels  396 us (95%)
  between operations  14.8 us (4%)
  local copies, waits for them, and re-layouts  5.78 us (1%)
    pallas_call x1, Pallas kernels, gather_weights(): pl.pallas_call(functools.partial(weights_kernel, n, rows), out_shape=(plt...  103 us
    pallas_call x2, Pallas kernels, gather_seq(): pl.pallas_call(functools.partial(gather_kernel, n, rows, count, (range(le...  80 us
    pallas_call x1, Pallas kernels, feed_forward(): pl.pallas_call(kernel, out_shape=(shape((tokens, width), f32), pltpu.HBM(...  64.7 us
    pallas_call x1, Pallas kernels, scatter_seq(): pl.pallas_call(functools.partial(scatter_kernel, n, rows), out_shape=(jax...  41.1 us
    pallas_call x1, Pallas kernels, sum_gradients(): pl.pallas_call(functools.partial(reduce_kernel, n, rows), out_shape=jax.S...  36.2 us
    pallas_call x1, Pallas kernels, project_qkv(): pl.pallas_call(functools.partial(project_kernel, (q_tiles, last)), out_sh...  15.6 us
    pallas_call x1, Pallas kernels, qkv_back(): pl.pallas_call(qkv_back_kernel, out_shape=(pltpu.HBM((rows, width), f32),...  12.3 us
    pallas_call x1, Pallas kernels, attend_back(): pl.pallas_call(attend_back_kernel, out_shape=(pltpu.HBM(q.shape, jnp.bflo...  11.4 us
  transfers between devices with their start and end apart: 4, of which 0 were waited for; matrix products, arithmetic and copies ran while one was open for 0% of the time, Pallas kernels for 54%

profile of v8, /device:TPU:0, one launch (start us, length us, event | category | flops | bytes accessed | tf_op | source)
XLA Modules:
  0.0 417.9 jit_solution(15094530310340397605)
XLA Ops:
  7.2 0.0 all-gather.5.cloned.1.call-start
  7.2 0.8 fusion
  8.0 1.9 slice_bitcast_fusion
  9.9 0.0 copy-start.14
  9.9 102.7 %gather_weights.1 = (bf16[2,8,4,64,2560]{4,3,2,1,0:T(8,128)(2,1)}, bf16[2,8,64,1024]{3,2,1,0:T(8,128)(2,1)}, bf16[2,2,4,64,1024]{4,3,2,1,0:T(8,128)(2,1)}, f32[1...) custom-call(bf16[2,4,64,2048]{3,2,1,0:T(8,128)(2,1)} %bitcast.68, ...), custom_call_target="tpu_custom_call" | custom-call | bytes 262144000 | tf_op jit(solution)/shard_map/gather_weights/pallas_call | solution.py:650
  112.7 0.0 copy-start.7
  112.7 0.0 copy-start.11
  112.7 0.0 all-gather.5.cloned.1.call-update
  112.7 0.0 all-gather.7.cloned.1.call-start
  112.8 0.1 multiply_sine_fusion
  113.0 0.1 tile.21
  113.1 0.1 copy.38.sin_ref
  113.3 0.1 tile.9
  113.4 0.1 copy.37.cos_ref
  113.5 0.0 copy-done.18
  113.5 0.0 copy-done.16
  113.5 0.0 copy-done.17
  113.6 0.0 copy-done.15
  113.6 0.0 copy-done.14
  113.6 0.8 pad_maximum_fusion.b_ref
  114.4 15.6 %project_qkv.1 = (f32[128,3072]{1,0:T(8,128)}, bf16[128,2048]{1,0:T(8,128)(2,1)}, bf16[128,1024]{1,0:T(8,128)(2,1)}, f32[1,5120]{1,0:T(1,128)}, f32[16,5120]{1,0:T(8,128)}) custom-call(bf16[128,2048]{1,0:T(8,128)(2,1)} %get-tuple-element.88.u_ref, bf16[3,128,16]{2,1,0:T(8,128)(2,1)S(1)} %get-tuple-element.89.inner_ref, ...), custom_call_target="tpu_custom_call" | custom-call | flops 2684354560 | bytes 20971520 | tf_op jit(solution)/shard_map/project_qkv/pallas_call | solution.py:131
  130.0 0.0 copy-start.19
  130.0 32.6 %gather_seq.2 = (bf16[8,128,1024]{2,1,0:T(8,128)(2,1)}, f32[8,1,2048]{2,1,0:T(1,128)}, bf16[8,64,1024]{2,1,0:T(8,128)(2,1)}, bf16[8,64,1024]{2,1,0:T(8,128)(2,1)}) custom-call(bf16[128,1024]{1,0:T(8,128)(2,1)} %get-tuple-element.94.refs_0_, f32[1,2048]{1,0:T(1,128)} %copy-done.11, bf16[2,8,64,1024]{3,2,1,0:T(8,128)(2,1)} %get-tuple-element.96.refs_2_.refs_0_), custom_call_target="tpu_custom_call" | custom-call | bytes 43253760 | tf_op jit(solution)/shard_map/gather_seq/pallas_call | solution.py:760
  162.6 0.0 all-gather.7.cloned.1.call-update
  162.6 0.0 reduce-scatter.3.cloned.1.call-start
  163.3 0.0 copy-start.1
  163.3 11.1 %attend.1 = (bf16[2,64,2048]{2,1,0:T(8,128)(2,1)}, bf16[2,4,512,512]{3,2,1,0:T(8,128)(2,1)}) custom-call(s32[2]{0:T(128)S(1)} %broadcast_add_fusion.valid_ref, bf16[2,64,2048]{2,1,0:T(8,128)(2,1)} %bitcast.60, bf16[8,2,64,1024]{3,2,1,0:T(8,128)(2,1)} %bitcast.52, bf16[8,2,64,1024]{3,2,1,0:T(8,128)(2,1)} %bitcast.53), custom_call_target="tpu_custom_call" | custom-call | flops 1073741824 | bytes 8388608 | tf_op jit(solution)/shard_map/attend/pallas_call | solution.py:833
  174.4 0.0 copy-done.1
  174.4 7.8 %project_out.1 = (f32[128,2048]{1,0:T(8,128)}, f32[128,2048]{1,0:T(8,128)}, bf16[128,2048]{1,0:T(8,128)(2,1)}, bf16[128,128]{1,0:T(8,128)(2,1)}) custom-call(bf16[128,2048]{1,0:T(8,128)(2,1)} %bitcast.62, f32[4,16,2048]{2,1,0:T(8,128)} %a_ref.7, bf16[2,2048,2560]{2,1,0:T(8,128)(2,1)} %bitcast.48, f32[16,5120]{1,0:T(8,128)} %pad_maximum_fusion.b_ref, ...), custom_call_target="tpu_custom_call" | custom-call | flops 1073741824 | bytes 8388608 | tf_op jit(solution)/shard_map/project_out/pallas_call | solution.py:198
  182.3 47.4 %gather_seq.3 = (bf16[8,128,2048]{2,1,0:T(8,128)(2,1)}, bf16[8,128,128]{2,1,0:T(8,128)(2,1)}, bf16[8,64,1024]{2,1,0:T(8,128)(2,1)}, bf16[8,64,1024]{2,1,0:T(8,12...) custom-call(bf16[128,2048]{1,0:T(8,128)(2,1)} %get-tuple-element.105.refs_0_, ...), custom_call_target="tpu_custom_call" | custom-call | bytes 89128960 | tf_op jit(solution)/shard_map/gather_seq/pallas_call | solution.py:760
  229.7 0.0 all-gather.5.cloned.1.call-done
  229.7 0.0 all-gather.7.cloned.1.call-done
  229.7 64.7 %feed_forward.1 = (f32[128,2048]{1,0:T(8,128)}, bf16[8,64,2048]{2,1,0:T(8,128)(2,1)}, bf16[8,64,2048]{2,1,0:T(8,128)(2,1)}, f32[2,16,2048]{2,1,0:T(8,128)}, f32[...) custom-call(bf16[2,8,64,1024]{3,2,1,0:T(8,128)(2,1)} %get-tuple-elem, ...), custom_call_target="tpu_custom_call" | custom-call | flops 25769803776 | bytes 33554432 | tf_op jit(solution)/shard_map/feed_forward/pallas_call | solution.py:1219
  294.5 0.0 reduce-scatter.3.cloned.1.call-update
  294.5 0.0 reduce-scatter.5.cloned.1.call-start
  294.5 1.1 copy-done
  295.7 9.6 %out_back.1 = (f32[128,2048]{1,0:T(8,128)}, bf16[128,2048]{1,0:T(8,128)(2,1)}, f32[16,2048]{1,0:T(8,128)S(1)}, f32[16,2048]{1,0:T(8,128)S(1)}, f32[1,2048]{1,0:T(1,128)S(1)}) custom-call(f32[128,2048]{1,0:T(8,128)S(1)} %copy-done, f32[128,2048]{1,0:T(8,128)} %get-tuple-element.117.x1_ref.x1, f32[1,2048]{1,0:T(1,128)S(1)} %get-tuple-element.197.gain_ref, ...), custom_call_target="tpu_custom_call" | custom-call | bytes 1048576 | tf_op jit(solution)/shard_map/out_back/pallas_call | solution.py:269
  305.3 11.4 %attend_back.1 = (bf16[2,64,2048]{2,1,0:T(8,128)(2,1)}, bf16[8,2,64,1024]{3,2,1,0:T(8,128)(2,1)}) custom-call(bf16[2,64,2048]{2,1,0:T(8,128)(2,1)} %bitcast.61, bf16[8,2,64,1024]{3,2,1,0:T(8,128)(2,1)} %bitcast.54, bf16[8,2,64,1024]{3,2,1,0:T(8,128)(2,1)} %bitcast.55, bf16[2,4,512,512]{3,2,1,0:T(8,128)(2,1)} %get-tuple-element.99.p_ref, ...), custom_call_target="tpu_custom_call" | custom-call | bytes 1048576 | tf_op jit(solution)/shard_map/attend_back/pallas_call | solution.py:887
  316.8 41.1 %scatter_seq.1 = (f32[128,1024]{1,0:T(8,128)S(1)}, bf16[4,2,4,16,1024]{4,3,2,1,0:T(8,128)(2,1)S(1)}) custom-call(bf16[8,128,1024]{2,1,0:T(8,128)(2,1)} %bitcast.67, f32[2,16,1024]{2,1,0:T(8,128)S(1)} %copy-done.3, f32[2,1,1024]{2,1,0:T(1,128)S(1)} %copy-done.12, f32[2,1,1024]{2,1,0:T(1,128)S(1)} %copy-done.13, f32[16,1024]{1,0:T(8,128)S(1)} %copy-done.6), custom_call_target="tpu_custom_call" | custom-call | bytes 1048576 | tf_op jit(solution)/shard_map/scatter_seq/pallas_call | solution.py:1451
  357.9 0.0 reduce-scatter.3.cloned.1.call-done.before_0
  357.9 0.0 reduce-scatter.5.cloned.1.call-update
  358.0 0.0 copy-start.5
  358.0 0.0 copy-start.8
  358.0 12.3 %qkv_back.1 = (f32[128,2048]{1,0:T(8,128)}, f32[3,16,2048]{2,1,0:T(8,128)S(1)}, f32[16,3072]{1,0:T(8,128)S(1)}, f32[1,3072]{1,0:T(1,128)S(1)}) custom-call(bf16[128,2048]{1,0:T(8,128)(2,1)} %bitcast.69, f32[128,1024]{1,0:T(8,128)S(1)} %get-tuple-element.130.gkv_ref, f32[128,128]{1,0:T(8,128)S(1)} %copy.37.cos_ref, f32[128,128]{1,0:T(8,128)S(1)} %copy.38.sin_ref, ...), custom_call_target="tpu_custom_call" | custom-call | bytes 1048576 | tf_op jit(solution)/shard_map/qkv_back/pallas_call | solution.py:357
  370.3 36.2 %sum_gradients.1.whole = bf16[4,2,4,40,256]{4,3,2,1,0:T(8,128)(2,1)S(1)} custom-call(f32[3,16,2048]{2,1,0:T(8,128)S(1)} %get-tuple-element.133.ga_qkv, f32[16,2048]{1,0:T(8,128)S(1)} %get-tuple-element.134.ga_o, f32[16,3072]{1,0:T(8,128)S(1)} %get-tuple-element.135.gb_qkv, f32[16,2048]{1,0:T(8,128)S(1)} %get-tuple-element.136.gb_o, ...), custom_call_target="tpu_custom_call" | custom-call | bytes 1048576 | tf_op jit(solution)/shard_map/sum_gradients/pallas_call | solution.py:1581
  406.5 0.0 reduce-scatter.5.cloned.1.call-done.before_1
  406.5 3.4 finish.1
  410.0 1.3 copy.41
  (35 shorter events, 0.2 us)
Async XLA Ops:
  7.2 222.5 %all-gather.5.cloned.1.call-start = ((), (), s32[]{:S(2)}) async-start(), calls=%async_computation.4 | async-start | bytes 2359296 | tf_op jit(solution)/shard_map/all_gather | solution.py:1728
  9.9 103.6 %copy-start.18 = (f32[2,512]{1,0:T(2,128)S(1)}, f32[2,512]{1,0:T(2,128)}, u32[]{:S(2)}) copy-start(f32[2,512]{1,0:T(2,128)} %param.32) | copy-start | bytes 12292
  9.9 103.6 %copy-start.16 = (f32[2048]{0:T(1024)S(1)}, f32[2048]{0:T(1024)}, u32[]{:S(2)}) copy-start(f32[2048]{0:T(1024)} %param.33) | copy-start | bytes 24580
  9.9 103.6 %copy-start.17 = (f32[2048]{0:T(1024)S(1)}, f32[2048]{0:T(1024)}, u32[]{:S(2)}) copy-start(f32[2048]{0:T(1024)} %param.31) | copy-start | bytes 24580
  9.9 103.6 %copy-start.15 = (f32[2,16,512]{2,1,0:T(8,128)S(1)}, f32[2,16,512]{2,1,0:T(8,128)}, u32[]{:S(2)}) copy-start(f32[2,16,512]{2,1,0:T(8,128)} %param.30) | copy-start | bytes 196612
  9.9 103.7 %copy-start.14 = (f32[2,16,2048]{2,1,0:T(8,128)S(1)}, f32[2,16,2048]{2,1,0:T(8,128)}, u32[]{:S(2)}) copy-start(f32[2,16,2048]{2,1,0:T(8,128)} %param.29) | copy-start | bytes 786436
  112.7 17.3 %copy-start.7 = (bf16[7,32,16]{2,1,0:T(8,128)(2,1)}, bf16[7,32,16]{2,1,0:T(8,128)(2,1)S(1)}, u32[]{:S(2)}) copy-start(bf16[7,32,16]{2,1,0:T(8,128)(2,1)S(1)} %get-tuple-element.90.gram_ref.refs_20_) | copy-start | bytes 21508
  112.7 17.3 %copy-start.11 = (f32[1,2048]{1,0:T(1,128)}, f32[1,2048]{1,0:T(1,128)S(1)}, u32[]{:S(2)}) copy-start(f32[1,2048]{1,0:T(1,128)S(1)} %get-tuple-element.95.refs_1_) | copy-start | bytes 24580
  112.7 117.0 %all-gather.7.cloned.1.call-start = ((), (), s32[]{:S(2)}) async-start(), calls=%async_computation.5 | async-start | bytes 2359296 | tf_op jit(solution)/shard_map/all_gather | solution.py:1759
  130.0 33.3 %copy-start.19 = (s32[2]{0:T(128)S(1)}, s32[2]{0:T(128)}, u32[]{:S(2)}) copy-start(s32[2]{0:T(128)} %param.41) | copy-start | bytes 28
  162.6 195.3 %reduce-scatter.3.cloned.1.call-start = ((), (), s32[]{:S(2)}) async-start(), calls=%async_computation.2 | async-start | bytes 2359296 | tf_op jit(solution)/shard_map/reduce_scatter | solution.py:1777
  163.3 11.1 %copy-start.1 = (f32[1,5120]{1,0:T(1,128)S(1)}, f32[1,5120]{1,0:T(1,128)}, u32[]{:S(2)}) copy-start(f32[1,5120]{1,0:T(1,128)} %get-tuple-element.104.n_ref.n_attn) | copy-start | bytes 61444
  294.5 1.2 copy-start
  294.5 112.0 %reduce-scatter.5.cloned.1.call-start = ((), (), s32[]{:S(2)}) async-start(), calls=%async_computation.3 | async-start | bytes 2359296 | tf_op jit(solution)/shard_map/reduce_scatter | solution.py:1789
  305.3 11.4 %copy-start.3 = (f32[2,16,1024]{2,1,0:T(8,128)S(1)}, f32[2,16,1024]{2,1,0:T(8,128)}, u32[]{:S(2)}) copy-start(f32[2,16,1024]{2,1,0:T(8,128)} %get-tuple-element.123.gb_gu) | copy-start | bytes 393220
  305.3 11.4 %copy-start.6 = (f32[16,1024]{1,0:T(8,128)S(1)}, f32[16,1024]{1,0:T(8,128)}, u32[]{:S(2)}) copy-start(f32[16,1024]{1,0:T(8,128)} %get-tuple-element.126.ga_d) | copy-start | bytes 196612
  305.3 11.4 %copy-start.12 = (f32[2,1,1024]{2,1,0:T(1,128)S(1)}, f32[2,1,1024]{2,1,0:T(1,128)}, u32[]{:S(2)}) copy-start(f32[2,1,1024]{2,1,0:T(1,128)} %get-tuple-element.124.gm_gu) | copy-start | bytes 24580
  305.3 11.4 %copy-start.13 = (f32[2,1,1024]{2,1,0:T(1,128)S(1)}, f32[2,1,1024]{2,1,0:T(1,128)}, u32[]{:S(2)}) copy-start(f32[2,1,1024]{2,1,0:T(1,128)} %get-tuple-element.125.n_gu) | copy-start | bytes 24580
  357.9 12.3 %copy-start.2 = (f32[2,16,2048]{2,1,0:T(8,128)S(1)}, f32[2,16,2048]{2,1,0:T(8,128)}, u32[]{:S(2)}) copy-start(f32[2,16,2048]{2,1,0:T(8,128)} %get-tuple-element.137.ga_gu) | copy-start | bytes 786436
  357.9 12.3 %copy-start.4 = (f32[16,2048]{1,0:T(8,128)S(1)}, f32[16,2048]{1,0:T(8,128)}, u32[]{:S(2)}) copy-start(f32[16,2048]{1,0:T(8,128)} %get-tuple-element.138.gb_d) | copy-start | bytes 393220
  357.9 12.3 %copy-start.10 = (f32[1,2048]{1,0:T(1,128)S(1)}, f32[1,2048]{1,0:T(1,128)}, u32[]{:S(2)}) copy-start(f32[1,2048]{1,0:T(1,128)} %get-tuple-element.141.gm_d) | copy-start | bytes 24580
  358.0 48.6 %copy-start.5 = (f32[2,8192]{1,0:T(2,128)S(1)}, f32[2,8192]{1,0:T(2,128)}, u32[]{:S(2)}) copy-start(f32[2,8192]{1,0:T(2,128)} %m_gu.1) | copy-start | bytes 196612
  358.0 48.6 %copy-start.8 = (f32[2048]{0:T(1024)S(1)}, f32[2048]{0:T(1024)}, u32[]{:S(2)}) copy-start(f32[2048]{0:T(1024)} %param.39) | copy-start | bytes 24580
  358.0 48.6 %copy-start.9 = (f32[1,2048]{1,0:T(1,128)S(1)}, f32[1,2048]{1,0:T(1,128)}, u32[]{:S(2)}) copy-start(f32[1,2048]{1,0:T(1,128)} %get-tuple-element.145.n_d) | copy-start | bytes 24580
Sparse Core Ops, SparseCore 0:
  112.8 30.7 all-gather.4
  162.7 28.9 all-gather.6
  294.6 37.1 reduce-scatter.2
  358.0 46.3 reduce-scatter.4

commit v9 on v8

--- a/solution.py
+++ b/solution.py
@@ -289,7 +289,7 @@
         compiler_params=pltpu.CompilerParams(vmem_limit_bytes=48 << 20),
         cost_estimate=pl.CostEstimate(flops=0, transcendentals=0, bytes_accessed=1 << 20),
         name="out_back",
-    )(in_grad, *in_hbm(x1), gain, *in_hbm(gy, before, att, a, b), m, norms, *in_hbm(cross, weights))
+    )(*in_hbm(in_grad, x1), gain, *in_hbm(gy, before, att, a, b), m, norms, *in_hbm(cross, weights))
 
 
 def qkv_back_kernel(gq_ref, gkv_ref, cos_ref, sin_ref, before_ref, u_ref, inner_ref, a_ref, b_ref, m_ref, n_ref, cross_ref,
@@ -802,24 +802,29 @@
     return jnp.concatenate(pairs, axis=1)
 
 
-def attend_kernel(valid_ref, q_ref, k_ref, v_ref, o_ref, p_ref):
+def key_blocks(kv_ref):
+    n, _, span, width = kv_ref.shape
+    at = pl.multiple_of(pl.program_id(1) * 128, 128)
+    pick = lambda start: kv_ref[:, 0, :, pl.ds(start, 128)].reshape(n * span, 128)
+    return pick(at), pick(width // 2 + at)
+
+
+def attend_kernel(valid_ref, q_ref, kv_ref, o_ref, p_ref, s_ref):
     span = q_ref.shape[1]
-    keys = k_ref.shape[0] * span
-    q8 = stack_heads(q_ref[0])
-    k2 = k_ref[:, 0].reshape(keys, 128)
-    v2 = v_ref[:, 0].reshape(keys, 128)
-    scores = lax.dot_general(q8, k2, last_last, preferred_element_type=jnp.float32)
-    scores = scores * HEAD_DIM**-0.5
-    first_pos = lax.axis_index("seq") * span
-    q_pos = first_pos + lax.broadcasted_iota(jnp.int32, (8, span, keys), 1).reshape(8 * span, keys)
-    k_pos = lax.broadcasted_iota(jnp.int32, (8 * span, keys), 1)
-    allowed = (k_pos <= q_pos) & (k_pos < valid_ref[pl.program_id(0)])
-    scores = jnp.where(allowed, scores, -1e30)
-    unscaled = jnp.exp(scores - jnp.max(scores, axis=1, keepdims=True))
-    shares = unscaled * (1.0 / jnp.sum(unscaled, axis=1, keepdims=True))
-    shares = shares.astype(jnp.bfloat16)
-    p_ref[0, 0] = shares
-    mixed = jnp.dot(shares, v2, preferred_element_type=jnp.float32)
+    keys = kv_ref.shape[0] * span
+    q8 = stack_heads(q_ref[0]) * jnp.bfloat16(HEAD_DIM**-0.5)
+    k2, v2 = key_blocks(kv_ref)
+    s_ref[...] = lax.dot_general(q8, k2, last_last, preferred_element_type=jnp.float32)
+    q_pos = lax.axis_index("seq") * span + lax.broadcasted_iota(jnp.int32, (span, 1), 0)
+    limit = jnp.minimum(q_pos + 1, valid_ref[pl.program_id(0)])
+    allowed = lax.broadcasted_iota(jnp.int32, (span, keys), 1) < limit
+    for h in range(8):
+        head = slice(h * span, (h + 1) * span)
+        scores = jnp.where(allowed, s_ref[head], -1e30)
+        unscaled = jnp.exp(scores - jnp.max(scores, axis=1, keepdims=True))
+        shares = unscaled * (1.0 / jnp.sum(unscaled, axis=1, keepdims=True))
+        p_ref[0, 0, head] = shares.astype(jnp.bfloat16)
+    mixed = jnp.dot(p_ref[0, 0], v2, preferred_element_type=jnp.float32)
     o_ref[0] = unstack_heads(mixed, span).astype(jnp.bfloat16)
 
 
@@ -841,41 +846,44 @@
             grid=(pair, groups),
             in_specs=[
                 q_spec,
-                pl.BlockSpec((n, 1, span, 128), lambda p, j, *_: (0, p, 0, j)),
-                pl.BlockSpec((n, 1, span, 128), lambda p, j, *_: (0, p, 0, groups + j)),
+                pl.BlockSpec((n, 1, span, 2 * kv_width), lambda p, j, *_: (0, p, 0, 0)),
             ],
             out_specs=(
                 q_spec,
                 pl.BlockSpec((1, 1, 8 * span, keys), lambda p, j, *_: (p, j, 0, 0)),
             ),
+            scratch_shapes=[pltpu.VMEM((8 * span, keys), jnp.float32)],
         ),
         compiler_params=pltpu.CompilerParams(vmem_limit_bytes=40 << 20),
         cost_estimate=pl.CostEstimate(
             flops=flops, transcendentals=flops // 512, bytes_accessed=8 << 20
         ),
         name="attend",
-    )(valid, *in_hbm(q, kv, kv))
-
-
-def attend_back_kernel(q_ref, k_ref, v_ref, p_ref, g_ref, gq_ref, gkv_ref):
+    )(valid, *in_hbm(q, kv))
+
+
+def attend_back_kernel(q_ref, kv_ref, p_ref, g_ref, gq_ref, gkv_ref, s_ref, g_scores):
     span = q_ref.shape[1]
-    keys = k_ref.shape[0] * span
-    q8 = stack_heads(q_ref[0])
+    keys = kv_ref.shape[0] * span
+    q8 = stack_heads(q_ref[0]) * jnp.bfloat16(HEAD_DIM**-0.5)
     g8 = stack_heads(g_ref[0])
-    k2 = k_ref[:, 0].reshape(keys, 128)
-    v2 = v_ref[:, 0].reshape(keys, 128)
+    k2, v2 = key_blocks(kv_ref)
     low = p_ref[0, 0]
-    shares = low.astype(jnp.float32)
-    grad_shares = lax.dot_general(g8, v2, last_last, preferred_element_type=jnp.float32)
-    weighted = shares * grad_shares
-    centre = jnp.sum(weighted, axis=1, keepdims=True)
-    grad_scores = (weighted - shares * centre).astype(jnp.bfloat16)
+    s_ref[...] = lax.dot_general(g8, v2, last_last, preferred_element_type=jnp.float32)
+    for h in range(8):
+        head = slice(h * span, (h + 1) * span)
+        shares = p_ref[0, 0, head].astype(jnp.float32)
+        weighted = shares * s_ref[head]
+        centre = jnp.sum(weighted, axis=1, keepdims=True)
+        g_scores[head] = (weighted - shares * centre).astype(jnp.bfloat16)
+    grad_scores = g_scores[...]
     gq = jnp.dot(grad_scores, k2, preferred_element_type=jnp.float32) * HEAD_DIM**-0.5
     gq_ref[0] = unstack_heads(gq, span).astype(jnp.bfloat16)
     gk = lax.dot_general(grad_scores, q8, first_first, preferred_element_type=jnp.float32)
     gv = lax.dot_general(low, g8, first_first, preferred_element_type=jnp.float32)
-    both = jnp.concatenate([gk * HEAD_DIM**-0.5, gv], axis=1).astype(jnp.bfloat16)
-    gkv_ref[:, 0] = both.reshape(gkv_ref.shape[0], span, 256)
+    both = jnp.concatenate([gk, gv], axis=1).astype(jnp.bfloat16)
+    at = pl.multiple_of(pl.program_id(1) * 256, 256)
+    gkv_ref[:, 0, :, pl.ds(at, 256)] = both.reshape(gkv_ref.shape[0], span, 256)
 
 
 def attend_back(q, kv, shares, g):
@@ -893,19 +901,22 @@
         grid=(pair, groups),
         in_specs=[
             q_spec,
-            pl.BlockSpec((n, 1, span, 128), lambda p, j: (0, p, 0, j)),
-            pl.BlockSpec((n, 1, span, 128), lambda p, j: (0, p, 0, groups + j)),
+            pl.BlockSpec((n, 1, span, 2 * kv_width), lambda p, j: (0, p, 0, 0)),
             pl.BlockSpec((1, 1, 8 * span, keys), lambda p, j: (p, j, 0, 0)),
             q_spec,
         ],
         out_specs=(
             q_spec,
-            pl.BlockSpec((n, 1, span, 256), lambda p, j: (0, p, 0, j)),
-        ),
+            pl.BlockSpec((n, 1, span, 2 * kv_width), lambda p, j: (0, p, 0, 0)),
+        ),
+        scratch_shapes=[
+            pltpu.VMEM((8 * span, keys), jnp.float32),
+            pltpu.VMEM((8 * span, keys), jnp.bfloat16),
+        ],
         compiler_params=pltpu.CompilerParams(vmem_limit_bytes=40 << 20),
         cost_estimate=pl.CostEstimate(flops=0, transcendentals=0, bytes_accessed=1 << 20),
         name="attend_back",
-    )(*in_hbm(q, kv, kv, shares, g))
+    )(*in_hbm(q, kv, shares, g))
 
 def by_distance(i, q, nc):
     room = nc - 1 - q
@@ -1373,10 +1384,9 @@
 
     for t in range(1, rows):
         unit_send(t).start()
+    sum_units()
     for step, p in enumerate(order):
         if step == 1:
-            sum_units()
-        if step == nc // 2:
             spread_units()
         load(p).wait()
         to_sibling(p).wait_recv()
@@ -1658,8 +1668,8 @@
     for p, (m, norm) in enumerate(both):
         drift = jnp.mean(jnp.square(m - norm), axis=1, keepdims=True)
         drift = jnp.sqrt(drift) / jnp.sqrt(jnp.mean(jnp.square(m), axis=1, keepdims=True) + 1e-06)
-        stats = jnp.where((row == p) & (col == 0), drift, stats)
-        stats = jnp.where((row == p) & (col == 1), jnp.mean(norm, axis=1, keepdims=True), stats)
+        stats = jnp.where((row == 0) & (col == p), drift, stats)
+        stats = jnp.where((row == 1) & (col == p), jnp.mean(norm, axis=1, keepdims=True), stats)
     o_stats[...] = stats
 
 
@@ -1674,7 +1684,7 @@
         out_shape=(
             pltpu.HBM((tokens, width), jnp.bfloat16), shape(4, 16, width), shape(2, 16, width), shape(2, 16, kv),
             shape(width), shape(2, kv), shape(width), shape(2, 16, width), shape(2, 16, wide_units), shape(2, wide_units),
-            shape(16, wide_units), shape(16, width), shape(width), shape(7, 2),
+            shape(16, wide_units), shape(16, width), shape(width), shape(2, 7),
         ),
         in_specs=[vmem] * 2 + [pl.BlockSpec()] * 8,
         scratch_shapes=[pltpu.VMEM((2, wide_units), jnp.float32)],
@@ -1801,7 +1811,7 @@
         seq_size, rows_size, sums, units, x1, before_0, before_1, m_attn, n_attn, m_d, n_d, gate_up_magnitude
     )
     shape = (pair_rows, span_len, model_width)
-    return (layer_result.reshape(shape), grad_inputs.reshape(shape), *summed, stats)
+    return (layer_result.reshape(shape), grad_inputs.reshape(shape), *summed, stats.T)
 
 def solution(mesh):
     return jax.shard_map(

time: 419 us -> 405 us (0.967)
  Pallas kernels: 396 us -> 385 us
    pallas_call x1, Pallas kernels: 36.2 us -> 25.5 us  [sum_gradients(): pl.pallas_call(functools.partial(reduce_kernel, n, rows), out_shape=jax.S...]
  transfers between devices with their start and end apart: 4 -> 4, of which waited for: 0 -> 0; matrix products, arithmetic and copies ran while one was open for 0% -> 0% of each run, Pallas kernels for 54% -> 53%
where the time goes in v9:
time: 405 us; the launch traced here: 404 us
  Pallas kernels  385 us (95%)
  between operations  14.8 us (4%)
    pallas_call x1, Pallas kernels, gather_weights(): pl.pallas_call(functools.partial(weights_kernel, n, rows), out_shape=(plt...  103 us
    pallas_call x2, Pallas kernels, gather_seq(): pl.pallas_call(functools.partial(gather_kernel, n, rows, count, (range(le...  79.6 us
    pallas_call x1, Pallas kernels, feed_forward(): pl.pallas_call(kernel, out_shape=(shape((tokens, width), f32), pltpu.HBM(...  64.7 us
    pallas_call x1, Pallas kernels, scatter_seq(): pl.pallas_call(functools.partial(scatter_kernel, n, rows), out_shape=(jax...  39.6 us
    pallas_call x1, Pallas kernels, sum_gradients(): pl.pallas_call(functools.partial(reduce_kernel, n, rows), out_shape=jax.S...  25.5 us
    pallas_call x1, Pallas kernels, project_qkv(): pl.pallas_call(functools.partial(project_kernel, (q_tiles, last)), out_sh...  15.6 us
    pallas_call x1, Pallas kernels, qkv_back(): pl.pallas_call(qkv_back_kernel, out_shape=(pltpu.HBM((rows, width), f32),...  12.3 us
    pallas_call x1, Pallas kernels, attend_back(): pl.pallas_call(attend_back_kernel, out_shape=(pltpu.HBM(q.shape, jnp.bflo...  11.9 us
  transfers between devices with their start and end apart: 4, of which 0 were waited for; matrix products, arithmetic and copies ran while one was open for 0% of the time, Pallas kernels for 53%

profile of v9, /device:TPU:0, one launch (start us, length us, event | category | flops | bytes accessed | tf_op | source)
XLA Modules:
  0.0 404.0 jit_solution(252385829539391271)
XLA Ops:
  7.2 0.0 all-gather.5.cloned.1.call-start
  7.2 0.8 fusion
  8.0 1.9 slice_bitcast_fusion
  9.9 0.0 copy-start.13
  9.9 102.7 %gather_weights.1 = (bf16[2,8,4,64,2560]{4,3,2,1,0:T(8,128)(2,1)}, bf16[2,8,64,1024]{3,2,1,0:T(8,128)(2,1)}, bf16[2,2,4,64,1024]{4,3,2,1,0:T(8,128)(2,1)}, f32[1...) custom-call(bf16[2,4,64,2048]{3,2,1,0:T(8,128)(2,1)} %bitcast.65, ...), custom_call_target="tpu_custom_call" | custom-call | bytes 262144000 | tf_op jit(solution)/shard_map/gather_weights/pallas_call | solution.py:650
  112.7 0.0 copy-start.6
  112.7 0.0 copy-start.10
  112.7 0.0 all-gather.5.cloned.1.call-update
  112.7 0.0 all-gather.7.cloned.1.call-start
  112.8 0.1 multiply_sine_fusion
  113.0 0.1 tile.21
  113.1 0.1 copy.37.sin_ref
  113.3 0.1 tile.9
  113.4 0.1 copy.36.cos_ref
  113.6 0.8 pad_maximum_fusion.b_ref
  114.4 15.6 %project_qkv.1 = (f32[128,3072]{1,0:T(8,128)}, bf16[128,2048]{1,0:T(8,128)(2,1)}, bf16[128,1024]{1,0:T(8,128)(2,1)}, f32[1,5120]{1,0:T(1,128)}, f32[16,5120]{1,0:T(8,128)}) custom-call(bf16[128,2048]{1,0:T(8,128)(2,1)} %get-tuple-element.88.u_ref, bf16[3,128,16]{2,1,0:T(8,128)(2,1)S(1)} %get-tuple-element.89.inner_ref, ...), custom_call_target="tpu_custom_call" | custom-call | flops 2684354560 | bytes 20971520 | tf_op jit(solution)/shard_map/project_qkv/pallas_call | solution.py:131
  130.0 0.0 copy-done.6
  130.0 0.0 copy-start.18
  130.0 32.6 %gather_seq.2 = (bf16[8,128,1024]{2,1,0:T(8,128)(2,1)}, f32[8,1,2048]{2,1,0:T(1,128)}, bf16[8,64,1024]{2,1,0:T(8,128)(2,1)}, bf16[8,64,1024]{2,1,0:T(8,128)(2,1)}) custom-call(bf16[128,1024]{1,0:T(8,128)(2,1)} %get-tuple-element.94.refs_0_, f32[1,2048]{1,0:T(1,128)} %copy-done.10, bf16[2,8,64,1024]{3,2,1,0:T(8,128)(2,1)} %get-tuple-element.96.refs_2_.refs_0_), custom_call_target="tpu_custom_call" | custom-call | bytes 43253760 | tf_op jit(solution)/shard_map/gather_seq/pallas_call | solution.py:760
  162.6 0.0 copy-start
  162.6 0.0 all-gather.7.cloned.1.call-update
  162.6 0.0 reduce-scatter.3.cloned.1.call-start
  163.3 0.0 copy-done.18
  163.3 11.6 %attend.1 = (bf16[2,64,2048]{2,1,0:T(8,128)(2,1)}, bf16[2,4,512,512]{3,2,1,0:T(8,128)(2,1)}) custom-call(s32[2]{0:T(128)S(1)} %broadcast_add_fusion.valid_ref, bf16[2,64,2048]{2,1,0:T(8,128)(2,1)} %bitcast.67, bf16[8,2,64,1024]{3,2,1,0:T(8,128)(2,1)} %bitcast.57), custom_call_target="tpu_custom_call" | custom-call | flops 1073741824 | bytes 8388608 | tf_op jit(solution)/shard_map/attend/pallas_call | solution.py:838
  174.9 7.8 %project_out.1 = (f32[128,2048]{1,0:T(8,128)}, f32[128,2048]{1,0:T(8,128)}, bf16[128,2048]{1,0:T(8,128)(2,1)}, bf16[128,128]{1,0:T(8,128)(2,1)}) custom-call(bf16[128,2048]{1,0:T(8,128)(2,1)} %bitcast.59, f32[4,16,2048]{2,1,0:T(8,128)} %a_ref.7, bf16[2,2048,2560]{2,1,0:T(8,128)(2,1)} %bitcast.49, f32[16,5120]{1,0:T(8,128)} %pad_maximum_fusion.b_ref, ...), custom_call_target="tpu_custom_call" | custom-call | flops 1073741824 | bytes 8388608 | tf_op jit(solution)/shard_map/project_out/pallas_call | solution.py:198
  182.7 47.0 %gather_seq.3 = (bf16[8,128,2048]{2,1,0:T(8,128)(2,1)}, bf16[8,128,128]{2,1,0:T(8,128)(2,1)}, bf16[8,64,1024]{2,1,0:T(8,128)(2,1)}, bf16[8,64,1024]{2,1,0:T(8,12...) custom-call(bf16[128,2048]{1,0:T(8,128)(2,1)} %get-tuple-element.105.refs_0_, ...), custom_call_target="tpu_custom_call" | custom-call | bytes 89128960 | tf_op jit(solution)/shard_map/gather_seq/pallas_call | solution.py:760
  229.7 0.0 all-gather.5.cloned.1.call-done
  229.7 0.0 all-gather.7.cloned.1.call-done
  229.8 64.7 %feed_forward.1 = (f32[128,2048]{1,0:T(8,128)}, bf16[8,64,2048]{2,1,0:T(8,128)(2,1)}, bf16[8,64,2048]{2,1,0:T(8,128)(2,1)}, f32[2,16,2048]{2,1,0:T(8,128)}, f32[...) custom-call(bf16[2,8,64,1024]{3,2,1,0:T(8,128)(2,1)} %get-tuple-elem, ...), custom_call_target="tpu_custom_call" | custom-call | flops 25769803776 | bytes 33554432 | tf_op jit(solution)/shard_map/feed_forward/pallas_call | solution.py:1230
  294.5 0.0 reduce-scatter.3.cloned.1.call-update
  294.5 0.0 reduce-scatter.5.cloned.1.call-start
  294.6 9.9 %out_back.1 = (f32[128,2048]{1,0:T(8,128)}, bf16[128,2048]{1,0:T(8,128)(2,1)}, f32[16,2048]{1,0:T(8,128)S(1)}, f32[16,2048]{1,0:T(8,128)S(1)}, f32[1,2048]{1,0:T(1,128)S(1)}) custom-call(f32[128,2048]{1,0:T(8,128)} %get-tuple-element.116.in_ref, f32[128,2048]{1,0:T(8,128)} %get-tuple-element.117.x1_ref.x1, f32[1,2048]{1,0:T(1,128)S(1)} %get-tuple-element.167.gain_ref, ...), custom_call_target="tpu_custom_call" | custom-call | bytes 1048576 | tf_op jit(solution)/shard_map/out_back/pallas_call | solution.py:269
  304.5 0.0 copy-start.11
  304.5 0.0 copy-start.12
  304.5 11.9 %attend_back.1 = (bf16[2,64,2048]{2,1,0:T(8,128)(2,1)}, bf16[8,2,64,1024]{3,2,1,0:T(8,128)(2,1)}) custom-call(bf16[2,64,2048]{2,1,0:T(8,128)(2,1)} %bitcast.68, bf16[8,2,64,1024]{3,2,1,0:T(8,128)(2,1)} %bitcast.58, bf16[2,4,512,512]{3,2,1,0:T(8,128)(2,1)} %get-tuple-element.99.p_ref, bf16[2,64,2048]{2,1,0:T(8,128)(2,1)} %bitcast.69), custom_call_target="tpu_custom_call" | custom-call | bytes 1048576 | tf_op jit(solution)/shard_map/attend_back/pallas_call | solution.py:895
  316.4 0.0 copy-done.11
  316.4 0.0 copy-done.12
  316.4 39.6 %scatter_seq.1 = (f32[128,1024]{1,0:T(8,128)S(1)}, bf16[4,2,4,16,1024]{4,3,2,1,0:T(8,128)(2,1)S(1)}) custom-call(bf16[8,128,1024]{2,1,0:T(8,128)(2,1)} %bitcast.64, f32[2,16,1024]{2,1,0:T(8,128)S(1)} %copy-done.2, f32[2,1,1024]{2,1,0:T(1,128)S(1)} %copy-done.11, f32[2,1,1024]{2,1,0:T(1,128)S(1)} %copy-done.12, f32[16,1024]{1,0:T(8,128)S(1)} %copy-done.5), custom_call_target="tpu_custom_call" | custom-call | bytes 1048576 | tf_op jit(solution)/shard_map/scatter_seq/pallas_call | solution.py:1461
  356.1 0.0 reduce-scatter.3.cloned.1.call-done.before_0
  356.1 0.0 reduce-scatter.5.cloned.1.call-update
  356.2 0.0 copy-start.4
  356.2 0.0 copy-start.7
  356.2 0.0 copy-start.8
  356.2 12.3 %qkv_back.1 = (f32[128,2048]{1,0:T(8,128)}, f32[3,16,2048]{2,1,0:T(8,128)S(1)}, f32[16,3072]{1,0:T(8,128)S(1)}, f32[1,3072]{1,0:T(1,128)S(1)}) custom-call(bf16[128,2048]{1,0:T(8,128)(2,1)} %bitcast.66, f32[128,1024]{1,0:T(8,128)S(1)} %get-tuple-element.130.gkv_ref, f32[128,128]{1,0:T(8,128)S(1)} %copy.36.cos_ref, f32[128,128]{1,0:T(8,128)S(1)} %copy.37.sin_ref, ...), custom_call_target="tpu_custom_call" | custom-call | bytes 1048576 | tf_op jit(solution)/shard_map/qkv_back/pallas_call | solution.py:357
  368.5 0.0 copy-done.9
  368.5 25.5 %sum_gradients.1.whole = bf16[4,2,4,40,256]{4,3,2,1,0:T(8,128)(2,1)S(1)} custom-call(f32[3,16,2048]{2,1,0:T(8,128)S(1)} %get-tuple-element.133.ga_qkv, f32[16,2048]{1,0:T(8,128)S(1)} %get-tuple-element.134.ga_o, f32[16,3072]{1,0:T(8,128)S(1)} %get-tuple-element.135.gb_qkv, f32[16,2048]{1,0:T(8,128)S(1)} %get-tuple-element.136.gb_o, ...), custom_call_target="tpu_custom_call" | custom-call | bytes 1048576 | tf_op jit(solution)/shard_map/sum_gradients/pallas_call | solution.py:1591
  394.0 0.0 reduce-scatter.5.cloned.1.call-done.before_1
  394.0 3.4 finish.1
  (32 shorter events, 0.2 us)
Async XLA Ops:
  7.2 222.6 %all-gather.5.cloned.1.call-start = ((), (), s32[]{:S(2)}) async-start(), calls=%async_computation.4 | async-start | bytes 2359296 | tf_op jit(solution)/shard_map/all_gather | solution.py:1738
  9.9 103.6 %copy-start.17 = (f32[2,512]{1,0:T(2,128)S(1)}, f32[2,512]{1,0:T(2,128)}, u32[]{:S(2)}) copy-start(f32[2,512]{1,0:T(2,128)} %param.32) | copy-start | bytes 12292
  9.9 103.6 %copy-start.15 = (f32[2048]{0:T(1024)S(1)}, f32[2048]{0:T(1024)}, u32[]{:S(2)}) copy-start(f32[2048]{0:T(1024)} %param.33) | copy-start | bytes 24580
  9.9 103.6 %copy-start.16 = (f32[2048]{0:T(1024)S(1)}, f32[2048]{0:T(1024)}, u32[]{:S(2)}) copy-start(f32[2048]{0:T(1024)} %param.31) | copy-start | bytes 24580
  9.9 103.6 %copy-start.14 = (f32[2,16,512]{2,1,0:T(8,128)S(1)}, f32[2,16,512]{2,1,0:T(8,128)}, u32[]{:S(2)}) copy-start(f32[2,16,512]{2,1,0:T(8,128)} %param.30) | copy-start | bytes 196612
  9.9 103.7 %copy-start.13 = (f32[2,16,2048]{2,1,0:T(8,128)S(1)}, f32[2,16,2048]{2,1,0:T(8,128)}, u32[]{:S(2)}) copy-start(f32[2,16,2048]{2,1,0:T(8,128)} %param.29) | copy-start | bytes 786436
  112.7 17.3 %copy-start.6 = (bf16[7,32,16]{2,1,0:T(8,128)(2,1)}, bf16[7,32,16]{2,1,0:T(8,128)(2,1)S(1)}, u32[]{:S(2)}) copy-start(bf16[7,32,16]{2,1,0:T(8,128)(2,1)S(1)} %get-tuple-element.90.gram_ref.refs_20_) | copy-start | bytes 21508
  112.7 17.3 %copy-start.10 = (f32[1,2048]{1,0:T(1,128)}, f32[1,2048]{1,0:T(1,128)S(1)}, u32[]{:S(2)}) copy-start(f32[1,2048]{1,0:T(1,128)S(1)} %get-tuple-element.95.refs_1_) | copy-start | bytes 24580
  112.7 117.0 %all-gather.7.cloned.1.call-start = ((), (), s32[]{:S(2)}) async-start(), calls=%async_computation.5 | async-start | bytes 2359296 | tf_op jit(solution)/shard_map/all_gather | solution.py:1769
  130.0 33.3 %copy-start.18 = (s32[2]{0:T(128)S(1)}, s32[2]{0:T(128)}, u32[]{:S(2)}) copy-start(s32[2]{0:T(128)} %param.41) | copy-start | bytes 28
  162.6 12.3 %copy-start = (f32[1,5120]{1,0:T(1,128)S(1)}, f32[1,5120]{1,0:T(1,128)}, u32[]{:S(2)}) copy-start(f32[1,5120]{1,0:T(1,128)} %get-tuple-element.104.n_ref.n_attn) | copy-start | bytes 61444
  162.6 193.5 %reduce-scatter.3.cloned.1.call-start = ((), (), s32[]{:S(2)}) async-start(), calls=%async_computation.2 | async-start | bytes 2359296 | tf_op jit(solution)/shard_map/reduce_scatter | solution.py:1787
  294.5 99.5 %reduce-scatter.5.cloned.1.call-start = ((), (), s32[]{:S(2)}) async-start(), calls=%async_computation.3 | async-start | bytes 2359296 | tf_op jit(solution)/shard_map/reduce_scatter | solution.py:1799
  304.5 11.9 %copy-start.2 = (f32[2,16,1024]{2,1,0:T(8,128)S(1)}, f32[2,16,1024]{2,1,0:T(8,128)}, u32[]{:S(2)}) copy-start(f32[2,16,1024]{2,1,0:T(8,128)} %get-tuple-element.123.gb_gu) | copy-start | bytes 393220
  304.5 11.9 %copy-start.5 = (f32[16,1024]{1,0:T(8,128)S(1)}, f32[16,1024]{1,0:T(8,128)}, u32[]{:S(2)}) copy-start(f32[16,1024]{1,0:T(8,128)} %get-tuple-element.126.ga_d) | copy-start | bytes 196612
  304.5 11.9 %copy-start.11 = (f32[2,1,1024]{2,1,0:T(1,128)S(1)}, f32[2,1,1024]{2,1,0:T(1,128)}, u32[]{:S(2)}) copy-start(f32[2,1,1024]{2,1,0:T(1,128)} %get-tuple-element.124.gm_gu) | copy-start | bytes 24580
  304.5 11.9 %copy-start.12 = (f32[2,1,1024]{2,1,0:T(1,128)S(1)}, f32[2,1,1024]{2,1,0:T(1,128)}, u32[]{:S(2)}) copy-start(f32[2,1,1024]{2,1,0:T(1,128)} %get-tuple-element.125.n_gu) | copy-start | bytes 24580
  356.1 12.3 %copy-start.1 = (f32[2,16,2048]{2,1,0:T(8,128)S(1)}, f32[2,16,2048]{2,1,0:T(8,128)}, u32[]{:S(2)}) copy-start(f32[2,16,2048]{2,1,0:T(8,128)} %get-tuple-element.137.ga_gu) | copy-start | bytes 786436
  356.2 12.3 %copy-start.3 = (f32[16,2048]{1,0:T(8,128)S(1)}, f32[16,2048]{1,0:T(8,128)}, u32[]{:S(2)}) copy-start(f32[16,2048]{1,0:T(8,128)} %get-tuple-element.138.gb_d) | copy-start | bytes 393220
  356.2 12.3 %copy-start.9 = (f32[1,2048]{1,0:T(1,128)S(1)}, f32[1,2048]{1,0:T(1,128)}, u32[]{:S(2)}) copy-start(f32[1,2048]{1,0:T(1,128)} %get-tuple-element.141.gm_d) | copy-start | bytes 24580
  356.2 37.8 %copy-start.4 = (f32[2,8192]{1,0:T(2,128)S(1)}, f32[2,8192]{1,0:T(2,128)}, u32[]{:S(2)}) copy-start(f32[2,8192]{1,0:T(2,128)} %m_gu.1) | copy-start | bytes 196612
  356.2 37.8 %copy-start.7 = (f32[2048]{0:T(1024)S(1)}, f32[2048]{0:T(1024)}, u32[]{:S(2)}) copy-start(f32[2048]{0:T(1024)} %param.39) | copy-start | bytes 24580
  356.2 37.8 %copy-start.8 = (f32[1,2048]{1,0:T(1,128)S(1)}, f32[1,2048]{1,0:T(1,128)}, u32[]{:S(2)}) copy-start(f32[1,2048]{1,0:T(1,128)} %get-tuple-element.145.n_d) | copy-start | bytes 24580
Sparse Core Ops, SparseCore 0:
  112.8 30.8 all-gather.4
  162.7 28.8 all-gather.6
  294.7 35.1 reduce-scatter.2
  356.3 36.1 reduce-scatter.4

commit v10 on v9

--- a/solution.py
+++ b/solution.py
@@ -79,89 +79,187 @@
     return jnp.sqrt(squares + 1e-06), cross + SCALE * gram_b
 
 
-def project_kernel(kv_tiles, u_ref, inner_ref, gram_ref, a_ref, w_ref, b_ref, m_ref, cos_ref, sin_ref,
-                   before_ref, q_ref, kv_ref, n_ref, cross_ref):
+def project_kernel(n, rows, plan, k_tiles, q_tiles, u_ref, inner_ref, gram_ref, a_ref, w_ref, b_ref, m_ref, cos_ref,
+                   sin_ref, sq_ref, held, before_ref, q_ref, n_ref, cross_ref, kv_all, sq_all, *refs):
+    swapped = refs[: len(plan)]
+    kv_ref, keep_sem, to_sib, to_left, to_right, recv, share_out, share_in = refs[len(plan) :]
     j = pl.program_id(0)
-    q_tiles, last = kv_tiles
+    last = pl.num_programs(0) - 1
+    nc = n // 2
+    s, q, c = place_in_seq()
+    sibling = s + 1 - 2 * c
+    r, b_row, a_row, _ = place_in_rows(rows)
+    order = [near_first(i, q, nc) for i in range(nc)]
+    sources, outs = (kv_ref, sq_ref), (kv_all, sq_all)
+
+    def copy(k, src, slot, sems, target):
+        return remote(src, outs[k].at[slot], sems.at[k, slot], recv.at[k, slot], r, target)
+
+    def share(i, chip):
+        _, piece, turn = plan[i]
+        pair = pl.ds(2 * chip, 2)
+        target = b_row if turn == 0 else a_row(turn)
+        return remote(
+            held.at[piece, pair], swapped[i].at[pair], share_out.at[i, chip], share_in.at[i, chip], target, s
+        )
+
+    def keep(k):
+        return pltpu.make_async_copy(sources[k], outs[k].at[s], keep_sem.at[k])
+
+    @pl.when(j == 0)
+    def _():
+        greet_all(n, rows)
+        for chip in order[1:]:
+            for i in range(len(plan)):
+                share(i, chip).start()
+
     a = a_ref[0].astype(jnp.bfloat16)
     b = b_ref[...].astype(jnp.bfloat16)
     w = w_ref[0]
-    rows = u_ref.shape[0]
-
-    @pl.when(j <= last)
+    height = u_ref.shape[0]
+
+    @pl.when(j < 2 * k_tiles + q_tiles)
     def _():
         both = dot_f32(jnp.concatenate([u_ref[...], a], axis=0), w)
-        norm, cross = column_norms(w, gram_ref[0], b, both[rows:])
+        norm, cross = column_norms(w, gram_ref[0], b, both[height:])
         n_ref[...] = norm
         cross_ref[...] = cross
-        before = both[:rows] + SCALE * dot_f32(inner_ref[0], b)
+        before = both[:height] + SCALE * dot_f32(inner_ref[0], b)
         before_ref[...] = before
         y = before * (m_ref[...] / norm)
 
-        @pl.when(j < q_tiles)
+        @pl.when(j >= 2 * k_tiles)
         def _():
             q_ref[...] = turn(y, cos_ref[...], sin_ref[...]).astype(jnp.bfloat16)
 
-        @pl.when(j == q_tiles)
-        def _():
-            kv_ref[...] = turn(y, cos_ref[...], sin_ref[...]).astype(jnp.bfloat16)
-
-        @pl.when(j > q_tiles)
-        def _():
-            kv_ref[...] = y.astype(jnp.bfloat16)
-
-    @pl.when(j > last)
+        for t in range(2 * k_tiles):
+
+            @pl.when(j == t)
+            def _(t=t):
+                z = turn(y, cos_ref[...], sin_ref[...]) if t < k_tiles else y
+                kv_ref[:, TILE * t : TILE * (t + 1)] = z.astype(jnp.bfloat16)
+
+    @pl.when(j >= 2 * k_tiles + q_tiles)
     def _():
         norm, cross = column_norms(w, gram_ref[0], b, dot_f32(a, w))
         n_ref[...] = norm
         cross_ref[...] = cross
 
-
-def project_qkv(u, inner, grams, a, weights, b, m, cosine, sine):
-    rows, width = u.shape
+    @pl.when(j == 2 * k_tiles - 1)
+    def _():
+        for k in range(2):
+            pl.when(q > 0)(lambda k=k: copy(k, sources[k], s, to_left, s - 2).start())
+            pl.when(q < nc - 1)(lambda k=k: copy(k, sources[k], s, to_right, s + 2).start())
+            copy(k, sources[k], s, to_sib, sibling).start()
+            keep(k).start()
+
+    def pass_on(chip):
+        slot = 2 * chip + c
+        for k in range(2):
+            src = outs[k].at[slot]
+            copy(k, src, slot, to_right, s).wait_recv()
+            pl.when((chip < q) & (q < nc - 1))(
+                lambda k=k, src=src: copy(k, src, slot, to_right, s + 2).start()
+            )
+            pl.when((chip > q) & (q > 0))(
+                lambda k=k, src=src: copy(k, src, slot, to_left, s - 2).start()
+            )
+            copy(k, src, slot, to_sib, sibling).start()
+
+    for i in range(1, nc):
+        at = min(2 * k_tiles + 2 * i, 2 * k_tiles + 2 * q_tiles - 1)
+        pl.when(j == at)(lambda i=i: pass_on(order[i]))
+
+    @pl.when(j == last)
+    def _():
+        for k in range(2):
+            keep(k).wait()
+            for chip in range(nc):
+                mine, theirs = 2 * chip + c, 2 * chip + 1 - c
+                copy(k, outs[k].at[theirs], theirs, to_sib, sibling).wait_recv()
+                copy(k, outs[k].at[mine], mine, to_sib, sibling).wait_send()
+                pl.when((q < nc - 1) & (chip <= q))(
+                    lambda k=k, mine=mine: copy(k, outs[k].at[mine], mine, to_right, s).wait_send()
+                )
+                pl.when((q > 0) & (chip >= q))(
+                    lambda k=k, mine=mine: copy(k, outs[k].at[mine], mine, to_left, s).wait_send()
+                )
+        for chip in order[1:]:
+            for i in range(len(plan)):
+                share(i, chip).wait_send()
+                share(i, chip).wait_recv()
+
+
+def project_qkv(n, rows, u, inner, grams, a, weights, b, m, cosine, sine, sq, held, plan, collective_id):
+    tokens, width = u.shape
     cols = b.shape[1]
+    nc = n // 2
     per_half = weights.shape[2] // TILE
     q_tiles = width // TILE
     k_cols = weights.shape[2] - width
-    last = q_tiles + 2 * k_cols // TILE - 1
+    k_tiles = k_cols // TILE
+    kv_tiles = 2 * k_tiles
     full = lambda shape: pl.BlockSpec(shape, lambda j: (0,) * len(shape))
-    col = lambda height: pl.BlockSpec((height, TILE), lambda j: (0, j))
-    which = lambda j: jnp.where(j < q_tiles, 0, jnp.where(j > last, 3, 1 + j - q_tiles))
+
+    def column(j):
+        return jnp.where(j < kv_tiles, q_tiles + j, jnp.where(j < kv_tiles + q_tiles, j - kv_tiles, j))
+
+    def which(j):
+        return jnp.where(
+            j < k_tiles, 1, jnp.where(j < kv_tiles, 2, jnp.where(j < kv_tiles + q_tiles, 0, 3))
+        )
+
+    def before_tile(j):
+        return (0, column(jnp.minimum(j, kv_tiles + q_tiles - 1)))
+
+    col = lambda height: pl.BlockSpec((height, TILE), lambda j: (0, column(j)))
     f32, low = jnp.float32, jnp.bfloat16
-    return pl.pallas_call(
-        functools.partial(project_kernel, (q_tiles, last)),
+    hbm = pl.BlockSpec(memory_space=pltpu.HBM)
+    dma = pltpu.SemaphoreType.DMA
+    got = pl.pallas_call(
+        functools.partial(project_kernel, n, rows, plan, k_tiles, q_tiles),
         out_shape=(
-            pltpu.HBM((rows, width + 2 * k_cols), f32),
-            pltpu.HBM((rows, width), low),
-            pltpu.HBM((rows, 2 * k_cols), low),
+            pltpu.HBM((tokens, width + 2 * k_cols), f32),
+            pltpu.HBM((tokens, width), low),
             pltpu.HBM((1, cols), f32),
             pltpu.HBM((16, cols), f32),
+            pltpu.HBM((n, tokens, 2 * k_cols), low),
+            pltpu.HBM((n, *sq.shape), f32),
+            *(pltpu.HBM(held.shape[-3:], low) for _ in plan),
         ),
         grid=(cols // TILE,),
         in_specs=[
-            full((rows, width)),
-            pl.BlockSpec((1, rows, 16), lambda j: (jnp.minimum(which(j), 2), 0, 0)),
+            full((tokens, width)),
+            pl.BlockSpec((1, tokens, 16), lambda j: (jnp.minimum(which(j), 2), 0, 0)),
             pl.BlockSpec((1, 32, 16), lambda j: (which(j), 0, 0)),
             pl.BlockSpec((1, 16, width), lambda j: (which(j), 0, 0)),
-            pl.BlockSpec((1, width, TILE), lambda j: (j // per_half, 0, j % per_half)),
+            pl.BlockSpec((1, width, TILE), lambda j: (column(j) // per_half, 0, lax.rem(column(j), per_half))),
             col(16),
             col(1),
             full(cosine.shape),
             full(sine.shape),
+            hbm,
+            hbm,
         ],
         out_specs=(
-            pl.BlockSpec((rows, TILE), lambda j: (0, jnp.minimum(j, last))),
-            pl.BlockSpec((rows, TILE), lambda j: (0, jnp.minimum(j, q_tiles - 1))),
-            pl.BlockSpec((rows, TILE), lambda j: (0, jnp.clip(j - q_tiles, 0, last - q_tiles))),
+            pl.BlockSpec((tokens, TILE), before_tile),
+            pl.BlockSpec((tokens, TILE), lambda j: (0, jnp.clip(j - kv_tiles, 0, q_tiles - 1))),
             col(1),
             col(16),
-        ),
-        compiler_params=pltpu.CompilerParams(vmem_limit_bytes=40 << 20),
+            *([hbm] * (2 + len(plan))),
+        ),
+        scratch_shapes=[pltpu.VMEM((tokens, 2 * k_cols), low), dma((2,))]
+        + [dma((2, n))] * 4
+        + [dma((len(plan), nc))] * 2,
+        compiler_params=pltpu.CompilerParams(
+            collective_id=collective_id, has_side_effects=True, vmem_limit_bytes=40 << 20
+        ),
         cost_estimate=pl.CostEstimate(
-            flops=2 * rows * width * cols, transcendentals=0, bytes_accessed=2 * width * cols
+            flops=2 * tokens * width * cols, transcendentals=0, bytes_accessed=64 << 20
         ),
         name="project_qkv",
-    )(*in_hbm(u), inner, grams, *in_hbm(a, weights, b), m, cosine, sine)
+    )(*in_hbm(u), inner, grams, *in_hbm(a, weights, b), m, cosine, sine, *in_hbm(sq, held))
+    return (*got[:6], got[6:])
 
 
 def out_kernel(att_ref, a_ref, w_ref, b_ref, m_ref, n_ref, x_ref, gain_ref, next_ref,
@@ -179,7 +277,7 @@
     @pl.when(t == pl.num_programs(0) - 1)
     def _():
         v = x1_ref[...]
-        u2 = (v * unit_rms(v) * gain_ref[...]).astype(jnp.bfloat16)
+        u2 = (v * unit_rms(v) * gain_ref[1:]).astype(jnp.bfloat16)
         u2_ref[...] = u2
         following = next_ref[...].reshape(-1, u2.shape[1]).astype(jnp.bfloat16)
         inner_ref[...] = jnp.zeros_like(inner_ref)
@@ -212,7 +310,7 @@
             later(1),
             later(1),
             col(rows),
-            full((1, width)),
+            full((2, width)),
             full(following.shape),
         ],
         out_specs=(col(rows), full((rows, width)), full((rows, width)), full((rows, 128))),
@@ -234,7 +332,7 @@
 
     @pl.when(t == 0)
     def _():
-        gx = gy_ref[...].astype(jnp.float32) + rms_back(x1_ref[...], gain_ref[...], in_ref[...])
+        gx = gy_ref[...].astype(jnp.float32) + rms_back(x1_ref[...], gain_ref[1:], in_ref[...])
         gx_ref[...] = gx
         norm, m = n_ref[:, o_cols], m_ref[:, o_cols]
         gb = (gx * (m / norm)).astype(low)
@@ -276,7 +374,7 @@
             jax.ShapeDtypeStruct((1, width), f32),
         ),
         grid=(tiles,),
-        in_specs=[wide, wide, full((1, width)), wide, wide, wide,
+        in_specs=[wide, wide, full((2, width)), wide, wide, wide,
                   pl.BlockSpec((1, 16, width), lambda t: (3, 0, 0)),
                   full(b.shape), full(m.shape), full(norms.shape), full(cross.shape),
                   pl.BlockSpec((1, TILE, weights.shape[2]), lambda t: (1, t, 0))],
@@ -343,7 +441,7 @@
     @pl.when(t == pl.num_programs(0) - 1)
     def _():
         v = x_ref[...].astype(jnp.float32)
-        out_ref[...] = gx_ref[...] + rms_back(v, gain_ref[...], out_ref[...])
+        out_ref[...] = gx_ref[...] + rms_back(v, gain_ref[:1], out_ref[...])
 
 
 def qkv_back(gq, gkv, cosine, sine, before, u, inner, a, b, m, norms, cross, x, gain, gx, weights):
@@ -365,7 +463,7 @@
         grid=(tiles,),
         in_specs=[wide, full(gkv.shape), full(cosine.shape), full(sine.shape), full((rows, cols)), wide, full(inner.shape),
                   full(a.shape), full(b.shape), full(m.shape), full(norms.shape), full(cross.shape),
-                  wide, full((1, width)), wide,
+                  wide, full((2, width)), wide,
                   pl.BlockSpec((1, TILE, width + k_cols), lambda t: (0, t, 0)),
                   pl.BlockSpec((1, TILE, k_cols), lambda t: (1, t, 0))],
         out_specs=(wide, pl.BlockSpec((3, 16, TILE), lambda t: (0, 0, t)), full((16, cols)), full((1, cols))),
@@ -425,9 +523,9 @@
     )
 
 
-def weights_kernel(n, rows, qo, kv, xg, wd_hbm, ad_hbm, bd_hbm, x_hbm, gain_ref, aa_hbm, ag_hbm,
-                   wa, gz, near, sq_ref, gram_ref, u_hbm, inner_ref,
-                   wd, ad_ref, bd_ref, x_ref, aa_ref, ag_ref, own_ref, cols_ref, local, edge, a_in, a_sib_in, a_out, a_sib_out, z_in, z_out):
+def weights_kernel(n, rows, qo, kv, xg, wd_hbm, ad_hbm, bd_hbm, x_hbm, gain_ref, aa_hbm, ag_hbm, gy_hbm,
+                   wa, gz, near, sq_ref, gram_ref, u_hbm, inner_ref, gy0_hbm, gy1_hbm,
+                   wd, ad_ref, bd_ref, x_ref, aa_ref, ag_ref, gy_ref, own_ref, cols_ref, local, edge, a_in, a_sib_in, a_out, a_sib_out, z_in, z_out):
     nc, half = n // 2, rows // 2
     others = half - 1
     units = gz.shape[-1]
@@ -536,31 +634,39 @@
     own_blocks(
         all_parts,
         lambda src, i, cols: pltpu.make_async_copy(
-            src, own_ref.at[i, :, :, cols], local.at[9]
+            src, own_ref.at[i, :, :, cols], local.at[12]
         ).start(),
     )
-    take_cols = pltpu.make_async_copy(xg.at[:, :, :, columns(s)], cols_ref, local.at[10])
+    take_cols = pltpu.make_async_copy(xg.at[:, :, :, columns(s)], cols_ref, local.at[13])
     take_cols.start()
     takes = [
-        pltpu.make_async_copy(src, dst, local.at[3 + i])
+        pltpu.make_async_copy(src, dst, local.at[5 + i])
         for i, (src, dst) in enumerate(
-            [(x_hbm, x_ref), (aa_hbm, aa_ref), (ag_hbm, ag_ref), (ad_hbm, ad_ref), (bd_hbm, bd_ref), (wd_hbm, wd)]
+            [(x_hbm, x_ref), (aa_hbm, aa_ref), (ag_hbm, ag_ref), (ad_hbm, ad_ref), (bd_hbm, bd_ref), (wd_hbm, wd),
+             (gy_hbm, gy_ref)]
         )
     ]
     for cp in takes:
         cp.start()
     for cp in takes:
         cp.wait()
-    pltpu.make_async_copy(own_ref, own_ref, local.at[9]).wait()
+    pltpu.make_async_copy(own_ref, own_ref, local.at[12]).wait()
     keep_a.start()
     take_cols.wait()
     keep_g.start()
     low = jnp.bfloat16
     v = x_ref[...].astype(jnp.float32)
-    u = (v * unit_rms(v) * gain_ref[...]).astype(low)
+    u = (v * unit_rms(v) * gain_ref[:1]).astype(low)
     x_ref[...] = u
     keep_u = pltpu.make_async_copy(x_ref, u_hbm, local.at[2])
     keep_u.start()
+    tokens = x_ref.shape[0] // 2
+    halves = [
+        pltpu.make_async_copy(gy_ref.at[pl.ds(tokens * k, tokens)], out, local.at[3 + k])
+        for k, out in enumerate((gy0_hbm, gy1_hbm))
+    ]
+    for cp in halves:
+        cp.start()
     for g in range(4):
         a = aa_ref[g].astype(low)
         gram_ref[g] = two_terms(dot_nt(a, a))
@@ -596,6 +702,8 @@
     sib_g().start()
     down_squares()
     keep_u.wait()
+    for cp in halves:
+        cp.wait()
     for p in order[1:]:
         a_arrival(p, FROM_B).wait_recv()
         for k in range(1, half):
@@ -633,7 +741,7 @@
             z_arrival(p, core).wait_recv()
 
 
-def gather_weights(n, rows, qo, kv, xg, wd, ad, bd, x, gain, aa, ag, collective_id):
+def gather_weights(n, rows, qo, kv, xg, wd, ad, bd, x, gains, aa, ag, gy, collective_id):
     nc = n // 2
     _, block, width = qo.shape
     part = block // rows
@@ -647,7 +755,7 @@
     anywhere = pl.BlockSpec(memory_space=pltpu.HBM)
     vmem = pl.BlockSpec(memory_space=pltpu.VMEM)
     low = qo.dtype
-    wa, gz, near, sq, grams, u, inner = pl.pallas_call(
+    wa, gz, near, sq, grams, u, inner, *halves = pl.pallas_call(
         functools.partial(weights_kernel, n, rows),
         out_shape=(
             pltpu.HBM((2, n, rows, part, cols), low),
@@ -657,12 +765,13 @@
             jax.ShapeDtypeStruct((7, 32, 16), low),
             pltpu.HBM(x.shape, low),
             jax.ShapeDtypeStruct((3, x.shape[0], 16), low),
-        ),
-        in_specs=[anywhere] * 7 + [vmem] + [anywhere] * 2,
-        out_specs=(anywhere,) * 3 + (vmem,) * 2 + (anywhere, vmem),
-        scratch_shapes=[pltpu.VMEM(v.shape, v.dtype) for v in (wd, ad, bd, x, aa, ag)]
+            *([pltpu.HBM((gy.shape[0] // 2, width), low)] * 2),
+        ),
+        in_specs=[anywhere] * 7 + [vmem] + [anywhere] * 3,
+        out_specs=(anywhere,) * 3 + (vmem,) * 2 + (anywhere, vmem) + (anywhere,) * 2,
+        scratch_shapes=[pltpu.VMEM(v.shape, v.dtype) for v in (wd, ad, bd, x, aa, ag, gy)]
         + [pltpu.VMEM((2, rows, part, cols), low), pltpu.VMEM((2, rows, part, units), low)]
-        + [dma((11,)), dma((6,))]
+        + [dma((14,)), dma((6,))]
         + [dma((nc, kinds))] * 4
         + [dma((nc, 2))] * 2,
         compiler_params=pltpu.CompilerParams(
@@ -672,8 +781,8 @@
             flops=0, transcendentals=0, bytes_accessed=250 * 1024 * 1024
         ),
         name="gather_weights",
-    )(*in_hbm(qo, kv, xg, wd, ad, bd, x), gain, *in_hbm(aa, ag))
-    return wa.reshape(2, n * block, cols), gz, near, sq, grams, u, inner
+    )(*in_hbm(qo, kv, xg, wd, ad, bd, x), gains, *in_hbm(aa, ag, gy))
+    return wa.reshape(2, n * block, cols), gz, near, sq, grams, u, inner, halves
 
 
 def gather_kernel(n, rows, count, shared, *refs):
@@ -1725,17 +1834,14 @@
     f32 = jnp.float32
 
     x = layer_input.reshape(token_count, model_width)
-    gain_attn, gain_ffn = norm_gain_vectors[:1], norm_gain_vectors[1:]
-    weights, gu_own, gu_near, sq_d, grams, u1, inner_1 = gather_weights(
+    grad_out_rows = output_gradient.reshape(token_count, model_width)
+    weights, gu_own, gu_near, sq_d, grams, u1, inner_1, gy_halves = gather_weights(
         seq_size, rows_size, query_output_frozen, key_value_frozen, gate_up_frozen,
-        down_frozen_weight, down_adapter_a, down_adapter_b, x, gain_attn, attention_adapter_a,
-        gate_up_adapter_a, 1,
+        down_frozen_weight, down_adapter_a, down_adapter_b, x, norm_gain_vectors,
+        attention_adapter_a, gate_up_adapter_a, grad_out_rows, 1,
     )
     shares_1, shares_2 = share_plan(rows_size)
-    grad_out_rows = output_gradient.reshape(token_count, model_width)
-    half_0, half_1 = jnp.split(grad_out_rows, 2)
-    weights, half_0 = lax.optimization_barrier((weights, half_0))
-    gy_0 = lax.all_gather(half_0, "seq", axis=0, tiled=False)
+    gy_0 = lax.all_gather(gy_halves[0], "seq", axis=0, tiled=False)
 
     b_attn = jnp.concatenate(
         [
@@ -1759,20 +1865,18 @@
     sine = jnp.tile(jnp.sin(angles), (pair_rows, 4))
     valid_len = prompt_length_list[0] + response_length_list
 
-    before_qkv, q, kv, n_attn, cross_attn = project_qkv(
-        u1, inner_1, grams, attention_adapter_a, weights, b_attn, m_attn, cosine, sine
-    )
-    (kv_all, sq_all), gu_1 = gather_seq(
-        seq_size, rows_size, [kv, sq_d], 2, (gu_own,), shares_1
-    )
-    kv_all, half_1 = lax.optimization_barrier((kv_all, half_1))
+    before_qkv, q, n_attn, cross_attn, kv_all, sq_all, gu_1 = project_qkv(
+        seq_size, rows_size, u1, inner_1, grams, attention_adapter_a, weights, b_attn, m_attn,
+        cosine, sine, sq_d, gu_own, shares_1, 2,
+    )
+    kv_all, half_1 = lax.optimization_barrier((kv_all, gy_halves[1]))
     gy_1 = lax.all_gather(half_1, "seq", axis=0, tiled=False)
     kv_all = kv_all.reshape(seq_size, pair_rows, span_len, 2 * kv_width)
     q = q.reshape(pair_rows, span_len, model_width)
     att, shares = attend(q, kv_all, valid_len)
     att = att.reshape(token_count, model_width)
     before_o, x1, u2, inner_2 = project_out(
-        att, attention_adapter_a, weights, b_attn, m_attn, n_attn, x, gain_ffn, gate_up_adapter_a
+        att, attention_adapter_a, weights, b_attn, m_attn, n_attn, x, norm_gain_vectors, gate_up_adapter_a
     )
 
     (u2_all, inner_all), gu_2 = gather_seq(
@@ -1787,7 +1891,7 @@
     before_0 = lax.psum_scatter(flat(down_0), "seq", scatter_dimension=0, tiled=True)
 
     gx1, grad_att, ga_o, gb_o, gm_o = out_back(
-        in_grad, x1, gain_ffn, grad_out_rows, before_o, att, attention_adapter_a, b_attn, m_attn,
+        in_grad, x1, norm_gain_vectors, grad_out_rows, before_o, att, attention_adapter_a, b_attn, m_attn,
         n_attn, cross_attn, weights,
     )
     gq, gkv = attend_back(q, kv_all, shares, grad_att.reshape(q.shape))
@@ -1799,7 +1903,7 @@
     before_1 = lax.psum_scatter(flat(down_1), "seq", scatter_dimension=0, tiled=True)
     grad_inputs, ga_qkv, gb_qkv, gm_qkv = qkv_back(
         gq.reshape(token_count, model_width), gkv, cosine, sine, before_qkv, u1, inner_1,
-        attention_adapter_a, b_attn, m_attn, n_attn, cross_attn, x, gain_attn, gx1, weights,
+        attention_adapter_a, b_attn, m_attn, n_attn, cross_attn, x, norm_gain_vectors, gx1, weights,
     )
 
     sums = sum_gradients(

time: 405 us -> 402 us (level)
    pallas_call x2 -> x1, Pallas kernels: 79.6 us -> 47 us  [gather_seq(): pl.pallas_call(functools.partial(gather_kernel, n, rows, count, (range(le...]
    pallas_call x1, Pallas kernels: 15.6 us -> 47.4 us  [project_qkv(): pl.pallas_call(functools.partial(project_kernel, n, rows, plan, k_tiles,...]
where the time goes in v10:
time: 402 us; the launch traced here: 401 us
  Pallas kernels  384 us (96%)
  between operations  14.8 us (4%)
    pallas_call x1, Pallas kernels, gather_weights(): pl.pallas_call(functools.partial(weights_kernel, n, rows), out_shape=(plt...  103 us
    pallas_call x1, Pallas kernels, feed_forward(): pl.pallas_call(kernel, out_shape=(shape((tokens, width), f32), pltpu.HBM(...  64.8 us
    pallas_call x1, Pallas kernels, project_qkv(): pl.pallas_call(functools.partial(project_kernel, n, rows, plan, k_tiles,...  47.4 us
    pallas_call x1, Pallas kernels, gather_seq(): pl.pallas_call(functools.partial(gather_kernel, n, rows, count, (range(le...  47 us
    pallas_call x1, Pallas kernels, scatter_seq(): pl.pallas_call(functools.partial(scatter_kernel, n, rows), out_shape=(jax...  39.8 us
    pallas_call x1, Pallas kernels, sum_gradients(): pl.pallas_call(functools.partial(reduce_kernel, n, rows), out_shape=jax.S...  25.4 us
    pallas_call x1, Pallas kernels, qkv_back(): pl.pallas_call(qkv_back_kernel, out_shape=(pltpu.HBM((rows, width), f32),...  12.3 us
    pallas_call x1, Pallas kernels, attend_back(): pl.pallas_call(attend_back_kernel, out_shape=(pltpu.HBM(q.shape, jnp.bflo...  11.9 us
  transfers between devices with their start and end apart: 4, of which 0 were waited for; matrix products, arithmetic and copies ran while one was open for 0% of the time, Pallas kernels for 53%

profile of v10, /device:TPU:0, one launch (start us, length us, event | category | flops | bytes accessed | tf_op | source)
XLA Modules:
  0.0 401.3 jit_solution(12921478990103508474)
XLA Ops:
  7.2 0.0 all-gather.5.cloned.1.call-start
  7.2 0.0 copy-start.2
  7.2 0.7 copy-done.2
  8.0 0.0 copy-start.15
  8.0 102.8 %gather_weights.1 = (bf16[2,8,4,64,2560]{4,3,2,1,0:T(8,128)(2,1)}, bf16[2,8,64,1024]{3,2,1,0:T(8,128)(2,1)}, bf16[2,2,4,64,1024]{4,3,2,1,0:T(8,128)(2,1)}, f32[1...) custom-call(bf16[2,4,64,2048]{3,2,1,0:T(8,128)(2,1)} %bitcast.53, ...), custom_call_target="tpu_custom_call" | custom-call | bytes 262144000 | tf_op jit(solution)/shard_map/gather_weights/pallas_call | solution.py:758
  110.7 0.0 copy-start.12
  110.8 0.0 copy-start.8
  110.8 0.0 all-gather.5.cloned.1.call-update
  110.8 0.0 all-gather.7.cloned.1.call-start
  110.9 0.1 multiply_sine_fusion
  111.1 0.1 tile.21
  111.2 0.1 copy.37.sin_ref
  111.3 0.1 tile.9
  111.5 0.1 copy.36.cos_ref
  111.6 0.0 copy-done.17
  111.6 0.0 copy-done.18
  111.6 0.0 copy-done.15
  111.7 0.7 pad_maximum_fusion.b_ref
  112.4 47.4 %project_qkv.1 = (f32[128,3072]{1,0:T(8,128)}, bf16[128,2048]{1,0:T(8,128)(2,1)}, f32[1,5120]{1,0:T(1,128)}, f32[16,5120]{1,0:T(8,128)}, bf16[8,128,1024]{2,1,0:...) custom-call(bf16[128,2048]{1,0:T(8,128)(2,1)} %get-tuple-element.87.u_ref, ...), custom_call_target="tpu_custom_call" | custom-call | flops 2684354560 | bytes 67108864 | tf_op jit(solution)/shard_map/project_qkv/pallas_call | solution.py:219
  159.8 0.0 copy-done.8
  159.8 0.0 copy-start
  159.8 0.0 copy-start.3
  159.8 0.0 all-gather.7.cloned.1.call-update
  159.9 0.0 reduce-scatter.3.cloned.1.call-start
  160.6 11.6 %attend.1 = (bf16[2,64,2048]{2,1,0:T(8,128)(2,1)}, bf16[2,4,512,512]{3,2,1,0:T(8,128)(2,1)}) custom-call(s32[2]{0:T(128)S(1)} %broadcast_add_fusion.valid_ref, bf16[2,64,2048]{2,1,0:T(8,128)(2,1)} %bitcast.64, bf16[8,2,64,1024]{3,2,1,0:T(8,128)(2,1)} %bitcast.54), custom_call_target="tpu_custom_call" | custom-call | flops 1073741824 | bytes 8388608 | tf_op jit(solution)/shard_map/attend/pallas_call | solution.py:947
  172.2 0.0 copy-done.3
  172.2 7.8 %project_out.1 = (f32[128,2048]{1,0:T(8,128)}, f32[128,2048]{1,0:T(8,128)}, bf16[128,2048]{1,0:T(8,128)(2,1)}, bf16[128,128]{1,0:T(8,128)(2,1)}) custom-call(bf16[128,2048]{1,0:T(8,128)(2,1)} %bitcast.58, f32[4,16,2048]{2,1,0:T(8,128)} %a_ref.7, bf16[2,2048,2560]{2,1,0:T(8,128)(2,1)} %bitcast.45, f32[16,5120]{1,0:T(8,128)} %pad_maximum_fusion.b_ref, ...), custom_call_target="tpu_custom_call" | custom-call | flops 1073741824 | bytes 8388608 | tf_op jit(solution)/shard_map/project_out/pallas_call | solution.py:296
  180.0 47.0 %gather_seq.1 = (bf16[8,128,2048]{2,1,0:T(8,128)(2,1)}, bf16[8,128,128]{2,1,0:T(8,128)(2,1)}, bf16[8,64,1024]{2,1,0:T(8,128)(2,1)}, bf16[8,64,1024]{2,1,0:T(8,12...) custom-call(bf16[128,2048]{1,0:T(8,128)(2,1)} %get-tuple-element.103.refs_0_, ...), custom_call_target="tpu_custom_call" | custom-call | bytes 89128960 | tf_op jit(solution)/shard_map/gather_seq/pallas_call | solution.py:869
  227.0 0.0 all-gather.5.cloned.1.call-done
  227.0 0.0 all-gather.7.cloned.1.call-done
  227.0 64.8 %feed_forward.1 = (f32[128,2048]{1,0:T(8,128)}, bf16[8,64,2048]{2,1,0:T(8,128)(2,1)}, bf16[8,64,2048]{2,1,0:T(8,128)(2,1)}, f32[2,16,2048]{2,1,0:T(8,128)}, f32[...) custom-call(bf16[2,8,64,1024]{3,2,1,0:T(8,128)(2,1)} %get-tuple-elem, ...), custom_call_target="tpu_custom_call" | custom-call | flops 25769803776 | bytes 33554432 | tf_op jit(solution)/shard_map/feed_forward/pallas_call | solution.py:1339
  291.8 0.0 reduce-scatter.3.cloned.1.call-update
  291.8 0.0 reduce-scatter.5.cloned.1.call-start
  291.8 9.9 %out_back.1 = (f32[128,2048]{1,0:T(8,128)}, bf16[128,2048]{1,0:T(8,128)(2,1)}, f32[16,2048]{1,0:T(8,128)S(1)}, f32[16,2048]{1,0:T(8,128)S(1)}, f32[1,2048]{1,0:T(1,128)S(1)}) custom-call(f32[128,2048]{1,0:T(8,128)} %get-tuple-element.114.in_ref, f32[128,2048]{1,0:T(8,128)} %get-tuple-element.115.x1_ref.x1, f32[2,2048]{1,0:T(2,128)S(1)} %copy-done.3, ...), custom_call_target="tpu_custom_call" | custom-call | bytes 1048576 | tf_op jit(solution)/shard_map/out_back/pallas_call | solution.py:367
  301.8 11.9 %attend_back.1 = (bf16[2,64,2048]{2,1,0:T(8,128)(2,1)}, bf16[8,2,64,1024]{3,2,1,0:T(8,128)(2,1)}) custom-call(bf16[2,64,2048]{2,1,0:T(8,128)(2,1)} %bitcast.65, bf16[8,2,64,1024]{3,2,1,0:T(8,128)(2,1)} %bitcast.55, bf16[2,4,512,512]{3,2,1,0:T(8,128)(2,1)} %get-tuple-element.97.p_ref, bf16[2,64,2048]{2,1,0:T(8,128)(2,1)} %bitcast.66), custom_call_target="tpu_custom_call" | custom-call | bytes 1048576 | tf_op jit(solution)/shard_map/attend_back/pallas_call | solution.py:1004
  313.7 39.8 %scatter_seq.1 = (f32[128,1024]{1,0:T(8,128)S(1)}, bf16[4,2,4,16,1024]{4,3,2,1,0:T(8,128)(2,1)S(1)}) custom-call(bf16[8,128,1024]{2,1,0:T(8,128)(2,1)} %bitcast.62, f32[2,16,1024]{2,1,0:T(8,128)S(1)} %copy-done.4, f32[2,1,1024]{2,1,0:T(1,128)S(1)} %copy-done.13, f32[2,1,1024]{2,1,0:T(1,128)S(1)} %copy-done.14, f32[16,1024]{1,0:T(8,128)S(1)} %copy-done.7), custom_call_target="tpu_custom_call" | custom-call | bytes 1048576 | tf_op jit(solution)/shard_map/scatter_seq/pallas_call | solution.py:1570
  353.5 0.0 reduce-scatter.3.cloned.1.call-done.before_0
  353.5 0.0 reduce-scatter.5.cloned.1.call-update
  353.6 0.0 copy-start.6
  353.6 0.0 copy-start.9
  353.6 0.0 copy-start.10
  353.6 12.3 %qkv_back.1 = (f32[128,2048]{1,0:T(8,128)}, f32[3,16,2048]{2,1,0:T(8,128)S(1)}, f32[16,3072]{1,0:T(8,128)S(1)}, f32[1,3072]{1,0:T(1,128)S(1)}) custom-call(bf16[128,2048]{1,0:T(8,128)(2,1)} %bitcast.63, f32[128,1024]{1,0:T(8,128)S(1)} %get-tuple-element.128.gkv_ref, f32[128,128]{1,0:T(8,128)S(1)} %copy.36.cos_ref, f32[128,128]{1,0:T(8,128)S(1)} %copy.37.sin_ref, ...), custom_call_target="tpu_custom_call" | custom-call | bytes 1048576 | tf_op jit(solution)/shard_map/qkv_back/pallas_call | solution.py:455
  365.9 0.0 copy-done.11
  365.9 25.4 %sum_gradients.1.whole = bf16[4,2,4,40,256]{4,3,2,1,0:T(8,128)(2,1)S(1)} custom-call(f32[3,16,2048]{2,1,0:T(8,128)S(1)} %get-tuple-element.131.ga_qkv, f32[16,2048]{1,0:T(8,128)S(1)} %get-tuple-element.132.ga_o, f32[16,3072]{1,0:T(8,128)S(1)} %get-tuple-element.133.gb_qkv, f32[16,2048]{1,0:T(8,128)S(1)} %get-tuple-element.134.gb_o, ...), custom_call_target="tpu_custom_call" | custom-call | bytes 1048576 | tf_op jit(solution)/shard_map/sum_gradients/pallas_call | solution.py:1700
  391.3 0.0 reduce-scatter.5.cloned.1.call-done.before_1
  391.3 0.0 copy-done.6
  391.3 0.0 copy-done.9
  391.3 3.4 finish.1
  (33 shorter events, 0.2 us)
Async XLA Ops:
  7.2 219.8 %all-gather.5.cloned.1.call-start = ((), (), s32[]{:S(2)}) async-start(), calls=%async_computation.4 | async-start | bytes 2359296 | tf_op jit(solution)/shard_map/all_gather | solution.py:1844
  7.2 0.7 copy-start.2
  7.9 103.6 %copy-start.19 = (f32[2,512]{1,0:T(2,128)S(1)}, f32[2,512]{1,0:T(2,128)}, u32[]{:S(2)}) copy-start(f32[2,512]{1,0:T(2,128)} %param.32) | copy-start | bytes 12292
  8.0 103.6 %copy-start.17 = (f32[2048]{0:T(1024)S(1)}, f32[2048]{0:T(1024)}, u32[]{:S(2)}) copy-start(f32[2048]{0:T(1024)} %param.33) | copy-start | bytes 24580
  8.0 103.6 %copy-start.18 = (f32[2048]{0:T(1024)S(1)}, f32[2048]{0:T(1024)}, u32[]{:S(2)}) copy-start(f32[2048]{0:T(1024)} %param.31) | copy-start | bytes 24580
  8.0 103.7 %copy-start.16 = (f32[2,16,512]{2,1,0:T(8,128)S(1)}, f32[2,16,512]{2,1,0:T(8,128)}, u32[]{:S(2)}) copy-start(f32[2,16,512]{2,1,0:T(8,128)} %param.30) | copy-start | bytes 196612
  8.0 103.7 %copy-start.15 = (f32[2,16,2048]{2,1,0:T(8,128)S(1)}, f32[2,16,2048]{2,1,0:T(8,128)}, u32[]{:S(2)}) copy-start(f32[2,16,2048]{2,1,0:T(8,128)} %param.29) | copy-start | bytes 786436
  110.7 1.7 copy-start.12
  110.8 49.1 %copy-start.8 = (bf16[7,32,16]{2,1,0:T(8,128)(2,1)}, bf16[7,32,16]{2,1,0:T(8,128)(2,1)S(1)}, u32[]{:S(2)}) copy-start(bf16[7,32,16]{2,1,0:T(8,128)(2,1)S(1)} %get-tuple-element.89.gram_ref.refs_20_) | copy-start | bytes 21508
  110.8 116.2 %all-gather.7.cloned.1.call-start = ((), (), s32[]{:S(2)}) async-start(), calls=%async_computation.5 | async-start | bytes 2359296 | tf_op jit(solution)/shard_map/all_gather | solution.py:1873
  112.4 48.1 %copy-start.20 = (s32[2]{0:T(128)S(1)}, s32[2]{0:T(128)}, u32[]{:S(2)}) copy-start(s32[2]{0:T(128)} %param.41) | copy-start | bytes 28
  159.8 12.3 %copy-start = (f32[1,5120]{1,0:T(1,128)S(1)}, f32[1,5120]{1,0:T(1,128)}, u32[]{:S(2)}) copy-start(f32[1,5120]{1,0:T(1,128)} %get-tuple-element.102.n_ref.n_attn) | copy-start | bytes 61444
  159.8 12.3 %copy-start.3 = (f32[2,2048]{1,0:T(2,128)S(1)}, f32[2,2048]{1,0:T(2,128)}, u32[]{:S(2)}) copy-start(f32[2,2048]{1,0:T(2,128)} %gain_ref.7) | copy-start | bytes 49156
  159.9 193.7 %reduce-scatter.3.cloned.1.call-start = ((), (), s32[]{:S(2)}) async-start(), calls=%async_computation.2 | async-start | bytes 2359296 | tf_op jit(solution)/shard_map/reduce_scatter | solution.py:1891
  291.8 99.5 %reduce-scatter.5.cloned.1.call-start = ((), (), s32[]{:S(2)}) async-start(), calls=%async_computation.3 | async-start | bytes 2359296 | tf_op jit(solution)/shard_map/reduce_scatter | solution.py:1903
  301.8 11.9 %copy-start.4 = (f32[2,16,1024]{2,1,0:T(8,128)S(1)}, f32[2,16,1024]{2,1,0:T(8,128)}, u32[]{:S(2)}) copy-start(f32[2,16,1024]{2,1,0:T(8,128)} %get-tuple-element.121.gb_gu) | copy-start | bytes 393220
  301.8 11.9 %copy-start.7 = (f32[16,1024]{1,0:T(8,128)S(1)}, f32[16,1024]{1,0:T(8,128)}, u32[]{:S(2)}) copy-start(f32[16,1024]{1,0:T(8,128)} %get-tuple-element.124.ga_d) | copy-start | bytes 196612
  301.8 11.9 %copy-start.13 = (f32[2,1,1024]{2,1,0:T(1,128)S(1)}, f32[2,1,1024]{2,1,0:T(1,128)}, u32[]{:S(2)}) copy-start(f32[2,1,1024]{2,1,0:T(1,128)} %get-tuple-element.122.gm_gu) | copy-start | bytes 24580
  301.8 11.9 %copy-start.14 = (f32[2,1,1024]{2,1,0:T(1,128)S(1)}, f32[2,1,1024]{2,1,0:T(1,128)}, u32[]{:S(2)}) copy-start(f32[2,1,1024]{2,1,0:T(1,128)} %get-tuple-element.123.n_gu) | copy-start | bytes 24580
  353.6 12.3 %copy-start.1 = (f32[2,16,2048]{2,1,0:T(8,128)S(1)}, f32[2,16,2048]{2,1,0:T(8,128)}, u32[]{:S(2)}) copy-start(f32[2,16,2048]{2,1,0:T(8,128)} %get-tuple-element.135.ga_gu) | copy-start | bytes 786436
  353.6 12.3 %copy-start.5 = (f32[16,2048]{1,0:T(8,128)S(1)}, f32[16,2048]{1,0:T(8,128)}, u32[]{:S(2)}) copy-start(f32[16,2048]{1,0:T(8,128)} %get-tuple-element.136.gb_d) | copy-start | bytes 393220
  353.6 12.3 %copy-start.11 = (f32[1,2048]{1,0:T(1,128)S(1)}, f32[1,2048]{1,0:T(1,128)}, u32[]{:S(2)}) copy-start(f32[1,2048]{1,0:T(1,128)} %get-tuple-element.139.gm_d) | copy-start | bytes 24580
  353.6 37.7 %copy-start.6 = (f32[2,8192]{1,0:T(2,128)S(1)}, f32[2,8192]{1,0:T(2,128)}, u32[]{:S(2)}) copy-start(f32[2,8192]{1,0:T(2,128)} %m_gu.1) | copy-start | bytes 196612
  353.6 37.7 %copy-start.9 = (f32[2048]{0:T(1024)S(1)}, f32[2048]{0:T(1024)}, u32[]{:S(2)}) copy-start(f32[2048]{0:T(1024)} %param.39) | copy-start | bytes 24580
  353.6 37.7 %copy-start.10 = (f32[1,2048]{1,0:T(1,128)S(1)}, f32[1,2048]{1,0:T(1,128)}, u32[]{:S(2)}) copy-start(f32[1,2048]{1,0:T(1,128)} %get-tuple-element.143.n_d) | copy-start | bytes 24580
Sparse Core Ops, SparseCore 0:
  110.9 35.9 all-gather.4
  160.0 28.8 all-gather.6
  291.9 35.2 reduce-scatter.2
  353.7 35.8 reduce-scatter.4

commit v11 on v10

--- a/solution.py
+++ b/solution.py
@@ -911,30 +911,30 @@
     return jnp.concatenate(pairs, axis=1)
 
 
-def key_blocks(kv_ref):
+def key_blocks(kv_ref, j):
     n, _, span, width = kv_ref.shape
-    at = pl.multiple_of(pl.program_id(1) * 128, 128)
-    pick = lambda start: kv_ref[:, 0, :, pl.ds(start, 128)].reshape(n * span, 128)
-    return pick(at), pick(width // 2 + at)
+    pick = lambda start: kv_ref[:, 0, :, start : start + 128].reshape(n * span, 128)
+    return pick(128 * j), pick(width // 2 + 128 * j)
 
 
 def attend_kernel(valid_ref, q_ref, kv_ref, o_ref, p_ref, s_ref):
     span = q_ref.shape[1]
     keys = kv_ref.shape[0] * span
-    q8 = stack_heads(q_ref[0]) * jnp.bfloat16(HEAD_DIM**-0.5)
-    k2, v2 = key_blocks(kv_ref)
-    s_ref[...] = lax.dot_general(q8, k2, last_last, preferred_element_type=jnp.float32)
     q_pos = lax.axis_index("seq") * span + lax.broadcasted_iota(jnp.int32, (span, 1), 0)
     limit = jnp.minimum(q_pos + 1, valid_ref[pl.program_id(0)])
     allowed = lax.broadcasted_iota(jnp.int32, (span, keys), 1) < limit
-    for h in range(8):
-        head = slice(h * span, (h + 1) * span)
-        scores = jnp.where(allowed, s_ref[head], -1e30)
-        unscaled = jnp.exp(scores - jnp.max(scores, axis=1, keepdims=True))
-        shares = unscaled * (1.0 / jnp.sum(unscaled, axis=1, keepdims=True))
-        p_ref[0, 0, head] = shares.astype(jnp.bfloat16)
-    mixed = jnp.dot(p_ref[0, 0], v2, preferred_element_type=jnp.float32)
-    o_ref[0] = unstack_heads(mixed, span).astype(jnp.bfloat16)
+    for j in range(p_ref.shape[1]):
+        at = slice(512 * j, 512 * (j + 1))
+        q8 = stack_heads(q_ref[0, :, at]) * jnp.bfloat16(HEAD_DIM**-0.5)
+        k2, v2 = key_blocks(kv_ref, j)
+        s_ref[j % 2] = dot_nt(q8, k2)
+        for h in range(8):
+            head = slice(h * span, (h + 1) * span)
+            scores = jnp.where(allowed, s_ref[j % 2, head], -1e30)
+            unscaled = jnp.exp(scores - jnp.max(scores, axis=1, keepdims=True))
+            shares = unscaled * (1.0 / jnp.sum(unscaled, axis=1, keepdims=True))
+            p_ref[0, j, head] = shares.astype(jnp.bfloat16)
+        o_ref[0, :, at] = unstack_heads(dot_f32(p_ref[0, j], v2), span).astype(jnp.bfloat16)
 
 
 def attend(q, kv, valid):
@@ -942,7 +942,7 @@
     n, kv_width = kv.shape[0], kv.shape[3] // 2
     groups = kv_width // 128
     keys = n * span
-    q_spec = pl.BlockSpec((1, span, 512), lambda p, j, *_: (p, 0, j))
+    q_spec = pl.BlockSpec((1, span, width), lambda p, *_: (p, 0, 0))
     flops = 4 * pair * groups * 8 * span * keys * 128
     return pl.pallas_call(
         attend_kernel,
@@ -952,16 +952,13 @@
         ),
         grid_spec=pltpu.PrefetchScalarGridSpec(
             num_scalar_prefetch=1,
-            grid=(pair, groups),
-            in_specs=[
-                q_spec,
-                pl.BlockSpec((n, 1, span, 2 * kv_width), lambda p, j, *_: (0, p, 0, 0)),
-            ],
+            grid=(pair,),
+            in_specs=[q_spec, pl.BlockSpec((n, 1, span, 2 * kv_width), lambda p, *_: (0, p, 0, 0))],
             out_specs=(
                 q_spec,
-                pl.BlockSpec((1, 1, 8 * span, keys), lambda p, j, *_: (p, j, 0, 0)),
+                pl.BlockSpec((1, groups, 8 * span, keys), lambda p, *_: (p, 0, 0, 0)),
             ),
-            scratch_shapes=[pltpu.VMEM((8 * span, keys), jnp.float32)],
+            scratch_shapes=[pltpu.VMEM((2, 8 * span, keys), jnp.float32)],
         ),
         compiler_params=pltpu.CompilerParams(vmem_limit_bytes=40 << 20),
         cost_estimate=pl.CostEstimate(
@@ -973,56 +970,52 @@
 
 def attend_back_kernel(q_ref, kv_ref, p_ref, g_ref, gq_ref, gkv_ref, s_ref, g_scores):
     span = q_ref.shape[1]
-    keys = kv_ref.shape[0] * span
-    q8 = stack_heads(q_ref[0]) * jnp.bfloat16(HEAD_DIM**-0.5)
-    g8 = stack_heads(g_ref[0])
-    k2, v2 = key_blocks(kv_ref)
-    low = p_ref[0, 0]
-    s_ref[...] = lax.dot_general(g8, v2, last_last, preferred_element_type=jnp.float32)
-    for h in range(8):
-        head = slice(h * span, (h + 1) * span)
-        shares = p_ref[0, 0, head].astype(jnp.float32)
-        weighted = shares * s_ref[head]
-        centre = jnp.sum(weighted, axis=1, keepdims=True)
-        g_scores[head] = (weighted - shares * centre).astype(jnp.bfloat16)
-    grad_scores = g_scores[...]
-    gq = jnp.dot(grad_scores, k2, preferred_element_type=jnp.float32) * HEAD_DIM**-0.5
-    gq_ref[0] = unstack_heads(gq, span).astype(jnp.bfloat16)
-    gk = lax.dot_general(grad_scores, q8, first_first, preferred_element_type=jnp.float32)
-    gv = lax.dot_general(low, g8, first_first, preferred_element_type=jnp.float32)
-    both = jnp.concatenate([gk, gv], axis=1).astype(jnp.bfloat16)
-    at = pl.multiple_of(pl.program_id(1) * 256, 256)
-    gkv_ref[:, 0, :, pl.ds(at, 256)] = both.reshape(gkv_ref.shape[0], span, 256)
+    n = kv_ref.shape[0]
+    for j in range(p_ref.shape[1]):
+        at = slice(512 * j, 512 * (j + 1))
+        q8 = stack_heads(q_ref[0, :, at]) * jnp.bfloat16(HEAD_DIM**-0.5)
+        g8 = stack_heads(g_ref[0, :, at])
+        k2, v2 = key_blocks(kv_ref, j)
+        s_ref[j % 2] = dot_nt(g8, v2)
+        for h in range(8):
+            head = slice(h * span, (h + 1) * span)
+            shares = p_ref[0, j, head].astype(jnp.float32)
+            weighted = shares * s_ref[j % 2, head]
+            centre = jnp.sum(weighted, axis=1, keepdims=True)
+            g_scores[j % 2, head] = (weighted - shares * centre).astype(jnp.bfloat16)
+        grad_scores = g_scores[j % 2]
+        gq = dot_f32(grad_scores, k2) * HEAD_DIM**-0.5
+        gq_ref[0, :, at] = unstack_heads(gq, span).astype(jnp.bfloat16)
+        both = jnp.concatenate([dot_tn(grad_scores, q8), dot_tn(p_ref[0, j], g8)], axis=1)
+        gkv_ref[:, 0, :, 256 * j : 256 * (j + 1)] = both.astype(jnp.bfloat16).reshape(n, span, 256)
 
 
 def attend_back(q, kv, shares, g):
-    pair, span, _ = q.shape
+    pair, span, width = q.shape
     n, kv_width = kv.shape[0], kv.shape[3] // 2
     groups = kv_width // 128
     keys = n * span
-    q_spec = pl.BlockSpec((1, span, 512), lambda p, j: (p, 0, j))
+    q_spec = pl.BlockSpec((1, span, width), lambda p: (p, 0, 0))
+    kv_spec = pl.BlockSpec((n, 1, span, 2 * kv_width), lambda p: (0, p, 0, 0))
     return pl.pallas_call(
         attend_back_kernel,
         out_shape=(
             pltpu.HBM(q.shape, jnp.bfloat16),
             pltpu.HBM(kv.shape, jnp.bfloat16),
         ),
-        grid=(pair, groups),
+        grid=(pair,),
         in_specs=[
             q_spec,
-            pl.BlockSpec((n, 1, span, 2 * kv_width), lambda p, j: (0, p, 0, 0)),
-            pl.BlockSpec((1, 1, 8 * span, keys), lambda p, j: (p, j, 0, 0)),
+            kv_spec,
+            pl.BlockSpec((1, groups, 8 * span, keys), lambda p: (p, 0, 0, 0)),
             q_spec,
         ],
-        out_specs=(
-            q_spec,
-            pl.BlockSpec((n, 1, span, 2 * kv_width), lambda p, j: (0, p, 0, 0)),
-        ),
+        out_specs=(q_spec, kv_spec),
         scratch_shapes=[
-            pltpu.VMEM((8 * span, keys), jnp.float32),
-            pltpu.VMEM((8 * span, keys), jnp.bfloat16),
+            pltpu.VMEM((2, 8 * span, keys), jnp.float32),
+            pltpu.VMEM((2, 8 * span, keys), jnp.bfloat16),
         ],
-        compiler_params=pltpu.CompilerParams(vmem_limit_bytes=40 << 20),
+        compiler_params=pltpu.CompilerParams(vmem_limit_bytes=48 << 20),
         cost_estimate=pl.CostEstimate(flops=0, transcendentals=0, bytes_accessed=1 << 20),
         name="attend_back",
     )(*in_hbm(q, kv, shares, g))
@@ -1399,35 +1392,38 @@
     f32, low = jnp.float32, jnp.bfloat16
     unit_rows, size = units.shape[1:]
 
+    cut = own.shape[1] // 2
+    part = lambda k: pl.ds(k * cut, cut)
+
     def load(p):
         return pltpu.make_async_copy(x_ref.at[2 * p + c], own.at[p], load_sem.at[p])
 
-    def to_sibling(p):
+    def to_sibling(p, k):
         return pltpu.make_async_remote_copy(
-            src_ref=x_ref.at[2 * p + theirs],
-            dst_ref=sib.at[p],
-            send_sem=to_sib.at[p],
-            recv_sem=sib_in.at[p],
+            src_ref=x_ref.at[2 * p + theirs, part(k)],
+            dst_ref=sib.at[p, part(k)],
+            send_sem=to_sib.at[p, k],
+            recv_sem=sib_in.at[p, k],
             device_id={"seq": sibling},
             device_id_type=MESH,
         )
 
-    def rightward(p, target):
+    def rightward(p, k, target):
         return pltpu.make_async_remote_copy(
-            src_ref=own.at[p],
-            dst_ref=from_left.at[p],
-            send_sem=to_right.at[p],
-            recv_sem=right_in.at[p],
+            src_ref=own.at[p, part(k)],
+            dst_ref=from_left.at[p, part(k)],
+            send_sem=to_right.at[p, k],
+            recv_sem=right_in.at[p, k],
             device_id={"seq": target},
             device_id_type=MESH,
         )
 
-    def leftward(p, target):
+    def leftward(p, k, target):
         return pltpu.make_async_remote_copy(
-            src_ref=own.at[p],
-            dst_ref=from_right.at[p],
-            send_sem=to_left.at[p],
-            recv_sem=left_in.at[p],
+            src_ref=own.at[p, part(k)],
+            dst_ref=from_right.at[p, part(k)],
+            send_sem=to_left.at[p, k],
+            recv_sem=left_in.at[p, k],
             device_id={"seq": target},
             device_id_type=MESH,
         )
@@ -1438,8 +1434,9 @@
             if p not in order:
                 order.append(p)
     for p in order:
-        to_sibling(p).start()
         load(p).start()
+        for k in range(2):
+            to_sibling(p, k).start()
 
     n_high = [n_gu[g].astype(low).astype(f32) for g in range(2)]
     n_rest = [n_gu[g] - n_high[g] for g in range(2)]
@@ -1493,51 +1490,45 @@
 
     for t in range(1, rows):
         unit_send(t).start()
+    def add_and_send(p, k, flow, arrived, more, target):
+        at = part(k)
+
+        @pl.when(more)
+        def _():
+            flow(p, k, s).wait_recv()
+            total = own[p, at].astype(f32) + sib[p, at].astype(f32) + arrived[p, at].astype(f32)
+            own[p, at] = total.astype(own.dtype)
+
+        @pl.when(jnp.logical_not(more))
+        def _():
+            own[p, at] = (own[p, at].astype(f32) + sib[p, at].astype(f32)).astype(own.dtype)
+
+        flow(p, k, target).start()
+
     sum_units()
-    for step, p in enumerate(order):
+    for step, p in enumerate(jnp.where(q <= nc - 1 - q, p, nc - 1 - p) for p in order):
         if step == 1:
             spread_units()
         load(p).wait()
-        to_sibling(p).wait_recv()
-
-        @pl.when(p > q)
-        def _(p=p):
-            @pl.when(q > 0)
-            def _():
-                rightward(p, s).wait_recv()
-                total = own[p].astype(f32) + sib[p].astype(f32) + from_left[p].astype(f32)
-                own[p] = total.astype(own.dtype)
-
-            @pl.when(q == 0)
-            def _():
-                own[p] = (own[p].astype(f32) + sib[p].astype(f32)).astype(own.dtype)
-
-            rightward(p, s + 2).start()
-
-        @pl.when(p < q)
-        def _(p=p):
-            @pl.when(q < nc - 1)
-            def _():
-                leftward(p, s).wait_recv()
-                total = own[p].astype(f32) + sib[p].astype(f32) + from_right[p].astype(f32)
-                own[p] = total.astype(own.dtype)
-
-            @pl.when(q == nc - 1)
-            def _():
-                own[p] = (own[p].astype(f32) + sib[p].astype(f32)).astype(own.dtype)
-
-            leftward(p, s - 2).start()
+        for k in range(2):
+            to_sibling(p, k).wait_recv()
+            pl.when(p > q)(lambda p=p, k=k: add_and_send(p, k, rightward, from_left, q > 0, s + 2))
+            pl.when(p < q)(
+                lambda p=p, k=k: add_and_send(p, k, leftward, from_right, q < nc - 1, s - 2)
+            )
 
     o_ref[...] = own[q].astype(f32) + sib[q].astype(f32)
 
     @pl.when(q > 0)
     def _():
-        rightward(q, s).wait_recv()
+        for k in range(2):
+            rightward(q, k, s).wait_recv()
         o_ref[...] += from_left[q].astype(f32)
 
     @pl.when(q < nc - 1)
     def _():
-        leftward(q, s).wait_recv()
+        for k in range(2):
+            leftward(q, k, s).wait_recv()
         o_ref[...] += from_right[q].astype(f32)
 
     for t in range(1, rows):
@@ -1552,9 +1543,10 @@
     for t in range(1, nc):
         unit_back(t, q).wait_send()
     for p in range(nc):
-        to_sibling(p).wait_send()
-        pl.when(p > q)(lambda p=p: rightward(p, s).wait_send())
-        pl.when(p < q)(lambda p=p: leftward(p, s).wait_send())
+        for k in range(2):
+            to_sibling(p, k).wait_send()
+            pl.when(p > q)(lambda p=p, k=k: rightward(p, k, s).wait_send())
+            pl.when(p < q)(lambda p=p, k=k: leftward(p, k, s).wait_send())
 
 
 def scatter_seq(n, rows, x, own_units, collective_id):
@@ -1575,7 +1567,7 @@
         ),
         in_specs=[pl.BlockSpec(memory_space=pltpu.HBM)] + [vmem] * 4,
         out_specs=(vmem,) * 2,
-        scratch_shapes=[buf] * 4 + [small] * 2 + [dma((nc,))] * 7
+        scratch_shapes=[buf] * 4 + [small] * 2 + [dma((nc,))] + [dma((nc, 2))] * 6
         + [dma((rows,))] * 2 + [dma((nc,))] * 2 + [dma((rows,))] * 4,
         compiler_params=pltpu.CompilerParams(
             collective_id=collective_id, has_side_effects=True, vmem_limit_bytes=32 << 20

time: 402 us -> 392 us (0.975)
  Pallas kernels: 384 us -> 374 us
    pallas_call x1, Pallas kernels: 39.8 us -> 29.6 us  [scatter_seq(): pl.pallas_call(functools.partial(scatter_kernel, n, rows), out_shape=(jax...]
    pallas_call x1, Pallas kernels: 47 us -> 51.1 us  [gather_seq(): pl.pallas_call(functools.partial(gather_kernel, n, rows, count, (range(le...]
    pallas_call x1, Pallas kernels: 11.6 us -> 7.52 us  [attend(): pl.pallas_call(attend_kernel, out_shape=(pltpu.HBM(q.shape, jnp.bfloat16)...]
  transfers between devices with their start and end apart: 4 -> 4, of which waited for: 0 -> 0; matrix products, arithmetic and copies ran while one was open for 0% -> 0% of each run, Pallas kernels for 53% -> 52%
where the time goes in v11:
time: 392 us
  Pallas kernels  374 us (95%)
  between operations  14.8 us (4%)
    pallas_call x1, Pallas kernels, gather_weights(): pl.pallas_call(functools.partial(weights_kernel, n, rows), out_shape=(plt...  103 us
    pallas_call x1, Pallas kernels, feed_forward(): pl.pallas_call(kernel, out_shape=(shape((tokens, width), f32), pltpu.HBM(...  64.7 us
    pallas_call x1, Pallas kernels, gather_seq(): pl.pallas_call(functools.partial(gather_kernel, n, rows, count, (range(le...  51.1 us
    pallas_call x1, Pallas kernels, project_qkv(): pl.pallas_call(functools.partial(project_kernel, n, rows, plan, k_tiles,...  47.4 us
    pallas_call x1, Pallas kernels, scatter_seq(): pl.pallas_call(functools.partial(scatter_kernel, n, rows), out_shape=(jax...  29.6 us
    pallas_call x1, Pallas kernels, sum_gradients(): pl.pallas_call(functools.partial(reduce_kernel, n, rows), out_shape=jax.S...  27.5 us
    pallas_call x1, Pallas kernels, qkv_back(): pl.pallas_call(qkv_back_kernel, out_shape=(pltpu.HBM((rows, width), f32),...  12.5 us
    pallas_call x1, Pallas kernels, attend_back(): pl.pallas_call(attend_back_kernel, out_shape=(pltpu.HBM(q.shape, jnp.bflo...  10.1 us
  transfers between devices with their start and end apart: 4, of which 0 were waited for; matrix products, arithmetic and copies ran while one was open for 0% of the time, Pallas kernels for 52%

profile of v11, /device:TPU:0, one launch (start us, length us, event | category | flops | bytes accessed | tf_op | source)
XLA Modules:
  0.0 391.8 jit_solution(1605626315740320333)
XLA Ops:
  7.2 0.0 all-gather.5.cloned.1.call-start
  7.2 0.0 copy-start.2
  7.2 0.7 copy-done.2
  8.0 0.0 copy-start.15
  8.0 102.8 %gather_weights.1 = (bf16[2,8,4,64,2560]{4,3,2,1,0:T(8,128)(2,1)}, bf16[2,8,64,1024]{3,2,1,0:T(8,128)(2,1)}, bf16[2,2,4,64,1024]{4,3,2,1,0:T(8,128)(2,1)}, f32[1...) custom-call(bf16[2,4,64,2048]{3,2,1,0:T(8,128)(2,1)} %bitcast.53, ...), custom_call_target="tpu_custom_call" | custom-call | bytes 262144000 | tf_op jit(solution)/shard_map/gather_weights/pallas_call | solution.py:758
  110.7 0.0 copy-start.12
  110.8 0.0 copy-start.8
  110.8 0.0 all-gather.5.cloned.1.call-update
  110.8 0.0 all-gather.7.cloned.1.call-start
  110.9 0.1 multiply_sine_fusion
  111.1 0.1 tile.21
  111.2 0.1 copy.37.sin_ref
  111.3 0.1 tile.9
  111.5 0.1 copy.36.cos_ref
  111.6 0.0 copy-done.19
  111.6 0.0 copy-done.17
  111.6 0.0 copy-done.18
  111.6 0.0 copy-done.16
  111.6 0.0 copy-done.15
  111.7 0.7 pad_maximum_fusion.b_ref
  112.4 47.4 %project_qkv.1 = (f32[128,3072]{1,0:T(8,128)}, bf16[128,2048]{1,0:T(8,128)(2,1)}, f32[1,5120]{1,0:T(1,128)}, f32[16,5120]{1,0:T(8,128)}, bf16[8,128,1024]{2,1,0:...) custom-call(bf16[128,2048]{1,0:T(8,128)(2,1)} %get-tuple-element.87.u_ref, ...), custom_call_target="tpu_custom_call" | custom-call | flops 2684354560 | bytes 67108864 | tf_op jit(solution)/shard_map/project_qkv/pallas_call | solution.py:219
  159.8 0.0 copy-done.8
  159.8 0.0 copy-start
  159.8 0.0 copy-start.3
  159.8 0.0 all-gather.7.cloned.1.call-update
  159.9 0.0 reduce-scatter.3.cloned.1.call-start
  160.6 7.5 %attend.1 = (bf16[2,64,2048]{2,1,0:T(8,128)(2,1)}, bf16[2,4,512,512]{3,2,1,0:T(8,128)(2,1)}) custom-call(s32[2]{0:T(128)S(1)} %broadcast_add_fusion.valid_ref, bf16[2,64,2048]{2,1,0:T(8,128)(2,1)} %bitcast.64, bf16[8,2,64,1024]{3,2,1,0:T(8,128)(2,1)} %bitcast.54), custom_call_target="tpu_custom_call" | custom-call | flops 1073741824 | bytes 8388608 | tf_op jit(solution)/shard_map/attend/pallas_call | solution.py:947
  168.1 7.8 %project_out.1 = (f32[128,2048]{1,0:T(8,128)}, f32[128,2048]{1,0:T(8,128)}, bf16[128,2048]{1,0:T(8,128)(2,1)}, bf16[128,128]{1,0:T(8,128)(2,1)}) custom-call(bf16[128,2048]{1,0:T(8,128)(2,1)} %bitcast.58, f32[4,16,2048]{2,1,0:T(8,128)} %a_ref.7, bf16[2,2048,2560]{2,1,0:T(8,128)(2,1)} %bitcast.45, f32[16,5120]{1,0:T(8,128)} %pad_maximum_fusion.b_ref, ...), custom_call_target="tpu_custom_call" | custom-call | flops 1073741824 | bytes 8388608 | tf_op jit(solution)/shard_map/project_out/pallas_call | solution.py:296
  175.9 51.1 %gather_seq.1 = (bf16[8,128,2048]{2,1,0:T(8,128)(2,1)}, bf16[8,128,128]{2,1,0:T(8,128)(2,1)}, bf16[8,64,1024]{2,1,0:T(8,128)(2,1)}, bf16[8,64,1024]{2,1,0:T(8,12...) custom-call(bf16[128,2048]{1,0:T(8,128)(2,1)} %get-tuple-element.103.refs_0_, ...), custom_call_target="tpu_custom_call" | custom-call | bytes 89128960 | tf_op jit(solution)/shard_map/gather_seq/pallas_call | solution.py:869
  227.0 0.0 all-gather.5.cloned.1.call-done
  227.0 0.0 all-gather.7.cloned.1.call-done
  227.0 64.7 %feed_forward.1 = (f32[128,2048]{1,0:T(8,128)}, bf16[8,64,2048]{2,1,0:T(8,128)(2,1)}, bf16[8,64,2048]{2,1,0:T(8,128)(2,1)}, f32[2,16,2048]{2,1,0:T(8,128)}, f32[...) custom-call(bf16[2,8,64,1024]{3,2,1,0:T(8,128)(2,1)} %get-tuple-elem, ...), custom_call_target="tpu_custom_call" | custom-call | flops 25769803776 | bytes 33554432 | tf_op jit(solution)/shard_map/feed_forward/pallas_call | solution.py:1332
  291.8 0.0 reduce-scatter.3.cloned.1.call-update
  291.8 0.0 reduce-scatter.5.cloned.1.call-start
  291.9 9.9 %out_back.1 = (f32[128,2048]{1,0:T(8,128)}, bf16[128,2048]{1,0:T(8,128)(2,1)}, f32[16,2048]{1,0:T(8,128)S(1)}, f32[16,2048]{1,0:T(8,128)S(1)}, f32[1,2048]{1,0:T(1,128)S(1)}) custom-call(f32[128,2048]{1,0:T(8,128)} %get-tuple-element.114.in_ref, f32[128,2048]{1,0:T(8,128)} %get-tuple-element.115.x1_ref.x1, f32[2,2048]{1,0:T(2,128)S(1)} %copy-done.3, ...), custom_call_target="tpu_custom_call" | custom-call | bytes 1048576 | tf_op jit(solution)/shard_map/out_back/pallas_call | solution.py:367
  301.8 10.1 %attend_back.1 = (bf16[2,64,2048]{2,1,0:T(8,128)(2,1)}, bf16[8,2,64,1024]{3,2,1,0:T(8,128)(2,1)}) custom-call(bf16[2,64,2048]{2,1,0:T(8,128)(2,1)} %bitcast.65, bf16[8,2,64,1024]{3,2,1,0:T(8,128)(2,1)} %bitcast.55, bf16[2,4,512,512]{3,2,1,0:T(8,128)(2,1)} %get-tuple-element.97.p_ref, bf16[2,64,2048]{2,1,0:T(8,128)(2,1)} %bitcast.66), custom_call_target="tpu_custom_call" | custom-call | bytes 1048576 | tf_op jit(solution)/shard_map/attend_back/pallas_call | solution.py:1000
  312.0 29.6 %scatter_seq.1 = (f32[128,1024]{1,0:T(8,128)S(1)}, bf16[4,2,4,16,1024]{4,3,2,1,0:T(8,128)(2,1)S(1)}) custom-call(bf16[8,128,1024]{2,1,0:T(8,128)(2,1)} %bitcast.62, f32[2,16,1024]{2,1,0:T(8,128)S(1)} %copy-done.4, f32[2,1,1024]{2,1,0:T(1,128)S(1)} %copy-done.13, f32[2,1,1024]{2,1,0:T(1,128)S(1)} %copy-done.14, f32[16,1024]{1,0:T(8,128)S(1)} %copy-done.7), custom_call_target="tpu_custom_call" | custom-call | bytes 1048576 | tf_op jit(solution)/shard_map/scatter_seq/pallas_call | solution.py:1562
  341.6 0.0 reduce-scatter.3.cloned.1.call-done.before_0
  341.6 0.0 reduce-scatter.5.cloned.1.call-update
  341.7 0.0 copy-start.6
  341.7 0.0 copy-start.9
  341.7 0.0 copy-start.10
  341.7 12.5 %qkv_back.1 = (f32[128,2048]{1,0:T(8,128)}, f32[3,16,2048]{2,1,0:T(8,128)S(1)}, f32[16,3072]{1,0:T(8,128)S(1)}, f32[1,3072]{1,0:T(1,128)S(1)}) custom-call(bf16[128,2048]{1,0:T(8,128)(2,1)} %bitcast.63, f32[128,1024]{1,0:T(8,128)S(1)} %get-tuple-element.128.gkv_ref, f32[128,128]{1,0:T(8,128)S(1)} %copy.36.cos_ref, f32[128,128]{1,0:T(8,128)S(1)} %copy.37.sin_ref, ...), custom_call_target="tpu_custom_call" | custom-call | bytes 1048576 | tf_op jit(solution)/shard_map/qkv_back/pallas_call | solution.py:455
  354.2 0.0 copy-done.5
  354.2 0.0 copy-done.11
  354.2 27.5 %sum_gradients.1.whole = bf16[4,2,4,40,256]{4,3,2,1,0:T(8,128)(2,1)S(1)} custom-call(f32[3,16,2048]{2,1,0:T(8,128)S(1)} %get-tuple-element.131.ga_qkv, f32[16,2048]{1,0:T(8,128)S(1)} %get-tuple-element.132.ga_o, f32[16,3072]{1,0:T(8,128)S(1)} %get-tuple-element.133.gb_qkv, f32[16,2048]{1,0:T(8,128)S(1)} %get-tuple-element.134.gb_o, ...), custom_call_target="tpu_custom_call" | custom-call | bytes 1048576 | tf_op jit(solution)/shard_map/sum_gradients/pallas_call | solution.py:1692
  381.8 0.0 reduce-scatter.5.cloned.1.call-done.before_1
  381.8 3.4 finish.1
  (33 shorter events, 0.2 us)
Async XLA Ops:
  7.2 219.8 %all-gather.5.cloned.1.call-start = ((), (), s32[]{:S(2)}) async-start(), calls=%async_computation.4 | async-start | bytes 2359296 | tf_op jit(solution)/shard_map/all_gather | solution.py:1836
  7.2 0.7 copy-start.2
  7.9 103.6 %copy-start.19 = (f32[2,512]{1,0:T(2,128)S(1)}, f32[2,512]{1,0:T(2,128)}, u32[]{:S(2)}) copy-start(f32[2,512]{1,0:T(2,128)} %param.32) | copy-start | bytes 12292
  8.0 103.6 %copy-start.17 = (f32[2048]{0:T(1024)S(1)}, f32[2048]{0:T(1024)}, u32[]{:S(2)}) copy-start(f32[2048]{0:T(1024)} %param.33) | copy-start | bytes 24580
  8.0 103.6 %copy-start.18 = (f32[2048]{0:T(1024)S(1)}, f32[2048]{0:T(1024)}, u32[]{:S(2)}) copy-start(f32[2048]{0:T(1024)} %param.31) | copy-start | bytes 24580
  8.0 103.7 %copy-start.16 = (f32[2,16,512]{2,1,0:T(8,128)S(1)}, f32[2,16,512]{2,1,0:T(8,128)}, u32[]{:S(2)}) copy-start(f32[2,16,512]{2,1,0:T(8,128)} %param.30) | copy-start | bytes 196612
  8.0 103.7 %copy-start.15 = (f32[2,16,2048]{2,1,0:T(8,128)S(1)}, f32[2,16,2048]{2,1,0:T(8,128)}, u32[]{:S(2)}) copy-start(f32[2,16,2048]{2,1,0:T(8,128)} %param.29) | copy-start | bytes 786436
  110.7 1.7 copy-start.12
  110.8 49.1 %copy-start.8 = (bf16[7,32,16]{2,1,0:T(8,128)(2,1)}, bf16[7,32,16]{2,1,0:T(8,128)(2,1)S(1)}, u32[]{:S(2)}) copy-start(bf16[7,32,16]{2,1,0:T(8,128)(2,1)S(1)} %get-tuple-element.89.gram_ref.refs_20_) | copy-start | bytes 21508
  110.8 116.2 %all-gather.7.cloned.1.call-start = ((), (), s32[]{:S(2)}) async-start(), calls=%async_computation.5 | async-start | bytes 2359296 | tf_op jit(solution)/shard_map/all_gather | solution.py:1865
  112.4 48.1 %copy-start.20 = (s32[2]{0:T(128)S(1)}, s32[2]{0:T(128)}, u32[]{:S(2)}) copy-start(s32[2]{0:T(128)} %param.41) | copy-start | bytes 28
  159.8 8.3 %copy-start = (f32[1,5120]{1,0:T(1,128)S(1)}, f32[1,5120]{1,0:T(1,128)}, u32[]{:S(2)}) copy-start(f32[1,5120]{1,0:T(1,128)} %get-tuple-element.102.n_ref.n_attn) | copy-start | bytes 61444
  159.8 8.3 %copy-start.3 = (f32[2,2048]{1,0:T(2,128)S(1)}, f32[2,2048]{1,0:T(2,128)}, u32[]{:S(2)}) copy-start(f32[2,2048]{1,0:T(2,128)} %gain_ref.7) | copy-start | bytes 49156
  159.9 181.8 %reduce-scatter.3.cloned.1.call-start = ((), (), s32[]{:S(2)}) async-start(), calls=%async_computation.2 | async-start | bytes 2359296 | tf_op jit(solution)/shard_map/reduce_scatter | solution.py:1883
  291.8 90.0 %reduce-scatter.5.cloned.1.call-start = ((), (), s32[]{:S(2)}) async-start(), calls=%async_computation.3 | async-start | bytes 2359296 | tf_op jit(solution)/shard_map/reduce_scatter | solution.py:1895
  301.8 10.2 %copy-start.4 = (f32[2,16,1024]{2,1,0:T(8,128)S(1)}, f32[2,16,1024]{2,1,0:T(8,128)}, u32[]{:S(2)}) copy-start(f32[2,16,1024]{2,1,0:T(8,128)} %get-tuple-element.121.gb_gu) | copy-start | bytes 393220
  301.8 10.2 %copy-start.7 = (f32[16,1024]{1,0:T(8,128)S(1)}, f32[16,1024]{1,0:T(8,128)}, u32[]{:S(2)}) copy-start(f32[16,1024]{1,0:T(8,128)} %get-tuple-element.124.ga_d) | copy-start | bytes 196612
  301.8 10.2 %copy-start.13 = (f32[2,1,1024]{2,1,0:T(1,128)S(1)}, f32[2,1,1024]{2,1,0:T(1,128)}, u32[]{:S(2)}) copy-start(f32[2,1,1024]{2,1,0:T(1,128)} %get-tuple-element.122.gm_gu) | copy-start | bytes 24580
  301.8 10.2 %copy-start.14 = (f32[2,1,1024]{2,1,0:T(1,128)S(1)}, f32[2,1,1024]{2,1,0:T(1,128)}, u32[]{:S(2)}) copy-start(f32[2,1,1024]{2,1,0:T(1,128)} %get-tuple-element.123.n_gu) | copy-start | bytes 24580
  341.7 12.6 %copy-start.1 = (f32[2,16,2048]{2,1,0:T(8,128)S(1)}, f32[2,16,2048]{2,1,0:T(8,128)}, u32[]{:S(2)}) copy-start(f32[2,16,2048]{2,1,0:T(8,128)} %get-tuple-element.135.ga_gu) | copy-start | bytes 786436
  341.7 12.5 %copy-start.5 = (f32[16,2048]{1,0:T(8,128)S(1)}, f32[16,2048]{1,0:T(8,128)}, u32[]{:S(2)}) copy-start(f32[16,2048]{1,0:T(8,128)} %get-tuple-element.136.gb_d) | copy-start | bytes 393220
  341.7 12.5 %copy-start.11 = (f32[1,2048]{1,0:T(1,128)S(1)}, f32[1,2048]{1,0:T(1,128)}, u32[]{:S(2)}) copy-start(f32[1,2048]{1,0:T(1,128)} %get-tuple-element.139.gm_d) | copy-start | bytes 24580
  341.7 40.1 %copy-start.6 = (f32[2,8192]{1,0:T(2,128)S(1)}, f32[2,8192]{1,0:T(2,128)}, u32[]{:S(2)}) copy-start(f32[2,8192]{1,0:T(2,128)} %m_gu.1) | copy-start | bytes 196612
  341.7 40.1 %copy-start.9 = (f32[2048]{0:T(1024)S(1)}, f32[2048]{0:T(1024)}, u32[]{:S(2)}) copy-start(f32[2048]{0:T(1024)} %param.39) | copy-start | bytes 24580
  341.7 40.1 %copy-start.10 = (f32[1,2048]{1,0:T(1,128)S(1)}, f32[1,2048]{1,0:T(1,128)}, u32[]{:S(2)}) copy-start(f32[1,2048]{1,0:T(1,128)} %get-tuple-element.143.n_d) | copy-start | bytes 24580
Sparse Core Ops, SparseCore 0:
  110.9 35.9 all-gather.4
  160.0 30.2 all-gather.6
  291.9 36.9 reduce-scatter.2
  341.8 38.1 reduce-scatter.4
